TPU v7x, 32 devices: a whole 2x2x4 slice. The times are simulated.
32 devices in a mesh: copies: 2 (over y), grid: 4 (over z), slab: 4 (over x, core).
Axes of the slice: x: 2, y: 2, z: 4, core: 2. Of those that a mesh axis runs over, the one named last changes fastest.
Arguments:
- field: float32 [8, 128, 64, 128], P(('copies', 'grid'), 'slab'), parts along dimension 0, may hold values from -6 to 6
- levels: int32 [8, 5], P(('copies', 'grid')), parts along dimension 0, may hold values from 1 to 3
- owner: int32 [256], P('copies'), parts along dimension 0, may hold values from 0 to 127, each once
Outputs:
- combined: float32 [256, 64, 128], P(('copies', 'grid'), 'slab'), parts along dimension 0
There are 2 independent parts, one for each index of `copies`. A program takes and returns all parts, laid end to end along the dimension named above; each array names one. Nothing has to cross between parts.
All inputs are finite; a program needn't handle non-finite values.
Results may differ from a plain program's by a relative error of at most 0.0003.
Values sent between devices are 32-bit elements; how exact they have to be, the bound alone decides.
No kernel may reach another device: no remote copies, remote signals or barrier semaphores. Data moves between devices by JAX's collectives and lax.ppermute only.
A program may use at most 64 MiB of HBM per device.

v0:
```python
import math

import jax
import jax.numpy as jnp
import numpy as np
from jax import lax
from jax.sharding import PartitionSpec as P

N0 = 128
N1 = 2
N2 = 8
N3 = 4
N4 = 128
STEPS = 4
Q = 64


ADVECT = 0.08
DIFFUSE = 0.03


def extended_2(value, sides, width):
    for axis, dim in sides:
        count, length = (lax.axis_size(axis), value.shape[dim])
        up = [(i, (i + 1) % count) for i in range(count)]
        down = [(j, i) for i, j in up]
        last = lax.slice_in_dim(value, length - width, length, axis=dim)
        first = lax.slice_in_dim(value, 0, width, axis=dim)
        before = lax.ppermute(last, axis, up)
        after = lax.ppermute(first, axis, down)
        value = jnp.concatenate([before, value, after], axis=dim)
    return value


def build_tables(count):
    depth = count.bit_length() - 1
    matrix = np.eye(count)
    inverse = np.zeros((count, count))
    inverse[0, 0] = 1.0
    level_rows = np.zeros(count, np.int32)
    for index in range(1, count):
        zeros = (index & -index).bit_length() - 1
        spacing = 1 << zeros
        matrix[index, index - spacing] -= 0.5
        matrix[index, (index + spacing) % count] -= 0.5
        level_rows[index] = depth - zeros
    for zeros in range(depth - 1, -1, -1):
        spacing = 1 << zeros
        for index in range(spacing, count, 2 * spacing):
            inverse[index] = 0.5 * (inverse[index - spacing] + inverse[(index + spacing) % count])
            inverse[index, index] += 1.0
    return (matrix.astype(np.float32), inverse.astype(np.float32), level_rows)


def advance(extended, scales, padded):
    length = extended.shape[padded] - 2
    centre = lax.slice_in_dim(extended, 1, length + 1, axis=padded)
    speed = 1.0 + 0.5 * jnp.tanh(centre)
    change = jnp.zeros_like(centre)
    for axis in range(5):
        if axis == padded:
            back = lax.slice_in_dim(extended, 0, length, axis=padded)
            ahead = lax.slice_in_dim(extended, 2, length + 2, axis=padded)
        else:
            back = jnp.roll(centre, 1, axis)
            ahead = jnp.roll(centre, -1, axis)
        change = (
            change
            - ADVECT * scales[axis] * speed * (centre - back)
            + DIFFUSE * scales[axis] ** 2 * (ahead - 2.0 * centre + back)
        )
    return centre + change


def regroup_rows(stepped):
    return lax.all_to_all(stepped, "slab", split_axis=1, concat_axis=0, tiled=True)


def local(field, levels, owner):
    matrix, inverse, level_rows = build_tables(N0)
    matrix = jnp.asarray(matrix)
    inverse = jnp.asarray(inverse)
    depth = N0.bit_length() - 1
    level_vec = levels[0]
    scales = jnp.exp2(level_vec.astype(jnp.float32)) / 8.0
    weight = jnp.where(jnp.sum(level_vec) % 2 == 0, 1.0, -1.0).astype(jnp.float32) / math.sqrt(
        lax.axis_size("grid")
    )
    keep = (jnp.asarray(level_rows) <= depth - 3 + level_vec[0]).astype(jnp.float32)[:, None, None]

    def evolve_rows(state):
        rows = state.shape[0]
        grid5 = state.reshape(rows, N1, N2, N3, N4)
        for step in range(STEPS):
            extended = extended_2(grid5, (("slab", 0),), 1)
            grid5 = advance(extended, scales, 0)
        return grid5.reshape(rows, Q, N4)

    def hierarchise(whole):
        hier = jnp.dot(matrix, whole.reshape(N0, -1), precision=lax.Precision.HIGHEST)
        return weight * keep * hier.reshape(whole.shape)

    def reduce_terms(terms):
        return lax.psum_scatter(terms[owner], "grid", scatter_dimension=0, tiled=True)

    stepped = evolve_rows(field[0])
    summed = reduce_terms(hierarchise(regroup_rows(stepped)))
    ordered = lax.all_gather(summed, "grid", axis=0, tiled=True)
    position = jnp.zeros((N0,), jnp.int32).at[owner].set(jnp.arange(N0, dtype=jnp.int32))
    combined = ordered[position]
    masked = (keep * combined).reshape(N0, -1)
    nodal = jnp.dot(inverse, masked, precision=lax.Precision.HIGHEST).reshape(combined.shape)
    state = lax.all_to_all(nodal, "slab", split_axis=0, concat_axis=1, tiled=True)
    stepped = evolve_rows(state)
    summed = reduce_terms(hierarchise(regroup_rows(stepped)))
    return summed


def solution(mesh):
    in_specs = (P(("copies", "grid"), "slab", None, None), P(("copies", "grid"), None), P("copies"))
    out_specs = P(("copies", "grid"), "slab", None)
    return jax.shard_map(local, mesh=mesh, in_specs=in_specs, out_specs=out_specs, check_vma=False)
```

profile of v0, /device:TPU:0, one launch (start us, length us, event | category | flops | bytes accessed | tf_op | source)
XLA Modules:
  0.0 231.8 jit_solution(14325692422374188094)
XLA Ops:
  6.5 0.8 fusion.255
  7.3 2.4 %collective-permute-start.1 = (f32[1,2,8,4,128]{4,0,3,2,1:T(1,128)S(1)}, f32[1,2,8,4,128]{4,0,3,2,1:T(1,128)S(1)}, u32[]{:S(2)}, u32[]{:S(2)}) collective-permute-start(f32[1,2,8,4,128]{4,0,3,2,1:T(1,128)S(1)} %bitcast.80), channel_id=1, source_target_pairs={{1,0},{2,1},{3,2},{0,3},{5,4},{6,5},{7,6},{4,7},{9,8},{10,9},{11,1... | collective-permute-start | bytes 98312 | tf_op jit(solution)/shard_map/ppermute | solution.py:30
  9.7 1.8 copy.37
  12.1 0.4 fusion.253
  12.5 0.4 fusion.254
  12.9 0.6 copy-done.3
  13.5 0.7 fusion.256
  23.8 2.3 %fusion.8 = f32[32,2,8,4,128]{4,0,3,2,1:T(8,128)S(1)} fusion(f32[32,2,8,4,128]{4,0,3,2,1:T(8,128)S(1)} %copy.37, f32[1,2,8,4,128]{4,0,3,2,1:T(1,128)S(1)} %collective-permute-done.1, f32[1,2,8,4,128]{4,0,3,2,1:T(1,128)S(1)} %collective-permute-done, f32[32,2,1,4,128]{4,0,3,2,1:T(8,128)S(1)} %get-tuple-element.120, ...), kind=kLoop, calls=%fused_computation.23 | loop fusion | flops 13893632 | bytes 9502760 | tf_op jit(solution)/shard_map/add | solution.py:72
  26.7 0.4 fusion.245
  27.1 0.4 fusion.246
  27.6 1.8 collective-permute-start.3
  29.4 1.7 collective-permute-done.3
  31.1 1.6 collective-permute-done.2
  32.7 2.3 fusion.17
  35.5 0.4 fusion.237
  35.9 0.4 fusion.238
  36.4 0.7 collective-permute-start.5
  37.1 1.6 collective-permute-done.5
  38.7 1.7 collective-permute-done.4
  40.4 2.3 fusion.26
  43.2 0.4 fusion.229
  43.6 0.4 fusion.230
  44.7 1.3 collective-permute-done.7
  46.0 1.7 collective-permute-done.6
  47.8 3.1 %fusion.35 = f32[32,2,8,4,128]{4,0,3,2,1:T(8,128)} fusion(f32[32,2,8,4,128]{4,0,3,2,1:T(8,128)S(1)} %fusion.26, f32[1,2,8,4,128]{4,0,3,2,1:T(1,128)S(1)} %collective-permute-done.7, f32[1,2,8,4,128]{4,0,3,2,1:T(1,128)S(1)} %collective-permute-done.6, f32[32,2,1,4,128]{4,0,3,2,1:T(8,128)S(1)} %get-tuple-element.72, ...), kind=kLoop, calls=%fused_computation.50 | loop fusion | flops 13893632 | bytes 9502760 | tf_op jit(solution)/shard_map/add | solution.py:72
  50.8 3.5 %all-to-all-start = ((f32[32,64,128]{2,0,1:T(8,128)}), f32[32,64,128]{2,0,1:T(8,128)S(1)}, u32[]{:S(2)}, u32[]{:S(2)}) async-start(f32[32,64,128]{2,0,1:T(8,128)} %bitcast.16), calls=%async_computation | async-start | bytes 2097152 | tf_op jit(solution)/shard_map/all_to_all | solution.py:76
  54.6 0.6 reduce_sum.9
  57.2 0.6 copy-done.4
  57.8 0.6 copy-done.2
  58.5 10.3 %all-to-all-done = f32[32,64,128]{2,0,1:T(8,128)S(1)} async-done(((f32[32,64,128]{2,0,1:T(8,128)}), f32[32,64,128]{2,0,1:T(8,128)S(1)}, u32[]{:S(2)}, u32[]{:S(2)}) %all-to-all-start) | async-done | bytes 1048608 | tf_op jit(solution)/shard_map/all_to_all | solution.py:76
  68.8 0.6 copy.39
  69.6 1.3 convolution_bitcast_fusion.2
  71.3 1.7 gather_fusion
  73.1 27.7 %reduce-scatter.3.cloned.1.call-done = f32[32,16,128]{2,1,0:T(8,128)} async-done(((f32[128,16,128]{2,1,0:T(8,128)}), f32[32,16,128]{2,1,0:T(8,128)}) %reduce-scatter.3.cloned.1.call-update) | async-done | bytes 262160 | tf_op jit(solution)/shard_map/reduce_scatter | solution.py:104
  100.9 1.0 scatter_custom_fusion
  102.0 27.0 %all-gather.2.cloned.1.call-done = f32[128,16,128]{2,1,0:T(8,128)} async-done(((f32[32,16,128]{2,1,0:T(8,128)}), f32[128,16,128]{2,1,0:T(8,128)}) %all-gather.2.cloned.1.call-update) | async-done | bytes 1048592 | tf_op jit(solution)/shard_map/all_gather | solution.py:108
  128.9 1.9 gather_fusion.1
  130.8 1.3 convolution_bitcast_fusion.1
  132.3 17.0 %all_to_all.45 = f32[128,16,128]{2,1,0:T(8,128)S(1)} all-to-all(f32[128,16,128]{2,1,0:T(8,128)S(1)} %bitcast.75), channel_id=1, replica_groups=mesh['copies'=2,'grid'=4,'slab'=4] {'slab'}, dimensions={0} | all-to-all | bytes 2097152 | tf_op jit(solution)/shard_map/all_to_all | solution.py:113
  150.1 0.4 fusion.221
  151.0 0.5 collective-permute-start.8
  151.5 1.1 collective-permute-done.9
  152.6 1.8 collective-permute-done.8
  154.4 2.3 fusion.44
  157.3 0.4 fusion.213
  158.2 0.5 collective-permute-start.10
  158.7 1.1 collective-permute-done.11
  159.8 1.8 collective-permute-done.10
  161.6 2.3 fusion.53
  164.4 0.4 fusion.205
  165.4 0.5 collective-permute-start.12
  165.9 1.1 collective-permute-done.13
  166.9 2.0 collective-permute-done.12
  169.0 2.3 fusion.62
  171.8 0.4 fusion.197
  172.7 0.5 collective-permute-start.14
  173.3 1.1 collective-permute-done.15
  174.3 1.8 collective-permute-done.14
  176.1 2.3 fusion.71
  178.4 16.9 %all_to_all.46 = f32[32,64,128]{2,0,1:T(8,128)S(1)} all-to-all(f32[32,64,128]{2,0,1:T(8,128)S(1)} %bitcast.77), channel_id=1, replica_groups=mesh['copies'=2,'grid'=4,'slab'=4] {'slab'}, dimensions={1} | all-to-all | bytes 2097152 | tf_op jit(solution)/shard_map/all_to_all | solution.py:76
  195.3 0.6 copy.42
  195.9 1.3 convolution_bitcast_fusion
  197.6 1.7 gather_fusion.2
  199.3 25.9 %reduce-scatter.5.cloned.1.call-done = f32[32,16,128]{2,1,0:T(8,128)} async-done(((f32[128,16,128]{2,1,0:T(8,128)}), f32[32,16,128]{2,1,0:T(8,128)}) %reduce-scatter.5.cloned.1.call-update) | async-done | bytes 262160 | tf_op jit(solution)/shard_map/reduce_scatter | solution.py:104
  (89 shorter events, 9.1 us)
Async XLA Ops:
  7.3 16.5 %collective-permute-start.1 = (f32[1,2,8,4,128]{4,0,3,2,1:T(1,128)S(1)}, f32[1,2,8,4,128]{4,0,3,2,1:T(1,128)S(1)}, u32[]{:S(2)}, u32[]{:S(2)}) collective-permute-start(f32[1,2,8,4,128]{4,0,3,2,1:T(1,128)S(1)} %bitcast.80), channel_id=1, source_target_pairs={{1,0},{2,1},{3,2},{0,3},{5,4},{6,5},{7,6},{4,7},{9,8},{10,9},{11,1... | collective-permute-start | bytes 98312 | tf_op jit(solution)/shard_map/ppermute | solution.py:30
  9.7 14.1 %collective-permute-start = (f32[1,2,8,4,128]{4,0,3,2,1:T(1,128)S(1)}, f32[1,2,8,4,128]{4,0,3,2,1:T(1,128)S(1)}, u32[]{:S(2)}, u32[]{:S(2)}) collective-permute-start(f32[1,2,8,4,128]{4,0,3,2,1:T(1,128)S(1)} %bitcast.79), channel_id=1, source_target_pairs={{0,1},{1,2},{2,3},{3,0},{4,5},{5,6},{6,7},{7,4},{8,9},{9,10},{10,1... | collective-permute-start | bytes 98312 | tf_op jit(solution)/shard_map/ppermute | solution.py:29
  12.8 0.7 copy-start.3
  27.6 3.5 %collective-permute-start.3 = (f32[1,2,8,4,128]{4,0,3,2,1:T(1,128)S(1)}, f32[1,2,8,4,128]{4,0,3,2,1:T(1,128)S(1)}, u32[]{:S(2)}, u32[]{:S(2)}) collective-permute-start(f32[1,2,8,4,128]{4,0,3,2,1:T(1,128)S(1)} %get-tuple-element.116), channel_id=1, source_target_pairs={{1,0},{2,1},{3,2},{0,3},{5,4},{6,5},{7,6},{4,7},{9,8},{10,9},{11,1... | collective-permute-start | bytes 98312 | tf_op jit(solution)/shard_map/ppermute | solution.py:30
  29.4 3.3 %collective-permute-start.2 = (f32[1,2,8,4,128]{4,0,3,2,1:T(1,128)S(1)}, f32[1,2,8,4,128]{4,0,3,2,1:T(1,128)S(1)}, u32[]{:S(2)}, u32[]{:S(2)}) collective-permute-start(f32[1,2,8,4,128]{4,0,3,2,1:T(1,128)S(1)} %get-tuple-element.115), channel_id=1, source_target_pairs={{0,1},{1,2},{2,3},{3,0},{4,5},{5,6},{6,7},{7,4},{8,9},{9,10},{10,1... | collective-permute-start | bytes 98312 | tf_op jit(solution)/shard_map/ppermute | solution.py:29
  36.4 2.3 collective-permute-start.5
  37.1 3.3 %collective-permute-start.4 = (f32[1,2,8,4,128]{4,0,3,2,1:T(1,128)S(1)}, f32[1,2,8,4,128]{4,0,3,2,1:T(1,128)S(1)}, u32[]{:S(2)}, u32[]{:S(2)}) collective-permute-start(f32[1,2,8,4,128]{4,0,3,2,1:T(1,128)S(1)} %get-tuple-element.99), channel_id=1, source_target_pairs={{0,1},{1,2},{2,3},{3,0},{4,5},{5,6},{6,7},{7,4},{8,9},{9,10},{10,1... | collective-permute-start | bytes 98312 | tf_op jit(solution)/shard_map/ppermute | solution.py:29
  44.1 1.9 collective-permute-start.7
  44.4 3.3 %collective-permute-start.6 = (f32[1,2,8,4,128]{4,0,3,2,1:T(1,128)S(1)}, f32[1,2,8,4,128]{4,0,3,2,1:T(1,128)S(1)}, u32[]{:S(2)}, u32[]{:S(2)}) collective-permute-start(f32[1,2,8,4,128]{4,0,3,2,1:T(1,128)S(1)} %get-tuple-element.83), channel_id=1, source_target_pairs={{0,1},{1,2},{2,3},{3,0},{4,5},{5,6},{6,7},{7,4},{8,9},{9,10},{10,1... | collective-permute-start | bytes 98312 | tf_op jit(solution)/shard_map/ppermute | solution.py:29
  50.8 17.9 %all-to-all-start = ((f32[32,64,128]{2,0,1:T(8,128)}), f32[32,64,128]{2,0,1:T(8,128)S(1)}, u32[]{:S(2)}, u32[]{:S(2)}) async-start(f32[32,64,128]{2,0,1:T(8,128)} %bitcast.16), calls=%async_computation | async-start | bytes 2097152 | tf_op jit(solution)/shard_map/all_to_all | solution.py:76
  54.4 46.5 %reduce-scatter.3.cloned.1.call-start = ((), (), s32[]{:S(2)}) async-start(), calls=%async_computation.5 | async-start | bytes 1310720 | tf_op jit(solution)/shard_map/reduce_scatter | solution.py:104
  57.1 0.7 copy-start.4
  57.8 0.7 copy-start.2
  68.8 0.8 copy-start
  73.1 55.9 %all-gather.2.cloned.1.call-start = ((), (), s32[]{:S(2)}) async-start(), calls=%async_computation.6 | async-start | bytes 1310720 | tf_op jit(solution)/shard_map/all_gather | solution.py:108
  100.9 124.4 %reduce-scatter.5.cloned.1.call-start = ((), (), s32[]{:S(2)}) async-start(), calls=%async_computation.7 | async-start | bytes 1310720 | tf_op jit(solution)/shard_map/reduce_scatter | solution.py:104
  101.9 28.8 %copy-start.1 = (f32[128,128]{1,0:T(8,128)S(1)}, f32[128,128]{1,0:T(8,128)}, u32[]{:S(2)}) copy-start(f32[128,128]{1,0:T(8,128)} %constant.60.clone) | copy-start | bytes 196612
  151.0 1.7 collective-permute-start.9
  151.0 3.4 %collective-permute-start.8 = (f32[1,2,8,4,128]{4,0,3,2,1:T(1,128)S(1)}, f32[1,2,8,4,128]{4,0,3,2,1:T(1,128)S(1)}, u32[]{:S(2)}, u32[]{:S(2)}) collective-permute-start(f32[1,2,8,4,128]{4,0,3,2,1:T(1,128)S(1)} %bitcast.81), channel_id=1, source_target_pairs={{0,1},{1,2},{2,3},{3,0},{4,5},{5,6},{6,7},{7,4},{8,9},{9,10},{10,1... | collective-permute-start | bytes 98312 | tf_op jit(solution)/shard_map/ppermute | solution.py:29
  158.1 1.7 collective-permute-start.11
  158.2 3.4 %collective-permute-start.10 = (f32[1,2,8,4,128]{4,0,3,2,1:T(1,128)S(1)}, f32[1,2,8,4,128]{4,0,3,2,1:T(1,128)S(1)}, u32[]{:S(2)}, u32[]{:S(2)}) collective-permute-start(f32[1,2,8,4,128]{4,0,3,2,1:T(1,128)S(1)} %get-tuple-element.51), channel_id=1, source_target_pairs={{0,1},{1,2},{2,3},{3,0},{4,5},{5,6},{6,7},{7,4},{8,9},{9,10},{10,1... | collective-permute-start | bytes 98312 | tf_op jit(solution)/shard_map/ppermute | solution.py:29
  165.3 1.7 collective-permute-start.13
  165.4 3.6 %collective-permute-start.12 = (f32[1,2,8,4,128]{4,0,3,2,1:T(1,128)S(1)}, f32[1,2,8,4,128]{4,0,3,2,1:T(1,128)S(1)}, u32[]{:S(2)}, u32[]{:S(2)}) collective-permute-start(f32[1,2,8,4,128]{4,0,3,2,1:T(1,128)S(1)} %get-tuple-element.35), channel_id=1, source_target_pairs={{0,1},{1,2},{2,3},{3,0},{4,5},{5,6},{6,7},{7,4},{8,9},{9,10},{10,1... | collective-permute-start | bytes 98312 | tf_op jit(solution)/shard_map/ppermute | solution.py:29
  172.7 1.7 collective-permute-start.15
  172.7 3.4 %collective-permute-start.14 = (f32[1,2,8,4,128]{4,0,3,2,1:T(1,128)S(1)}, f32[1,2,8,4,128]{4,0,3,2,1:T(1,128)S(1)}, u32[]{:S(2)}, u32[]{:S(2)}) collective-permute-start(f32[1,2,8,4,128]{4,0,3,2,1:T(1,128)S(1)} %get-tuple-element.19), channel_id=1, source_target_pairs={{0,1},{1,2},{2,3},{3,0},{4,5},{5,6},{6,7},{7,4},{8,9},{9,10},{10,1... | collective-permute-start | bytes 98312 | tf_op jit(solution)/shard_map/ppermute | solution.py:29
Sparse Core Ops, SparseCore 0:
  73.2 27.6 reduce-scatter.2
  102.4 26.4 all-gather.1
  199.5 25.7 reduce-scatter.4
where the time goes:
time: 232 us
  waiting for transfers between devices  112 us (48%)
  blocking collectives  33.8 us (15%)
  between operations  25.4 us (11%)
  local copies, waits for them, and re-layouts  24.6 us (11%)
  other arithmetic  20.2 us (9%)
  starting transfers between devices  11.5 us (5%)
  matrix products  3.88 us (2%)
    reduce_scatter x2, waiting for transfers between devices, reduce_terms(): lax.psum_scatter(terms[owner], 'grid', scatter_dimension=0, tiled=True)  53.7 us
    all_gather x1, waiting for transfers between devices, local(): ordered = lax.all_gather(summed, 'grid', axis=0, tiled=True)  27 us
    add x8, other arithmetic, advance(): return centre + change  19.2 us
    all_to_all x1, blocking collectives, local(): lax.all_to_all(nodal, 'slab', split_axis=0, concat_axis=1, tiled=True)  17 us
    all_to_all x1, blocking collectives, regroup_rows(): lax.all_to_all(stepped, 'slab', split_axis=1, concat_axis=0, tiled=True)  16.9 us
    ppermute x8, waiting for transfers between devices, extended_2(): before = lax.ppermute(last, axis, up)  12.5 us
    slice x56, local copies, waits for them, and re-layouts, advance(): back = jnp.roll(centre, 1, axis)  10.6 us
    all_to_all x1, waiting for transfers between devices, regroup_rows(): lax.all_to_all(stepped, 'slab', split_axis=1, concat_axis=0, tiled=True)  10.3 us
  transfers between devices with their start and end apart: 20, of which 18 were waited for; matrix products, arithmetic and copies ran while one was open for 2% of the time, Pallas kernels for 0%

commit v1 on v0

--- a/solution.py
+++ b/solution.py
@@ -1,9 +1,12 @@
+import functools
 import math
 
 import jax
 import jax.numpy as jnp
 import numpy as np
 from jax import lax
+from jax.experimental import pallas as pl
+from jax.experimental.pallas import tpu as pltpu
 from jax.sharding import PartitionSpec as P
 
 N0 = 128
@@ -14,9 +17,12 @@
 STEPS = 4
 Q = 64
 
-
 ADVECT = 0.08
 DIFFUSE = 0.03
+
+LOW = STEPS
+HIGH = STEPS + 1
+TILES = N1 * N3
 
 
 def extended_2(value, sides, width):
@@ -76,7 +82,7 @@
     return lax.all_to_all(stepped, "slab", split_axis=1, concat_axis=0, tiled=True)
 
 
-def local(field, levels, owner):
+def local_general(field, levels, owner):
     matrix, inverse, level_rows = build_tables(N0)
     matrix = jnp.asarray(matrix)
     inverse = jnp.asarray(inverse)
@@ -116,6 +122,285 @@
     return summed
 
 
+def step_rows(src, dst, first, groups, unroll, get):
+    advect, spread, centre_spread, centre_advect = get
+
+    def body(group, carry):
+        base = first + group * unroll
+        for offset in range(unroll):
+            row = base + offset
+            tiles = [src[row, t] for t in range(TILES)]
+            for n1 in range(N1):
+                for n3 in range(N3):
+                    t = n1 * N3 + n3
+                    u = tiles[t]
+                    neighbours = (
+                        (src[row - 1, t], src[row + 1, t]),
+                        (tiles[(1 - n1) * N3 + n3], None),
+                        (pltpu.roll(u, 1, 0), pltpu.roll(u, N2 - 1, 0)),
+                        (tiles[n1 * N3 + (n3 - 1) % N3], tiles[n1 * N3 + (n3 + 1) % N3]),
+                        (pltpu.roll(u, 1, 1), pltpu.roll(u, N4 - 1, 1)),
+                    )
+                    drift = -centre_advect * u
+                    update = centre_spread * u
+                    for d, (back, ahead) in enumerate(neighbours):
+                        drift = drift + advect[d] * back
+                        if ahead is None:
+                            update = update + (spread[d] + spread[d]) * back
+                        else:
+                            update = update + spread[d] * (back + ahead)
+                    dst[row, t] = update + (2.0 + jnp.tanh(u)) * drift
+        return carry
+
+    lax.fori_loop(0, groups, body, 0)
+
+
+def coefficients(coef, g):
+    advect = [coef[g, d] for d in range(5)]
+    spread = [coef[g, 5 + d] for d in range(5)]
+    return advect, spread, coef[g, 10], coef[g, 11]
+
+
+def interpolate(nodes, level):
+    u0, u1, u2, u3, u4 = nodes
+    fine, middle = level >= 3, level >= 2
+    v2 = jnp.where(middle, u2, 0.5 * (u0 + u4))
+    v1 = jnp.where(fine, u1, 0.5 * (u0 + v2))
+    v3 = jnp.where(fine, u3, 0.5 * (v2 + u4))
+    return u0, v1, v2, v3
+
+
+def padded_rows(rows, unroll):
+    return rows + LOW + HIGH + unroll
+
+
+def run_steps(bufs, rows, unroll, get):
+    for step in range(STEPS):
+        count = rows + LOW + HIGH - 2 * (step + 1)
+        step_rows(bufs[step % 2], bufs[(step + 1) % 2], step + 1, -(-count // unroll), unroll, get)
+    return bufs[STEPS % 2]
+
+
+def first_kernel(rows, pieces, unroll, coef, level, order, before, field, after, *rest):
+    outs, bufs = rest[:pieces], rest[pieces:]
+    start = bufs[0]
+
+    def load(ref, at):
+        def body(i, carry):
+            for n1 in range(N1):
+                for n3 in range(N3):
+                    start[at + i, n1 * N3 + n3] = ref[i, pl.ds(n1 * N2 * N3 + n3, N2, stride=N3), :]
+            return carry
+
+        lax.fori_loop(0, ref.shape[0], body, 0)
+
+    load(before, 0)
+    load(field, LOW)
+    load(after, LOW + rows)
+    done = run_steps(bufs, rows, unroll, coefficients(coef, 0))
+    weight = coef[0, 12]
+    piece = rows // pieces
+    for j, out in enumerate(outs):
+        for quad in range(0, piece, 4):
+            base = LOW + order[j] * piece + quad
+            for t in range(TILES):
+                values = interpolate([done[base + i, t] for i in range(5)], level[0])
+                for i, value in enumerate(values):
+                    out[quad + i, t] = weight * value
+
+
+def second_kernel(rows, grids, unroll, coef, level, before, own, after, out, total, wide, *bufs):
+    extent = rows + LOW + HIGH
+    wide[0:LOW] = before[...]
+    wide[LOW : LOW + rows] = own[...]
+    wide[LOW + rows : extent] = after[...]
+    for g in range(grids):
+        start = bufs[0]
+        for quad in range(0, extent - 1, 4):
+            for t in range(TILES):
+                values = interpolate([wide[quad + i, t] for i in range(5)], level[g])
+                for i, value in enumerate(values):
+                    start[quad + i, t] = value
+        start[extent - 1] = wide[extent - 1]
+        done = run_steps(bufs, rows, unroll, coefficients(coef, g))
+        weight = coef[g, 12]
+        for quad in range(0, rows, 4):
+            for t in range(TILES):
+                values = interpolate([done[LOW + quad + i, t] for i in range(5)], level[g])
+                for i, value in enumerate(values):
+                    at = pl.ds(((quad + i) * TILES + t) * N2, N2)
+                    total[at, :] = weight * value + (total[at, :] if g else 0.0)
+    half = N2 // 2
+    for n3 in range(N3):
+        for n1 in range(N1):
+            for n2 in range(N2):
+                at = (n3 * N1 + n1) * 2 + n2 // half
+                out[at, n2 % half] = total[pl.ds((n1 * N3 + n3) * N2 + n2, rows, stride=TILES * N2), :]
+
+
+def hier_kernel(groups, matrix, rows, out):
+    parts, lanes = rows.shape[1], rows.shape[3]
+    for n in range(parts):
+        whole = rows[:, n].reshape(matrix.shape[1], lanes)
+        hier = jnp.dot(matrix[...], whole, precision=lax.Precision.HIGHEST, preferred_element_type=jnp.float32)
+        out[:, n] = hier.reshape(groups, -1, lanes)
+
+
+def place_kernel(parts, received, out):
+    count = received.shape[2]
+    for n3 in range(received.shape[0]):
+        for n in range(parts):
+            q = n * N3 + n3
+            out[pl.ds(q, count, stride=parts * N3), :] = received[n3, n]
+
+
+VMEM = pl.BlockSpec(memory_space=pltpu.VMEM)
+SMEM = pl.BlockSpec(memory_space=pltpu.SMEM)
+
+
+def coefficient_table(levels):
+    scales = jnp.exp2(levels.astype(jnp.float32)) / 8.0
+    advect = 0.5 * ADVECT * scales
+    spread = DIFFUSE * scales**2
+    return advect, spread
+
+
+def table_of(levels, grids):
+    advect, spread = coefficient_table(levels)
+    weight = jnp.where(jnp.sum(levels, 1) % 2 == 0, 1.0, -1.0).astype(jnp.float32) / math.sqrt(grids)
+    centre_spread = 1.0 - 2.0 * jnp.sum(spread, 1)
+    centre_advect = jnp.sum(advect, 1)
+    return jnp.concatenate(
+        [advect, spread, centre_spread[:, None], centre_advect[:, None], weight[:, None]], axis=1
+    )
+
+
+def row_tile(rows):
+    return jax.ShapeDtypeStruct((rows, TILES, N2, N4), jnp.float32)
+
+
+def fast_sizes(grids, slabs):
+    rows = N0 // slabs
+    block = rows // grids
+    return rows, block
+
+
+def fast_fits(grids, slabs):
+    rows, block = fast_sizes(grids, slabs)
+    return grids == 4 and grids == N3 and slabs == 2 * N1 and block >= HIGH and block % 4 == 0
+
+
+def local_fast(field, levels, owner):
+    grids, slabs = lax.axis_size("grid"), lax.axis_size("slab")
+    rows, block = fast_sizes(grids, slabs)
+    me, at = lax.axis_index("grid"), lax.axis_index("slab")
+    state = field[0]
+
+    up = [(i, (i + 1) % slabs) for i in range(slabs)]
+    down = [(j, i) for i, j in up]
+    before = lax.ppermute(state[rows - LOW :], "slab", up)
+    after = lax.ppermute(state[:HIGH], "slab", down)
+
+    shift = lambda d: lax.ppermute(levels, "grid", [(i, (i + d) % grids) for i in range(grids)])
+    every = jnp.concatenate([levels] + [shift(d) for d in range(1, grids)], axis=0)
+
+    def block_of(g):
+        return jnp.where(at % 2 == 0, g, grids - 1 - g)
+
+    low = me < grids // 2
+    targets = jnp.stack(
+        [
+            block_of(jnp.where(low, 3, 0)),
+            block_of(jnp.where(low, 2, 1)),
+            block_of(jnp.where(low, 1, 2)),
+            block_of(jnp.where(low, 0, 3)),
+        ]
+    ).astype(jnp.int32)
+
+    unroll = 2
+    space = lambda r: pltpu.VMEM((padded_rows(r, unroll), TILES, N2, N4), jnp.float32)
+    far, middle, near, rear = pl.pallas_call(
+        functools.partial(first_kernel, rows, grids, unroll),
+        out_shape=[row_tile(block)] * grids,
+        in_specs=[SMEM, SMEM, SMEM, VMEM, VMEM, VMEM],
+        out_specs=[VMEM] * grids,
+        scratch_shapes=[space(rows), space(rows)],
+        name="first_cycle",
+    )(table_of(levels, grids), levels[:, 0], targets, before, state, after)
+
+    inwards, across, outwards = [(0, 1), (3, 2)], [(1, 2), (2, 1)], [(1, 0), (2, 3)]
+    a1 = lax.ppermute(far, "grid", inwards)
+    a2 = lax.ppermute(middle, "grid", inwards)
+    a3 = lax.ppermute(near, "grid", inwards)
+    b1 = lax.ppermute(a1 + far, "grid", across)
+    b2 = lax.ppermute(a2 + middle, "grid", across)
+    c1 = lax.ppermute(b1 + rear, "grid", outwards)
+    inner = (me == 1) | (me == 2)
+    own = jnp.where(inner, near + a3 + b2, rear + c1)
+
+    chain = []
+    for k in range(slabs):
+        chain += [(g if k % 2 == 0 else grids - 1 - g) * slabs + k for g in range(grids)]
+    forward = [(chain[i], chain[(i + 1) % len(chain)]) for i in range(len(chain))]
+    backward = [(j, i) for i, j in forward]
+    both = ("grid", "slab")
+    before = lax.ppermute(own[block - LOW :], both, forward)
+    after = lax.ppermute(own[:HIGH], both, backward)
+
+    half = N2 // 2
+    sent = pl.pallas_call(
+        functools.partial(second_kernel, block, grids, unroll),
+        out_shape=jax.ShapeDtypeStruct((N3 * N1 * 2, half, block, N4), jnp.float32),
+        in_specs=[SMEM, SMEM, VMEM, VMEM, VMEM],
+        out_specs=VMEM,
+        scratch_shapes=[
+            pltpu.VMEM((block * TILES * N2, N4), jnp.float32),
+            pltpu.VMEM((block + LOW + HIGH, TILES, N2, N4), jnp.float32),
+            space(block),
+            space(block),
+        ],
+        name="second_cycle",
+    )(table_of(every, grids), every[:, 0], before, own, after)
+
+    spread = lax.all_to_all(sent, both, split_axis=0, concat_axis=0, tiled=True)
+
+    source = np.zeros(N0, np.int32)
+    for place, device in enumerate(chain):
+        source[device * block : (device + 1) * block] = place * block + np.arange(block)
+    column = jnp.asarray(source)[None, :]
+    row = owner[:, None]
+    reach = jnp.where(row > 0, row & -row, 0)
+    part = jnp.where(row > 0, -0.5, 0.0)
+    matrix = (
+        (column == row).astype(jnp.float32)
+        + part * (column == row - reach)
+        + part * (column == (row + reach) % N0)
+    )
+    group = N0 // grids
+    hier = pl.pallas_call(
+        functools.partial(hier_kernel, grids),
+        out_shape=jax.ShapeDtypeStruct((grids, half, group, N4), jnp.float32),
+        in_specs=[VMEM, VMEM],
+        out_specs=VMEM,
+        name="hierarchise",
+    )(matrix, spread)
+    received = lax.all_to_all(hier, "grid", split_axis=0, concat_axis=0, tiled=True)
+    out = pl.pallas_call(
+        functools.partial(place_kernel, half),
+        out_shape=jax.ShapeDtypeStruct((group * half * N3, N4), jnp.float32),
+        in_specs=[VMEM],
+        out_specs=VMEM,
+        name="place",
+    )(received)
+    return out.reshape(group, Q // slabs, N4)
+
+
+def local(field, levels, owner):
+    if fast_fits(lax.axis_size("grid"), lax.axis_size("slab")):
+        return local_fast(field, levels, owner)
+    return local_general(field, levels, owner)
+
+
 def solution(mesh):
     in_specs = (P(("copies", "grid"), "slab", None, None), P(("copies", "grid"), None), P("copies"))
     out_specs = P(("copies", "grid"), "slab", None)

time: 232 us -> 112 us (0.48)
  waiting for transfers between devices: 112 us -> 25.6 us
  Pallas kernels: 0 us -> 28.1 us
  between operations: 25.4 us -> 2.64 us
  blocking collectives: 33.8 us -> 13.3 us
  starting transfers between devices: 11.5 us -> 28.3 us
  other arithmetic: 20.2 us -> 4.11 us
  local copies, waits for them, and re-layouts: 24.6 us -> 8.9 us
  matrix products: 3.88 us -> 0 us
    reduce_scatter x2 -> x0, waiting for transfers between devices: 53.7 us -> none  [reduce_terms(): lax.psum_scatter(terms[owner], 'grid', scatter_dimension=0, tiled=True)]
    pallas_call x0 -> x4, Pallas kernels: none -> 28.1 us  [the longest x1 13.2 us: local_fast(): pl.pallas_call(functools.partial(second_kernel, block, grids, unroll), ou...]
    all_gather x1 -> x0, waiting for transfers between devices: 27 us -> none  [local(): ordered = lax.all_gather(summed, 'grid', axis=0, tiled=True)]
    all_to_all x2 -> x1, blocking collectives: 33.8 us -> 13.3 us  [local_fast(): lax.all_to_all(hier, 'grid', split_axis=0, concat_axis=0, tiled=True)]
    add x8 -> x4, other arithmetic: 19.2 us -> 1.81 us  [the longest x1 0.98 us: local_fast(): b1 = lax.ppermute(a1 + far, 'grid', across)]
    ppermute x16 -> x13, starting transfers between devices: 7.64 us -> 22.8 us  [the longest x3 8.05 us: local_fast(): lax.ppermute(levels, 'grid', [(i, (i + d) % grids) for i in range(grids)])]
    slice x65 -> x5, local copies, waits for them, and re-layouts: 12.3 us -> 2.55 us  [the longest x1 0.93 us: local_fast(): after = lax.ppermute(state[:HIGH], 'slab', down)]
    gather x3 -> x0, local copies, waits for them, and re-layouts: 5.31 us -> none  [the longest x2 3.45 us: reduce_terms(): terms[owner]]
  transfers between devices with their start and end apart: 20 -> 14, of which waited for: 18 -> 6; matrix products, arithmetic and copies ran while one was open for 2% -> 7% of each run, Pallas kernels for 0% -> 0%
where the time goes in v1:
time: 112 us; the launch traced here: 111 us
  starting transfers between devices  28.3 us (25%)
  Pallas kernels  28.1 us (25%)
  waiting for transfers between devices  25.6 us (23%)
  blocking collectives  13.3 us (12%)
  local copies, waits for them, and re-layouts  8.9 us (8%)
  other arithmetic  4.11 us (4%)
  between operations  2.64 us (2%)
    all_to_all x1, blocking collectives, local_fast(): lax.all_to_all(hier, 'grid', split_axis=0, concat_axis=0, tiled=True)  13.3 us
    pallas_call x1, Pallas kernels, local_fast(): pl.pallas_call(functools.partial(second_kernel, block, grids, unroll), ou...  13.2 us
    pallas_call x1, Pallas kernels, local_fast(): pl.pallas_call(functools.partial(first_kernel, rows, grids, unroll), out_...  11 us
    all_to_all x1, waiting for transfers between devices, local_fast(): spread = lax.all_to_all(sent, both, split_axis=0, concat_axis=0, tiled=True)  8.56 us
    ppermute x3, starting transfers between devices, local_fast(): lax.ppermute(levels, 'grid', [(i, (i + d) % grids) for i in range(grids)])  8.05 us
    ppermute x1, waiting for transfers between devices, local_fast(): a1 = lax.ppermute(far, 'grid', inwards)  5.5 us
    all_to_all x1, starting transfers between devices, local_fast(): spread = lax.all_to_all(sent, both, split_axis=0, concat_axis=0, tiled=True)  5.46 us
    ppermute x1, waiting for transfers between devices, local_fast(): c1 = lax.ppermute(b1 + rear, 'grid', outwards)  4.93 us
  transfers between devices with their start and end apart: 14, of which 6 were waited for; matrix products, arithmetic and copies ran while one was open for 7% of the time, Pallas kernels for 0%

profile of v1, /device:TPU:0, one launch (start us, length us, event | category | flops | bytes accessed | tf_op | source)
XLA Modules:
  0.0 111.0 jit_solution(2577680866340185037)
XLA Ops:
  0.0 0.9 slice_bitcast_fusion
  0.9 0.0 copy-start.9
  0.9 2.5 %collective-permute-start.4 = (f32[5,64,128]{2,1,0:T(8,128)S(1)}, f32[5,64,128]{2,1,0:T(8,128)S(1)}, u32[]{:S(2)}, u32[]{:S(2)}) collective-permute-start(f32[5,64,128]{2,1,0:T(8,128)S(1)} %slice_bitcast_fusion), channel_id=1, source_target_pairs={{1,0},{2,1},{3,2},{0,3},{5,4},{6,5},{7,6},{4,7},{9,8},{10,9},{11,1... | collective-permute-start | bytes 491528 | tf_op jit(solution)/shard_map/ppermute | solution.py:302
  3.4 0.9 slice_bitcast_fusion.1
  4.3 0.1 collective-permute-start.3
  4.4 0.0 copy-done.9
  4.4 0.6 fusion.8
  5.0 0.6 reduce_sum.64
  8.1 1.3 %concatenate.11.coef = f32[1,13]{1,0:T(1,128)} concatenate(f32[1,5]{1,0:T(1,128)S(1)} %get-tuple-element.22, f32[1,5]{1,0:T(1,128)S(1)} %get-tuple-element.16, f32[1,1]{1,0:T(1,128)} %bitcast.3, f32[1,1]{1,0:T(1,128)} %bitcast.4, f32[1,1]{1,0:T(1,128)} %bitcast.6), dimensions={1} | concatenate | bytes 104 | tf_op jit(solution)/shard_map/concatenate | solution.py:273
  9.4 0.6 pad_add_fusion.1.order
  10.0 0.0 collective-permute-done.3.before
  10.0 0.0 collective-permute-done.4.after
  10.0 0.6 copy-done.8
  10.7 0.1 copy-done.6
  10.7 11.0 %first_cycle.1 = (f32[8,8,8,128]{3,2,1,0:T(8,128)}, f32[8,8,8,128]{3,2,1,0:T(8,128)}, f32[8,8,8,128]{3,2,1,0:T(8,128)}, f32[8,8,8,128]{3,2,1,0:T(8,128)}) custom-call(f32[1,13]{1,0:T(1,128)} %concatenate.11.coef, s32[1]{0:T(128)} %bitcast.21, s32[4]{0:T(128)} %pad_add_fusion.1.order, f32[4,64,128]{2,1,0:T(8,128)} %copy-done.8, f32[32,64,128]{2,1,0:T(8,128)} %bitcast.20, ...), custom_call_target="tpu_custom_call" | custom-call | tf_op jit(solution)/shard_map/first_cycle/pallas_call | solution.py:322
  21.7 3.5 %collective-permute-start.8 = (f32[8,8,8,128]{3,2,1,0:T(8,128)}, f32[8,8,8,128]{3,2,1,0:T(8,128)S(1)}, u32[]{:S(2)}, u32[]{:S(2)}) collective-permute-start(f32[8,8,8,128]{3,2,1,0:T(8,128)} %get-tuple-element.12), channel_id=1, source_target_pairs={{0,4},{12,8},{1,5},{13,9},{2,6},{14,10},{3,7},{15,11},{16,20},{28,... | collective-permute-start | bytes 786440 | tf_op jit(solution)/shard_map/ppermute | solution.py:332
  25.2 0.0 copy-start.10
  25.2 1.4 %collective-permute-start.6 = (f32[8,8,8,128]{3,2,1,0:T(8,128)}, f32[8,8,8,128]{3,2,1,0:T(8,128)S(1)}, u32[]{:S(2)}, u32[]{:S(2)}) collective-permute-start(f32[8,8,8,128]{3,2,1,0:T(8,128)} %get-tuple-element.10), channel_id=1, source_target_pairs={{0,4},{12,8},{1,5},{13,9},{2,6},{14,10},{3,7},{15,11},{16,20},{28,... | collective-permute-start | bytes 786440 | tf_op jit(solution)/shard_map/ppermute | solution.py:333
  26.7 5.5 %collective-permute-done.8 = f32[8,8,8,128]{3,2,1,0:T(8,128)S(1)} collective-permute-done((f32[8,8,8,128]{3,2,1,0:T(8,128)}, f32[8,8,8,128]{3,2,1,0:T(8,128)S(1)}, u32[]{:S(2)}, u32[]{:S(2)}) %collective-permute-start.8) | collective-permute-done | bytes 262176 | tf_op jit(solution)/shard_map/ppermute | solution.py:332
  32.2 1.0 add.71
  33.2 0.7 collective-permute-start.9
  33.9 0.0 copy-done.10
  33.9 5.2 %collective-permute-start = (s32[1,5]{1,0:T(1,128)S(1)}, s32[1,5]{1,0:T(1,128)S(1)}, u32[]{:S(2)}, u32[]{:S(2)}) collective-permute-start(s32[1,5]{1,0:T(1,128)S(1)} %copy-done.10), channel_id=1, source_target_pairs={{0,4},{4,8},{8,12},{12,0},{1,5},{5,9},{9,13},{13,1},{2,6},{6,10},{... | collective-permute-start | bytes 68 | tf_op jit(solution)/shard_map/ppermute | solution.py:304
  39.1 0.0 collective-permute-start.1
  39.1 2.8 %collective-permute-start.2 = (s32[1,5]{1,0:T(1,128)S(1)}, s32[1,5]{1,0:T(1,128)S(1)}, u32[]{:S(2)}, u32[]{:S(2)}) collective-permute-start(s32[1,5]{1,0:T(1,128)S(1)} %copy-done.10), channel_id=1, source_target_pairs={{0,12},{4,0},{8,4},{12,8},{1,13},{5,1},{9,5},{13,9},{2,14},{6,2},{... | collective-permute-start | bytes 68 | tf_op jit(solution)/shard_map/ppermute | solution.py:304
  41.9 0.0 collective-permute-done
  41.9 2.7 %collective-permute-done.1 = s32[1,5]{1,0:T(1,128)S(1)} collective-permute-done((s32[1,5]{1,0:T(1,128)S(1)}, s32[1,5]{1,0:T(1,128)S(1)}, u32[]{:S(2)}, u32[]{:S(2)}) %collective-permute-start.1) | collective-permute-done | bytes 52 | tf_op jit(solution)/shard_map/ppermute | solution.py:304
  44.6 0.0 collective-permute-done.2
  44.6 0.1 fusion.9
  44.8 0.1 copy.10
  44.9 0.0 copy-done.4
  44.9 2.7 %collective-permute-start.5 = (f32[8,8,8,128]{3,2,1,0:T(8,128)S(1)}, f32[8,8,8,128]{3,2,1,0:T(8,128)S(1)}, u32[]{:S(2)}, u32[]{:S(2)}) collective-permute-start(f32[8,8,8,128]{3,2,1,0:T(8,128)S(1)} %copy-done.4), channel_id=1, source_target_pairs={{0,4},{12,8},{1,5},{13,9},{2,6},{14,10},{3,7},{15,11},{16,20},{28,... | collective-permute-start | bytes 786440 | tf_op jit(solution)/shard_map/ppermute | solution.py:334
  47.6 0.0 collective-permute-done.6
  47.6 0.7 collective-permute-start.7
  48.3 0.0 collective-permute-done.9
  48.4 1.3 %collective-permute-start.10 = (f32[8,8,8,128]{3,2,1,0:T(8,128)S(1)}, f32[8,8,8,128]{3,2,1,0:T(8,128)S(1)}, u32[]{:S(2)}, u32[]{:S(2)}) collective-permute-start(f32[8,8,8,128]{3,2,1,0:T(8,128)S(1)} %add.72), channel_id=1, source_target_pairs={{4,0},{8,12},{5,1},{9,13},{6,2},{10,14},{7,3},{11,15},{20,16},{24,... | collective-permute-start | bytes 786440 | tf_op jit(solution)/shard_map/ppermute | solution.py:337
  49.7 0.2 fusion.6
  49.8 2.0 %collective-permute-done.5 = f32[8,8,8,128]{3,2,1,0:T(8,128)S(1)} collective-permute-done((f32[8,8,8,128]{3,2,1,0:T(8,128)S(1)}, f32[8,8,8,128]{3,2,1,0:T(8,128)S(1)}, u32[]{:S(2)}, u32[]{:S(2)}) %collective-permute-start.5) | collective-permute-done | bytes 262176 | tf_op jit(solution)/shard_map/ppermute | solution.py:334
  51.8 0.0 collective-permute-done.7
  51.9 4.9 %collective-permute-done.10 = f32[8,8,8,128]{3,2,1,0:T(8,128)S(1)} collective-permute-done((f32[8,8,8,128]{3,2,1,0:T(8,128)S(1)}, f32[8,8,8,128]{3,2,1,0:T(8,128)S(1)}, u32[]{:S(2)}, u32[]{:S(2)}) %collective-permute-start.10) | collective-permute-done | bytes 262176 | tf_op jit(solution)/shard_map/ppermute | solution.py:337
  56.8 0.1 add_select_fusion.own
  56.9 0.0 copy-start
  56.9 0.7 copy-done
  57.6 0.4 collective-permute-start.12
  58.0 1.6 %collective-permute-start.11 = (f32[4,8,8,128]{3,2,1,0:T(8,128)S(1)}, f32[4,8,8,128]{3,2,1,0:T(8,128)S(1)}, u32[]{:S(2)}, u32[]{:S(2)}) collective-permute-start(f32[4,8,8,128]{3,2,1,0:T(8,128)S(1)} %slice.32), channel_id=1, source_target_pairs={{0,4},{4,8},{8,12},{12,13},{13,9},{9,5},{5,1},{1,2},{2,6},{6,10},{... | collective-permute-start | bytes 393224 | tf_op jit(solution)/shard_map/ppermute | solution.py:347
  59.6 0.1 copy.13
  59.7 0.1 copy.14
  59.8 0.7 concatenate.10.coef
  60.5 0.7 slice_reduce_fusion.level
  61.2 1.9 %collective-permute-done.11.before = f32[4,8,8,128]{3,2,1,0:T(8,128)S(1)} collective-permute-done((f32[4,8,8,128]{3,2,1,0:T(8,128)S(1)}, f32[4,8,8,128]{3,2,1,0:T(8,128)S(1)}, u32[]{:S(2)}, u32[]{:S(2)}) %collective-permute-start.11) | collective-permute-done | bytes 131104 | tf_op jit(solution)/shard_map/ppermute | solution.py:347
  63.1 0.0 collective-permute-done.12.after
  63.1 0.6 copy-done.7
  63.7 0.7 copy-done.5
  64.4 13.2 %second_cycle.1 = f32[16,4,8,128]{3,2,1,0:T(8,128)} custom-call(f32[4,13]{1,0:T(4,128)} %concatenate.10.coef, s32[4]{0:T(128)} %slice_reduce_fusion.level, f32[4,8,8,128]{3,2,1,0:T(8,128)} %copy-done.7, f32[8,8,8,128]{3,2,1,0:T(8,128)} %copy-done, f32[5,8,8,128]{3,2,1,0:T(8,128)} %copy-done.5), custom_call_target="tpu_custom_call" | custom-call | tf_op jit(solution)/shard_map/second_cycle/pallas_call | solution.py:351
  77.6 5.5 %all-to-all-start = ((f32[16,4,8,128]{3,2,1,0:T(8,128)}), f32[16,4,8,128]{3,2,1,0:T(8,128)S(1)}, u32[]{:S(2)}, u32[]{:S(2)}) async-start(f32[16,4,8,128]{3,2,1,0:T(8,128)} %second_cycle.1), calls=%async_computation | async-start | bytes 524288 | tf_op jit(solution)/shard_map/all_to_all | solution.py:365
  83.1 0.0 copy-done.11
  83.1 0.0 copy-start.12
  83.1 0.6 copy-done.12
  83.8 0.8 select_add_fusion.matrix
  84.6 8.6 %all-to-all-done.rows = f32[16,4,8,128]{3,2,1,0:T(8,128)S(1)} async-done(((f32[16,4,8,128]{3,2,1,0:T(8,128)}), f32[16,4,8,128]{3,2,1,0:T(8,128)S(1)}, u32[]{:S(2)}, u32[]{:S(2)}) %all-to-all-start) | async-done | bytes 262176 | tf_op jit(solution)/shard_map/all_to_all | solution.py:365
  93.1 0.7 copy-done.2
  93.8 2.1 %hierarchise.1 = f32[4,4,32,128]{3,2,1,0:T(8,128)} custom-call(f32[128,128]{1,0:T(8,128)} %select_add_fusion.matrix, f32[16,4,8,128]{3,2,1,0:T(8,128)} %copy-done.2), custom_call_target="tpu_custom_call" | custom-call | tf_op jit(solution)/shard_map/hierarchise/pallas_call | solution.py:380
  95.9 13.3 %all_to_all.10.received = f32[4,4,32,128]{3,2,1,0:T(8,128)} all-to-all(f32[4,4,32,128]{3,2,1,0:T(8,128)} %hierarchise.1), channel_id=1, replica_groups=mesh['copies'=2,'grid'=4,'slab'=4] {'grid'}, dimensions={0} | all-to-all | bytes 524288 | tf_op jit(solution)/shard_map/all_to_all | solution.py:387
  109.2 1.8 %place.1 = f32[512,128]{1,0:T(8,128)} custom-call(f32[4,4,32,128]{3,2,1,0:T(8,128)} %all_to_all.10.received), custom_call_target="tpu_custom_call" | custom-call | tf_op jit(solution)/shard_map/place/pallas_call | solution.py:388
  (19 shorter events, 0.2 us)
Async XLA Ops:
  0.9 3.5 %copy-start.9 = (s32[1,5]{1,0:T(1,128)S(1)}, s32[1,5]{1,0:T(1,128)}, u32[]{:S(2)}) copy-start(s32[1,5]{1,0:T(1,128)} %param.5) | copy-start | bytes 64
  0.9 9.1 %collective-permute-start.4 = (f32[5,64,128]{2,1,0:T(8,128)S(1)}, f32[5,64,128]{2,1,0:T(8,128)S(1)}, u32[]{:S(2)}, u32[]{:S(2)}) collective-permute-start(f32[5,64,128]{2,1,0:T(8,128)S(1)} %slice_bitcast_fusion), channel_id=1, source_target_pairs={{1,0},{2,1},{3,2},{0,3},{5,4},{6,5},{7,6},{4,7},{9,8},{10,9},{11,1... | collective-permute-start | bytes 491528 | tf_op jit(solution)/shard_map/ppermute | solution.py:302
  4.3 5.7 %collective-permute-start.3 = (f32[4,64,128]{2,1,0:T(8,128)S(1)}, f32[4,64,128]{2,1,0:T(8,128)S(1)}, u32[]{:S(2)}, u32[]{:S(2)}) collective-permute-start(f32[4,64,128]{2,1,0:T(8,128)S(1)} %slice_bitcast_fusion.1), channel_id=1, source_target_pairs={{0,1},{1,2},{2,3},{3,0},{4,5},{5,6},{6,7},{7,4},{8,9},{9,10},{10,1... | collective-permute-start | bytes 393224 | tf_op jit(solution)/shard_map/ppermute | solution.py:301
  10.0 0.7 copy-start.8
  10.0 0.7 copy-start.6
  21.7 10.5 %collective-permute-start.8 = (f32[8,8,8,128]{3,2,1,0:T(8,128)}, f32[8,8,8,128]{3,2,1,0:T(8,128)S(1)}, u32[]{:S(2)}, u32[]{:S(2)}) collective-permute-start(f32[8,8,8,128]{3,2,1,0:T(8,128)} %get-tuple-element.12), channel_id=1, source_target_pairs={{0,4},{12,8},{1,5},{13,9},{2,6},{14,10},{3,7},{15,11},{16,20},{28,... | collective-permute-start | bytes 786440 | tf_op jit(solution)/shard_map/ppermute | solution.py:332
  25.2 8.6 %copy-start.10 = (s32[1,5]{1,0:T(1,128)S(1)}, s32[1,5]{1,0:T(1,128)}, u32[]{:S(2)}) copy-start(s32[1,5]{1,0:T(1,128)} %param.5) | copy-start | bytes 64
  25.2 19.6 %copy-start.4 = (f32[8,8,8,128]{3,2,1,0:T(8,128)S(1)}, f32[8,8,8,128]{3,2,1,0:T(8,128)}, u32[]{:S(2)}) copy-start(f32[8,8,8,128]{3,2,1,0:T(8,128)} %get-tuple-element.9) | copy-start | bytes 786436
  25.2 22.4 %copy-start.3 = (f32[8,8,8,128]{3,2,1,0:T(8,128)S(1)}, f32[8,8,8,128]{3,2,1,0:T(8,128)}, u32[]{:S(2)}) copy-start(f32[8,8,8,128]{3,2,1,0:T(8,128)} %get-tuple-element.10) | copy-start | bytes 786436
  25.2 22.3 %collective-permute-start.6 = (f32[8,8,8,128]{3,2,1,0:T(8,128)}, f32[8,8,8,128]{3,2,1,0:T(8,128)S(1)}, u32[]{:S(2)}, u32[]{:S(2)}) collective-permute-start(f32[8,8,8,128]{3,2,1,0:T(8,128)} %get-tuple-element.10), channel_id=1, source_target_pairs={{0,4},{12,8},{1,5},{13,9},{2,6},{14,10},{3,7},{15,11},{16,20},{28,... | collective-permute-start | bytes 786440 | tf_op jit(solution)/shard_map/ppermute | solution.py:333
  33.2 15.1 %collective-permute-start.9 = (f32[8,8,8,128]{3,2,1,0:T(8,128)S(1)}, f32[8,8,8,128]{3,2,1,0:T(8,128)S(1)}, u32[]{:S(2)}, u32[]{:S(2)}) collective-permute-start(f32[8,8,8,128]{3,2,1,0:T(8,128)S(1)} %add.71), channel_id=1, source_target_pairs={{4,8},{8,4},{5,9},{9,5},{6,10},{10,6},{7,11},{11,7},{20,24},{24,20... | collective-permute-start | bytes 786440 | tf_op jit(solution)/shard_map/ppermute | solution.py:335
  33.9 8.1 %collective-permute-start = (s32[1,5]{1,0:T(1,128)S(1)}, s32[1,5]{1,0:T(1,128)S(1)}, u32[]{:S(2)}, u32[]{:S(2)}) collective-permute-start(s32[1,5]{1,0:T(1,128)S(1)} %copy-done.10), channel_id=1, source_target_pairs={{0,4},{4,8},{8,12},{12,0},{1,5},{5,9},{9,13},{13,1},{2,6},{6,10},{... | collective-permute-start | bytes 68 | tf_op jit(solution)/shard_map/ppermute | solution.py:304
  39.1 5.5 %collective-permute-start.1 = (s32[1,5]{1,0:T(1,128)S(1)}, s32[1,5]{1,0:T(1,128)S(1)}, u32[]{:S(2)}, u32[]{:S(2)}) collective-permute-start(s32[1,5]{1,0:T(1,128)S(1)} %copy-done.10), channel_id=1, source_target_pairs={{0,8},{4,12},{8,0},{12,4},{1,9},{5,13},{9,1},{13,5},{2,10},{6,14},... | collective-permute-start | bytes 68 | tf_op jit(solution)/shard_map/ppermute | solution.py:304
  39.1 5.5 %collective-permute-start.2 = (s32[1,5]{1,0:T(1,128)S(1)}, s32[1,5]{1,0:T(1,128)S(1)}, u32[]{:S(2)}, u32[]{:S(2)}) collective-permute-start(s32[1,5]{1,0:T(1,128)S(1)} %copy-done.10), channel_id=1, source_target_pairs={{0,12},{4,0},{8,4},{12,8},{1,13},{5,1},{9,5},{13,9},{2,14},{6,2},{... | collective-permute-start | bytes 68 | tf_op jit(solution)/shard_map/ppermute | solution.py:304
  44.9 3.5 %copy-start.1 = (f32[8,8,8,128]{3,2,1,0:T(8,128)S(1)}, f32[8,8,8,128]{3,2,1,0:T(8,128)}, u32[]{:S(2)}) copy-start(f32[8,8,8,128]{3,2,1,0:T(8,128)} %get-tuple-element.11) | copy-start | bytes 786436
  44.9 7.0 %collective-permute-start.5 = (f32[8,8,8,128]{3,2,1,0:T(8,128)S(1)}, f32[8,8,8,128]{3,2,1,0:T(8,128)S(1)}, u32[]{:S(2)}, u32[]{:S(2)}) collective-permute-start(f32[8,8,8,128]{3,2,1,0:T(8,128)S(1)} %copy-done.4), channel_id=1, source_target_pairs={{0,4},{12,8},{1,5},{13,9},{2,6},{14,10},{3,7},{15,11},{16,20},{28,... | collective-permute-start | bytes 786440 | tf_op jit(solution)/shard_map/ppermute | solution.py:334
  47.6 4.2 %collective-permute-start.7 = (f32[8,8,8,128]{3,2,1,0:T(8,128)S(1)}, f32[8,8,8,128]{3,2,1,0:T(8,128)S(1)}, u32[]{:S(2)}, u32[]{:S(2)}) collective-permute-start(f32[8,8,8,128]{3,2,1,0:T(8,128)S(1)} %add.69), channel_id=1, source_target_pairs={{4,8},{8,4},{5,9},{9,5},{6,10},{10,6},{7,11},{11,7},{20,24},{24,20... | collective-permute-start | bytes 786440 | tf_op jit(solution)/shard_map/ppermute | solution.py:336
  48.4 8.4 %collective-permute-start.10 = (f32[8,8,8,128]{3,2,1,0:T(8,128)S(1)}, f32[8,8,8,128]{3,2,1,0:T(8,128)S(1)}, u32[]{:S(2)}, u32[]{:S(2)}) collective-permute-start(f32[8,8,8,128]{3,2,1,0:T(8,128)S(1)} %add.72), channel_id=1, source_target_pairs={{4,0},{8,12},{5,1},{9,13},{6,2},{10,14},{7,3},{11,15},{20,16},{24,... | collective-permute-start | bytes 786440 | tf_op jit(solution)/shard_map/ppermute | solution.py:337
  56.9 0.7 copy-start
  57.6 5.5 %collective-permute-start.12 = (f32[5,8,8,128]{3,2,1,0:T(8,128)S(1)}, f32[5,8,8,128]{3,2,1,0:T(8,128)S(1)}, u32[]{:S(2)}, u32[]{:S(2)}) collective-permute-start(f32[5,8,8,128]{3,2,1,0:T(8,128)S(1)} %slice.33), channel_id=1, source_target_pairs={{4,0},{8,4},{12,8},{13,12},{9,13},{5,9},{1,5},{2,1},{6,2},{10,6},{... | collective-permute-start | bytes 491528 | tf_op jit(solution)/shard_map/ppermute | solution.py:348
  58.0 5.1 %collective-permute-start.11 = (f32[4,8,8,128]{3,2,1,0:T(8,128)S(1)}, f32[4,8,8,128]{3,2,1,0:T(8,128)S(1)}, u32[]{:S(2)}, u32[]{:S(2)}) collective-permute-start(f32[4,8,8,128]{3,2,1,0:T(8,128)S(1)} %slice.32), channel_id=1, source_target_pairs={{0,4},{4,8},{8,12},{12,13},{13,9},{9,5},{5,1},{1,2},{2,6},{6,10},{... | collective-permute-start | bytes 393224 | tf_op jit(solution)/shard_map/ppermute | solution.py:347
  63.1 0.6 copy-start.7
  63.7 0.7 copy-start.5
  77.6 5.5 %copy-start.11 = (s32[128]{0:T(128)S(1)}, s32[128]{0:T(128)}, u32[]{:S(2)}) copy-start(s32[128]{0:T(128)} %param.6) | copy-start | bytes 1540
  77.6 15.5 %all-to-all-start = ((f32[16,4,8,128]{3,2,1,0:T(8,128)}), f32[16,4,8,128]{3,2,1,0:T(8,128)S(1)}, u32[]{:S(2)}, u32[]{:S(2)}) async-start(f32[16,4,8,128]{3,2,1,0:T(8,128)} %second_cycle.1), calls=%async_computation | async-start | bytes 524288 | tf_op jit(solution)/shard_map/all_to_all | solution.py:365
  83.1 0.7 copy-start.12
  93.1 0.7 copy-start.2

commit v2 on v0

--- a/solution.py
+++ b/solution.py
@@ -1,9 +1,12 @@
+import functools
 import math
 
 import jax
 import jax.numpy as jnp
 import numpy as np
 from jax import lax
+from jax.experimental import pallas as pl
+from jax.experimental.pallas import tpu as pltpu
 from jax.sharding import PartitionSpec as P
 
 N0 = 128
@@ -14,9 +17,12 @@
 STEPS = 4
 Q = 64
 
-
 ADVECT = 0.08
 DIFFUSE = 0.03
+
+LOW = STEPS
+HIGH = STEPS + 1
+TILES = N1 * N3
 
 
 def extended_2(value, sides, width):
@@ -76,7 +82,7 @@
     return lax.all_to_all(stepped, "slab", split_axis=1, concat_axis=0, tiled=True)
 
 
-def local(field, levels, owner):
+def local_general(field, levels, owner):
     matrix, inverse, level_rows = build_tables(N0)
     matrix = jnp.asarray(matrix)
     inverse = jnp.asarray(inverse)
@@ -116,6 +122,326 @@
     return summed
 
 
+VMEM = pl.BlockSpec(memory_space=pltpu.VMEM)
+SMEM = pl.BlockSpec(memory_space=pltpu.SMEM)
+HBM = pl.BlockSpec(memory_space=pltpu.HBM)
+UNROLL = 2
+
+
+def step_rows(src, dst, first, groups, factors):
+    advect, spread, centre_spread, centre_advect = factors
+    twice = spread[1] + spread[1]
+
+    def body(group, carry):
+        base = first + group * UNROLL
+        for offset in range(UNROLL):
+            row = base + offset
+            tiles = [src[row, t] for t in range(TILES)]
+            for n1 in range(N1):
+                for n3 in range(N3):
+                    t = n1 * N3 + n3
+                    u = tiles[t]
+                    other = tiles[(1 - n1) * N3 + n3]
+                    neighbours = (
+                        (0, src[row - 1, t], src[row + 1, t]),
+                        (2, pltpu.roll(u, 1, 0), pltpu.roll(u, N2 - 1, 0)),
+                        (3, tiles[n1 * N3 + (n3 - 1) % N3], tiles[n1 * N3 + (n3 + 1) % N3]),
+                        (4, pltpu.roll(u, 1, 1), pltpu.roll(u, N4 - 1, 1)),
+                    )
+                    drift = advect[1] * other - centre_advect * u
+                    update = twice * other + centre_spread * u
+                    for d, back, ahead in neighbours:
+                        drift = drift + advect[d] * back
+                        update = update + spread[d] * (back + ahead)
+                    dst[row, t] = update + (2.0 + jnp.tanh(u)) * drift
+        return carry
+
+    lax.fori_loop(0, groups, body, 0)
+
+
+def factors_of(scales):
+    advect = [(0.5 * ADVECT) * s for s in scales]
+    spread = [DIFFUSE * (s * s) for s in scales]
+    total = spread[0]
+    for value in spread[1:]:
+        total = total + value
+    centre = advect[0]
+    for value in advect[1:]:
+        centre = centre + value
+    return advect, spread, 1.0 - 2.0 * total, centre
+
+
+def interpolate(nodes, fine, middle):
+    u0, u1, u2, u3, u4 = nodes
+    v2 = jnp.where(middle, u2, 0.5 * (u0 + u4))
+    v1 = jnp.where(fine, u1, 0.5 * (u0 + v2))
+    v3 = jnp.where(fine, u3, 0.5 * (v2 + u4))
+    return u0, v1, v2, v3
+
+
+def state_space(rows):
+    return pltpu.VMEM((rows + LOW + HIGH + UNROLL, TILES, N2, N4), jnp.float32)
+
+
+def run_steps(bufs, rows, factors):
+    for step in range(STEPS):
+        count = rows + LOW + HIGH - 2 * (step + 1)
+        step_rows(bufs[step % 2], bufs[(step + 1) % 2], step + 1, -(-count // UNROLL), factors)
+    return bufs[STEPS % 2]
+
+
+def ends_kernel(field, last, first, sems):
+    rows = field.shape[0]
+    one = pltpu.make_async_copy(field.at[pl.ds(rows - LOW, LOW)], last, sems.at[0])
+    two = pltpu.make_async_copy(field.at[pl.ds(0, HIGH)], first, sems.at[1])
+    one.start()
+    two.start()
+    one.wait()
+    two.wait()
+
+
+def first_kernel(rows, later, level, before, field, after, outer, inner, *bufs):
+    half, start = field.shape[0] // 2, bufs[0]
+    me = lax.axis_index("grid")
+    upper = lax.rem(me + lax.axis_index("slab") + later, 2) == 0
+
+    def load(ref, first, count, at):
+        def body(i, carry):
+            for n1 in range(N1):
+                for n3 in range(N3):
+                    start[at + i, n1 * N3 + n3] = ref[first + i, pl.ds(n1 * N2 * N3 + n3, N2, stride=N3), :]
+            return carry
+
+        lax.fori_loop(0, count, body, 0)
+
+    @pl.when(upper)
+    def _():
+        load(field, half - LOW, half + LOW, 0)
+        load(after, 0, HIGH, LOW + half)
+
+    @pl.when(jnp.logical_not(upper))
+    def _():
+        load(before, 0, LOW, 0)
+        load(field, 0, half + HIGH, LOW)
+
+    levels = [level[0, d] for d in range(5)]
+    scales = [lax.shift_left(1, v).astype(jnp.float32) * 0.125 for v in levels]
+    parity = lax.rem(levels[0] + levels[1] + levels[2] + levels[3] + levels[4], 2)
+    weight = (1 - 2 * parity).astype(jnp.float32) * (1.0 / math.sqrt(lax.axis_size("grid")))
+    done = run_steps(bufs, half, factors_of(scales))
+    fine, middle = levels[0] >= 3, levels[0] >= 2
+    block = half // 2
+    edge = jnp.where(upper, block, 0)
+    for out, first in ((outer, edge), (inner, block - edge)):
+        for quad in range(0, block, 4):
+            base = LOW + first + quad
+            for t in range(TILES):
+                values = interpolate([done[base + i, t] for i in range(5)], fine, middle)
+                for i, value in enumerate(values):
+                    out[(quad + i) * TILES + t] = weight * value
+        lane = lax.broadcasted_iota(jnp.int32, (N2, N4), 1)
+        tile = jnp.zeros((N2, N4), jnp.float32)
+        for d, value in enumerate(scales + [levels[0].astype(jnp.float32), weight]):
+            tile = jnp.where(lane == d, value, tile)
+        sublane = lax.broadcasted_iota(jnp.int32, (N2, N4), 0)
+        out[block * TILES] = jnp.where(sublane == me, tile, 0.0)
+
+
+def second_kernel(rows, grids, before, own, after, out, total, wide, *bufs):
+    extent = rows + LOW + HIGH
+    for i in range(LOW * TILES):
+        wide[i] = before[i]
+    for i in range(rows * TILES):
+        wide[LOW * TILES + i] = own[i]
+    for i in range(HIGH * TILES):
+        wide[(LOW + rows) * TILES + i] = after[i]
+    for g in range(grids):
+        spread = lambda d: jnp.broadcast_to(own[rows * TILES, g : g + 1, d : d + 1], (N2, N4))
+        factors = factors_of([spread(d) for d in range(5)])
+        fine, middle, weight = spread(5) > 2.5, spread(5) > 1.5, spread(6)
+        start = bufs[0]
+        for quad in range(0, extent - 1, 4):
+            for t in range(TILES):
+                values = interpolate([wide[(quad + i) * TILES + t] for i in range(5)], fine, middle)
+                for i, value in enumerate(values):
+                    start[quad + i, t] = value
+        for t in range(TILES):
+            start[extent - 1, t] = wide[(extent - 1) * TILES + t]
+        done = run_steps(bufs, rows, factors)
+        for quad in range(0, rows, 4):
+            for t in range(TILES):
+                values = interpolate([done[LOW + quad + i, t] for i in range(5)], fine, middle)
+                for i, value in enumerate(values):
+                    at = pl.ds(((quad + i) * TILES + t) * N2, N2)
+                    total[at, :] = weight * value + (total[at, :] if g else 0.0)
+    half = N2 // 2
+    for n3 in range(N3):
+        for n1 in range(N1):
+            for n2 in range(N2):
+                at = (n3 * N1 + n1) * 2 + n2 // half
+                out[at, n2 % half] = total[pl.ds((n1 * N3 + n3) * N2 + n2, rows, stride=TILES * N2), :]
+
+
+def hier_kernel(groups, matrix, rows, *outs):
+    me = lax.axis_index("grid")
+    lanes = rows.shape[3]
+    count = matrix.shape[0] // groups
+    for n in range(rows.shape[1]):
+        whole = rows[:, n].reshape(matrix.shape[1], lanes)
+        high = whole.astype(jnp.bfloat16)
+        rest = (whole - high.astype(jnp.float32)).astype(jnp.bfloat16)
+        for d, out in enumerate(outs):
+            part = matrix[pl.ds(lax.rem(me + d, groups) * count, count), :]
+            out[n] = jnp.dot(part, high, preferred_element_type=jnp.float32) + jnp.dot(
+                part, rest, preferred_element_type=jnp.float32
+            )
+
+
+def place_kernel(groups, *refs):
+    received, out = refs[:-1], refs[-1]
+    me = lax.axis_index("grid")
+    parts, count = received[0].shape[0], received[0].shape[1]
+    for d, ref in enumerate(received):
+        n3 = lax.rem(me + groups - d, groups)
+        for n in range(parts):
+            out[pl.ds(n * N3 + n3, count, stride=parts * N3), :] = ref[n]
+
+
+def kernel(body, name, out_shape, in_specs, scratch=(), limit=4, flops=0):
+    single = not isinstance(out_shape, (list, tuple))
+    return pl.pallas_call(
+        body,
+        out_shape=out_shape,
+        in_specs=in_specs,
+        out_specs=VMEM if single else [VMEM] * len(out_shape),
+        scratch_shapes=list(scratch),
+        compiler_params=pltpu.CompilerParams(vmem_limit_bytes=limit << 20),
+        cost_estimate=pl.CostEstimate(flops=flops, bytes_accessed=1 << 20, transcendentals=flops // 30),
+        name=name,
+    )
+
+
+def fast_sizes(grids, slabs):
+    rows = N0 // slabs
+    return rows, rows // grids
+
+
+def fast_fits(grids, slabs):
+    rows, block = fast_sizes(grids, slabs)
+    return grids == 4 and grids == N3 and slabs == 2 * N1 and block >= HIGH and block % 4 == 0
+
+
+def floats(*shape):
+    return jax.ShapeDtypeStruct(shape, jnp.float32)
+
+
+def local_fast(field, levels, owner):
+    grids, slabs = lax.axis_size("grid"), lax.axis_size("slab")
+    rows, block = fast_sizes(grids, slabs)
+    me = lax.axis_index("grid")
+    state = field[0]
+
+    up = [(i, (i + 1) % slabs) for i in range(slabs)]
+    down = [(j, i) for i, j in up]
+    last, first = kernel(
+        ends_kernel,
+        "ends",
+        [floats(LOW, Q, N4), floats(HIGH, Q, N4)],
+        [HBM],
+        [pltpu.SemaphoreType.DMA((2,))],
+    )(state)
+    before = lax.ppermute(last, "slab", up)
+    after = lax.ppermute(first, "slab", down)
+
+    piece = floats(block * TILES + 1, N2, N4)
+
+    def half_slab(later):
+        return kernel(
+            functools.partial(first_kernel, rows, later),
+            "first_cycle",
+            [piece, piece],
+            [SMEM, VMEM, VMEM, VMEM],
+            [state_space(rows // 2)] * 2,
+            limit=8,
+            flops=160 * 8192 * 40,
+        )(levels, before, state, after)
+
+    edge = (me == 0) | (me == grids - 1)
+    a_outer, a_inner = half_slab(0)
+    swapped = lax.ppermute(a_outer, "grid", [(0, 1), (1, 0), (2, 3), (3, 2)])
+    b_outer, b_inner = half_slab(1)
+    inwards = lax.ppermute(b_inner, "grid", [(0, 1), (3, 2)])
+    across = lax.ppermute(b_inner, "grid", [(1, 2), (2, 1)])
+    joined = swapped + b_outer
+    passed = lax.ppermute(jnp.where(edge, a_inner, joined), "grid", [(0, 2), (3, 1), (1, 3), (2, 0)])
+    own = jnp.where(edge, joined, a_inner) + inwards + across + passed
+
+    chain = []
+    for k in range(slabs):
+        chain += [(g if k % 2 == 0 else grids - 1 - g) * slabs + k for g in range(grids)]
+    forward = [(chain[i], chain[(i + 1) % len(chain)]) for i in range(len(chain))]
+    backward = [(j, i) for i, j in forward]
+    both = ("grid", "slab")
+    before = lax.ppermute(own[(block - LOW) * TILES : block * TILES], both, forward)
+    after = lax.ppermute(own[: HIGH * TILES], both, backward)
+
+    half = N2 // 2
+    sent = kernel(
+        functools.partial(second_kernel, block, grids),
+        "second_cycle",
+        floats(N3 * N1 * 2, half, block, N4),
+        [VMEM, VMEM, VMEM],
+        [
+            pltpu.VMEM((block * TILES * N2, N4), jnp.float32),
+            pltpu.VMEM(((block + LOW + HIGH) * TILES, N2, N4), jnp.float32),
+            state_space(block),
+            state_space(block),
+        ],
+        limit=8,
+        flops=400 * 8192 * 40,
+    )(before, own, after)
+
+    spread = lax.all_to_all(sent, both, split_axis=0, concat_axis=0, tiled=True)
+
+    source = np.zeros(N0, np.int32)
+    for place, device in enumerate(chain):
+        source[device * block : (device + 1) * block] = place * block + np.arange(block)
+    column = jnp.asarray(source)[None, :]
+    row = owner[:, None]
+    reach = jnp.where(row > 0, row & -row, 0)
+    part = jnp.where(row > 0, -0.5, 0.0)
+    matrix = (
+        (column == row).astype(jnp.float32)
+        + part * (column == row - reach)
+        + part * (column == (row + reach) % N0)
+    ).astype(jnp.bfloat16)
+    group = N0 // grids
+    hier = kernel(
+        functools.partial(hier_kernel, grids),
+        "hierarchise",
+        [floats(half, group, N4)] * grids,
+        [VMEM, VMEM],
+    )(matrix, spread)
+    others = lax.optimization_barrier(tuple(hier[1:]))
+    received = [hier[0]] + [
+        lax.ppermute(value, "grid", [(i, (i + d) % grids) for i in range(grids)])
+        for d, value in enumerate(others, 1)
+    ]
+    out = kernel(
+        functools.partial(place_kernel, grids),
+        "place",
+        floats(group * half * N3, N4),
+        [VMEM] * grids,
+    )(*received)
+    return out.reshape(group, Q // slabs, N4)
+
+
+def local(field, levels, owner):
+    if fast_fits(lax.axis_size("grid"), lax.axis_size("slab")):
+        return local_fast(field, levels, owner)
+    return local_general(field, levels, owner)
+
+
 def solution(mesh):
     in_specs = (P(("copies", "grid"), "slab", None, None), P(("copies", "grid"), None), P("copies"))
     out_specs = P(("copies", "grid"), "slab", None)

time: 232 us -> 88.6 us (0.38)
  waiting for transfers between devices: 112 us -> 41.8 us
  blocking collectives: 33.8 us -> 0 us
  between operations: 25.4 us -> 0.12 us
  Pallas kernels: 0 us -> 24.7 us
  local copies, waits for them, and re-layouts: 24.6 us -> 1.91 us
  other arithmetic: 20.2 us -> 0.33 us
  starting transfers between devices: 11.5 us -> 19.4 us
  matrix products: 3.88 us -> 0 us
    reduce_scatter x2 -> x0, waiting for transfers between devices: 53.7 us -> none  [reduce_terms(): lax.psum_scatter(terms[owner], 'grid', scatter_dimension=0, tiled=True)]
    all_to_all x2 -> x0, blocking collectives: 33.8 us -> none  [the longest x1 17 us: local(): lax.all_to_all(nodal, 'slab', split_axis=0, concat_axis=1, tiled=True)]
    all_gather x1 -> x0, waiting for transfers between devices: 27 us -> none  [local(): ordered = lax.all_gather(summed, 'grid', axis=0, tiled=True)]
    pallas_call x0 -> x6, Pallas kernels: none -> 24.7 us  [the longest x1 12.7 us: local_fast(): kernel(functools.partial(second_kernel, block, grids), 'second_cycle', fl...]
    add x8 -> x1, other arithmetic: 19.2 us -> 0.13 us  [local_fast(): own = jnp.where(edge, joined, a_inner) + inwards + across + passed]
    slice x65 -> x2, local copies, waits for them, and re-layouts: 12.3 us -> 0.02 us  [the longest x1 0.01 us: local_fast(): after = lax.ppermute(own[:HIGH * TILES], both, backward)]
    ppermute x16 -> x11, waiting for transfers between devices: 21.4 us -> 32.6 us  [the longest x1 13.9 us: local_fast(): lax.ppermute(jnp.where(edge, a_inner, joined), 'grid', [(0, 2), (3, 1), (...]
    ppermute x16 -> x11, starting transfers between devices: 7.64 us -> 15.2 us  [the longest x3 3.1 us: local_fast(): lax.ppermute(value, 'grid', [(i, (i + d) % grids) for i in range(grids)])]
  transfers between devices with their start and end apart: 20 -> 12, of which waited for: 18 -> 8; matrix products, arithmetic and copies ran while one was open for 2% -> 0% of each run, Pallas kernels for 0% -> 6%
where the time goes in v2:
time: 88.6 us; the launch traced here: 88.3 us
  waiting for transfers between devices  41.8 us (47%)
  Pallas kernels  24.7 us (28%)
  starting transfers between devices  19.4 us (22%)
  local copies, waits for them, and re-layouts  1.91 us (2%)
    ppermute x1, waiting for transfers between devices, local_fast(): lax.ppermute(jnp.where(edge, a_inner, joined), 'grid', [(0, 2), (3, 1), (...  13.9 us
    pallas_call x1, Pallas kernels, local_fast(): kernel(functools.partial(second_kernel, block, grids), 'second_cycle', fl...  12.7 us
    pallas_call x2, Pallas kernels, half_slab(): kernel(functools.partial(first_kernel, rows, later), 'first_cycle', [piec...  10.4 us
    all_to_all x1, waiting for transfers between devices, local_fast(): spread = lax.all_to_all(sent, both, split_axis=0, concat_axis=0, tiled=True)  9.17 us
    ppermute x3, waiting for transfers between devices, local_fast(): lax.ppermute(value, 'grid', [(i, (i + d) % grids) for i in range(grids)])  6 us
    ppermute x1, waiting for transfers between devices, local_fast(): before = lax.ppermute(last, 'slab', up)  5.26 us
    ppermute x1, waiting for transfers between devices, local_fast(): lax.ppermute(own[(block - LOW) * TILES:block * TILES], both, forward)  4.3 us
    all_to_all x1, starting transfers between devices, local_fast(): spread = lax.all_to_all(sent, both, split_axis=0, concat_axis=0, tiled=True)  4.2 us
  transfers between devices with their start and end apart: 12, of which 8 were waited for; matrix products, arithmetic and copies ran while one was open for 0% of the time, Pallas kernels for 6%

profile of v2, /device:TPU:0, one launch (start us, length us, event | category | flops | bytes accessed | tf_op | source)
XLA Modules:
  0.0 88.3 jit_solution(14475558146480386638)
XLA Ops:
  0.0 0.0 copy-start
  0.0 1.2 %copy-done = f32[1,32,64,128]{3,2,1,0:T(8,128)S(1)} copy-done((f32[1,32,64,128]{3,2,1,0:T(8,128)S(1)}, f32[1,32,64,128]{3,2,1,0:T(8,128)}, u32[]{:S(2)}) %copy-start) | copy-done | bytes 1048600
  1.2 0.0 copy-start.1
  1.2 0.4 ends.1
  1.6 0.0 copy-start.2
  1.6 2.5 %collective-permute-start.1 = (f32[5,64,128]{2,1,0:T(8,128)S(1)}, f32[5,64,128]{2,1,0:T(8,128)S(1)}, u32[]{:S(2)}, u32[]{:S(2)}) collective-permute-start(f32[5,64,128]{2,1,0:T(8,128)S(1)} %get-tuple-element.19), channel_id=1, source_target_pairs={{1,0},{2,1},{3,2},{0,3},{5,4},{6,5},{7,6},{4,7},{9,8},{10,9},{11,1... | collective-permute-start | bytes 491528 | tf_op jit(solution)/shard_map/ppermute | solution.py:354
  4.1 0.0 collective-permute-start
  4.1 5.3 %collective-permute-done.before = f32[4,64,128]{2,1,0:T(8,128)S(1)} collective-permute-done((f32[4,64,128]{2,1,0:T(8,128)S(1)}, f32[4,64,128]{2,1,0:T(8,128)S(1)}, u32[]{:S(2)}, u32[]{:S(2)}) %collective-permute-start) | collective-permute-done | bytes 131104 | tf_op jit(solution)/shard_map/ppermute | solution.py:353
  9.3 0.0 collective-permute-done.1.after
  9.3 0.0 copy-done.1
  9.3 0.0 copy-done.2
  9.4 5.2 %first_cycle.2 = (f32[65,8,128]{2,1,0:T(8,128)S(1)}, f32[65,8,128]{2,1,0:T(8,128)S(1)}) custom-call(s32[1,5]{1,0:T(1,128)S(1)} %copy-done.2, f32[4,64,128]{2,1,0:T(8,128)S(1)} %collective-permute-done.before, f32[32,64,128]{2,1,0:T(8,128)S(1)} %bitcast.3, f32[5,64,128]{2,1,0:T(8,128)S(1)} %collective-permute-done.1.after), custom_call_target="tpu_custom_call" | custom-call | flops 52428800 | bytes 1048576 | tf_op jit(solution)/shard_map/first_cycle/pallas_call | solution.py:359
  14.6 1.7 %collective-permute-start.2 = (f32[65,8,128]{2,1,0:T(8,128)S(1)}, f32[65,8,128]{2,1,0:T(8,128)S(1)}, u32[]{:S(2)}, u32[]{:S(2)}) collective-permute-start(f32[65,8,128]{2,1,0:T(8,128)S(1)} %get-tuple-element.20), channel_id=1, source_target_pairs={{0,4},{4,0},{8,12},{12,8},{1,5},{5,1},{9,13},{13,9},{2,6},{6,2},{1... | collective-permute-start | bytes 798728 | tf_op jit(solution)/shard_map/ppermute | solution.py:371
  16.2 5.2 %first_cycle.3 = (f32[65,8,128]{2,1,0:T(8,128)S(1)}, f32[65,8,128]{2,1,0:T(8,128)S(1)}) custom-call(s32[1,5]{1,0:T(1,128)S(1)} %copy-done.2, f32[4,64,128]{2,1,0:T(8,128)S(1)} %collective-permute-done.before, f32[32,64,128]{2,1,0:T(8,128)S(1)} %bitcast.4, f32[5,64,128]{2,1,0:T(8,128)S(1)} %collective-permute-done.1.after), custom_call_target="tpu_custom_call" | custom-call | flops 52428800 | bytes 1048576 | tf_op jit(solution)/shard_map/first_cycle/pallas_call | solution.py:359
  21.5 2.3 %collective-permute-start.3 = (f32[65,8,128]{2,1,0:T(8,128)S(1)}, f32[65,8,128]{2,1,0:T(8,128)S(1)}, u32[]{:S(2)}, u32[]{:S(2)}) collective-permute-start(f32[65,8,128]{2,1,0:T(8,128)S(1)} %get-tuple-element.23), channel_id=1, source_target_pairs={{0,4},{12,8},{1,5},{13,9},{2,6},{14,10},{3,7},{15,11},{16,20},{28,... | collective-permute-start | bytes 798728 | tf_op jit(solution)/shard_map/ppermute | solution.py:373
  23.8 0.7 collective-permute-start.4
  24.5 0.0 collective-permute-done.2
  24.5 0.1 broadcast_select_fusion
  24.5 2.9 %collective-permute-start.5 = (f32[65,8,128]{2,1,0:T(8,128)S(1)}, f32[65,8,128]{2,1,0:T(8,128)S(1)}, u32[]{:S(2)}, u32[]{:S(2)}) collective-permute-start(f32[65,8,128]{2,1,0:T(8,128)S(1)} %broadcast_select_fusion), channel_id=1, source_target_pairs={{0,8},{12,4},{4,12},{8,0},{1,9},{13,5},{5,13},{9,1},{2,10},{14,6},... | collective-permute-start | bytes 798728 | tf_op jit(solution)/shard_map/ppermute | solution.py:376
  27.4 3.1 %collective-permute-done.3 = f32[65,8,128]{2,1,0:T(8,128)S(1)} collective-permute-done((f32[65,8,128]{2,1,0:T(8,128)S(1)}, f32[65,8,128]{2,1,0:T(8,128)S(1)}, u32[]{:S(2)}, u32[]{:S(2)}) %collective-permute-start.3) | collective-permute-done | bytes 266272 | tf_op jit(solution)/shard_map/ppermute | solution.py:373
  30.5 0.0 collective-permute-done.4
  30.5 13.9 %collective-permute-done.5 = f32[65,8,128]{2,1,0:T(8,128)S(1)} collective-permute-done((f32[65,8,128]{2,1,0:T(8,128)S(1)}, f32[65,8,128]{2,1,0:T(8,128)S(1)}, u32[]{:S(2)}, u32[]{:S(2)}) %collective-permute-start.5) | collective-permute-done | bytes 266272 | tf_op jit(solution)/shard_map/ppermute | solution.py:376
  44.5 0.1 add_add_fusion.own
  44.6 0.6 collective-permute-start.7
  45.2 1.6 %collective-permute-start.6 = (f32[32,8,128]{2,1,0:T(8,128)S(1)}, f32[32,8,128]{2,1,0:T(8,128)S(1)}, u32[]{:S(2)}, u32[]{:S(2)}) collective-permute-start(f32[32,8,128]{2,1,0:T(8,128)S(1)} %slice.8), channel_id=1, source_target_pairs={{0,4},{4,8},{8,12},{12,13},{13,9},{9,5},{5,1},{1,2},{2,6},{6,10},{... | collective-permute-start | bytes 393224 | tf_op jit(solution)/shard_map/ppermute | solution.py:385
  46.8 4.3 %collective-permute-done.6.before = f32[32,8,128]{2,1,0:T(8,128)S(1)} collective-permute-done((f32[32,8,128]{2,1,0:T(8,128)S(1)}, f32[32,8,128]{2,1,0:T(8,128)S(1)}, u32[]{:S(2)}, u32[]{:S(2)}) %collective-permute-start.6) | collective-permute-done | bytes 131104 | tf_op jit(solution)/shard_map/ppermute | solution.py:385
  51.1 0.0 collective-permute-done.7.after
  51.1 12.7 %second_cycle.1 = f32[16,4,8,128]{3,2,1,0:T(8,128)} custom-call(f32[32,8,128]{2,1,0:T(8,128)S(1)} %collective-permute-done.6.before, f32[65,8,128]{2,1,0:T(8,128)S(1)} %add_add_fusion.own, f32[40,8,128]{2,1,0:T(8,128)S(1)} %collective-permute-done.7.after), custom_call_target="tpu_custom_call" | custom-call | flops 131072000 | bytes 1048576 | tf_op jit(solution)/shard_map/second_cycle/pallas_call | solution.py:389
  63.8 0.0 copy-start.3
  63.8 4.2 %all-to-all-start = ((f32[16,4,8,128]{3,2,1,0:T(8,128)}), f32[16,4,8,128]{3,2,1,0:T(8,128)S(1)}, u32[]{:S(2)}, u32[]{:S(2)}) async-start(f32[16,4,8,128]{3,2,1,0:T(8,128)} %second_cycle.1), calls=%async_computation | async-start | bytes 524288 | tf_op jit(solution)/shard_map/all_to_all | solution.py:404
  68.0 0.0 copy-done.3
  68.0 0.0 copy-start.4
  68.0 0.6 copy-done.4
  68.7 0.1 add_convert_fusion.matrix
  68.8 9.2 %all-to-all-done.rows = f32[16,4,8,128]{3,2,1,0:T(8,128)S(1)} async-done(((f32[16,4,8,128]{3,2,1,0:T(8,128)}), f32[16,4,8,128]{3,2,1,0:T(8,128)S(1)}, u32[]{:S(2)}, u32[]{:S(2)}) %all-to-all-start) | async-done | bytes 262176 | tf_op jit(solution)/shard_map/all_to_all | solution.py:404
  78.0 0.4 hierarchise.1
  78.4 1.0 %collective-permute-start.10 = (f32[4,32,128]{2,1,0:T(8,128)S(1)}, f32[4,32,128]{2,1,0:T(8,128)S(1)}, u32[]{:S(2)}, u32[]{:S(2)}) collective-permute-start(f32[4,32,128]{2,1,0:T(8,128)S(1)} %get-tuple-element.30), channel_id=1, source_target_pairs={{0,12},{4,0},{8,4},{12,8},{1,13},{5,1},{9,5},{13,9},{2,14},{6,2},{... | collective-permute-start | bytes 196616 | tf_op jit(solution)/shard_map/ppermute | solution.py:427
  79.4 1.0 %collective-permute-start.8 = (f32[4,32,128]{2,1,0:T(8,128)S(1)}, f32[4,32,128]{2,1,0:T(8,128)S(1)}, u32[]{:S(2)}, u32[]{:S(2)}) collective-permute-start(f32[4,32,128]{2,1,0:T(8,128)S(1)} %get-tuple-element.28), channel_id=1, source_target_pairs={{0,4},{4,8},{8,12},{12,0},{1,5},{5,9},{9,13},{13,1},{2,6},{6,10},{... | collective-permute-start | bytes 196616 | tf_op jit(solution)/shard_map/ppermute | solution.py:427
  80.4 1.1 %collective-permute-start.9 = (f32[4,32,128]{2,1,0:T(8,128)S(1)}, f32[4,32,128]{2,1,0:T(8,128)S(1)}, u32[]{:S(2)}, u32[]{:S(2)}) collective-permute-start(f32[4,32,128]{2,1,0:T(8,128)S(1)} %get-tuple-element.29), channel_id=1, source_target_pairs={{0,8},{4,12},{8,0},{12,4},{1,9},{5,13},{9,1},{13,5},{2,10},{6,14},... | collective-permute-start | bytes 196616 | tf_op jit(solution)/shard_map/ppermute | solution.py:427
  81.5 1.2 %collective-permute-done.10.refs_3_ = f32[4,32,128]{2,1,0:T(8,128)S(1)} collective-permute-done((f32[4,32,128]{2,1,0:T(8,128)S(1)}, f32[4,32,128]{2,1,0:T(8,128)S(1)}, u32[]{:S(2)}, u32[]{:S(2)}) %collective-permute-start.10) | collective-permute-done | bytes 65568 | tf_op jit(solution)/shard_map/ppermute | solution.py:427
  82.7 3.4 %collective-permute-done.8.refs_1_ = f32[4,32,128]{2,1,0:T(8,128)S(1)} collective-permute-done((f32[4,32,128]{2,1,0:T(8,128)S(1)}, f32[4,32,128]{2,1,0:T(8,128)S(1)}, u32[]{:S(2)}, u32[]{:S(2)}) %collective-permute-start.8) | collective-permute-done | bytes 65568 | tf_op jit(solution)/shard_map/ppermute | solution.py:427
  86.1 1.4 %collective-permute-done.9.refs_2_ = f32[4,32,128]{2,1,0:T(8,128)S(1)} collective-permute-done((f32[4,32,128]{2,1,0:T(8,128)S(1)}, f32[4,32,128]{2,1,0:T(8,128)S(1)}, u32[]{:S(2)}, u32[]{:S(2)}) %collective-permute-start.9) | collective-permute-done | bytes 65568 | tf_op jit(solution)/shard_map/ppermute | solution.py:427
  87.5 0.8 place.1
  (4 shorter events, 0.0 us)
Async XLA Ops:
  0.0 1.2 %copy-start = (f32[1,32,64,128]{3,2,1,0:T(8,128)S(1)}, f32[1,32,64,128]{3,2,1,0:T(8,128)}, u32[]{:S(2)}) copy-start(f32[1,32,64,128]{3,2,1,0:T(8,128)} %param.4) | copy-start | bytes 3145732
  1.2 8.1 %copy-start.1 = (f32[1,32,64,128]{3,2,1,0:T(8,128)S(1)}, f32[1,32,64,128]{3,2,1,0:T(8,128)}, u32[]{:S(2)}) copy-start(f32[1,32,64,128]{3,2,1,0:T(8,128)} %param.4) | copy-start | bytes 3145732
  1.6 7.7 %copy-start.2 = (s32[1,5]{1,0:T(1,128)S(1)}, s32[1,5]{1,0:T(1,128)}, u32[]{:S(2)}) copy-start(s32[1,5]{1,0:T(1,128)} %level.3) | copy-start | bytes 64
  1.6 7.7 %collective-permute-start.1 = (f32[5,64,128]{2,1,0:T(8,128)S(1)}, f32[5,64,128]{2,1,0:T(8,128)S(1)}, u32[]{:S(2)}, u32[]{:S(2)}) collective-permute-start(f32[5,64,128]{2,1,0:T(8,128)S(1)} %get-tuple-element.19), channel_id=1, source_target_pairs={{1,0},{2,1},{3,2},{0,3},{5,4},{6,5},{7,6},{4,7},{9,8},{10,9},{11,1... | collective-permute-start | bytes 491528 | tf_op jit(solution)/shard_map/ppermute | solution.py:354
  4.1 5.3 %collective-permute-start = (f32[4,64,128]{2,1,0:T(8,128)S(1)}, f32[4,64,128]{2,1,0:T(8,128)S(1)}, u32[]{:S(2)}, u32[]{:S(2)}) collective-permute-start(f32[4,64,128]{2,1,0:T(8,128)S(1)} %get-tuple-element.18), channel_id=1, source_target_pairs={{0,1},{1,2},{2,3},{3,0},{4,5},{5,6},{6,7},{7,4},{8,9},{9,10},{10,1... | collective-permute-start | bytes 393224 | tf_op jit(solution)/shard_map/ppermute | solution.py:353
  14.6 9.9 %collective-permute-start.2 = (f32[65,8,128]{2,1,0:T(8,128)S(1)}, f32[65,8,128]{2,1,0:T(8,128)S(1)}, u32[]{:S(2)}, u32[]{:S(2)}) collective-permute-start(f32[65,8,128]{2,1,0:T(8,128)S(1)} %get-tuple-element.20), channel_id=1, source_target_pairs={{0,4},{4,0},{8,12},{12,8},{1,5},{5,1},{9,13},{13,9},{2,6},{6,2},{1... | collective-permute-start | bytes 798728 | tf_op jit(solution)/shard_map/ppermute | solution.py:371
  21.5 9.1 %collective-permute-start.3 = (f32[65,8,128]{2,1,0:T(8,128)S(1)}, f32[65,8,128]{2,1,0:T(8,128)S(1)}, u32[]{:S(2)}, u32[]{:S(2)}) collective-permute-start(f32[65,8,128]{2,1,0:T(8,128)S(1)} %get-tuple-element.23), channel_id=1, source_target_pairs={{0,4},{12,8},{1,5},{13,9},{2,6},{14,10},{3,7},{15,11},{16,20},{28,... | collective-permute-start | bytes 798728 | tf_op jit(solution)/shard_map/ppermute | solution.py:373
  23.8 6.8 %collective-permute-start.4 = (f32[65,8,128]{2,1,0:T(8,128)S(1)}, f32[65,8,128]{2,1,0:T(8,128)S(1)}, u32[]{:S(2)}, u32[]{:S(2)}) collective-permute-start(f32[65,8,128]{2,1,0:T(8,128)S(1)} %get-tuple-element.23), channel_id=1, source_target_pairs={{4,8},{8,4},{5,9},{9,5},{6,10},{10,6},{7,11},{11,7},{20,24},{24,20... | collective-permute-start | bytes 798728 | tf_op jit(solution)/shard_map/ppermute | solution.py:374
  24.5 19.9 %collective-permute-start.5 = (f32[65,8,128]{2,1,0:T(8,128)S(1)}, f32[65,8,128]{2,1,0:T(8,128)S(1)}, u32[]{:S(2)}, u32[]{:S(2)}) collective-permute-start(f32[65,8,128]{2,1,0:T(8,128)S(1)} %broadcast_select_fusion), channel_id=1, source_target_pairs={{0,8},{12,4},{4,12},{8,0},{1,9},{13,5},{5,13},{9,1},{2,10},{14,6},... | collective-permute-start | bytes 798728 | tf_op jit(solution)/shard_map/ppermute | solution.py:376
  44.6 6.5 %collective-permute-start.7 = (f32[40,8,128]{2,1,0:T(8,128)S(1)}, f32[40,8,128]{2,1,0:T(8,128)S(1)}, u32[]{:S(2)}, u32[]{:S(2)}) collective-permute-start(f32[40,8,128]{2,1,0:T(8,128)S(1)} %slice.9), channel_id=1, source_target_pairs={{4,0},{8,4},{12,8},{13,12},{9,13},{5,9},{1,5},{2,1},{6,2},{10,6},{... | collective-permute-start | bytes 491528 | tf_op jit(solution)/shard_map/ppermute | solution.py:386
  45.2 5.9 %collective-permute-start.6 = (f32[32,8,128]{2,1,0:T(8,128)S(1)}, f32[32,8,128]{2,1,0:T(8,128)S(1)}, u32[]{:S(2)}, u32[]{:S(2)}) collective-permute-start(f32[32,8,128]{2,1,0:T(8,128)S(1)} %slice.8), channel_id=1, source_target_pairs={{0,4},{4,8},{8,12},{12,13},{13,9},{9,5},{5,1},{1,2},{2,6},{6,10},{... | collective-permute-start | bytes 393224 | tf_op jit(solution)/shard_map/ppermute | solution.py:385
  63.8 4.2 %copy-start.3 = (s32[128]{0:T(128)S(1)}, s32[128]{0:T(128)}, u32[]{:S(2)}) copy-start(s32[128]{0:T(128)} %param.6) | copy-start | bytes 1540
  63.8 14.2 %all-to-all-start = ((f32[16,4,8,128]{3,2,1,0:T(8,128)}), f32[16,4,8,128]{3,2,1,0:T(8,128)S(1)}, u32[]{:S(2)}, u32[]{:S(2)}) async-start(f32[16,4,8,128]{3,2,1,0:T(8,128)} %second_cycle.1), calls=%async_computation | async-start | bytes 524288 | tf_op jit(solution)/shard_map/all_to_all | solution.py:404
  68.0 0.7 copy-start.4
  78.4 4.3 %collective-permute-start.10 = (f32[4,32,128]{2,1,0:T(8,128)S(1)}, f32[4,32,128]{2,1,0:T(8,128)S(1)}, u32[]{:S(2)}, u32[]{:S(2)}) collective-permute-start(f32[4,32,128]{2,1,0:T(8,128)S(1)} %get-tuple-element.30), channel_id=1, source_target_pairs={{0,12},{4,0},{8,4},{12,8},{1,13},{5,1},{9,5},{13,9},{2,14},{6,2},{... | collective-permute-start | bytes 196616 | tf_op jit(solution)/shard_map/ppermute | solution.py:427
  79.4 6.7 %collective-permute-start.8 = (f32[4,32,128]{2,1,0:T(8,128)S(1)}, f32[4,32,128]{2,1,0:T(8,128)S(1)}, u32[]{:S(2)}, u32[]{:S(2)}) collective-permute-start(f32[4,32,128]{2,1,0:T(8,128)S(1)} %get-tuple-element.28), channel_id=1, source_target_pairs={{0,4},{4,8},{8,12},{12,0},{1,5},{5,9},{9,13},{13,1},{2,6},{6,10},{... | collective-permute-start | bytes 196616 | tf_op jit(solution)/shard_map/ppermute | solution.py:427
  80.4 7.1 %collective-permute-start.9 = (f32[4,32,128]{2,1,0:T(8,128)S(1)}, f32[4,32,128]{2,1,0:T(8,128)S(1)}, u32[]{:S(2)}, u32[]{:S(2)}) collective-permute-start(f32[4,32,128]{2,1,0:T(8,128)S(1)} %get-tuple-element.29), channel_id=1, source_target_pairs={{0,8},{4,12},{8,0},{12,4},{1,9},{5,13},{9,1},{13,5},{2,10},{6,14},... | collective-permute-start | bytes 196616 | tf_op jit(solution)/shard_map/ppermute | solution.py:427

commit v3 on v2

--- a/solution.py
+++ b/solution.py
@@ -200,10 +200,10 @@
     two.wait()
 
 
-def first_kernel(rows, later, level, before, field, after, outer, inner, *bufs):
+def first_kernel(later, level, before, field, after, one, two, *bufs):
     half, start = field.shape[0] // 2, bufs[0]
-    me = lax.axis_index("grid")
-    upper = lax.rem(me + lax.axis_index("slab") + later, 2) == 0
+    me, grids = lax.axis_index("grid"), lax.axis_size("grid")
+    upper = lax.rem(lax.div(2 * me, grids) + lax.axis_index("slab") + later, 2) == 0
 
     def load(ref, first, count, at):
         def body(i, carry):
@@ -231,8 +231,11 @@
     done = run_steps(bufs, half, factors_of(scales))
     fine, middle = levels[0] >= 3, levels[0] >= 2
     block = half // 2
-    edge = jnp.where(upper, block, 0)
-    for out, first in ((outer, edge), (inner, block - edge)):
+    ends = jnp.logical_or(me == 0, me == grids - 1)
+    at = jnp.where(upper, block, 0)
+    if later:
+        at = jnp.where(ends, block - at, at)
+    for out, first in ((one, at), (two, block - at)):
         for quad in range(0, block, 4):
             base = LOW + first + quad
             for t in range(TILES):
@@ -338,7 +341,6 @@
 def local_fast(field, levels, owner):
     grids, slabs = lax.axis_size("grid"), lax.axis_size("slab")
     rows, block = fast_sizes(grids, slabs)
-    me = lax.axis_index("grid")
     state = field[0]
 
     up = [(i, (i + 1) % slabs) for i in range(slabs)]
@@ -357,7 +359,7 @@
 
     def half_slab(later):
         return kernel(
-            functools.partial(first_kernel, rows, later),
+            functools.partial(first_kernel, later),
             "first_cycle",
             [piece, piece],
             [SMEM, VMEM, VMEM, VMEM],
@@ -366,15 +368,14 @@
             flops=160 * 8192 * 40,
         )(levels, before, state, after)
 
-    edge = (me == 0) | (me == grids - 1)
-    a_outer, a_inner = half_slab(0)
-    swapped = lax.ppermute(a_outer, "grid", [(0, 1), (1, 0), (2, 3), (3, 2)])
-    b_outer, b_inner = half_slab(1)
-    inwards = lax.ppermute(b_inner, "grid", [(0, 1), (3, 2)])
-    across = lax.ppermute(b_inner, "grid", [(1, 2), (2, 1)])
-    joined = swapped + b_outer
-    passed = lax.ppermute(jnp.where(edge, a_inner, joined), "grid", [(0, 2), (3, 1), (1, 3), (2, 0)])
-    own = jnp.where(edge, joined, a_inner) + inwards + across + passed
+    far, middle = half_slab(0)
+    joined = lax.ppermute(far, "grid", [(0, 1), (3, 2)]) + far
+    across = lax.ppermute(middle, "grid", [(1, 2), (2, 1)])
+    skipped = lax.ppermute(middle, "grid", [(0, 2), (3, 1)])
+    near, own = half_slab(1)
+    swapped = lax.ppermute(near, "grid", [(0, 1), (1, 0), (2, 3), (3, 2)])
+    passed = lax.ppermute(joined, "grid", [(1, 3), (2, 0)])
+    own = own + across + skipped + swapped + passed
 
     chain = []
     for k in range(slabs):

time: 88.6 us -> 84.2 us (0.950)
  waiting for transfers between devices: 41.8 us -> 35 us
  starting transfers between devices: 19.4 us -> 21.8 us
    ppermute x4 -> x5, waiting for transfers between devices: 17.1 us -> 11.6 us  [the longest x1 10.6 us: local_fast(): swapped = lax.ppermute(near, 'grid', [(0, 1), (1, 0), (2, 3), (3, 2)])]
    ppermute x4 -> x5, starting transfers between devices: 7.53 us -> 9.52 us  [the longest x1 3.98 us: local_fast(): skipped = lax.ppermute(middle, 'grid', [(0, 2), (3, 1)])]
  transfers between devices with their start and end apart: 12 -> 13, of which waited for: 8 -> 8; matrix products, arithmetic and copies ran while one was open for 0% -> 0% of each run, Pallas kernels for 6% -> 6%
where the time goes in v3:
time: 84.2 us; the launch traced here: 83.9 us
  waiting for transfers between devices  35 us (42%)
  Pallas kernels  24.7 us (29%)
  starting transfers between devices  21.8 us (26%)
  local copies, waits for them, and re-layouts  1.91 us (2%)
    pallas_call x1, Pallas kernels, local_fast(): kernel(functools.partial(second_kernel, block, grids), 'second_cycle', fl...  12.7 us
    ppermute x1, waiting for transfers between devices, local_fast(): swapped = lax.ppermute(near, 'grid', [(0, 1), (1, 0), (2, 3), (3, 2)])  10.6 us
    pallas_call x2, Pallas kernels, half_slab(): kernel(functools.partial(first_kernel, later), 'first_cycle', [piece, pie...  10.4 us
    all_to_all x1, waiting for transfers between devices, local_fast(): spread = lax.all_to_all(sent, both, split_axis=0, concat_axis=0, tiled=True)  9.17 us
    ppermute x3, waiting for transfers between devices, local_fast(): lax.ppermute(value, 'grid', [(i, (i + d) % grids) for i in range(grids)])  5.32 us
    ppermute x1, waiting for transfers between devices, local_fast(): before = lax.ppermute(last, 'slab', up)  5.26 us
    all_to_all x1, starting transfers between devices, local_fast(): spread = lax.all_to_all(sent, both, split_axis=0, concat_axis=0, tiled=True)  4.56 us
    ppermute x1, starting transfers between devices, local_fast(): skipped = lax.ppermute(middle, 'grid', [(0, 2), (3, 1)])  3.98 us
  transfers between devices with their start and end apart: 13, of which 8 were waited for; matrix products, arithmetic and copies ran while one was open for 0% of the time, Pallas kernels for 6%

profile of v3, /device:TPU:0, one launch (start us, length us, event | category | flops | bytes accessed | tf_op | source)
XLA Modules:
  0.0 83.9 jit_solution(16828202842184012692)
XLA Ops:
  0.0 0.0 copy-start
  0.0 1.2 %copy-done = f32[1,32,64,128]{3,2,1,0:T(8,128)S(1)} copy-done((f32[1,32,64,128]{3,2,1,0:T(8,128)S(1)}, f32[1,32,64,128]{3,2,1,0:T(8,128)}, u32[]{:S(2)}) %copy-start) | copy-done | bytes 1048600
  1.2 0.0 copy-start.1
  1.2 0.4 ends.1
  1.6 0.0 copy-start.2
  1.6 2.5 %collective-permute-start.1 = (f32[5,64,128]{2,1,0:T(8,128)S(1)}, f32[5,64,128]{2,1,0:T(8,128)S(1)}, u32[]{:S(2)}, u32[]{:S(2)}) collective-permute-start(f32[5,64,128]{2,1,0:T(8,128)S(1)} %get-tuple-element.19), channel_id=1, source_target_pairs={{1,0},{2,1},{3,2},{0,3},{5,4},{6,5},{7,6},{4,7},{9,8},{10,9},{11,1... | collective-permute-start | bytes 491528 | tf_op jit(solution)/shard_map/ppermute | solution.py:356
  4.1 0.0 collective-permute-start
  4.1 5.3 %collective-permute-done.before = f32[4,64,128]{2,1,0:T(8,128)S(1)} collective-permute-done((f32[4,64,128]{2,1,0:T(8,128)S(1)}, f32[4,64,128]{2,1,0:T(8,128)S(1)}, u32[]{:S(2)}, u32[]{:S(2)}) %collective-permute-start) | collective-permute-done | bytes 131104 | tf_op jit(solution)/shard_map/ppermute | solution.py:355
  9.3 0.0 collective-permute-done.1.after
  9.3 0.0 copy-done.1
  9.3 0.0 copy-done.2
  9.4 5.2 %first_cycle.3 = (f32[65,8,128]{2,1,0:T(8,128)S(1)}, f32[65,8,128]{2,1,0:T(8,128)S(1)}) custom-call(s32[1,5]{1,0:T(1,128)S(1)} %copy-done.2, f32[4,64,128]{2,1,0:T(8,128)S(1)} %collective-permute-done.before, f32[32,64,128]{2,1,0:T(8,128)S(1)} %bitcast.3, f32[5,64,128]{2,1,0:T(8,128)S(1)} %collective-permute-done.1.after), custom_call_target="tpu_custom_call" | custom-call | flops 52428800 | bytes 1048576 | tf_op jit(solution)/shard_map/first_cycle/pallas_call | solution.py:361
  14.6 3.5 %collective-permute-start.5 = (f32[65,8,128]{2,1,0:T(8,128)S(1)}, f32[65,8,128]{2,1,0:T(8,128)S(1)}, u32[]{:S(2)}, u32[]{:S(2)}) collective-permute-start(f32[65,8,128]{2,1,0:T(8,128)S(1)} %get-tuple-element.23), channel_id=1, source_target_pairs={{0,4},{12,8},{1,5},{13,9},{2,6},{14,10},{3,7},{15,11},{16,20},{28,... | collective-permute-start | bytes 798728 | tf_op jit(solution)/shard_map/ppermute | solution.py:372
  18.1 0.7 collective-permute-start.2
  18.8 4.0 %collective-permute-start.3 = (f32[65,8,128]{2,1,0:T(8,128)S(1)}, f32[65,8,128]{2,1,0:T(8,128)S(1)}, u32[]{:S(2)}, u32[]{:S(2)}) collective-permute-start(f32[65,8,128]{2,1,0:T(8,128)S(1)} %get-tuple-element.21), channel_id=1, source_target_pairs={{0,8},{12,4},{1,9},{13,5},{2,10},{14,6},{3,11},{15,7},{16,24},{28,... | collective-permute-start | bytes 798728 | tf_op jit(solution)/shard_map/ppermute | solution.py:374
  22.8 5.2 %first_cycle.2 = (f32[65,8,128]{2,1,0:T(8,128)S(1)}, f32[65,8,128]{2,1,0:T(8,128)S(1)}) custom-call(s32[1,5]{1,0:T(1,128)S(1)} %copy-done.2, f32[4,64,128]{2,1,0:T(8,128)S(1)} %collective-permute-done.before, f32[32,64,128]{2,1,0:T(8,128)S(1)} %bitcast.4, f32[5,64,128]{2,1,0:T(8,128)S(1)} %collective-permute-done.1.after), custom_call_target="tpu_custom_call" | custom-call | flops 52428800 | bytes 1048576 | tf_op jit(solution)/shard_map/first_cycle/pallas_call | solution.py:361
  28.0 0.1 collective-permute-start.4
  28.1 0.0 collective-permute-done.5
  28.1 1.3 %collective-permute-start.6 = (f32[65,8,128]{2,1,0:T(8,128)S(1)}, f32[65,8,128]{2,1,0:T(8,128)S(1)}, u32[]{:S(2)}, u32[]{:S(2)}) collective-permute-start(f32[65,8,128]{2,1,0:T(8,128)S(1)} %add.39), channel_id=1, source_target_pairs={{4,12},{8,0},{5,13},{9,1},{6,14},{10,2},{7,15},{11,3},{20,28},{24,... | collective-permute-start | bytes 798728 | tf_op jit(solution)/shard_map/ppermute | solution.py:377
  29.4 0.0 collective-permute-done.2
  29.4 1.1 %collective-permute-done.3 = f32[65,8,128]{2,1,0:T(8,128)S(1)} collective-permute-done((f32[65,8,128]{2,1,0:T(8,128)S(1)}, f32[65,8,128]{2,1,0:T(8,128)S(1)}, u32[]{:S(2)}, u32[]{:S(2)}) %collective-permute-start.3) | collective-permute-done | bytes 266272 | tf_op jit(solution)/shard_map/ppermute | solution.py:374
  30.5 10.6 %collective-permute-done.4 = f32[65,8,128]{2,1,0:T(8,128)S(1)} collective-permute-done((f32[65,8,128]{2,1,0:T(8,128)S(1)}, f32[65,8,128]{2,1,0:T(8,128)S(1)}, u32[]{:S(2)}, u32[]{:S(2)}) %collective-permute-start.4) | collective-permute-done | bytes 266272 | tf_op jit(solution)/shard_map/ppermute | solution.py:376
  41.1 0.0 collective-permute-done.6
  41.1 0.1 add_add_fusion.own
  41.2 0.1 collective-permute-start.8
  41.3 2.1 %collective-permute-start.7 = (f32[32,8,128]{2,1,0:T(8,128)S(1)}, f32[32,8,128]{2,1,0:T(8,128)S(1)}, u32[]{:S(2)}, u32[]{:S(2)}) collective-permute-start(f32[32,8,128]{2,1,0:T(8,128)S(1)} %slice.8), channel_id=1, source_target_pairs={{0,4},{4,8},{8,12},{12,13},{13,9},{9,5},{5,1},{1,2},{2,6},{6,10},{... | collective-permute-start | bytes 393224 | tf_op jit(solution)/shard_map/ppermute | solution.py:386
  43.4 3.6 %collective-permute-done.7.before = f32[32,8,128]{2,1,0:T(8,128)S(1)} collective-permute-done((f32[32,8,128]{2,1,0:T(8,128)S(1)}, f32[32,8,128]{2,1,0:T(8,128)S(1)}, u32[]{:S(2)}, u32[]{:S(2)}) %collective-permute-start.7) | collective-permute-done | bytes 131104 | tf_op jit(solution)/shard_map/ppermute | solution.py:386
  47.0 0.0 collective-permute-done.8.after
  47.0 12.7 %second_cycle.1 = f32[16,4,8,128]{3,2,1,0:T(8,128)} custom-call(f32[32,8,128]{2,1,0:T(8,128)S(1)} %collective-permute-done.7.before, f32[65,8,128]{2,1,0:T(8,128)S(1)} %add_add_fusion.own, f32[40,8,128]{2,1,0:T(8,128)S(1)} %collective-permute-done.8.after), custom_call_target="tpu_custom_call" | custom-call | flops 131072000 | bytes 1048576 | tf_op jit(solution)/shard_map/second_cycle/pallas_call | solution.py:390
  59.7 0.0 copy-start.3
  59.7 4.6 %all-to-all-start = ((f32[16,4,8,128]{3,2,1,0:T(8,128)}), f32[16,4,8,128]{3,2,1,0:T(8,128)S(1)}, u32[]{:S(2)}, u32[]{:S(2)}) async-start(f32[16,4,8,128]{3,2,1,0:T(8,128)} %second_cycle.1), calls=%async_computation | async-start | bytes 524288 | tf_op jit(solution)/shard_map/all_to_all | solution.py:405
  64.2 0.0 copy-done.3
  64.3 0.0 copy-start.4
  64.3 0.6 copy-done.4
  64.9 0.1 add_convert_fusion.matrix
  65.1 9.2 %all-to-all-done.rows = f32[16,4,8,128]{3,2,1,0:T(8,128)S(1)} async-done(((f32[16,4,8,128]{3,2,1,0:T(8,128)}), f32[16,4,8,128]{3,2,1,0:T(8,128)S(1)}, u32[]{:S(2)}, u32[]{:S(2)}) %all-to-all-start) | async-done | bytes 262176 | tf_op jit(solution)/shard_map/all_to_all | solution.py:405
  74.3 0.4 hierarchise.1
  74.6 1.1 %collective-permute-start.10 = (f32[4,32,128]{2,1,0:T(8,128)S(1)}, f32[4,32,128]{2,1,0:T(8,128)S(1)}, u32[]{:S(2)}, u32[]{:S(2)}) collective-permute-start(f32[4,32,128]{2,1,0:T(8,128)S(1)} %get-tuple-element.29), channel_id=1, source_target_pairs={{0,8},{4,12},{8,0},{12,4},{1,9},{5,13},{9,1},{13,5},{2,10},{6,14},... | collective-permute-start | bytes 196616 | tf_op jit(solution)/shard_map/ppermute | solution.py:428
  75.7 0.8 collective-permute-start.11
  76.5 1.2 %collective-permute-start.9 = (f32[4,32,128]{2,1,0:T(8,128)S(1)}, f32[4,32,128]{2,1,0:T(8,128)S(1)}, u32[]{:S(2)}, u32[]{:S(2)}) collective-permute-start(f32[4,32,128]{2,1,0:T(8,128)S(1)} %get-tuple-element.28), channel_id=1, source_target_pairs={{0,4},{4,8},{8,12},{12,0},{1,5},{5,9},{9,13},{13,1},{2,6},{6,10},{... | collective-permute-start | bytes 196616 | tf_op jit(solution)/shard_map/ppermute | solution.py:428
  77.7 3.2 %collective-permute-done.10.refs_2_ = f32[4,32,128]{2,1,0:T(8,128)S(1)} collective-permute-done((f32[4,32,128]{2,1,0:T(8,128)S(1)}, f32[4,32,128]{2,1,0:T(8,128)S(1)}, u32[]{:S(2)}, u32[]{:S(2)}) %collective-permute-start.10) | collective-permute-done | bytes 65568 | tf_op jit(solution)/shard_map/ppermute | solution.py:428
  81.0 0.3 collective-permute-done.11.refs_3_
  81.3 1.8 %collective-permute-done.9.refs_1_ = f32[4,32,128]{2,1,0:T(8,128)S(1)} collective-permute-done((f32[4,32,128]{2,1,0:T(8,128)S(1)}, f32[4,32,128]{2,1,0:T(8,128)S(1)}, u32[]{:S(2)}, u32[]{:S(2)}) %collective-permute-start.9) | collective-permute-done | bytes 65568 | tf_op jit(solution)/shard_map/ppermute | solution.py:428
  83.1 0.8 place.1
  (5 shorter events, 0.1 us)
Async XLA Ops:
  0.0 1.2 %copy-start = (f32[1,32,64,128]{3,2,1,0:T(8,128)S(1)}, f32[1,32,64,128]{3,2,1,0:T(8,128)}, u32[]{:S(2)}) copy-start(f32[1,32,64,128]{3,2,1,0:T(8,128)} %param.4) | copy-start | bytes 3145732
  1.2 8.1 %copy-start.1 = (f32[1,32,64,128]{3,2,1,0:T(8,128)S(1)}, f32[1,32,64,128]{3,2,1,0:T(8,128)}, u32[]{:S(2)}) copy-start(f32[1,32,64,128]{3,2,1,0:T(8,128)} %param.4) | copy-start | bytes 3145732
  1.6 7.7 %copy-start.2 = (s32[1,5]{1,0:T(1,128)S(1)}, s32[1,5]{1,0:T(1,128)}, u32[]{:S(2)}) copy-start(s32[1,5]{1,0:T(1,128)} %level.3) | copy-start | bytes 64
  1.6 7.7 %collective-permute-start.1 = (f32[5,64,128]{2,1,0:T(8,128)S(1)}, f32[5,64,128]{2,1,0:T(8,128)S(1)}, u32[]{:S(2)}, u32[]{:S(2)}) collective-permute-start(f32[5,64,128]{2,1,0:T(8,128)S(1)} %get-tuple-element.19), channel_id=1, source_target_pairs={{1,0},{2,1},{3,2},{0,3},{5,4},{6,5},{7,6},{4,7},{9,8},{10,9},{11,1... | collective-permute-start | bytes 491528 | tf_op jit(solution)/shard_map/ppermute | solution.py:356
  4.1 5.3 %collective-permute-start = (f32[4,64,128]{2,1,0:T(8,128)S(1)}, f32[4,64,128]{2,1,0:T(8,128)S(1)}, u32[]{:S(2)}, u32[]{:S(2)}) collective-permute-start(f32[4,64,128]{2,1,0:T(8,128)S(1)} %get-tuple-element.18), channel_id=1, source_target_pairs={{0,1},{1,2},{2,3},{3,0},{4,5},{5,6},{6,7},{7,4},{8,9},{9,10},{10,1... | collective-permute-start | bytes 393224 | tf_op jit(solution)/shard_map/ppermute | solution.py:355
  14.6 13.5 %collective-permute-start.5 = (f32[65,8,128]{2,1,0:T(8,128)S(1)}, f32[65,8,128]{2,1,0:T(8,128)S(1)}, u32[]{:S(2)}, u32[]{:S(2)}) collective-permute-start(f32[65,8,128]{2,1,0:T(8,128)S(1)} %get-tuple-element.23), channel_id=1, source_target_pairs={{0,4},{12,8},{1,5},{13,9},{2,6},{14,10},{3,7},{15,11},{16,20},{28,... | collective-permute-start | bytes 798728 | tf_op jit(solution)/shard_map/ppermute | solution.py:372
  18.1 11.3 %collective-permute-start.2 = (f32[65,8,128]{2,1,0:T(8,128)S(1)}, f32[65,8,128]{2,1,0:T(8,128)S(1)}, u32[]{:S(2)}, u32[]{:S(2)}) collective-permute-start(f32[65,8,128]{2,1,0:T(8,128)S(1)} %get-tuple-element.21), channel_id=1, source_target_pairs={{4,8},{8,4},{5,9},{9,5},{6,10},{10,6},{7,11},{11,7},{20,24},{24,20... | collective-permute-start | bytes 798728 | tf_op jit(solution)/shard_map/ppermute | solution.py:373
  18.8 11.7 %collective-permute-start.3 = (f32[65,8,128]{2,1,0:T(8,128)S(1)}, f32[65,8,128]{2,1,0:T(8,128)S(1)}, u32[]{:S(2)}, u32[]{:S(2)}) collective-permute-start(f32[65,8,128]{2,1,0:T(8,128)S(1)} %get-tuple-element.21), channel_id=1, source_target_pairs={{0,8},{12,4},{1,9},{13,5},{2,10},{14,6},{3,11},{15,7},{16,24},{28,... | collective-permute-start | bytes 798728 | tf_op jit(solution)/shard_map/ppermute | solution.py:374
  28.0 13.1 %collective-permute-start.4 = (f32[65,8,128]{2,1,0:T(8,128)S(1)}, f32[65,8,128]{2,1,0:T(8,128)S(1)}, u32[]{:S(2)}, u32[]{:S(2)}) collective-permute-start(f32[65,8,128]{2,1,0:T(8,128)S(1)} %get-tuple-element.22), channel_id=1, source_target_pairs={{0,4},{4,0},{8,12},{12,8},{1,5},{5,1},{9,13},{13,9},{2,6},{6,2},{1... | collective-permute-start | bytes 798728 | tf_op jit(solution)/shard_map/ppermute | solution.py:376
  28.1 13.0 %collective-permute-start.6 = (f32[65,8,128]{2,1,0:T(8,128)S(1)}, f32[65,8,128]{2,1,0:T(8,128)S(1)}, u32[]{:S(2)}, u32[]{:S(2)}) collective-permute-start(f32[65,8,128]{2,1,0:T(8,128)S(1)} %add.39), channel_id=1, source_target_pairs={{4,12},{8,0},{5,13},{9,1},{6,14},{10,2},{7,15},{11,3},{20,28},{24,... | collective-permute-start | bytes 798728 | tf_op jit(solution)/shard_map/ppermute | solution.py:377
  41.2 5.8 %collective-permute-start.8 = (f32[40,8,128]{2,1,0:T(8,128)S(1)}, f32[40,8,128]{2,1,0:T(8,128)S(1)}, u32[]{:S(2)}, u32[]{:S(2)}) collective-permute-start(f32[40,8,128]{2,1,0:T(8,128)S(1)} %slice.9), channel_id=1, source_target_pairs={{4,0},{8,4},{12,8},{13,12},{9,13},{5,9},{1,5},{2,1},{6,2},{10,6},{... | collective-permute-start | bytes 491528 | tf_op jit(solution)/shard_map/ppermute | solution.py:387
  41.3 5.7 %collective-permute-start.7 = (f32[32,8,128]{2,1,0:T(8,128)S(1)}, f32[32,8,128]{2,1,0:T(8,128)S(1)}, u32[]{:S(2)}, u32[]{:S(2)}) collective-permute-start(f32[32,8,128]{2,1,0:T(8,128)S(1)} %slice.8), channel_id=1, source_target_pairs={{0,4},{4,8},{8,12},{12,13},{13,9},{9,5},{5,1},{1,2},{2,6},{6,10},{... | collective-permute-start | bytes 393224 | tf_op jit(solution)/shard_map/ppermute | solution.py:386
  59.7 4.6 %copy-start.3 = (s32[128]{0:T(128)S(1)}, s32[128]{0:T(128)}, u32[]{:S(2)}) copy-start(s32[128]{0:T(128)} %param.6) | copy-start | bytes 1540
  59.7 14.6 %all-to-all-start = ((f32[16,4,8,128]{3,2,1,0:T(8,128)}), f32[16,4,8,128]{3,2,1,0:T(8,128)S(1)}, u32[]{:S(2)}, u32[]{:S(2)}) async-start(f32[16,4,8,128]{3,2,1,0:T(8,128)} %second_cycle.1), calls=%async_computation | async-start | bytes 524288 | tf_op jit(solution)/shard_map/all_to_all | solution.py:405
  64.3 0.7 copy-start.4
  74.6 6.3 %collective-permute-start.10 = (f32[4,32,128]{2,1,0:T(8,128)S(1)}, f32[4,32,128]{2,1,0:T(8,128)S(1)}, u32[]{:S(2)}, u32[]{:S(2)}) collective-permute-start(f32[4,32,128]{2,1,0:T(8,128)S(1)} %get-tuple-element.29), channel_id=1, source_target_pairs={{0,8},{4,12},{8,0},{12,4},{1,9},{5,13},{9,1},{13,5},{2,10},{6,14},... | collective-permute-start | bytes 196616 | tf_op jit(solution)/shard_map/ppermute | solution.py:428
  75.7 5.6 %collective-permute-start.11 = (f32[4,32,128]{2,1,0:T(8,128)S(1)}, f32[4,32,128]{2,1,0:T(8,128)S(1)}, u32[]{:S(2)}, u32[]{:S(2)}) collective-permute-start(f32[4,32,128]{2,1,0:T(8,128)S(1)} %get-tuple-element.30), channel_id=1, source_target_pairs={{0,12},{4,0},{8,4},{12,8},{1,13},{5,1},{9,5},{13,9},{2,14},{6,2},{... | collective-permute-start | bytes 196616 | tf_op jit(solution)/shard_map/ppermute | solution.py:428
  76.5 6.6 %collective-permute-start.9 = (f32[4,32,128]{2,1,0:T(8,128)S(1)}, f32[4,32,128]{2,1,0:T(8,128)S(1)}, u32[]{:S(2)}, u32[]{:S(2)}) collective-permute-start(f32[4,32,128]{2,1,0:T(8,128)S(1)} %get-tuple-element.28), channel_id=1, source_target_pairs={{0,4},{4,8},{8,12},{12,0},{1,5},{5,9},{9,13},{13,1},{2,6},{6,10},{... | collective-permute-start | bytes 196616 | tf_op jit(solution)/shard_map/ppermute | solution.py:428

commit v4 on v3

--- a/solution.py
+++ b/solution.py
@@ -128,47 +128,54 @@
 UNROLL = 2
 
 
-def step_rows(src, dst, first, groups, factors):
-    advect, spread, centre_spread, centre_advect = factors
-    twice = spread[1] + spread[1]
-
-    def body(group, carry):
+def stencil(scales):
+    size = TILES * N2
+    shape = (size, 2 * size)
+    row = lax.broadcasted_iota(jnp.int32, shape, 0)
+    column = lax.bitwise_and(lax.broadcasted_iota(jnp.int32, shape, 1), size - 1)
+    total = sum(scales[1:], scales[0])
+    squares = [value * value for value in scales]
+    square = sum(squares[1:], squares[0])
+    drift = jnp.where(row == column, -total, 0.0)
+    second = jnp.where(row == column, -2.0 * square, 0.0)
+    for d, unit, count in ((1, N3 * N2, N1), (2, 1, N2), (3, N2, N3)):
+        digit = lax.bitwise_and(lax.div(row, unit), count - 1)
+        rest = row - digit * unit
+        back = column == rest + lax.bitwise_and(digit + count - 1, count - 1) * unit
+        ahead = column == rest + lax.bitwise_and(digit + 1, count - 1) * unit
+        drift = drift + jnp.where(back, scales[d], 0.0)
+        second = second + jnp.where(back, squares[d], 0.0) + jnp.where(ahead, squares[d], 0.0)
+    return jnp.concatenate([second, drift], axis=0).astype(jnp.bfloat16)
+
+
+def step_rows(src, dst, first, groups, matrix, factors, products):
+    s0, q0, s4, q4 = factors
+    size = TILES * N2
+
+    def multiply(group):
         base = first + group * UNROLL
-        for offset in range(UNROLL):
-            row = base + offset
-            tiles = [src[row, t] for t in range(TILES)]
-            for n1 in range(N1):
-                for n3 in range(N3):
-                    t = n1 * N3 + n3
-                    u = tiles[t]
-                    other = tiles[(1 - n1) * N3 + n3]
-                    neighbours = (
-                        (0, src[row - 1, t], src[row + 1, t]),
-                        (2, pltpu.roll(u, 1, 0), pltpu.roll(u, N2 - 1, 0)),
-                        (3, tiles[n1 * N3 + (n3 - 1) % N3], tiles[n1 * N3 + (n3 + 1) % N3]),
-                        (4, pltpu.roll(u, 1, 1), pltpu.roll(u, N4 - 1, 1)),
-                    )
-                    drift = advect[1] * other - centre_advect * u
-                    update = twice * other + centre_spread * u
-                    for d, back, ahead in neighbours:
-                        drift = drift + advect[d] * back
-                        update = update + spread[d] * (back + ahead)
-                    dst[row, t] = update + (2.0 + jnp.tanh(u)) * drift
-        return carry
-
-    lax.fori_loop(0, groups, body, 0)
-
-
-def factors_of(scales):
-    advect = [(0.5 * ADVECT) * s for s in scales]
-    spread = [DIFFUSE * (s * s) for s in scales]
-    total = spread[0]
-    for value in spread[1:]:
-        total = total + value
-    centre = advect[0]
-    for value in advect[1:]:
-        centre = centre + value
-    return advect, spread, 1.0 - 2.0 * total, centre
+        value = jnp.concatenate([src[base + i].reshape(size, N4) for i in range(UNROLL)], axis=1)
+        high = value.astype(jnp.bfloat16)
+        rest = (value - high.astype(jnp.float32)).astype(jnp.bfloat16)
+        products[group % 2][...] = jnp.dot(
+            matrix[...], jnp.concatenate([high, rest], axis=0), preferred_element_type=jnp.float32
+        )
+
+    multiply(0)
+    for group in range(groups):
+        if group + 1 < groups:
+            multiply(group + 1)
+        product = products[group % 2]
+        for i in range(UNROLL):
+            row = first + group * UNROLL + i
+            lanes = slice(i * N4, (i + 1) * N4)
+            for t in range(TILES):
+                u, below, above = src[row, t], src[row - 1, t], src[row + 1, t]
+                left, right = pltpu.roll(u, 1, 1), pltpu.roll(u, N4 - 1, 1)
+                second = product[t * N2 : (t + 1) * N2, lanes] + q0 * (below + above) + q4 * (left + right)
+                drift = product[size + t * N2 : size + (t + 1) * N2, lanes] + s0 * below + s4 * left
+                speed = ADVECT + (0.5 * ADVECT) * jnp.tanh(u)
+                dst[row, t] = (u + DIFFUSE * second) + speed * drift
 
 
 def interpolate(nodes, fine, middle):
@@ -179,15 +186,22 @@
     return u0, v1, v2, v3
 
 
-def state_space(rows):
-    return pltpu.VMEM((rows + LOW + HIGH + UNROLL, TILES, N2, N4), jnp.float32)
-
-
-def run_steps(bufs, rows, factors):
+def spaces(rows):
+    state = pltpu.VMEM((rows + LOW + HIGH + UNROLL, TILES, N2, N4), jnp.float32)
+    size = TILES * N2
+    product = pltpu.VMEM((2 * size, UNROLL * N4), jnp.float32)
+    return [state, state, product, product, pltpu.VMEM((2 * size, 2 * size), jnp.bfloat16)]
+
+
+def run_steps(bufs, rows, scales):
+    states, products, matrix = bufs[0:2], bufs[2:4], bufs[4]
+    matrix[...] = stencil(scales)
+    factors = (scales[0], scales[0] * scales[0], scales[4], scales[4] * scales[4])
     for step in range(STEPS):
         count = rows + LOW + HIGH - 2 * (step + 1)
-        step_rows(bufs[step % 2], bufs[(step + 1) % 2], step + 1, -(-count // UNROLL), factors)
-    return bufs[STEPS % 2]
+        groups = -(-count // UNROLL)
+        step_rows(states[step % 2], states[(step + 1) % 2], step + 1, groups, matrix, factors, products)
+    return states[STEPS % 2]
 
 
 def ends_kernel(field, last, first, sems):
@@ -228,7 +242,7 @@
     scales = [lax.shift_left(1, v).astype(jnp.float32) * 0.125 for v in levels]
     parity = lax.rem(levels[0] + levels[1] + levels[2] + levels[3] + levels[4], 2)
     weight = (1 - 2 * parity).astype(jnp.float32) * (1.0 / math.sqrt(lax.axis_size("grid")))
-    done = run_steps(bufs, half, factors_of(scales))
+    done = run_steps(bufs, half, scales)
     fine, middle = levels[0] >= 3, levels[0] >= 2
     block = half // 2
     ends = jnp.logical_or(me == 0, me == grids - 1)
@@ -258,10 +272,13 @@
         wide[LOW * TILES + i] = own[i]
     for i in range(HIGH * TILES):
         wide[(LOW + rows) * TILES + i] = after[i]
-    for g in range(grids):
-        spread = lambda d: jnp.broadcast_to(own[rows * TILES, g : g + 1, d : d + 1], (N2, N4))
-        factors = factors_of([spread(d) for d in range(5)])
-        fine, middle, weight = spread(5) > 2.5, spread(5) > 1.5, spread(6)
+    total[...] = jnp.zeros_like(total)
+
+    def grid(g, carry):
+        spread = lambda d: jnp.broadcast_to(own[rows * TILES, pl.ds(g, 1), d : d + 1], (1, N4))
+        scales = [spread(d) for d in range(5)]
+        wide_of = lambda value: jnp.broadcast_to(value, (N2, N4))
+        fine, middle, weight = wide_of(spread(5)) > 2.5, wide_of(spread(5)) > 1.5, wide_of(spread(6))
         start = bufs[0]
         for quad in range(0, extent - 1, 4):
             for t in range(TILES):
@@ -270,13 +287,16 @@
                     start[quad + i, t] = value
         for t in range(TILES):
             start[extent - 1, t] = wide[(extent - 1) * TILES + t]
-        done = run_steps(bufs, rows, factors)
+        done = run_steps(bufs, rows, scales)
         for quad in range(0, rows, 4):
             for t in range(TILES):
                 values = interpolate([done[LOW + quad + i, t] for i in range(5)], fine, middle)
                 for i, value in enumerate(values):
                     at = pl.ds(((quad + i) * TILES + t) * N2, N2)
-                    total[at, :] = weight * value + (total[at, :] if g else 0.0)
+                    total[at, :] = weight * value + total[at, :]
+        return carry
+
+    lax.fori_loop(0, grids, grid, 0)
     half = N2 // 2
     for n3 in range(N3):
         for n1 in range(N1):
@@ -363,7 +383,7 @@
             "first_cycle",
             [piece, piece],
             [SMEM, VMEM, VMEM, VMEM],
-            [state_space(rows // 2)] * 2,
+            spaces(rows // 2),
             limit=8,
             flops=160 * 8192 * 40,
         )(levels, before, state, after)
@@ -395,9 +415,8 @@
         [
             pltpu.VMEM((block * TILES * N2, N4), jnp.float32),
             pltpu.VMEM(((block + LOW + HIGH) * TILES, N2, N4), jnp.float32),
-            state_space(block),
-            state_space(block),
-        ],
+        ]
+        + spaces(block),
         limit=8,
         flops=400 * 8192 * 40,
     )(before, own, after)

time: 84.2 us -> 73.8 us (0.88)
  Pallas kernels: 24.7 us -> 14.3 us
    pallas_call x1, Pallas kernels: 12.7 us -> 6.82 us  [local_fast(): kernel(functools.partial(second_kernel, block, grids), 'second_cycle', fl...]
    pallas_call x2, Pallas kernels: 10.4 us -> 5.93 us  [half_slab(): kernel(functools.partial(first_kernel, later), 'first_cycle', [piece, pie...]
    ppermute x1, waiting for transfers between devices: 10.6 us -> 8.31 us  [local_fast(): swapped = lax.ppermute(near, 'grid', [(0, 1), (1, 0), (2, 3), (3, 2)])]
    ppermute x1, waiting for transfers between devices: 1.08 us -> 3.32 us  [local_fast(): skipped = lax.ppermute(middle, 'grid', [(0, 2), (3, 1)])]
  transfers between devices with their start and end apart: 13 -> 13, of which waited for: 8 -> 8; matrix products, arithmetic and copies ran while one was open for 0% -> 0% of each run, Pallas kernels for 6% -> 4%
where the time goes in v4:
time: 73.8 us; the launch traced here: 73.5 us
  waiting for transfers between devices  35.7 us (48%)
  starting transfers between devices  21.1 us (29%)
  Pallas kernels  14.3 us (19%)
  local copies, waits for them, and re-layouts  1.91 us (3%)
    all_to_all x1, waiting for transfers between devices, local_fast(): spread = lax.all_to_all(sent, both, split_axis=0, concat_axis=0, tiled=True)  9.17 us
    ppermute x1, waiting for transfers between devices, local_fast(): swapped = lax.ppermute(near, 'grid', [(0, 1), (1, 0), (2, 3), (3, 2)])  8.31 us
    pallas_call x1, Pallas kernels, local_fast(): kernel(functools.partial(second_kernel, block, grids), 'second_cycle', fl...  6.82 us
    pallas_call x2, Pallas kernels, half_slab(): kernel(functools.partial(first_kernel, later), 'first_cycle', [piece, pie...  5.93 us
    ppermute x3, waiting for transfers between devices, local_fast(): lax.ppermute(value, 'grid', [(i, (i + d) % grids) for i in range(grids)])  5.32 us
    ppermute x1, waiting for transfers between devices, local_fast(): before = lax.ppermute(last, 'slab', up)  5.26 us
    ppermute x1, waiting for transfers between devices, local_fast(): lax.ppermute(own[(block - LOW) * TILES:block * TILES], both, forward)  4.29 us
    ppermute x1, starting transfers between devices, local_fast(): skipped = lax.ppermute(middle, 'grid', [(0, 2), (3, 1)])  3.98 us
  transfers between devices with their start and end apart: 13, of which 8 were waited for; matrix products, arithmetic and copies ran while one was open for 0% of the time, Pallas kernels for 4%

profile of v4, /device:TPU:0, one launch (start us, length us, event | category | flops | bytes accessed | tf_op | source)
XLA Modules:
  0.0 73.5 jit_solution(11263372855519370899)
XLA Ops:
  0.0 0.0 copy-start
  0.0 1.2 %copy-done = f32[1,32,64,128]{3,2,1,0:T(8,128)S(1)} copy-done((f32[1,32,64,128]{3,2,1,0:T(8,128)S(1)}, f32[1,32,64,128]{3,2,1,0:T(8,128)}, u32[]{:S(2)}) %copy-start) | copy-done | bytes 1048600
  1.2 0.0 copy-start.1
  1.2 0.4 ends.1
  1.6 0.0 copy-start.2
  1.6 2.5 %collective-permute-start.1 = (f32[5,64,128]{2,1,0:T(8,128)S(1)}, f32[5,64,128]{2,1,0:T(8,128)S(1)}, u32[]{:S(2)}, u32[]{:S(2)}) collective-permute-start(f32[5,64,128]{2,1,0:T(8,128)S(1)} %get-tuple-element.19), channel_id=1, source_target_pairs={{1,0},{2,1},{3,2},{0,3},{5,4},{6,5},{7,6},{4,7},{9,8},{10,9},{11,1... | collective-permute-start | bytes 491528 | tf_op jit(solution)/shard_map/ppermute | solution.py:376
  4.1 0.0 collective-permute-start
  4.1 5.3 %collective-permute-done.before = f32[4,64,128]{2,1,0:T(8,128)S(1)} collective-permute-done((f32[4,64,128]{2,1,0:T(8,128)S(1)}, f32[4,64,128]{2,1,0:T(8,128)S(1)}, u32[]{:S(2)}, u32[]{:S(2)}) %collective-permute-start) | collective-permute-done | bytes 131104 | tf_op jit(solution)/shard_map/ppermute | solution.py:375
  9.3 0.0 collective-permute-done.1.after
  9.3 0.0 copy-done.1
  9.3 0.0 copy-done.2
  9.4 3.0 %first_cycle.3 = (f32[65,8,128]{2,1,0:T(8,128)S(1)}, f32[65,8,128]{2,1,0:T(8,128)S(1)}) custom-call(s32[1,5]{1,0:T(1,128)S(1)} %copy-done.2, f32[4,64,128]{2,1,0:T(8,128)S(1)} %collective-permute-done.before, f32[32,64,128]{2,1,0:T(8,128)S(1)} %bitcast.3, f32[5,64,128]{2,1,0:T(8,128)S(1)} %collective-permute-done.1.after), custom_call_target="tpu_custom_call" | custom-call | flops 52428800 | bytes 1048576 | tf_op jit(solution)/shard_map/first_cycle/pallas_call | solution.py:381
  12.3 3.5 %collective-permute-start.5 = (f32[65,8,128]{2,1,0:T(8,128)S(1)}, f32[65,8,128]{2,1,0:T(8,128)S(1)}, u32[]{:S(2)}, u32[]{:S(2)}) collective-permute-start(f32[65,8,128]{2,1,0:T(8,128)S(1)} %get-tuple-element.23), channel_id=1, source_target_pairs={{0,4},{12,8},{1,5},{13,9},{2,6},{14,10},{3,7},{15,11},{16,20},{28,... | collective-permute-start | bytes 798728 | tf_op jit(solution)/shard_map/ppermute | solution.py:392
  15.8 0.7 collective-permute-start.2
  16.5 4.0 %collective-permute-start.3 = (f32[65,8,128]{2,1,0:T(8,128)S(1)}, f32[65,8,128]{2,1,0:T(8,128)S(1)}, u32[]{:S(2)}, u32[]{:S(2)}) collective-permute-start(f32[65,8,128]{2,1,0:T(8,128)S(1)} %get-tuple-element.21), channel_id=1, source_target_pairs={{0,8},{12,4},{1,9},{13,5},{2,10},{14,6},{3,11},{15,7},{16,24},{28,... | collective-permute-start | bytes 798728 | tf_op jit(solution)/shard_map/ppermute | solution.py:394
  20.5 3.0 %first_cycle.2 = (f32[65,8,128]{2,1,0:T(8,128)S(1)}, f32[65,8,128]{2,1,0:T(8,128)S(1)}) custom-call(s32[1,5]{1,0:T(1,128)S(1)} %copy-done.2, f32[4,64,128]{2,1,0:T(8,128)S(1)} %collective-permute-done.before, f32[32,64,128]{2,1,0:T(8,128)S(1)} %bitcast.4, f32[5,64,128]{2,1,0:T(8,128)S(1)} %collective-permute-done.1.after), custom_call_target="tpu_custom_call" | custom-call | flops 52428800 | bytes 1048576 | tf_op jit(solution)/shard_map/first_cycle/pallas_call | solution.py:381
  23.5 0.1 collective-permute-start.4
  23.6 0.0 collective-permute-done.5
  23.6 1.3 %collective-permute-start.6 = (f32[65,8,128]{2,1,0:T(8,128)S(1)}, f32[65,8,128]{2,1,0:T(8,128)S(1)}, u32[]{:S(2)}, u32[]{:S(2)}) collective-permute-start(f32[65,8,128]{2,1,0:T(8,128)S(1)} %add.39), channel_id=1, source_target_pairs={{4,12},{8,0},{5,13},{9,1},{6,14},{10,2},{7,15},{11,3},{20,28},{24,... | collective-permute-start | bytes 798728 | tf_op jit(solution)/shard_map/ppermute | solution.py:397
  24.9 0.0 collective-permute-done.2
  24.9 3.3 %collective-permute-done.3 = f32[65,8,128]{2,1,0:T(8,128)S(1)} collective-permute-done((f32[65,8,128]{2,1,0:T(8,128)S(1)}, f32[65,8,128]{2,1,0:T(8,128)S(1)}, u32[]{:S(2)}, u32[]{:S(2)}) %collective-permute-start.3) | collective-permute-done | bytes 266272 | tf_op jit(solution)/shard_map/ppermute | solution.py:394
  28.2 8.3 %collective-permute-done.4 = f32[65,8,128]{2,1,0:T(8,128)S(1)} collective-permute-done((f32[65,8,128]{2,1,0:T(8,128)S(1)}, f32[65,8,128]{2,1,0:T(8,128)S(1)}, u32[]{:S(2)}, u32[]{:S(2)}) %collective-permute-start.4) | collective-permute-done | bytes 266272 | tf_op jit(solution)/shard_map/ppermute | solution.py:396
  36.6 0.0 collective-permute-done.6
  36.6 0.1 add_add_fusion.own
  36.7 0.6 collective-permute-start.8
  37.3 1.6 %collective-permute-start.7 = (f32[32,8,128]{2,1,0:T(8,128)S(1)}, f32[32,8,128]{2,1,0:T(8,128)S(1)}, u32[]{:S(2)}, u32[]{:S(2)}) collective-permute-start(f32[32,8,128]{2,1,0:T(8,128)S(1)} %slice.8), channel_id=1, source_target_pairs={{0,4},{4,8},{8,12},{12,13},{13,9},{9,5},{5,1},{1,2},{2,6},{6,10},{... | collective-permute-start | bytes 393224 | tf_op jit(solution)/shard_map/ppermute | solution.py:406
  38.8 4.3 %collective-permute-done.7.before = f32[32,8,128]{2,1,0:T(8,128)S(1)} collective-permute-done((f32[32,8,128]{2,1,0:T(8,128)S(1)}, f32[32,8,128]{2,1,0:T(8,128)S(1)}, u32[]{:S(2)}, u32[]{:S(2)}) %collective-permute-start.7) | collective-permute-done | bytes 131104 | tf_op jit(solution)/shard_map/ppermute | solution.py:406
  43.1 0.0 collective-permute-done.8.after
  43.1 6.8 %second_cycle.1 = f32[16,4,8,128]{3,2,1,0:T(8,128)} custom-call(f32[32,8,128]{2,1,0:T(8,128)S(1)} %collective-permute-done.7.before, f32[65,8,128]{2,1,0:T(8,128)S(1)} %add_add_fusion.own, f32[40,8,128]{2,1,0:T(8,128)S(1)} %collective-permute-done.8.after), custom_call_target="tpu_custom_call" | custom-call | flops 131072000 | bytes 1048576 | tf_op jit(solution)/shard_map/second_cycle/pallas_call | solution.py:410
  50.0 0.0 copy-start.3
  50.0 3.9 %all-to-all-start = ((f32[16,4,8,128]{3,2,1,0:T(8,128)}), f32[16,4,8,128]{3,2,1,0:T(8,128)S(1)}, u32[]{:S(2)}, u32[]{:S(2)}) async-start(f32[16,4,8,128]{3,2,1,0:T(8,128)} %second_cycle.1), calls=%async_computation | async-start | bytes 524288 | tf_op jit(solution)/shard_map/all_to_all | solution.py:424
  53.9 0.0 copy-done.3
  53.9 0.0 copy-start.4
  53.9 0.6 copy-done.4
  54.6 0.1 add_convert_fusion.matrix
  54.7 9.2 %all-to-all-done.rows = f32[16,4,8,128]{3,2,1,0:T(8,128)S(1)} async-done(((f32[16,4,8,128]{3,2,1,0:T(8,128)}), f32[16,4,8,128]{3,2,1,0:T(8,128)S(1)}, u32[]{:S(2)}, u32[]{:S(2)}) %all-to-all-start) | async-done | bytes 262176 | tf_op jit(solution)/shard_map/all_to_all | solution.py:424
  63.9 0.4 hierarchise.1
  64.3 1.1 %collective-permute-start.10 = (f32[4,32,128]{2,1,0:T(8,128)S(1)}, f32[4,32,128]{2,1,0:T(8,128)S(1)}, u32[]{:S(2)}, u32[]{:S(2)}) collective-permute-start(f32[4,32,128]{2,1,0:T(8,128)S(1)} %get-tuple-element.29), channel_id=1, source_target_pairs={{0,8},{4,12},{8,0},{12,4},{1,9},{5,13},{9,1},{13,5},{2,10},{6,14},... | collective-permute-start | bytes 196616 | tf_op jit(solution)/shard_map/ppermute | solution.py:447
  65.3 0.8 %collective-permute-start.11 = (f32[4,32,128]{2,1,0:T(8,128)S(1)}, f32[4,32,128]{2,1,0:T(8,128)S(1)}, u32[]{:S(2)}, u32[]{:S(2)}) collective-permute-start(f32[4,32,128]{2,1,0:T(8,128)S(1)} %get-tuple-element.30), channel_id=1, source_target_pairs={{0,12},{4,0},{8,4},{12,8},{1,13},{5,1},{9,5},{13,9},{2,14},{6,2},{... | collective-permute-start | bytes 196616 | tf_op jit(solution)/shard_map/ppermute | solution.py:447
  66.1 1.2 %collective-permute-start.9 = (f32[4,32,128]{2,1,0:T(8,128)S(1)}, f32[4,32,128]{2,1,0:T(8,128)S(1)}, u32[]{:S(2)}, u32[]{:S(2)}) collective-permute-start(f32[4,32,128]{2,1,0:T(8,128)S(1)} %get-tuple-element.28), channel_id=1, source_target_pairs={{0,4},{4,8},{8,12},{12,0},{1,5},{5,9},{9,13},{13,1},{2,6},{6,10},{... | collective-permute-start | bytes 196616 | tf_op jit(solution)/shard_map/ppermute | solution.py:447
  67.4 3.2 %collective-permute-done.10.refs_2_ = f32[4,32,128]{2,1,0:T(8,128)S(1)} collective-permute-done((f32[4,32,128]{2,1,0:T(8,128)S(1)}, f32[4,32,128]{2,1,0:T(8,128)S(1)}, u32[]{:S(2)}, u32[]{:S(2)}) %collective-permute-start.10) | collective-permute-done | bytes 65568 | tf_op jit(solution)/shard_map/ppermute | solution.py:447
  70.6 0.3 collective-permute-done.11.refs_3_
  70.9 1.8 %collective-permute-done.9.refs_1_ = f32[4,32,128]{2,1,0:T(8,128)S(1)} collective-permute-done((f32[4,32,128]{2,1,0:T(8,128)S(1)}, f32[4,32,128]{2,1,0:T(8,128)S(1)}, u32[]{:S(2)}, u32[]{:S(2)}) %collective-permute-start.9) | collective-permute-done | bytes 65568 | tf_op jit(solution)/shard_map/ppermute | solution.py:447
  72.7 0.8 %place.1 = f32[512,128]{1,0:T(8,128)} custom-call(f32[4,32,128]{2,1,0:T(8,128)S(1)} %get-tuple-element.24.refs_0_, f32[4,32,128]{2,1,0:T(8,128)S(1)} %collective-permute-done.9.refs_1_, f32[4,32,128]{2,1,0:T(8,128)S(1)} %collective-permute-done.10.refs_2_, f32[4,32,128]{2,1,0:T(8,128)S(1)} %collective-permute-done.11.refs_3_), custom_call_target="tpu_custom_call" | custom-call | bytes 1048576 | tf_op jit(solution)/shard_map/place/pallas_call | solution.py:450
  (5 shorter events, 0.1 us)
Async XLA Ops:
  0.0 1.2 %copy-start = (f32[1,32,64,128]{3,2,1,0:T(8,128)S(1)}, f32[1,32,64,128]{3,2,1,0:T(8,128)}, u32[]{:S(2)}) copy-start(f32[1,32,64,128]{3,2,1,0:T(8,128)} %param.4) | copy-start | bytes 3145732
  1.2 8.1 %copy-start.1 = (f32[1,32,64,128]{3,2,1,0:T(8,128)S(1)}, f32[1,32,64,128]{3,2,1,0:T(8,128)}, u32[]{:S(2)}) copy-start(f32[1,32,64,128]{3,2,1,0:T(8,128)} %param.4) | copy-start | bytes 3145732
  1.6 7.7 %copy-start.2 = (s32[1,5]{1,0:T(1,128)S(1)}, s32[1,5]{1,0:T(1,128)}, u32[]{:S(2)}) copy-start(s32[1,5]{1,0:T(1,128)} %level.3) | copy-start | bytes 64
  1.6 7.7 %collective-permute-start.1 = (f32[5,64,128]{2,1,0:T(8,128)S(1)}, f32[5,64,128]{2,1,0:T(8,128)S(1)}, u32[]{:S(2)}, u32[]{:S(2)}) collective-permute-start(f32[5,64,128]{2,1,0:T(8,128)S(1)} %get-tuple-element.19), channel_id=1, source_target_pairs={{1,0},{2,1},{3,2},{0,3},{5,4},{6,5},{7,6},{4,7},{9,8},{10,9},{11,1... | collective-permute-start | bytes 491528 | tf_op jit(solution)/shard_map/ppermute | solution.py:376
  4.1 5.3 %collective-permute-start = (f32[4,64,128]{2,1,0:T(8,128)S(1)}, f32[4,64,128]{2,1,0:T(8,128)S(1)}, u32[]{:S(2)}, u32[]{:S(2)}) collective-permute-start(f32[4,64,128]{2,1,0:T(8,128)S(1)} %get-tuple-element.18), channel_id=1, source_target_pairs={{0,1},{1,2},{2,3},{3,0},{4,5},{5,6},{6,7},{7,4},{8,9},{9,10},{10,1... | collective-permute-start | bytes 393224 | tf_op jit(solution)/shard_map/ppermute | solution.py:375
  12.3 11.2 %collective-permute-start.5 = (f32[65,8,128]{2,1,0:T(8,128)S(1)}, f32[65,8,128]{2,1,0:T(8,128)S(1)}, u32[]{:S(2)}, u32[]{:S(2)}) collective-permute-start(f32[65,8,128]{2,1,0:T(8,128)S(1)} %get-tuple-element.23), channel_id=1, source_target_pairs={{0,4},{12,8},{1,5},{13,9},{2,6},{14,10},{3,7},{15,11},{16,20},{28,... | collective-permute-start | bytes 798728 | tf_op jit(solution)/shard_map/ppermute | solution.py:392
  15.8 9.1 %collective-permute-start.2 = (f32[65,8,128]{2,1,0:T(8,128)S(1)}, f32[65,8,128]{2,1,0:T(8,128)S(1)}, u32[]{:S(2)}, u32[]{:S(2)}) collective-permute-start(f32[65,8,128]{2,1,0:T(8,128)S(1)} %get-tuple-element.21), channel_id=1, source_target_pairs={{4,8},{8,4},{5,9},{9,5},{6,10},{10,6},{7,11},{11,7},{20,24},{24,20... | collective-permute-start | bytes 798728 | tf_op jit(solution)/shard_map/ppermute | solution.py:393
  16.5 11.7 %collective-permute-start.3 = (f32[65,8,128]{2,1,0:T(8,128)S(1)}, f32[65,8,128]{2,1,0:T(8,128)S(1)}, u32[]{:S(2)}, u32[]{:S(2)}) collective-permute-start(f32[65,8,128]{2,1,0:T(8,128)S(1)} %get-tuple-element.21), channel_id=1, source_target_pairs={{0,8},{12,4},{1,9},{13,5},{2,10},{14,6},{3,11},{15,7},{16,24},{28,... | collective-permute-start | bytes 798728 | tf_op jit(solution)/shard_map/ppermute | solution.py:394
  23.5 13.1 %collective-permute-start.4 = (f32[65,8,128]{2,1,0:T(8,128)S(1)}, f32[65,8,128]{2,1,0:T(8,128)S(1)}, u32[]{:S(2)}, u32[]{:S(2)}) collective-permute-start(f32[65,8,128]{2,1,0:T(8,128)S(1)} %get-tuple-element.22), channel_id=1, source_target_pairs={{0,4},{4,0},{8,12},{12,8},{1,5},{5,1},{9,13},{13,9},{2,6},{6,2},{1... | collective-permute-start | bytes 798728 | tf_op jit(solution)/shard_map/ppermute | solution.py:396
  23.6 12.9 %collective-permute-start.6 = (f32[65,8,128]{2,1,0:T(8,128)S(1)}, f32[65,8,128]{2,1,0:T(8,128)S(1)}, u32[]{:S(2)}, u32[]{:S(2)}) collective-permute-start(f32[65,8,128]{2,1,0:T(8,128)S(1)} %add.39), channel_id=1, source_target_pairs={{4,12},{8,0},{5,13},{9,1},{6,14},{10,2},{7,15},{11,3},{20,28},{24,... | collective-permute-start | bytes 798728 | tf_op jit(solution)/shard_map/ppermute | solution.py:397
  36.7 6.5 %collective-permute-start.8 = (f32[40,8,128]{2,1,0:T(8,128)S(1)}, f32[40,8,128]{2,1,0:T(8,128)S(1)}, u32[]{:S(2)}, u32[]{:S(2)}) collective-permute-start(f32[40,8,128]{2,1,0:T(8,128)S(1)} %slice.9), channel_id=1, source_target_pairs={{4,0},{8,4},{12,8},{13,12},{9,13},{5,9},{1,5},{2,1},{6,2},{10,6},{... | collective-permute-start | bytes 491528 | tf_op jit(solution)/shard_map/ppermute | solution.py:407
  37.3 5.9 %collective-permute-start.7 = (f32[32,8,128]{2,1,0:T(8,128)S(1)}, f32[32,8,128]{2,1,0:T(8,128)S(1)}, u32[]{:S(2)}, u32[]{:S(2)}) collective-permute-start(f32[32,8,128]{2,1,0:T(8,128)S(1)} %slice.8), channel_id=1, source_target_pairs={{0,4},{4,8},{8,12},{12,13},{13,9},{9,5},{5,1},{1,2},{2,6},{6,10},{... | collective-permute-start | bytes 393224 | tf_op jit(solution)/shard_map/ppermute | solution.py:406
  50.0 3.9 %copy-start.3 = (s32[128]{0:T(128)S(1)}, s32[128]{0:T(128)}, u32[]{:S(2)}) copy-start(s32[128]{0:T(128)} %param.6) | copy-start | bytes 1540
  50.0 13.9 %all-to-all-start = ((f32[16,4,8,128]{3,2,1,0:T(8,128)}), f32[16,4,8,128]{3,2,1,0:T(8,128)S(1)}, u32[]{:S(2)}, u32[]{:S(2)}) async-start(f32[16,4,8,128]{3,2,1,0:T(8,128)} %second_cycle.1), calls=%async_computation | async-start | bytes 524288 | tf_op jit(solution)/shard_map/all_to_all | solution.py:424
  53.9 0.7 copy-start.4
  64.3 6.3 %collective-permute-start.10 = (f32[4,32,128]{2,1,0:T(8,128)S(1)}, f32[4,32,128]{2,1,0:T(8,128)S(1)}, u32[]{:S(2)}, u32[]{:S(2)}) collective-permute-start(f32[4,32,128]{2,1,0:T(8,128)S(1)} %get-tuple-element.29), channel_id=1, source_target_pairs={{0,8},{4,12},{8,0},{12,4},{1,9},{5,13},{9,1},{13,5},{2,10},{6,14},... | collective-permute-start | bytes 196616 | tf_op jit(solution)/shard_map/ppermute | solution.py:447
  65.3 5.6 %collective-permute-start.11 = (f32[4,32,128]{2,1,0:T(8,128)S(1)}, f32[4,32,128]{2,1,0:T(8,128)S(1)}, u32[]{:S(2)}, u32[]{:S(2)}) collective-permute-start(f32[4,32,128]{2,1,0:T(8,128)S(1)} %get-tuple-element.30), channel_id=1, source_target_pairs={{0,12},{4,0},{8,4},{12,8},{1,13},{5,1},{9,5},{13,9},{2,14},{6,2},{... | collective-permute-start | bytes 196616 | tf_op jit(solution)/shard_map/ppermute | solution.py:447
  66.1 6.6 %collective-permute-start.9 = (f32[4,32,128]{2,1,0:T(8,128)S(1)}, f32[4,32,128]{2,1,0:T(8,128)S(1)}, u32[]{:S(2)}, u32[]{:S(2)}) collective-permute-start(f32[4,32,128]{2,1,0:T(8,128)S(1)} %get-tuple-element.28), channel_id=1, source_target_pairs={{0,4},{4,8},{8,12},{12,0},{1,5},{5,9},{9,13},{13,1},{2,6},{6,10},{... | collective-permute-start | bytes 196616 | tf_op jit(solution)/shard_map/ppermute | solution.py:447

commit v5 on v4

--- a/solution.py
+++ b/solution.py
@@ -8,6 +8,7 @@
 from jax.experimental import pallas as pl
 from jax.experimental.pallas import tpu as pltpu
 from jax.sharding import PartitionSpec as P
+
 
 N0 = 128
 N1 = 2
@@ -97,7 +98,7 @@
     def evolve_rows(state):
         rows = state.shape[0]
         grid5 = state.reshape(rows, N1, N2, N3, N4)
-        for step in range(STEPS):
+        for _ in range(STEPS):
             extended = extended_2(grid5, (("slab", 0),), 1)
             grid5 = advance(extended, scales, 0)
         return grid5.reshape(rows, Q, N4)
@@ -148,26 +149,28 @@
     return jnp.concatenate([second, drift], axis=0).astype(jnp.bfloat16)
 
 
-def step_rows(src, dst, first, groups, matrix, factors, products):
+def step_rows(src, dst, first, count, matrix, factors, products):
     s0, q0, s4, q4 = factors
     size = TILES * N2
 
+    def rows_of(group):
+        return range(first + group * UNROLL, first + min(count, (group + 1) * UNROLL))
+
     def multiply(group):
-        base = first + group * UNROLL
-        value = jnp.concatenate([src[base + i].reshape(size, N4) for i in range(UNROLL)], axis=1)
+        value = jnp.concatenate([src[row].reshape(size, N4) for row in rows_of(group)], axis=1)
         high = value.astype(jnp.bfloat16)
         rest = (value - high.astype(jnp.float32)).astype(jnp.bfloat16)
-        products[group % 2][...] = jnp.dot(
+        products[group % 2][:, : value.shape[1]] = jnp.dot(
             matrix[...], jnp.concatenate([high, rest], axis=0), preferred_element_type=jnp.float32
         )
 
+    groups = -(-count // UNROLL)
     multiply(0)
     for group in range(groups):
         if group + 1 < groups:
             multiply(group + 1)
         product = products[group % 2]
-        for i in range(UNROLL):
-            row = first + group * UNROLL + i
+        for i, row in enumerate(rows_of(group)):
             lanes = slice(i * N4, (i + 1) * N4)
             for t in range(TILES):
                 u, below, above = src[row, t], src[row - 1, t], src[row + 1, t]
@@ -187,7 +190,7 @@
 
 
 def spaces(rows):
-    state = pltpu.VMEM((rows + LOW + HIGH + UNROLL, TILES, N2, N4), jnp.float32)
+    state = pltpu.VMEM((rows + LOW + HIGH, TILES, N2, N4), jnp.float32)
     size = TILES * N2
     product = pltpu.VMEM((2 * size, UNROLL * N4), jnp.float32)
     return [state, state, product, product, pltpu.VMEM((2 * size, 2 * size), jnp.bfloat16)]
@@ -199,8 +202,7 @@
     factors = (scales[0], scales[0] * scales[0], scales[4], scales[4] * scales[4])
     for step in range(STEPS):
         count = rows + LOW + HIGH - 2 * (step + 1)
-        groups = -(-count // UNROLL)
-        step_rows(states[step % 2], states[(step + 1) % 2], step + 1, groups, matrix, factors, products)
+        step_rows(states[step % 2], states[(step + 1) % 2], step + 1, count, matrix, factors, products)
     return states[STEPS % 2]
 
 
@@ -214,42 +216,26 @@
     two.wait()
 
 
-def first_kernel(later, level, before, field, after, one, two, *bufs):
-    half, start = field.shape[0] // 2, bufs[0]
+def load_rows(ref, first, count, state, at):
+    def body(i, carry):
+        for n1 in range(N1):
+            for n3 in range(N3):
+                state[at + i, n1 * N3 + n3] = ref[first + i, pl.ds(n1 * N2 * N3 + n3, N2, stride=N3), :]
+        return carry
+
+    lax.fori_loop(0, count, body, 0)
+
+
+def first_cycle(level, rows, outs, bufs):
     me, grids = lax.axis_index("grid"), lax.axis_size("grid")
-    upper = lax.rem(lax.div(2 * me, grids) + lax.axis_index("slab") + later, 2) == 0
-
-    def load(ref, first, count, at):
-        def body(i, carry):
-            for n1 in range(N1):
-                for n3 in range(N3):
-                    start[at + i, n1 * N3 + n3] = ref[first + i, pl.ds(n1 * N2 * N3 + n3, N2, stride=N3), :]
-            return carry
-
-        lax.fori_loop(0, count, body, 0)
-
-    @pl.when(upper)
-    def _():
-        load(field, half - LOW, half + LOW, 0)
-        load(after, 0, HIGH, LOW + half)
-
-    @pl.when(jnp.logical_not(upper))
-    def _():
-        load(before, 0, LOW, 0)
-        load(field, 0, half + HIGH, LOW)
-
     levels = [level[0, d] for d in range(5)]
     scales = [lax.shift_left(1, v).astype(jnp.float32) * 0.125 for v in levels]
     parity = lax.rem(levels[0] + levels[1] + levels[2] + levels[3] + levels[4], 2)
-    weight = (1 - 2 * parity).astype(jnp.float32) * (1.0 / math.sqrt(lax.axis_size("grid")))
-    done = run_steps(bufs, half, scales)
+    weight = (1 - 2 * parity).astype(jnp.float32) * (1.0 / math.sqrt(grids))
+    done = run_steps(bufs, rows, scales)
     fine, middle = levels[0] >= 3, levels[0] >= 2
-    block = half // 2
-    ends = jnp.logical_or(me == 0, me == grids - 1)
-    at = jnp.where(upper, block, 0)
-    if later:
-        at = jnp.where(ends, block - at, at)
-    for out, first in ((one, at), (two, block - at)):
+    block = outs[0][1].shape[0] // TILES
+    for first, out in outs:
         for quad in range(0, block, 4):
             base = LOW + first + quad
             for t in range(TILES):
@@ -262,6 +248,34 @@
             tile = jnp.where(lane == d, value, tile)
         sublane = lax.broadcasted_iota(jnp.int32, (N2, N4), 0)
         out[block * TILES] = jnp.where(sublane == me, tile, 0.0)
+
+
+def middle_kernel(level, field, middle, near, *bufs):
+    rows = field.shape[0] // 2
+    block = rows // 2
+    load_rows(field, block - LOW, rows + LOW + HIGH, bufs[0], 0)
+    side = lax.div(2 * lax.axis_index("grid"), lax.axis_size("grid"))
+    upper = lax.rem(side + lax.axis_index("slab"), 2) == 0
+    first = jnp.where(upper, block, 0)
+    first_cycle(level, rows, ((first, middle), (block - first, near)), bufs)
+
+
+def outer_kernel(later, level, before, field, after, out, *bufs):
+    total = field.shape[0]
+    block = out.shape[0] // TILES
+    top = lax.rem(lax.axis_index("grid") + lax.axis_index("slab") + later, 2) == 0
+
+    @pl.when(top)
+    def _():
+        load_rows(field, total - block - LOW, block + LOW, bufs[0], 0)
+        load_rows(after, 0, HIGH, bufs[0], block + LOW)
+
+    @pl.when(jnp.logical_not(top))
+    def _():
+        load_rows(before, 0, LOW, bufs[0], 0)
+        load_rows(field, 0, block + HIGH, bufs[0], LOW)
+
+    first_cycle(level, block, ((0, out),), bufs)
 
 
 def second_kernel(rows, grids, before, own, after, out, total, wide, *bufs):
@@ -330,7 +344,7 @@
             out[pl.ds(n * N3 + n3, count, stride=parts * N3), :] = ref[n]
 
 
-def kernel(body, name, out_shape, in_specs, scratch=(), limit=4, flops=0):
+def kernel(body, out_shape, in_specs, scratch=(), limit=4, flops=0):
     single = not isinstance(out_shape, (list, tuple))
     return pl.pallas_call(
         body,
@@ -340,7 +354,6 @@
         scratch_shapes=list(scratch),
         compiler_params=pltpu.CompilerParams(vmem_limit_bytes=limit << 20),
         cost_estimate=pl.CostEstimate(flops=flops, bytes_accessed=1 << 20, transcendentals=flops // 30),
-        name=name,
     )
 
 
@@ -350,7 +363,7 @@
 
 
 def fast_fits(grids, slabs):
-    rows, block = fast_sizes(grids, slabs)
+    _, block = fast_sizes(grids, slabs)
     return grids == 4 and grids == N3 and slabs == 2 * N1 and block >= HIGH and block % 4 == 0
 
 
@@ -367,35 +380,42 @@
     down = [(j, i) for i, j in up]
     last, first = kernel(
         ends_kernel,
-        "ends",
         [floats(LOW, Q, N4), floats(HIGH, Q, N4)],
         [HBM],
         [pltpu.SemaphoreType.DMA((2,))],
-    )(state)
+    )(pltpu.with_memory_space_constraint(state, pltpu.HBM))
     before = lax.ppermute(last, "slab", up)
     after = lax.ppermute(first, "slab", down)
 
     piece = floats(block * TILES + 1, N2, N4)
-
-    def half_slab(later):
+    work = 8192 * 40
+    middle, near = kernel(
+        middle_kernel, [piece, piece], [SMEM, VMEM], spaces(rows // 2), limit=6, flops=80 * work
+    )(levels, state)
+
+    ready = lax.optimization_barrier((before, after, middle))
+
+    def outer_block(later):
         return kernel(
-            functools.partial(first_kernel, later),
-            "first_cycle",
-            [piece, piece],
+            functools.partial(outer_kernel, later),
+            piece,
             [SMEM, VMEM, VMEM, VMEM],
-            spaces(rows // 2),
-            limit=8,
-            flops=160 * 8192 * 40,
-        )(levels, before, state, after)
-
-    far, middle = half_slab(0)
-    joined = lax.ppermute(far, "grid", [(0, 1), (3, 2)]) + far
+            spaces(block),
+            limit=6,
+            flops=48 * work,
+        )(levels, ready[0], state, ready[1])
+
+    edge = (lax.axis_index("grid") == 0) | (lax.axis_index("grid") == grids - 1)
     across = lax.ppermute(middle, "grid", [(1, 2), (2, 1)])
+    first_out = outer_block(0)
+    swapped = lax.ppermute(first_out, "grid", [(0, 1), (1, 0), (2, 3), (3, 2)])
+    middle, near, _ = lax.optimization_barrier((middle, near, first_out))
     skipped = lax.ppermute(middle, "grid", [(0, 2), (3, 1)])
-    near, own = half_slab(1)
-    swapped = lax.ppermute(near, "grid", [(0, 1), (1, 0), (2, 3), (3, 2)])
+    inwards = lax.ppermute(near, "grid", [(0, 1), (3, 2)])
+    second_out = outer_block(1)
+    joined = swapped + second_out
     passed = lax.ppermute(joined, "grid", [(1, 3), (2, 0)])
-    own = own + across + skipped + swapped + passed
+    own = jnp.where(edge, joined, near) + across + skipped + inwards + passed
 
     chain = []
     for k in range(slabs):
@@ -409,7 +429,6 @@
     half = N2 // 2
     sent = kernel(
         functools.partial(second_kernel, block, grids),
-        "second_cycle",
         floats(N3 * N1 * 2, half, block, N4),
         [VMEM, VMEM, VMEM],
         [
@@ -437,10 +456,7 @@
     ).astype(jnp.bfloat16)
     group = N0 // grids
     hier = kernel(
-        functools.partial(hier_kernel, grids),
-        "hierarchise",
-        [floats(half, group, N4)] * grids,
-        [VMEM, VMEM],
+        functools.partial(hier_kernel, grids), [floats(half, group, N4)] * grids, [VMEM, VMEM]
     )(matrix, spread)
     others = lax.optimization_barrier(tuple(hier[1:]))
     received = [hier[0]] + [
@@ -448,10 +464,7 @@
         for d, value in enumerate(others, 1)
     ]
     out = kernel(
-        functools.partial(place_kernel, grids),
-        "place",
-        floats(group * half * N3, N4),
-        [VMEM] * grids,
+        functools.partial(place_kernel, grids), floats(group * half * N3, N4), [VMEM] * grids
     )(*received)
     return out.reshape(group, Q // slabs, N4)
 

time: 73.8 us -> 74.3 us (level)
  starting transfers between devices: 21.1 us -> 22.5 us
  local copies, waits for them, and re-layouts: 1.91 us -> 0.69 us
  Pallas kernels: 14.3 us -> 15.4 us
  waiting for transfers between devices: 35.7 us -> 34.9 us
    ppermute x1, waiting for transfers between devices: 0.01 us -> 7.58 us  [local_fast(): passed = lax.ppermute(joined, 'grid', [(1, 3), (2, 0)])]
    ppermute x2, waiting for transfers between devices: 8.31 us -> 2.1 us  [the longest x1 2.09 us: local_fast(): inwards = lax.ppermute(near, 'grid', [(0, 1), (3, 2)])]
    ppermute x2, starting transfers between devices: 3.57 us -> 7.96 us  [the longest x1 6.3 us: local_fast(): inwards = lax.ppermute(near, 'grid', [(0, 1), (3, 2)])]
    ppermute x1, waiting for transfers between devices: 5.26 us -> 2.4 us  [local_fast(): before = lax.ppermute(last, 'slab', up)]
    ppermute x1, starting transfers between devices: 3.98 us -> 1.31 us  [local_fast(): skipped = lax.ppermute(middle, 'grid', [(0, 2), (3, 1)])]
    unnamed x10 -> x8, local copies, waits for them, and re-layouts: 1.89 us -> 0.66 us
    pallas_call x6 -> x7, Pallas kernels: 14.3 us -> 15.4 us  [the longest x1 6.33 us: local_fast(): kernel(functools.partial(second_kernel, block, grids), floats(N3 * N1 * 2...]
    ppermute x1, starting transfers between devices: 1.56 us -> 0.63 us  [local_fast(): lax.ppermute(own[(block - LOW) * TILES:block * TILES], both, forward)]
  transfers between devices with their start and end apart: 13 -> 13, of which waited for: 8 -> 9; matrix products, arithmetic and copies ran while one was open for 0% -> 0% of each run, Pallas kernels for 4% -> 7%
where the time goes in v5:
time: 74.3 us; the launch traced here: 74 us
  waiting for transfers between devices  34.9 us (47%)
  starting transfers between devices  22.5 us (30%)
  Pallas kernels  15.4 us (21%)
    all_to_all x1, waiting for transfers between devices, local_fast(): spread = lax.all_to_all(sent, both, split_axis=0, concat_axis=0, tiled=True)  9.14 us
    ppermute x1, waiting for transfers between devices, local_fast(): passed = lax.ppermute(joined, 'grid', [(1, 3), (2, 0)])  7.58 us
    pallas_call x1, Pallas kernels, local_fast(): kernel(functools.partial(second_kernel, block, grids), floats(N3 * N1 * 2...  6.33 us
    ppermute x1, starting transfers between devices, local_fast(): inwards = lax.ppermute(near, 'grid', [(0, 1), (3, 2)])  6.3 us
    ppermute x3, waiting for transfers between devices, local_fast(): lax.ppermute(value, 'grid', [(i, (i + d) % grids) for i in range(grids)])  5.35 us
    ppermute x1, waiting for transfers between devices, local_fast(): lax.ppermute(own[(block - LOW) * TILES:block * TILES], both, forward)  4.54 us
    pallas_call x2, Pallas kernels, outer_block(): kernel(functools.partial(outer_kernel, later), piece, [SMEM, VMEM, VMEM,...  3.93 us
    ppermute x1, waiting for transfers between devices, local_fast(): skipped = lax.ppermute(middle, 'grid', [(0, 2), (3, 1)])  3.78 us
  transfers between devices with their start and end apart: 13, of which 9 were waited for; matrix products, arithmetic and copies ran while one was open for 0% of the time, Pallas kernels for 7%

profile of v5, /device:TPU:0, one launch (start us, length us, event | category | flops | bytes accessed | tf_op | source)
XLA Modules:
  0.0 74.0 jit_solution(10683987222616596173)
XLA Ops:
  0.0 0.0 copy-start
  0.0 1.1 %shard_map.46 = (f32[4,64,128]{2,1,0:T(8,128)S(1)}, f32[5,64,128]{2,1,0:T(8,128)S(1)}) custom-call(f32[32,64,128]{2,1,0:T(8,128)} %bitcast.2), custom_call_target="tpu_custom_call" | custom-call | bytes 1048576 | tf_op jit(solution)/shard_map/pallas_call | solution.py:381
  1.1 0.0 copy-start.1
  1.1 2.5 %collective-permute-start.1 = (f32[5,64,128]{2,1,0:T(8,128)S(1)}, f32[5,64,128]{2,1,0:T(8,128)S(1)}, u32[]{:S(2)}, u32[]{:S(2)}) collective-permute-start(f32[5,64,128]{2,1,0:T(8,128)S(1)} %get-tuple-element.21), channel_id=1, source_target_pairs={{1,0},{2,1},{3,2},{0,3},{5,4},{6,5},{7,6},{4,7},{9,8},{10,9},{11,1... | collective-permute-start | bytes 491528 | tf_op jit(solution)/shard_map/ppermute | solution.py:388
  3.6 0.0 collective-permute-start
  3.6 0.0 copy-done
  3.6 0.0 copy-done.1
  3.6 2.8 %shard_map.47 = (f32[65,8,128]{2,1,0:T(8,128)S(1)}, f32[65,8,128]{2,1,0:T(8,128)S(1)}) custom-call(s32[1,5]{1,0:T(1,128)S(1)} %copy-done.1, f32[32,64,128]{2,1,0:T(8,128)S(1)} %bitcast.3), custom_call_target="tpu_custom_call" | custom-call | flops 26214400 | bytes 1048576 | tf_op jit(solution)/shard_map/pallas_call | solution.py:392
  6.4 2.4 %collective-permute-done.before = f32[4,64,128]{2,1,0:T(8,128)S(1)} collective-permute-done((f32[4,64,128]{2,1,0:T(8,128)S(1)}, f32[4,64,128]{2,1,0:T(8,128)S(1)}, u32[]{:S(2)}, u32[]{:S(2)}) %collective-permute-start) | collective-permute-done | bytes 131104 | tf_op jit(solution)/shard_map/ppermute | solution.py:387
  8.8 0.0 collective-permute-done.1.after
  8.8 2.0 %shard_map.48 = f32[65,8,128]{2,1,0:T(8,128)S(1)} custom-call(s32[1,5]{1,0:T(1,128)S(1)} %copy-done.1, f32[4,64,128]{2,1,0:T(8,128)S(1)} %collective-permute-done.before, f32[32,64,128]{2,1,0:T(8,128)S(1)} %bitcast.4, f32[5,64,128]{2,1,0:T(8,128)S(1)} %collective-permute-done.1.after), custom_call_target="tpu_custom_call" | custom-call | flops 15728640 | bytes 1048576 | tf_op jit(solution)/shard_map/pallas_call | solution.py:399
  10.8 1.7 %collective-permute-start.2 = (f32[65,8,128]{2,1,0:T(8,128)S(1)}, f32[65,8,128]{2,1,0:T(8,128)S(1)}, u32[]{:S(2)}, u32[]{:S(2)}) collective-permute-start(f32[65,8,128]{2,1,0:T(8,128)S(1)} %shard_map.48), channel_id=1, source_target_pairs={{0,4},{4,0},{8,12},{12,8},{1,5},{5,1},{9,13},{13,9},{2,6},{6,2},{1... | collective-permute-start | bytes 798728 | tf_op jit(solution)/shard_map/ppermute | solution.py:411
  12.4 0.7 collective-permute-start.3
  13.1 6.3 %collective-permute-start.5 = (f32[65,8,128]{2,1,0:T(8,128)S(1)}, f32[65,8,128]{2,1,0:T(8,128)S(1)}, u32[]{:S(2)}, u32[]{:S(2)}) collective-permute-start(f32[65,8,128]{2,1,0:T(8,128)S(1)} %get-tuple-element.26), channel_id=1, source_target_pairs={{0,4},{12,8},{1,5},{13,9},{2,6},{14,10},{3,7},{15,11},{16,20},{28,... | collective-permute-start | bytes 798728 | tf_op jit(solution)/shard_map/ppermute | solution.py:414
  19.4 2.0 %shard_map.49 = f32[65,8,128]{2,1,0:T(8,128)S(1)} custom-call(s32[1,5]{1,0:T(1,128)S(1)} %copy-done.1, f32[4,64,128]{2,1,0:T(8,128)S(1)} %collective-permute-done.before, f32[32,64,128]{2,1,0:T(8,128)S(1)} %bitcast.5, f32[5,64,128]{2,1,0:T(8,128)S(1)} %collective-permute-done.1.after), custom_call_target="tpu_custom_call" | custom-call | flops 15728640 | bytes 1048576 | tf_op jit(solution)/shard_map/pallas_call | solution.py:399
  21.4 1.3 %collective-permute-start.4 = (f32[65,8,128]{2,1,0:T(8,128)S(1)}, f32[65,8,128]{2,1,0:T(8,128)S(1)}, u32[]{:S(2)}, u32[]{:S(2)}) collective-permute-start(f32[65,8,128]{2,1,0:T(8,128)S(1)} %get-tuple-element.27), channel_id=1, source_target_pairs={{0,8},{12,4},{1,9},{13,5},{2,10},{14,6},{3,11},{15,7},{16,24},{28,... | collective-permute-start | bytes 798728 | tf_op jit(solution)/shard_map/ppermute | solution.py:413
  22.7 0.0 collective-permute-done.2
  22.8 1.3 %collective-permute-start.6 = (f32[65,8,128]{2,1,0:T(8,128)S(1)}, f32[65,8,128]{2,1,0:T(8,128)S(1)}, u32[]{:S(2)}, u32[]{:S(2)}) collective-permute-start(f32[65,8,128]{2,1,0:T(8,128)S(1)} %add.36), channel_id=1, source_target_pairs={{4,12},{8,0},{5,13},{9,1},{6,14},{10,2},{7,15},{11,3},{20,28},{24,... | collective-permute-start | bytes 798728 | tf_op jit(solution)/shard_map/ppermute | solution.py:417
  24.1 0.0 collective-permute-done.3
  24.1 2.1 %collective-permute-done.5 = f32[65,8,128]{2,1,0:T(8,128)S(1)} collective-permute-done((f32[65,8,128]{2,1,0:T(8,128)S(1)}, f32[65,8,128]{2,1,0:T(8,128)S(1)}, u32[]{:S(2)}, u32[]{:S(2)}) %collective-permute-start.5) | collective-permute-done | bytes 266272 | tf_op jit(solution)/shard_map/ppermute | solution.py:414
  26.2 3.8 %collective-permute-done.4 = f32[65,8,128]{2,1,0:T(8,128)S(1)} collective-permute-done((f32[65,8,128]{2,1,0:T(8,128)S(1)}, f32[65,8,128]{2,1,0:T(8,128)S(1)}, u32[]{:S(2)}, u32[]{:S(2)}) %collective-permute-start.4) | collective-permute-done | bytes 266272 | tf_op jit(solution)/shard_map/ppermute | solution.py:413
  30.0 7.6 %collective-permute-done.6 = f32[65,8,128]{2,1,0:T(8,128)S(1)} collective-permute-done((f32[65,8,128]{2,1,0:T(8,128)S(1)}, f32[65,8,128]{2,1,0:T(8,128)S(1)}, u32[]{:S(2)}, u32[]{:S(2)}) %collective-permute-start.6) | collective-permute-done | bytes 266272 | tf_op jit(solution)/shard_map/ppermute | solution.py:417
  37.5 0.1 add_add_fusion.own
  37.7 1.5 %collective-permute-start.8 = (f32[40,8,128]{2,1,0:T(8,128)S(1)}, f32[40,8,128]{2,1,0:T(8,128)S(1)}, u32[]{:S(2)}, u32[]{:S(2)}) collective-permute-start(f32[40,8,128]{2,1,0:T(8,128)S(1)} %slice.9), channel_id=1, source_target_pairs={{4,0},{8,4},{12,8},{13,12},{9,13},{5,9},{1,5},{2,1},{6,2},{10,6},{... | collective-permute-start | bytes 491528 | tf_op jit(solution)/shard_map/ppermute | solution.py:427
  39.2 0.6 collective-permute-start.7
  39.9 4.5 %collective-permute-done.7.before = f32[32,8,128]{2,1,0:T(8,128)S(1)} collective-permute-done((f32[32,8,128]{2,1,0:T(8,128)S(1)}, f32[32,8,128]{2,1,0:T(8,128)S(1)}, u32[]{:S(2)}, u32[]{:S(2)}) %collective-permute-start.7) | collective-permute-done | bytes 131104 | tf_op jit(solution)/shard_map/ppermute | solution.py:426
  44.4 0.0 collective-permute-done.8.after
  44.4 6.3 %shard_map.50 = f32[16,4,8,128]{3,2,1,0:T(8,128)} custom-call(f32[32,8,128]{2,1,0:T(8,128)S(1)} %collective-permute-done.7.before, f32[65,8,128]{2,1,0:T(8,128)S(1)} %add_add_fusion.own, f32[40,8,128]{2,1,0:T(8,128)S(1)} %collective-permute-done.8.after), custom_call_target="tpu_custom_call" | custom-call | flops 131072000 | bytes 1048576 | tf_op jit(solution)/shard_map/pallas_call | solution.py:430
  50.7 0.0 copy-start.2
  50.7 3.7 %all-to-all-start = ((f32[16,4,8,128]{3,2,1,0:T(8,128)}), f32[16,4,8,128]{3,2,1,0:T(8,128)S(1)}, u32[]{:S(2)}, u32[]{:S(2)}) async-start(f32[16,4,8,128]{3,2,1,0:T(8,128)} %shard_map.50), calls=%async_computation | async-start | bytes 524288 | tf_op jit(solution)/shard_map/all_to_all | solution.py:443
  54.4 0.0 copy-done.2
  54.5 0.0 copy-start.3
  54.5 0.6 copy-done.3
  55.1 0.1 add_convert_fusion.matrix
  55.3 9.1 %all-to-all-done.rows = f32[16,4,8,128]{3,2,1,0:T(8,128)S(1)} async-done(((f32[16,4,8,128]{3,2,1,0:T(8,128)}), f32[16,4,8,128]{3,2,1,0:T(8,128)S(1)}, u32[]{:S(2)}, u32[]{:S(2)}) %all-to-all-start) | async-done | bytes 262176 | tf_op jit(solution)/shard_map/all_to_all | solution.py:443
  64.4 0.4 shard_map.51
  64.8 1.0 %collective-permute-start.10 = (f32[4,32,128]{2,1,0:T(8,128)S(1)}, f32[4,32,128]{2,1,0:T(8,128)S(1)}, u32[]{:S(2)}, u32[]{:S(2)}) collective-permute-start(f32[4,32,128]{2,1,0:T(8,128)S(1)} %get-tuple-element.33), channel_id=1, source_target_pairs={{0,8},{4,12},{8,0},{12,4},{1,9},{5,13},{9,1},{13,5},{2,10},{6,14},... | collective-permute-start | bytes 196616 | tf_op jit(solution)/shard_map/ppermute | solution.py:463
  65.8 0.8 %collective-permute-start.11 = (f32[4,32,128]{2,1,0:T(8,128)S(1)}, f32[4,32,128]{2,1,0:T(8,128)S(1)}, u32[]{:S(2)}, u32[]{:S(2)}) collective-permute-start(f32[4,32,128]{2,1,0:T(8,128)S(1)} %get-tuple-element.34), channel_id=1, source_target_pairs={{0,12},{4,0},{8,4},{12,8},{1,13},{5,1},{9,5},{13,9},{2,14},{6,2},{... | collective-permute-start | bytes 196616 | tf_op jit(solution)/shard_map/ppermute | solution.py:463
  66.6 1.2 %collective-permute-start.9 = (f32[4,32,128]{2,1,0:T(8,128)S(1)}, f32[4,32,128]{2,1,0:T(8,128)S(1)}, u32[]{:S(2)}, u32[]{:S(2)}) collective-permute-start(f32[4,32,128]{2,1,0:T(8,128)S(1)} %get-tuple-element.32), channel_id=1, source_target_pairs={{0,4},{4,8},{8,12},{12,0},{1,5},{5,9},{9,13},{13,1},{2,6},{6,10},{... | collective-permute-start | bytes 196616 | tf_op jit(solution)/shard_map/ppermute | solution.py:463
  67.8 3.3 %collective-permute-done.10.refs_2_ = f32[4,32,128]{2,1,0:T(8,128)S(1)} collective-permute-done((f32[4,32,128]{2,1,0:T(8,128)S(1)}, f32[4,32,128]{2,1,0:T(8,128)S(1)}, u32[]{:S(2)}, u32[]{:S(2)}) %collective-permute-start.10) | collective-permute-done | bytes 65568 | tf_op jit(solution)/shard_map/ppermute | solution.py:463
  71.1 0.3 collective-permute-done.11.refs_3_
  71.4 1.8 %collective-permute-done.9.refs_1_ = f32[4,32,128]{2,1,0:T(8,128)S(1)} collective-permute-done((f32[4,32,128]{2,1,0:T(8,128)S(1)}, f32[4,32,128]{2,1,0:T(8,128)S(1)}, u32[]{:S(2)}, u32[]{:S(2)}) %collective-permute-start.9) | collective-permute-done | bytes 65568 | tf_op jit(solution)/shard_map/ppermute | solution.py:463
  73.2 0.8 %shard_map.52 = f32[512,128]{1,0:T(8,128)} custom-call(f32[4,32,128]{2,1,0:T(8,128)S(1)} %get-tuple-element.28.refs_0_, f32[4,32,128]{2,1,0:T(8,128)S(1)} %collective-permute-done.9.refs_1_, f32[4,32,128]{2,1,0:T(8,128)S(1)} %collective-permute-done.10.refs_2_, f32[4,32,128]{2,1,0:T(8,128)S(1)} %collective-permute-done.11.refs_3_), custom_call_target="tpu_custom_call" | custom-call | bytes 1048576 | tf_op jit(solution)/shard_map/pallas_call | solution.py:466
  (5 shorter events, 0.1 us)
Async XLA Ops:
  0.0 3.6 %copy-start = (f32[1,32,64,128]{3,2,1,0:T(8,128)S(1)}, f32[1,32,64,128]{3,2,1,0:T(8,128)}, u32[]{:S(2)}) copy-start(f32[1,32,64,128]{3,2,1,0:T(8,128)} %param.4) | copy-start | bytes 3145732
  1.1 2.5 %copy-start.1 = (s32[1,5]{1,0:T(1,128)S(1)}, s32[1,5]{1,0:T(1,128)}, u32[]{:S(2)}) copy-start(s32[1,5]{1,0:T(1,128)} %level.5) | copy-start | bytes 64
  1.1 7.7 %collective-permute-start.1 = (f32[5,64,128]{2,1,0:T(8,128)S(1)}, f32[5,64,128]{2,1,0:T(8,128)S(1)}, u32[]{:S(2)}, u32[]{:S(2)}) collective-permute-start(f32[5,64,128]{2,1,0:T(8,128)S(1)} %get-tuple-element.21), channel_id=1, source_target_pairs={{1,0},{2,1},{3,2},{0,3},{5,4},{6,5},{7,6},{4,7},{9,8},{10,9},{11,1... | collective-permute-start | bytes 491528 | tf_op jit(solution)/shard_map/ppermute | solution.py:388
  3.6 5.3 %collective-permute-start = (f32[4,64,128]{2,1,0:T(8,128)S(1)}, f32[4,64,128]{2,1,0:T(8,128)S(1)}, u32[]{:S(2)}, u32[]{:S(2)}) collective-permute-start(f32[4,64,128]{2,1,0:T(8,128)S(1)} %get-tuple-element.20), channel_id=1, source_target_pairs={{0,1},{1,2},{2,3},{3,0},{4,5},{5,6},{6,7},{7,4},{8,9},{9,10},{10,1... | collective-permute-start | bytes 393224 | tf_op jit(solution)/shard_map/ppermute | solution.py:387
  10.8 11.9 %collective-permute-start.2 = (f32[65,8,128]{2,1,0:T(8,128)S(1)}, f32[65,8,128]{2,1,0:T(8,128)S(1)}, u32[]{:S(2)}, u32[]{:S(2)}) collective-permute-start(f32[65,8,128]{2,1,0:T(8,128)S(1)} %shard_map.48), channel_id=1, source_target_pairs={{0,4},{4,0},{8,12},{12,8},{1,5},{5,1},{9,13},{13,9},{2,6},{6,2},{1... | collective-permute-start | bytes 798728 | tf_op jit(solution)/shard_map/ppermute | solution.py:411
  12.4 11.6 %collective-permute-start.3 = (f32[65,8,128]{2,1,0:T(8,128)S(1)}, f32[65,8,128]{2,1,0:T(8,128)S(1)}, u32[]{:S(2)}, u32[]{:S(2)}) collective-permute-start(f32[65,8,128]{2,1,0:T(8,128)S(1)} %get-tuple-element.27), channel_id=1, source_target_pairs={{4,8},{8,4},{5,9},{9,5},{6,10},{10,6},{7,11},{11,7},{20,24},{24,20... | collective-permute-start | bytes 798728 | tf_op jit(solution)/shard_map/ppermute | solution.py:409
  13.1 13.1 %collective-permute-start.5 = (f32[65,8,128]{2,1,0:T(8,128)S(1)}, f32[65,8,128]{2,1,0:T(8,128)S(1)}, u32[]{:S(2)}, u32[]{:S(2)}) collective-permute-start(f32[65,8,128]{2,1,0:T(8,128)S(1)} %get-tuple-element.26), channel_id=1, source_target_pairs={{0,4},{12,8},{1,5},{13,9},{2,6},{14,10},{3,7},{15,11},{16,20},{28,... | collective-permute-start | bytes 798728 | tf_op jit(solution)/shard_map/ppermute | solution.py:414
  21.4 8.6 %collective-permute-start.4 = (f32[65,8,128]{2,1,0:T(8,128)S(1)}, f32[65,8,128]{2,1,0:T(8,128)S(1)}, u32[]{:S(2)}, u32[]{:S(2)}) collective-permute-start(f32[65,8,128]{2,1,0:T(8,128)S(1)} %get-tuple-element.27), channel_id=1, source_target_pairs={{0,8},{12,4},{1,9},{13,5},{2,10},{14,6},{3,11},{15,7},{16,24},{28,... | collective-permute-start | bytes 798728 | tf_op jit(solution)/shard_map/ppermute | solution.py:413
  22.8 14.8 %collective-permute-start.6 = (f32[65,8,128]{2,1,0:T(8,128)S(1)}, f32[65,8,128]{2,1,0:T(8,128)S(1)}, u32[]{:S(2)}, u32[]{:S(2)}) collective-permute-start(f32[65,8,128]{2,1,0:T(8,128)S(1)} %add.36), channel_id=1, source_target_pairs={{4,12},{8,0},{5,13},{9,1},{6,14},{10,2},{7,15},{11,3},{20,28},{24,... | collective-permute-start | bytes 798728 | tf_op jit(solution)/shard_map/ppermute | solution.py:417
  37.7 6.7 %collective-permute-start.8 = (f32[40,8,128]{2,1,0:T(8,128)S(1)}, f32[40,8,128]{2,1,0:T(8,128)S(1)}, u32[]{:S(2)}, u32[]{:S(2)}) collective-permute-start(f32[40,8,128]{2,1,0:T(8,128)S(1)} %slice.9), channel_id=1, source_target_pairs={{4,0},{8,4},{12,8},{13,12},{9,13},{5,9},{1,5},{2,1},{6,2},{10,6},{... | collective-permute-start | bytes 491528 | tf_op jit(solution)/shard_map/ppermute | solution.py:427
  39.2 5.2 %collective-permute-start.7 = (f32[32,8,128]{2,1,0:T(8,128)S(1)}, f32[32,8,128]{2,1,0:T(8,128)S(1)}, u32[]{:S(2)}, u32[]{:S(2)}) collective-permute-start(f32[32,8,128]{2,1,0:T(8,128)S(1)} %slice.8), channel_id=1, source_target_pairs={{0,4},{4,8},{8,12},{12,13},{13,9},{9,5},{5,1},{1,2},{2,6},{6,10},{... | collective-permute-start | bytes 393224 | tf_op jit(solution)/shard_map/ppermute | solution.py:426
  50.7 3.7 %copy-start.2 = (s32[128]{0:T(128)S(1)}, s32[128]{0:T(128)}, u32[]{:S(2)}) copy-start(s32[128]{0:T(128)} %param.6) | copy-start | bytes 1540
  50.7 13.7 %all-to-all-start = ((f32[16,4,8,128]{3,2,1,0:T(8,128)}), f32[16,4,8,128]{3,2,1,0:T(8,128)S(1)}, u32[]{:S(2)}, u32[]{:S(2)}) async-start(f32[16,4,8,128]{3,2,1,0:T(8,128)} %shard_map.50), calls=%async_computation | async-start | bytes 524288 | tf_op jit(solution)/shard_map/all_to_all | solution.py:443
  54.5 0.7 copy-start.3
  64.8 6.3 %collective-permute-start.10 = (f32[4,32,128]{2,1,0:T(8,128)S(1)}, f32[4,32,128]{2,1,0:T(8,128)S(1)}, u32[]{:S(2)}, u32[]{:S(2)}) collective-permute-start(f32[4,32,128]{2,1,0:T(8,128)S(1)} %get-tuple-element.33), channel_id=1, source_target_pairs={{0,8},{4,12},{8,0},{12,4},{1,9},{5,13},{9,1},{13,5},{2,10},{6,14},... | collective-permute-start | bytes 196616 | tf_op jit(solution)/shard_map/ppermute | solution.py:463
  65.8 5.6 %collective-permute-start.11 = (f32[4,32,128]{2,1,0:T(8,128)S(1)}, f32[4,32,128]{2,1,0:T(8,128)S(1)}, u32[]{:S(2)}, u32[]{:S(2)}) collective-permute-start(f32[4,32,128]{2,1,0:T(8,128)S(1)} %get-tuple-element.34), channel_id=1, source_target_pairs={{0,12},{4,0},{8,4},{12,8},{1,13},{5,1},{9,5},{13,9},{2,14},{6,2},{... | collective-permute-start | bytes 196616 | tf_op jit(solution)/shard_map/ppermute | solution.py:463
  66.6 6.6 %collective-permute-start.9 = (f32[4,32,128]{2,1,0:T(8,128)S(1)}, f32[4,32,128]{2,1,0:T(8,128)S(1)}, u32[]{:S(2)}, u32[]{:S(2)}) collective-permute-start(f32[4,32,128]{2,1,0:T(8,128)S(1)} %get-tuple-element.32), channel_id=1, source_target_pairs={{0,4},{4,8},{8,12},{12,0},{1,5},{5,9},{9,13},{13,1},{2,6},{6,10},{... | collective-permute-start | bytes 196616 | tf_op jit(solution)/shard_map/ppermute | solution.py:463

commit v6 on v5

--- a/solution.py
+++ b/solution.py
@@ -129,14 +129,15 @@
 UNROLL = 2
 
 
-def stencil(scales):
+def fill_tables(scales, left, right):
     size = TILES * N2
+    squares = [value * value for value in scales]
+    total = sum(scales[1:], scales[0])
+    square = sum(squares[1:], squares[0])
+
     shape = (size, 2 * size)
     row = lax.broadcasted_iota(jnp.int32, shape, 0)
     column = lax.bitwise_and(lax.broadcasted_iota(jnp.int32, shape, 1), size - 1)
-    total = sum(scales[1:], scales[0])
-    squares = [value * value for value in scales]
-    square = sum(squares[1:], squares[0])
     drift = jnp.where(row == column, -total, 0.0)
     second = jnp.where(row == column, -2.0 * square, 0.0)
     for d, unit, count in ((1, N3 * N2, N1), (2, 1, N2), (3, N2, N3)):
@@ -146,22 +147,39 @@
         ahead = column == rest + lax.bitwise_and(digit + 1, count - 1) * unit
         drift = drift + jnp.where(back, scales[d], 0.0)
         second = second + jnp.where(back, squares[d], 0.0) + jnp.where(ahead, squares[d], 0.0)
-    return jnp.concatenate([second, drift], axis=0).astype(jnp.bfloat16)
-
-
-def step_rows(src, dst, first, count, matrix, factors, products):
-    s0, q0, s4, q4 = factors
+    left[...] = jnp.concatenate([second, drift], axis=0).astype(jnp.bfloat16)
+
+    shape = (N4, N4)
+    row = lax.broadcasted_iota(jnp.int32, shape, 0)
+    column = lax.broadcasted_iota(jnp.int32, shape, 1)
+    back = row == lax.bitwise_and(column + N4 - 1, N4 - 1)
+    ahead = row == lax.bitwise_and(column + 1, N4 - 1)
+    drift = jnp.where(back, scales[4], 0.0)
+    second = jnp.where(back, squares[4], 0.0) + jnp.where(ahead, squares[4], 0.0)
+    both = jnp.concatenate([second, drift], axis=1).astype(jnp.bfloat16)
+    right[...] = jnp.concatenate([both, both], axis=0)
+
+
+def step_rows(src, dst, first, count, tables, factors, products):
+    left, right = tables
+    s0, q0 = factors
     size = TILES * N2
 
     def rows_of(group):
         return range(first + group * UNROLL, first + min(count, (group + 1) * UNROLL))
 
     def multiply(group):
-        value = jnp.concatenate([src[row].reshape(size, N4) for row in rows_of(group)], axis=1)
-        high = value.astype(jnp.bfloat16)
-        rest = (value - high.astype(jnp.float32)).astype(jnp.bfloat16)
-        products[group % 2][:, : value.shape[1]] = jnp.dot(
-            matrix[...], jnp.concatenate([high, rest], axis=0), preferred_element_type=jnp.float32
+        values = [src[row].reshape(size, N4) for row in rows_of(group)]
+        high = [value.astype(jnp.bfloat16) for value in values]
+        rest = [(value - h.astype(jnp.float32)).astype(jnp.bfloat16) for value, h in zip(values, high)]
+        across, along = products[group % 2]
+        stacked = [jnp.concatenate(pair, axis=0) for pair in zip(high, rest)]
+        across[:, : len(values) * N4] = jnp.dot(
+            left[...], jnp.concatenate(stacked, axis=1), preferred_element_type=jnp.float32
+        )
+        beside = [jnp.concatenate(pair, axis=1) for pair in zip(high, rest)]
+        along[: len(values) * size] = jnp.dot(
+            jnp.concatenate(beside, axis=0), right[...], preferred_element_type=jnp.float32
         )
 
     groups = -(-count // UNROLL)
@@ -169,14 +187,16 @@
     for group in range(groups):
         if group + 1 < groups:
             multiply(group + 1)
-        product = products[group % 2]
+        across, along = products[group % 2]
         for i, row in enumerate(rows_of(group)):
             lanes = slice(i * N4, (i + 1) * N4)
             for t in range(TILES):
                 u, below, above = src[row, t], src[row - 1, t], src[row + 1, t]
-                left, right = pltpu.roll(u, 1, 1), pltpu.roll(u, N4 - 1, 1)
-                second = product[t * N2 : (t + 1) * N2, lanes] + q0 * (below + above) + q4 * (left + right)
-                drift = product[size + t * N2 : size + (t + 1) * N2, lanes] + s0 * below + s4 * left
+                here = slice(t * N2, (t + 1) * N2)
+                there = slice(size + t * N2, size + (t + 1) * N2)
+                beside = slice(i * size + t * N2, i * size + (t + 1) * N2)
+                second = (across[here, lanes] + along[beside, :N4]) + q0 * (below + above)
+                drift = (across[there, lanes] + along[beside, N4:]) + s0 * below
                 speed = ADVECT + (0.5 * ADVECT) * jnp.tanh(u)
                 dst[row, t] = (u + DIFFUSE * second) + speed * drift
 
@@ -192,17 +212,16 @@
 def spaces(rows):
     state = pltpu.VMEM((rows + LOW + HIGH, TILES, N2, N4), jnp.float32)
     size = TILES * N2
-    product = pltpu.VMEM((2 * size, UNROLL * N4), jnp.float32)
-    return [state, state, product, product, pltpu.VMEM((2 * size, 2 * size), jnp.bfloat16)]
-
-
-def run_steps(bufs, rows, scales):
-    states, products, matrix = bufs[0:2], bufs[2:4], bufs[4]
-    matrix[...] = stencil(scales)
-    factors = (scales[0], scales[0] * scales[0], scales[4], scales[4] * scales[4])
+    across = pltpu.VMEM((2 * size, UNROLL * N4), jnp.float32)
+    along = pltpu.VMEM((UNROLL * size, 2 * N4), jnp.float32)
+    return [state, state, across, along, across, along]
+
+
+def run_steps(bufs, rows, tables, s0):
+    states, products = bufs[0:2], (bufs[2:4], bufs[4:6])
     for step in range(STEPS):
         count = rows + LOW + HIGH - 2 * (step + 1)
-        step_rows(states[step % 2], states[(step + 1) % 2], step + 1, count, matrix, factors, products)
+        step_rows(states[step % 2], states[(step + 1) % 2], step + 1, count, tables, (s0, s0 * s0), products)
     return states[STEPS % 2]
 
 
@@ -226,13 +245,16 @@
     lax.fori_loop(0, count, body, 0)
 
 
-def first_cycle(level, rows, outs, bufs):
+def scales_of(level):
+    return [lax.shift_left(1, level[0, d]).astype(jnp.float32) * 0.125 for d in range(5)]
+
+
+def first_cycle(level, tables, rows, outs, bufs):
     me, grids = lax.axis_index("grid"), lax.axis_size("grid")
-    levels = [level[0, d] for d in range(5)]
-    scales = [lax.shift_left(1, v).astype(jnp.float32) * 0.125 for v in levels]
+    levels, scales = [level[0, d] for d in range(5)], scales_of(level)
     parity = lax.rem(levels[0] + levels[1] + levels[2] + levels[3] + levels[4], 2)
     weight = (1 - 2 * parity).astype(jnp.float32) * (1.0 / math.sqrt(grids))
-    done = run_steps(bufs, rows, scales)
+    done = run_steps(bufs, rows, tables, scales[0])
     fine, middle = levels[0] >= 3, levels[0] >= 2
     block = outs[0][1].shape[0] // TILES
     for first, out in outs:
@@ -250,17 +272,18 @@
         out[block * TILES] = jnp.where(sublane == me, tile, 0.0)
 
 
-def middle_kernel(level, field, middle, near, *bufs):
+def middle_kernel(level, field, middle, near, left, right, *bufs):
     rows = field.shape[0] // 2
     block = rows // 2
+    fill_tables(scales_of(level), left, right)
     load_rows(field, block - LOW, rows + LOW + HIGH, bufs[0], 0)
     side = lax.div(2 * lax.axis_index("grid"), lax.axis_size("grid"))
     upper = lax.rem(side + lax.axis_index("slab"), 2) == 0
     first = jnp.where(upper, block, 0)
-    first_cycle(level, rows, ((first, middle), (block - first, near)), bufs)
-
-
-def outer_kernel(later, level, before, field, after, out, *bufs):
+    first_cycle(level, (left, right), rows, ((first, middle), (block - first, near)), bufs)
+
+
+def outer_kernel(later, level, left, right, before, field, after, out, *bufs):
     total = field.shape[0]
     block = out.shape[0] // TILES
     top = lax.rem(lax.axis_index("grid") + lax.axis_index("slab") + later, 2) == 0
@@ -275,10 +298,22 @@
         load_rows(before, 0, LOW, bufs[0], 0)
         load_rows(field, 0, block + HIGH, bufs[0], LOW)
 
-    first_cycle(level, block, ((0, out),), bufs)
-
-
-def second_kernel(rows, grids, before, own, after, out, total, wide, *bufs):
+    first_cycle(level, (left, right), block, ((0, out),), bufs)
+
+
+def sent_value(own, g, d):
+    return jnp.broadcast_to(own[own.shape[0] - 1, pl.ds(g, 1), d : d + 1], (1, N4))
+
+
+def tables_kernel(grids, own, left, right):
+    def grid(g, carry):
+        fill_tables([sent_value(own, g, d) for d in range(5)], left.at[g], right.at[g])
+        return carry
+
+    lax.fori_loop(0, grids, grid, 0)
+
+
+def second_kernel(rows, grids, left, right, before, own, after, out, total, wide, *bufs):
     extent = rows + LOW + HIGH
     for i in range(LOW * TILES):
         wide[i] = before[i]
@@ -289,10 +324,8 @@
     total[...] = jnp.zeros_like(total)
 
     def grid(g, carry):
-        spread = lambda d: jnp.broadcast_to(own[rows * TILES, pl.ds(g, 1), d : d + 1], (1, N4))
-        scales = [spread(d) for d in range(5)]
-        wide_of = lambda value: jnp.broadcast_to(value, (N2, N4))
-        fine, middle, weight = wide_of(spread(5)) > 2.5, wide_of(spread(5)) > 1.5, wide_of(spread(6))
+        tile = lambda d: jnp.broadcast_to(sent_value(own, g, d), (N2, N4))
+        fine, middle, weight = tile(5) > 2.5, tile(5) > 1.5, tile(6)
         start = bufs[0]
         for quad in range(0, extent - 1, 4):
             for t in range(TILES):
@@ -301,7 +334,7 @@
                     start[quad + i, t] = value
         for t in range(TILES):
             start[extent - 1, t] = wide[(extent - 1) * TILES + t]
-        done = run_steps(bufs, rows, scales)
+        done = run_steps(bufs, rows, (left.at[g], right.at[g]), tile(0))
         for quad in range(0, rows, 4):
             for t in range(TILES):
                 values = interpolate([done[LOW + quad + i, t] for i in range(5)], fine, middle)
@@ -389,8 +422,19 @@
 
     piece = floats(block * TILES + 1, N2, N4)
     work = 8192 * 40
-    middle, near = kernel(
-        middle_kernel, [piece, piece], [SMEM, VMEM], spaces(rows // 2), limit=6, flops=80 * work
+    size = 2 * TILES * N2
+
+    def tables(*lead):
+        shapes = (lead + (size, size), lead + (2 * N4, 2 * N4))
+        return [jax.ShapeDtypeStruct(shape, jnp.bfloat16) for shape in shapes]
+
+    middle, near, left, right = kernel(
+        middle_kernel,
+        [piece, piece] + tables(),
+        [SMEM, VMEM],
+        spaces(rows // 2),
+        limit=6,
+        flops=80 * work,
     )(levels, state)
 
     ready = lax.optimization_barrier((before, after, middle))
@@ -399,11 +443,11 @@
         return kernel(
             functools.partial(outer_kernel, later),
             piece,
-            [SMEM, VMEM, VMEM, VMEM],
+            [SMEM] + [VMEM] * 5,
             spaces(block),
             limit=6,
             flops=48 * work,
-        )(levels, ready[0], state, ready[1])
+        )(levels, left, right, ready[0], state, ready[1])
 
     edge = (lax.axis_index("grid") == 0) | (lax.axis_index("grid") == grids - 1)
     across = lax.ppermute(middle, "grid", [(1, 2), (2, 1)])
@@ -426,11 +470,14 @@
     before = lax.ppermute(own[(block - LOW) * TILES : block * TILES], both, forward)
     after = lax.ppermute(own[: HIGH * TILES], both, backward)
 
+    left, right = kernel(
+        functools.partial(tables_kernel, grids), tables(grids), [VMEM], flops=30 * work
+    )(own)
     half = N2 // 2
     sent = kernel(
         functools.partial(second_kernel, block, grids),
         floats(N3 * N1 * 2, half, block, N4),
-        [VMEM, VMEM, VMEM],
+        [VMEM] * 5,
         [
             pltpu.VMEM((block * TILES * N2, N4), jnp.float32),
             pltpu.VMEM(((block + LOW + HIGH) * TILES, N2, N4), jnp.float32),
@@ -438,7 +485,7 @@
         + spaces(block),
         limit=8,
         flops=400 * 8192 * 40,
-    )(before, own, after)
+    )(left, right, before, own, after)
 
     spread = lax.all_to_all(sent, both, split_axis=0, concat_axis=0, tiled=True)
 

time: 74.3 us -> 74.7 us (level)
  Pallas kernels: 15.4 us -> 16.5 us
    pallas_call x3 -> x4, Pallas kernels: 6.77 us -> 7.48 us  [the longest x2 3.95 us: outer_block(): kernel(functools.partial(outer_kernel, later), piece, [SMEM] + [VMEM] * 5...]
where the time goes in v6:
time: 74.7 us; the launch traced here: 74.4 us
  waiting for transfers between devices  34.2 us (46%)
  starting transfers between devices  22.5 us (30%)
  Pallas kernels  16.5 us (22%)
    all_to_all x1, waiting for transfers between devices, local_fast(): spread = lax.all_to_all(sent, both, split_axis=0, concat_axis=0, tiled=True)  9.14 us
    ppermute x1, waiting for transfers between devices, local_fast(): passed = lax.ppermute(joined, 'grid', [(1, 3), (2, 0)])  7.58 us
    pallas_call x1, Pallas kernels, local_fast(): kernel(functools.partial(second_kernel, block, grids), floats(N3 * N1 * 2...  6.72 us
    ppermute x1, starting transfers between devices, local_fast(): inwards = lax.ppermute(near, 'grid', [(0, 1), (3, 2)])  6.31 us
    ppermute x3, waiting for transfers between devices, local_fast(): lax.ppermute(value, 'grid', [(i, (i + d) % grids) for i in range(grids)])  5.35 us
    pallas_call x2, Pallas kernels, outer_block(): kernel(functools.partial(outer_kernel, later), piece, [SMEM] + [VMEM] * 5...  3.95 us
    ppermute x1, waiting for transfers between devices, local_fast(): lax.ppermute(own[(block - LOW) * TILES:block * TILES], both, forward)  3.92 us
    ppermute x1, waiting for transfers between devices, local_fast(): skipped = lax.ppermute(middle, 'grid', [(0, 2), (3, 1)])  3.79 us
  transfers between devices with their start and end apart: 13, of which 9 were waited for; matrix products, arithmetic and copies ran while one was open for 0% of the time, Pallas kernels for 7%

profile of v6, /device:TPU:0, one launch (start us, length us, event | category | flops | bytes accessed | tf_op | source)
XLA Modules:
  0.0 74.4 jit_solution(4840828659907357821)
XLA Ops:
  0.0 0.0 copy-start
  0.0 1.1 %shard_map.47 = (f32[4,64,128]{2,1,0:T(8,128)S(1)}, f32[5,64,128]{2,1,0:T(8,128)S(1)}) custom-call(f32[32,64,128]{2,1,0:T(8,128)} %bitcast.2), custom_call_target="tpu_custom_call" | custom-call | bytes 1048576 | tf_op jit(solution)/shard_map/pallas_call | solution.py:414
  1.1 0.0 copy-start.1
  1.1 2.5 %collective-permute-start.1 = (f32[5,64,128]{2,1,0:T(8,128)S(1)}, f32[5,64,128]{2,1,0:T(8,128)S(1)}, u32[]{:S(2)}, u32[]{:S(2)}) collective-permute-start(f32[5,64,128]{2,1,0:T(8,128)S(1)} %get-tuple-element.27), channel_id=1, source_target_pairs={{1,0},{2,1},{3,2},{0,3},{5,4},{6,5},{7,6},{4,7},{9,8},{10,9},{11,1... | collective-permute-start | bytes 491528 | tf_op jit(solution)/shard_map/ppermute | solution.py:421
  3.6 0.0 collective-permute-start
  3.6 0.0 copy-done
  3.6 0.0 copy-done.1
  3.6 2.9 %shard_map.46 = (f32[65,8,128]{2,1,0:T(8,128)S(1)}, f32[65,8,128]{2,1,0:T(8,128)S(1)}, bf16[128,128]{1,0:T(8,128)(2,1)S(1)}, bf16[256,256]{1,0:T(8,128)(2,1)S(1)}) custom-call(s32[1,5]{1,0:T(1,128)S(1)} %copy-done.1, f32[32,64,128]{2,1,0:T(8,128)S(1)} %bitcast.3), custom_call_target="tpu_custom_call" | custom-call | flops 26214400 | bytes 1048576 | tf_op jit(solution)/shard_map/pallas_call | solution.py:431
  6.5 2.3 %collective-permute-done.before = f32[4,64,128]{2,1,0:T(8,128)S(1)} collective-permute-done((f32[4,64,128]{2,1,0:T(8,128)S(1)}, f32[4,64,128]{2,1,0:T(8,128)S(1)}, u32[]{:S(2)}, u32[]{:S(2)}) %collective-permute-start) | collective-permute-done | bytes 131104 | tf_op jit(solution)/shard_map/ppermute | solution.py:420
  8.8 0.0 collective-permute-done.1.after
  8.8 2.0 %shard_map.48 = f32[65,8,128]{2,1,0:T(8,128)S(1)} custom-call(s32[1,5]{1,0:T(1,128)S(1)} %copy-done.1, bf16[128,128]{1,0:T(8,128)(2,1)S(1)} %get-tuple-element.24.left, bf16[256,256]{1,0:T(8,128)(2,1)S(1)} %get-tuple-element.25.right, f32[4,64,128]{2,1,0:T(8,128)S(1)} %collective-permute-done.before, f32[32,64,128]{2,1,0:T(8,128)S(1)} %bitcast.4, ...), custom_call_target="tpu_custom_call" | custom-call | flops 15728640 | bytes 1048576 | tf_op jit(solution)/shard_map/pallas_call | solution.py:443
  10.8 1.7 %collective-permute-start.2 = (f32[65,8,128]{2,1,0:T(8,128)S(1)}, f32[65,8,128]{2,1,0:T(8,128)S(1)}, u32[]{:S(2)}, u32[]{:S(2)}) collective-permute-start(f32[65,8,128]{2,1,0:T(8,128)S(1)} %shard_map.48), channel_id=1, source_target_pairs={{0,4},{4,0},{8,12},{12,8},{1,5},{5,1},{9,13},{13,9},{2,6},{6,2},{1... | collective-permute-start | bytes 798728 | tf_op jit(solution)/shard_map/ppermute | solution.py:455
  12.5 0.7 collective-permute-start.3
  13.1 6.3 %collective-permute-start.5 = (f32[65,8,128]{2,1,0:T(8,128)S(1)}, f32[65,8,128]{2,1,0:T(8,128)S(1)}, u32[]{:S(2)}, u32[]{:S(2)}) collective-permute-start(f32[65,8,128]{2,1,0:T(8,128)S(1)} %get-tuple-element.32), channel_id=1, source_target_pairs={{0,4},{12,8},{1,5},{13,9},{2,6},{14,10},{3,7},{15,11},{16,20},{28,... | collective-permute-start | bytes 798728 | tf_op jit(solution)/shard_map/ppermute | solution.py:458
  19.4 2.0 %shard_map.49 = f32[65,8,128]{2,1,0:T(8,128)S(1)} custom-call(s32[1,5]{1,0:T(1,128)S(1)} %copy-done.1, bf16[128,128]{1,0:T(8,128)(2,1)S(1)} %get-tuple-element.24.left, bf16[256,256]{1,0:T(8,128)(2,1)S(1)} %get-tuple-element.25.right, f32[4,64,128]{2,1,0:T(8,128)S(1)} %collective-permute-done.before, f32[32,64,128]{2,1,0:T(8,128)S(1)} %bitcast.5, ...), custom_call_target="tpu_custom_call" | custom-call | flops 15728640 | bytes 1048576 | tf_op jit(solution)/shard_map/pallas_call | solution.py:443
  21.4 1.3 %collective-permute-start.4 = (f32[65,8,128]{2,1,0:T(8,128)S(1)}, f32[65,8,128]{2,1,0:T(8,128)S(1)}, u32[]{:S(2)}, u32[]{:S(2)}) collective-permute-start(f32[65,8,128]{2,1,0:T(8,128)S(1)} %get-tuple-element.33), channel_id=1, source_target_pairs={{0,8},{12,4},{1,9},{13,5},{2,10},{14,6},{3,11},{15,7},{16,24},{28,... | collective-permute-start | bytes 798728 | tf_op jit(solution)/shard_map/ppermute | solution.py:457
  22.8 0.0 collective-permute-done.2
  22.8 1.3 %collective-permute-start.6 = (f32[65,8,128]{2,1,0:T(8,128)S(1)}, f32[65,8,128]{2,1,0:T(8,128)S(1)}, u32[]{:S(2)}, u32[]{:S(2)}) collective-permute-start(f32[65,8,128]{2,1,0:T(8,128)S(1)} %add.36), channel_id=1, source_target_pairs={{4,12},{8,0},{5,13},{9,1},{6,14},{10,2},{7,15},{11,3},{20,28},{24,... | collective-permute-start | bytes 798728 | tf_op jit(solution)/shard_map/ppermute | solution.py:461
  24.1 0.0 collective-permute-done.3
  24.1 2.1 %collective-permute-done.5 = f32[65,8,128]{2,1,0:T(8,128)S(1)} collective-permute-done((f32[65,8,128]{2,1,0:T(8,128)S(1)}, f32[65,8,128]{2,1,0:T(8,128)S(1)}, u32[]{:S(2)}, u32[]{:S(2)}) %collective-permute-start.5) | collective-permute-done | bytes 266272 | tf_op jit(solution)/shard_map/ppermute | solution.py:458
  26.2 3.8 %collective-permute-done.4 = f32[65,8,128]{2,1,0:T(8,128)S(1)} collective-permute-done((f32[65,8,128]{2,1,0:T(8,128)S(1)}, f32[65,8,128]{2,1,0:T(8,128)S(1)}, u32[]{:S(2)}, u32[]{:S(2)}) %collective-permute-start.4) | collective-permute-done | bytes 266272 | tf_op jit(solution)/shard_map/ppermute | solution.py:457
  30.0 7.6 %collective-permute-done.6 = f32[65,8,128]{2,1,0:T(8,128)S(1)} collective-permute-done((f32[65,8,128]{2,1,0:T(8,128)S(1)}, f32[65,8,128]{2,1,0:T(8,128)S(1)}, u32[]{:S(2)}, u32[]{:S(2)}) %collective-permute-start.6) | collective-permute-done | bytes 266272 | tf_op jit(solution)/shard_map/ppermute | solution.py:461
  37.6 0.1 add_add_fusion.own
  37.7 1.5 %collective-permute-start.8 = (f32[40,8,128]{2,1,0:T(8,128)S(1)}, f32[40,8,128]{2,1,0:T(8,128)S(1)}, u32[]{:S(2)}, u32[]{:S(2)}) collective-permute-start(f32[40,8,128]{2,1,0:T(8,128)S(1)} %slice.9), channel_id=1, source_target_pairs={{4,0},{8,4},{12,8},{13,12},{9,13},{5,9},{1,5},{2,1},{6,2},{10,6},{... | collective-permute-start | bytes 491528 | tf_op jit(solution)/shard_map/ppermute | solution.py:471
  39.3 0.6 collective-permute-start.7
  39.9 0.6 shard_map.50
  40.5 3.9 %collective-permute-done.7.before = f32[32,8,128]{2,1,0:T(8,128)S(1)} collective-permute-done((f32[32,8,128]{2,1,0:T(8,128)S(1)}, f32[32,8,128]{2,1,0:T(8,128)S(1)}, u32[]{:S(2)}, u32[]{:S(2)}) %collective-permute-start.7) | collective-permute-done | bytes 131104 | tf_op jit(solution)/shard_map/ppermute | solution.py:470
  44.4 0.0 collective-permute-done.8.after
  44.4 6.7 %shard_map.51 = f32[16,4,8,128]{3,2,1,0:T(8,128)} custom-call(bf16[4,128,128]{2,1,0:T(8,128)(2,1)S(1)} %get-tuple-element.34.left, bf16[4,256,256]{2,1,0:T(8,128)(2,1)S(1)} %get-tuple-element.35.right, f32[32,8,128]{2,1,0:T(8,128)S(1)} %collective-permute-done.7.before, f32[65,8,128]{2,1,0:T(8,128)S(1)} %add_add_fusion.own, ...), custom_call_target="tpu_custom_call" | custom-call | flops 131072000 | bytes 1048576 | tf_op jit(solution)/shard_map/pallas_call | solution.py:477
  51.2 0.0 copy-start.2
  51.2 3.7 %all-to-all-start = ((f32[16,4,8,128]{3,2,1,0:T(8,128)}), f32[16,4,8,128]{3,2,1,0:T(8,128)S(1)}, u32[]{:S(2)}, u32[]{:S(2)}) async-start(f32[16,4,8,128]{3,2,1,0:T(8,128)} %shard_map.51), calls=%async_computation | async-start | bytes 524288 | tf_op jit(solution)/shard_map/all_to_all | solution.py:490
  54.8 0.0 copy-done.2
  54.9 0.0 copy-start.3
  54.9 0.6 copy-done.3
  55.5 0.1 add_convert_fusion.matrix
  55.7 9.1 %all-to-all-done.rows = f32[16,4,8,128]{3,2,1,0:T(8,128)S(1)} async-done(((f32[16,4,8,128]{3,2,1,0:T(8,128)}), f32[16,4,8,128]{3,2,1,0:T(8,128)S(1)}, u32[]{:S(2)}, u32[]{:S(2)}) %all-to-all-start) | async-done | bytes 262176 | tf_op jit(solution)/shard_map/all_to_all | solution.py:490
  64.8 0.4 shard_map.52
  65.2 1.0 %collective-permute-start.10 = (f32[4,32,128]{2,1,0:T(8,128)S(1)}, f32[4,32,128]{2,1,0:T(8,128)S(1)}, u32[]{:S(2)}, u32[]{:S(2)}) collective-permute-start(f32[4,32,128]{2,1,0:T(8,128)S(1)} %get-tuple-element.41), channel_id=1, source_target_pairs={{0,8},{4,12},{8,0},{12,4},{1,9},{5,13},{9,1},{13,5},{2,10},{6,14},... | collective-permute-start | bytes 196616 | tf_op jit(solution)/shard_map/ppermute | solution.py:510
  66.2 0.8 %collective-permute-start.11 = (f32[4,32,128]{2,1,0:T(8,128)S(1)}, f32[4,32,128]{2,1,0:T(8,128)S(1)}, u32[]{:S(2)}, u32[]{:S(2)}) collective-permute-start(f32[4,32,128]{2,1,0:T(8,128)S(1)} %get-tuple-element.42), channel_id=1, source_target_pairs={{0,12},{4,0},{8,4},{12,8},{1,13},{5,1},{9,5},{13,9},{2,14},{6,2},{... | collective-permute-start | bytes 196616 | tf_op jit(solution)/shard_map/ppermute | solution.py:510
  67.0 1.2 %collective-permute-start.9 = (f32[4,32,128]{2,1,0:T(8,128)S(1)}, f32[4,32,128]{2,1,0:T(8,128)S(1)}, u32[]{:S(2)}, u32[]{:S(2)}) collective-permute-start(f32[4,32,128]{2,1,0:T(8,128)S(1)} %get-tuple-element.40), channel_id=1, source_target_pairs={{0,4},{4,8},{8,12},{12,0},{1,5},{5,9},{9,13},{13,1},{2,6},{6,10},{... | collective-permute-start | bytes 196616 | tf_op jit(solution)/shard_map/ppermute | solution.py:510
  68.2 3.3 %collective-permute-done.10.refs_2_ = f32[4,32,128]{2,1,0:T(8,128)S(1)} collective-permute-done((f32[4,32,128]{2,1,0:T(8,128)S(1)}, f32[4,32,128]{2,1,0:T(8,128)S(1)}, u32[]{:S(2)}, u32[]{:S(2)}) %collective-permute-start.10) | collective-permute-done | bytes 65568 | tf_op jit(solution)/shard_map/ppermute | solution.py:510
  71.5 0.3 collective-permute-done.11.refs_3_
  71.8 1.8 %collective-permute-done.9.refs_1_ = f32[4,32,128]{2,1,0:T(8,128)S(1)} collective-permute-done((f32[4,32,128]{2,1,0:T(8,128)S(1)}, f32[4,32,128]{2,1,0:T(8,128)S(1)}, u32[]{:S(2)}, u32[]{:S(2)}) %collective-permute-start.9) | collective-permute-done | bytes 65568 | tf_op jit(solution)/shard_map/ppermute | solution.py:510
  73.6 0.8 %shard_map.53 = f32[512,128]{1,0:T(8,128)} custom-call(f32[4,32,128]{2,1,0:T(8,128)S(1)} %get-tuple-element.36.refs_0_, f32[4,32,128]{2,1,0:T(8,128)S(1)} %collective-permute-done.9.refs_1_, f32[4,32,128]{2,1,0:T(8,128)S(1)} %collective-permute-done.10.refs_2_, f32[4,32,128]{2,1,0:T(8,128)S(1)} %collective-permute-done.11.refs_3_), custom_call_target="tpu_custom_call" | custom-call | bytes 1048576 | tf_op jit(solution)/shard_map/pallas_call | solution.py:513
  (5 shorter events, 0.1 us)
Async XLA Ops:
  0.0 3.6 %copy-start = (f32[1,32,64,128]{3,2,1,0:T(8,128)S(1)}, f32[1,32,64,128]{3,2,1,0:T(8,128)}, u32[]{:S(2)}) copy-start(f32[1,32,64,128]{3,2,1,0:T(8,128)} %param.4) | copy-start | bytes 3145732
  1.1 2.5 %copy-start.1 = (s32[1,5]{1,0:T(1,128)S(1)}, s32[1,5]{1,0:T(1,128)}, u32[]{:S(2)}) copy-start(s32[1,5]{1,0:T(1,128)} %level.5) | copy-start | bytes 64
  1.1 7.7 %collective-permute-start.1 = (f32[5,64,128]{2,1,0:T(8,128)S(1)}, f32[5,64,128]{2,1,0:T(8,128)S(1)}, u32[]{:S(2)}, u32[]{:S(2)}) collective-permute-start(f32[5,64,128]{2,1,0:T(8,128)S(1)} %get-tuple-element.27), channel_id=1, source_target_pairs={{1,0},{2,1},{3,2},{0,3},{5,4},{6,5},{7,6},{4,7},{9,8},{10,9},{11,1... | collective-permute-start | bytes 491528 | tf_op jit(solution)/shard_map/ppermute | solution.py:421
  3.6 5.3 %collective-permute-start = (f32[4,64,128]{2,1,0:T(8,128)S(1)}, f32[4,64,128]{2,1,0:T(8,128)S(1)}, u32[]{:S(2)}, u32[]{:S(2)}) collective-permute-start(f32[4,64,128]{2,1,0:T(8,128)S(1)} %get-tuple-element.26), channel_id=1, source_target_pairs={{0,1},{1,2},{2,3},{3,0},{4,5},{5,6},{6,7},{7,4},{8,9},{9,10},{10,1... | collective-permute-start | bytes 393224 | tf_op jit(solution)/shard_map/ppermute | solution.py:420
  10.8 11.9 %collective-permute-start.2 = (f32[65,8,128]{2,1,0:T(8,128)S(1)}, f32[65,8,128]{2,1,0:T(8,128)S(1)}, u32[]{:S(2)}, u32[]{:S(2)}) collective-permute-start(f32[65,8,128]{2,1,0:T(8,128)S(1)} %shard_map.48), channel_id=1, source_target_pairs={{0,4},{4,0},{8,12},{12,8},{1,5},{5,1},{9,13},{13,9},{2,6},{6,2},{1... | collective-permute-start | bytes 798728 | tf_op jit(solution)/shard_map/ppermute | solution.py:455
  12.5 11.7 %collective-permute-start.3 = (f32[65,8,128]{2,1,0:T(8,128)S(1)}, f32[65,8,128]{2,1,0:T(8,128)S(1)}, u32[]{:S(2)}, u32[]{:S(2)}) collective-permute-start(f32[65,8,128]{2,1,0:T(8,128)S(1)} %get-tuple-element.33), channel_id=1, source_target_pairs={{4,8},{8,4},{5,9},{9,5},{6,10},{10,6},{7,11},{11,7},{20,24},{24,20... | collective-permute-start | bytes 798728 | tf_op jit(solution)/shard_map/ppermute | solution.py:453
  13.1 13.1 %collective-permute-start.5 = (f32[65,8,128]{2,1,0:T(8,128)S(1)}, f32[65,8,128]{2,1,0:T(8,128)S(1)}, u32[]{:S(2)}, u32[]{:S(2)}) collective-permute-start(f32[65,8,128]{2,1,0:T(8,128)S(1)} %get-tuple-element.32), channel_id=1, source_target_pairs={{0,4},{12,8},{1,5},{13,9},{2,6},{14,10},{3,7},{15,11},{16,20},{28,... | collective-permute-start | bytes 798728 | tf_op jit(solution)/shard_map/ppermute | solution.py:458
  21.4 8.5 %collective-permute-start.4 = (f32[65,8,128]{2,1,0:T(8,128)S(1)}, f32[65,8,128]{2,1,0:T(8,128)S(1)}, u32[]{:S(2)}, u32[]{:S(2)}) collective-permute-start(f32[65,8,128]{2,1,0:T(8,128)S(1)} %get-tuple-element.33), channel_id=1, source_target_pairs={{0,8},{12,4},{1,9},{13,5},{2,10},{14,6},{3,11},{15,7},{16,24},{28,... | collective-permute-start | bytes 798728 | tf_op jit(solution)/shard_map/ppermute | solution.py:457
  22.8 14.8 %collective-permute-start.6 = (f32[65,8,128]{2,1,0:T(8,128)S(1)}, f32[65,8,128]{2,1,0:T(8,128)S(1)}, u32[]{:S(2)}, u32[]{:S(2)}) collective-permute-start(f32[65,8,128]{2,1,0:T(8,128)S(1)} %add.36), channel_id=1, source_target_pairs={{4,12},{8,0},{5,13},{9,1},{6,14},{10,2},{7,15},{11,3},{20,28},{24,... | collective-permute-start | bytes 798728 | tf_op jit(solution)/shard_map/ppermute | solution.py:461
  37.7 6.7 %collective-permute-start.8 = (f32[40,8,128]{2,1,0:T(8,128)S(1)}, f32[40,8,128]{2,1,0:T(8,128)S(1)}, u32[]{:S(2)}, u32[]{:S(2)}) collective-permute-start(f32[40,8,128]{2,1,0:T(8,128)S(1)} %slice.9), channel_id=1, source_target_pairs={{4,0},{8,4},{12,8},{13,12},{9,13},{5,9},{1,5},{2,1},{6,2},{10,6},{... | collective-permute-start | bytes 491528 | tf_op jit(solution)/shard_map/ppermute | solution.py:471
  39.3 5.2 %collective-permute-start.7 = (f32[32,8,128]{2,1,0:T(8,128)S(1)}, f32[32,8,128]{2,1,0:T(8,128)S(1)}, u32[]{:S(2)}, u32[]{:S(2)}) collective-permute-start(f32[32,8,128]{2,1,0:T(8,128)S(1)} %slice.8), channel_id=1, source_target_pairs={{0,4},{4,8},{8,12},{12,13},{13,9},{9,5},{5,1},{1,2},{2,6},{6,10},{... | collective-permute-start | bytes 393224 | tf_op jit(solution)/shard_map/ppermute | solution.py:470
  51.2 3.7 %copy-start.2 = (s32[128]{0:T(128)S(1)}, s32[128]{0:T(128)}, u32[]{:S(2)}) copy-start(s32[128]{0:T(128)} %param.6) | copy-start | bytes 1540
  51.2 13.7 %all-to-all-start = ((f32[16,4,8,128]{3,2,1,0:T(8,128)}), f32[16,4,8,128]{3,2,1,0:T(8,128)S(1)}, u32[]{:S(2)}, u32[]{:S(2)}) async-start(f32[16,4,8,128]{3,2,1,0:T(8,128)} %shard_map.51), calls=%async_computation | async-start | bytes 524288 | tf_op jit(solution)/shard_map/all_to_all | solution.py:490
  54.9 0.7 copy-start.3
  65.2 6.3 %collective-permute-start.10 = (f32[4,32,128]{2,1,0:T(8,128)S(1)}, f32[4,32,128]{2,1,0:T(8,128)S(1)}, u32[]{:S(2)}, u32[]{:S(2)}) collective-permute-start(f32[4,32,128]{2,1,0:T(8,128)S(1)} %get-tuple-element.41), channel_id=1, source_target_pairs={{0,8},{4,12},{8,0},{12,4},{1,9},{5,13},{9,1},{13,5},{2,10},{6,14},... | collective-permute-start | bytes 196616 | tf_op jit(solution)/shard_map/ppermute | solution.py:510
  66.2 5.6 %collective-permute-start.11 = (f32[4,32,128]{2,1,0:T(8,128)S(1)}, f32[4,32,128]{2,1,0:T(8,128)S(1)}, u32[]{:S(2)}, u32[]{:S(2)}) collective-permute-start(f32[4,32,128]{2,1,0:T(8,128)S(1)} %get-tuple-element.42), channel_id=1, source_target_pairs={{0,12},{4,0},{8,4},{12,8},{1,13},{5,1},{9,5},{13,9},{2,14},{6,2},{... | collective-permute-start | bytes 196616 | tf_op jit(solution)/shard_map/ppermute | solution.py:510
  67.0 6.6 %collective-permute-start.9 = (f32[4,32,128]{2,1,0:T(8,128)S(1)}, f32[4,32,128]{2,1,0:T(8,128)S(1)}, u32[]{:S(2)}, u32[]{:S(2)}) collective-permute-start(f32[4,32,128]{2,1,0:T(8,128)S(1)} %get-tuple-element.40), channel_id=1, source_target_pairs={{0,4},{4,8},{8,12},{12,0},{1,5},{5,9},{9,13},{13,1},{2,6},{6,10},{... | collective-permute-start | bytes 196616 | tf_op jit(solution)/shard_map/ppermute | solution.py:510

commit v7 on v6

--- a/solution.py
+++ b/solution.py
@@ -129,12 +129,11 @@
 UNROLL = 2
 
 
-def fill_tables(scales, left, right):
+def fill_tables(scales, left):
     size = TILES * N2
     squares = [value * value for value in scales]
     total = sum(scales[1:], scales[0])
     square = sum(squares[1:], squares[0])
-
     shape = (size, 2 * size)
     row = lax.broadcasted_iota(jnp.int32, shape, 0)
     column = lax.bitwise_and(lax.broadcasted_iota(jnp.int32, shape, 1), size - 1)
@@ -147,39 +146,33 @@
         ahead = column == rest + lax.bitwise_and(digit + 1, count - 1) * unit
         drift = drift + jnp.where(back, scales[d], 0.0)
         second = second + jnp.where(back, squares[d], 0.0) + jnp.where(ahead, squares[d], 0.0)
-    left[...] = jnp.concatenate([second, drift], axis=0).astype(jnp.bfloat16)
-
-    shape = (N4, N4)
-    row = lax.broadcasted_iota(jnp.int32, shape, 0)
-    column = lax.broadcasted_iota(jnp.int32, shape, 1)
-    back = row == lax.bitwise_and(column + N4 - 1, N4 - 1)
-    ahead = row == lax.bitwise_and(column + 1, N4 - 1)
-    drift = jnp.where(back, scales[4], 0.0)
-    second = jnp.where(back, squares[4], 0.0) + jnp.where(ahead, squares[4], 0.0)
-    both = jnp.concatenate([second, drift], axis=1).astype(jnp.bfloat16)
-    right[...] = jnp.concatenate([both, both], axis=0)
-
-
-def step_rows(src, dst, first, count, tables, factors, products):
-    left, right = tables
-    s0, q0 = factors
+    left[:, : 2 * size] = jnp.concatenate([second, drift], axis=0).astype(jnp.bfloat16)
+    drift = jnp.where(row == column, scales[0], 0.0)
+    second = jnp.where(row == column, squares[0], 0.0)
+    left[:, 2 * size :] = jnp.concatenate([second, drift], axis=0).astype(jnp.bfloat16)
+
+
+def step_rows(src, dst, first, count, left, factors, products):
+    q0, s4, q4 = factors
     size = TILES * N2
 
     def rows_of(group):
         return range(first + group * UNROLL, first + min(count, (group + 1) * UNROLL))
 
+    def parts(row):
+        value = src[row].reshape(size, N4)
+        high = value.astype(jnp.bfloat16)
+        return jnp.concatenate([high, (value - high.astype(jnp.float32)).astype(jnp.bfloat16)], axis=0)
+
+    last = [parts(first - 1)]
+
     def multiply(group):
-        values = [src[row].reshape(size, N4) for row in rows_of(group)]
-        high = [value.astype(jnp.bfloat16) for value in values]
-        rest = [(value - h.astype(jnp.float32)).astype(jnp.bfloat16) for value, h in zip(values, high)]
-        across, along = products[group % 2]
-        stacked = [jnp.concatenate(pair, axis=0) for pair in zip(high, rest)]
-        across[:, : len(values) * N4] = jnp.dot(
-            left[...], jnp.concatenate(stacked, axis=1), preferred_element_type=jnp.float32
-        )
-        beside = [jnp.concatenate(pair, axis=1) for pair in zip(high, rest)]
-        along[: len(values) * size] = jnp.dot(
-            jnp.concatenate(beside, axis=0), right[...], preferred_element_type=jnp.float32
+        held = [parts(row) for row in rows_of(group)]
+        below = last + held
+        last[:] = [held[-1]]
+        held = [jnp.concatenate(pair, axis=0) for pair in zip(held, below)]
+        products[group % 2][:, : len(held) * N4] = jnp.dot(
+            left[...], jnp.concatenate(held, axis=1), preferred_element_type=jnp.float32
         )
 
     groups = -(-count // UNROLL)
@@ -187,16 +180,15 @@
     for group in range(groups):
         if group + 1 < groups:
             multiply(group + 1)
-        across, along = products[group % 2]
+        product = products[group % 2]
         for i, row in enumerate(rows_of(group)):
             lanes = slice(i * N4, (i + 1) * N4)
             for t in range(TILES):
-                u, below, above = src[row, t], src[row - 1, t], src[row + 1, t]
-                here = slice(t * N2, (t + 1) * N2)
-                there = slice(size + t * N2, size + (t + 1) * N2)
-                beside = slice(i * size + t * N2, i * size + (t + 1) * N2)
-                second = (across[here, lanes] + along[beside, :N4]) + q0 * (below + above)
-                drift = (across[there, lanes] + along[beside, N4:]) + s0 * below
+                u, above = src[row, t], src[row + 1, t]
+                back, ahead = pltpu.roll(u, 1, 1), pltpu.roll(u, N4 - 1, 1)
+                second = product[t * N2 : (t + 1) * N2, lanes] + q0 * above
+                drift = product[size + t * N2 : size + (t + 1) * N2, lanes] + s4 * back
+                second = second + q4 * (back + ahead)
                 speed = ADVECT + (0.5 * ADVECT) * jnp.tanh(u)
                 dst[row, t] = (u + DIFFUSE * second) + speed * drift
 
@@ -211,17 +203,16 @@
 
 def spaces(rows):
     state = pltpu.VMEM((rows + LOW + HIGH, TILES, N2, N4), jnp.float32)
-    size = TILES * N2
-    across = pltpu.VMEM((2 * size, UNROLL * N4), jnp.float32)
-    along = pltpu.VMEM((UNROLL * size, 2 * N4), jnp.float32)
-    return [state, state, across, along, across, along]
-
-
-def run_steps(bufs, rows, tables, s0):
-    states, products = bufs[0:2], (bufs[2:4], bufs[4:6])
+    product = pltpu.VMEM((2 * TILES * N2, UNROLL * N4), jnp.float32)
+    return [state, state, product, product]
+
+
+def run_steps(bufs, rows, left, scales):
+    states, products = bufs[0:2], bufs[2:4]
+    factors = (scales[0] * scales[0], scales[4], scales[4] * scales[4])
     for step in range(STEPS):
         count = rows + LOW + HIGH - 2 * (step + 1)
-        step_rows(states[step % 2], states[(step + 1) % 2], step + 1, count, tables, (s0, s0 * s0), products)
+        step_rows(states[step % 2], states[(step + 1) % 2], step + 1, count, left, factors, products)
     return states[STEPS % 2]
 
 
@@ -249,12 +240,12 @@
     return [lax.shift_left(1, level[0, d]).astype(jnp.float32) * 0.125 for d in range(5)]
 
 
-def first_cycle(level, tables, rows, outs, bufs):
+def first_cycle(level, left, rows, outs, bufs):
     me, grids = lax.axis_index("grid"), lax.axis_size("grid")
     levels, scales = [level[0, d] for d in range(5)], scales_of(level)
     parity = lax.rem(levels[0] + levels[1] + levels[2] + levels[3] + levels[4], 2)
     weight = (1 - 2 * parity).astype(jnp.float32) * (1.0 / math.sqrt(grids))
-    done = run_steps(bufs, rows, tables, scales[0])
+    done = run_steps(bufs, rows, left, scales)
     fine, middle = levels[0] >= 3, levels[0] >= 2
     block = outs[0][1].shape[0] // TILES
     for first, out in outs:
@@ -272,18 +263,18 @@
         out[block * TILES] = jnp.where(sublane == me, tile, 0.0)
 
 
-def middle_kernel(level, field, middle, near, left, right, *bufs):
+def middle_kernel(level, field, middle, near, left, *bufs):
     rows = field.shape[0] // 2
     block = rows // 2
-    fill_tables(scales_of(level), left, right)
+    fill_tables(scales_of(level), left)
     load_rows(field, block - LOW, rows + LOW + HIGH, bufs[0], 0)
     side = lax.div(2 * lax.axis_index("grid"), lax.axis_size("grid"))
     upper = lax.rem(side + lax.axis_index("slab"), 2) == 0
     first = jnp.where(upper, block, 0)
-    first_cycle(level, (left, right), rows, ((first, middle), (block - first, near)), bufs)
-
-
-def outer_kernel(later, level, left, right, before, field, after, out, *bufs):
+    first_cycle(level, left, rows, ((first, middle), (block - first, near)), bufs)
+
+
+def outer_kernel(later, level, left, before, field, after, out, *bufs):
     total = field.shape[0]
     block = out.shape[0] // TILES
     top = lax.rem(lax.axis_index("grid") + lax.axis_index("slab") + later, 2) == 0
@@ -298,22 +289,22 @@
         load_rows(before, 0, LOW, bufs[0], 0)
         load_rows(field, 0, block + HIGH, bufs[0], LOW)
 
-    first_cycle(level, (left, right), block, ((0, out),), bufs)
+    first_cycle(level, left, block, ((0, out),), bufs)
 
 
 def sent_value(own, g, d):
     return jnp.broadcast_to(own[own.shape[0] - 1, pl.ds(g, 1), d : d + 1], (1, N4))
 
 
-def tables_kernel(grids, own, left, right):
+def tables_kernel(grids, own, left):
     def grid(g, carry):
-        fill_tables([sent_value(own, g, d) for d in range(5)], left.at[g], right.at[g])
+        fill_tables([sent_value(own, g, d) for d in range(5)], left.at[g])
         return carry
 
     lax.fori_loop(0, grids, grid, 0)
 
 
-def second_kernel(rows, grids, left, right, before, own, after, out, total, wide, *bufs):
+def second_kernel(rows, grids, left, before, own, after, out, total, wide, *bufs):
     extent = rows + LOW + HIGH
     for i in range(LOW * TILES):
         wide[i] = before[i]
@@ -334,7 +325,7 @@
                     start[quad + i, t] = value
         for t in range(TILES):
             start[extent - 1, t] = wide[(extent - 1) * TILES + t]
-        done = run_steps(bufs, rows, (left.at[g], right.at[g]), tile(0))
+        done = run_steps(bufs, rows, left.at[g], [tile(d) for d in range(5)])
         for quad in range(0, rows, 4):
             for t in range(TILES):
                 values = interpolate([done[LOW + quad + i, t] for i in range(5)], fine, middle)
@@ -424,13 +415,12 @@
     work = 8192 * 40
     size = 2 * TILES * N2
 
-    def tables(*lead):
-        shapes = (lead + (size, size), lead + (2 * N4, 2 * N4))
-        return [jax.ShapeDtypeStruct(shape, jnp.bfloat16) for shape in shapes]
-
-    middle, near, left, right = kernel(
+    def table(*lead):
+        return jax.ShapeDtypeStruct(lead + (size, 2 * size), jnp.bfloat16)
+
+    middle, near, left = kernel(
         middle_kernel,
-        [piece, piece] + tables(),
+        [piece, piece, table()],
         [SMEM, VMEM],
         spaces(rows // 2),
         limit=6,
@@ -443,11 +433,11 @@
         return kernel(
             functools.partial(outer_kernel, later),
             piece,
-            [SMEM] + [VMEM] * 5,
+            [SMEM] + [VMEM] * 4,
             spaces(block),
             limit=6,
             flops=48 * work,
-        )(levels, left, right, ready[0], state, ready[1])
+        )(levels, left, ready[0], state, ready[1])
 
     edge = (lax.axis_index("grid") == 0) | (lax.axis_index("grid") == grids - 1)
     across = lax.ppermute(middle, "grid", [(1, 2), (2, 1)])
@@ -470,14 +460,14 @@
     before = lax.ppermute(own[(block - LOW) * TILES : block * TILES], both, forward)
     after = lax.ppermute(own[: HIGH * TILES], both, backward)
 
-    left, right = kernel(
-        functools.partial(tables_kernel, grids), tables(grids), [VMEM], flops=30 * work
+    left = kernel(
+        functools.partial(tables_kernel, grids), table(grids), [VMEM], flops=30 * work
     )(own)
     half = N2 // 2
     sent = kernel(
         functools.partial(second_kernel, block, grids),
         floats(N3 * N1 * 2, half, block, N4),
-        [VMEM] * 5,
+        [VMEM] * 4,
         [
             pltpu.VMEM((block * TILES * N2, N4), jnp.float32),
             pltpu.VMEM(((block + LOW + HIGH) * TILES, N2, N4), jnp.float32),
@@ -485,7 +475,7 @@
         + spaces(block),
         limit=8,
         flops=400 * 8192 * 40,
-    )(left, right, before, own, after)
+    )(left, before, own, after)
 
     spread = lax.all_to_all(sent, both, split_axis=0, concat_axis=0, tiled=True)
 

time: 74.7 us -> 73.9 us (0.989)
  Pallas kernels: 16.5 us -> 15.4 us
where the time goes in v7:
time: 73.9 us; the launch traced here: 73.6 us
  waiting for transfers between devices  34.4 us (47%)
  starting transfers between devices  22.5 us (30%)
  Pallas kernels  15.4 us (21%)
    all_to_all x1, waiting for transfers between devices, local_fast(): spread = lax.all_to_all(sent, both, split_axis=0, concat_axis=0, tiled=True)  9.14 us
    ppermute x1, waiting for transfers between devices, local_fast(): passed = lax.ppermute(joined, 'grid', [(1, 3), (2, 0)])  7.53 us
    ppermute x1, starting transfers between devices, local_fast(): inwards = lax.ppermute(near, 'grid', [(0, 1), (3, 2)])  6.31 us
    pallas_call x1, Pallas kernels, local_fast(): kernel(functools.partial(second_kernel, block, grids), floats(N3 * N1 * 2...  6.07 us
    ppermute x3, waiting for transfers between devices, local_fast(): lax.ppermute(value, 'grid', [(i, (i + d) % grids) for i in range(grids)])  5.35 us
    ppermute x1, waiting for transfers between devices, local_fast(): lax.ppermute(own[(block - LOW) * TILES:block * TILES], both, forward)  4.05 us
    ppermute x1, waiting for transfers between devices, local_fast(): skipped = lax.ppermute(middle, 'grid', [(0, 2), (3, 1)])  3.79 us
    pallas_call x2, Pallas kernels, outer_block(): kernel(functools.partial(outer_kernel, later), piece, [SMEM] + [VMEM] * 4...  3.75 us
  transfers between devices with their start and end apart: 13, of which 9 were waited for; matrix products, arithmetic and copies ran while one was open for 0% of the time, Pallas kernels for 7%

profile of v7, /device:TPU:0, one launch (start us, length us, event | category | flops | bytes accessed | tf_op | source)
XLA Modules:
  0.0 73.6 jit_solution(5099730892666154047)
XLA Ops:
  0.0 0.0 copy-start
  0.0 1.1 %shard_map.47 = (f32[4,64,128]{2,1,0:T(8,128)S(1)}, f32[5,64,128]{2,1,0:T(8,128)S(1)}) custom-call(f32[32,64,128]{2,1,0:T(8,128)} %bitcast.2), custom_call_target="tpu_custom_call" | custom-call | bytes 1048576 | tf_op jit(solution)/shard_map/pallas_call | solution.py:405
  1.1 0.0 copy-start.1
  1.1 2.5 %collective-permute-start.1 = (f32[5,64,128]{2,1,0:T(8,128)S(1)}, f32[5,64,128]{2,1,0:T(8,128)S(1)}, u32[]{:S(2)}, u32[]{:S(2)}) collective-permute-start(f32[5,64,128]{2,1,0:T(8,128)S(1)} %get-tuple-element.23), channel_id=1, source_target_pairs={{1,0},{2,1},{3,2},{0,3},{5,4},{6,5},{7,6},{4,7},{9,8},{10,9},{11,1... | collective-permute-start | bytes 491528 | tf_op jit(solution)/shard_map/ppermute | solution.py:412
  3.6 0.0 collective-permute-start
  3.6 0.0 copy-done
  3.6 0.0 copy-done.1
  3.6 2.8 %shard_map.46 = (f32[65,8,128]{2,1,0:T(8,128)S(1)}, f32[65,8,128]{2,1,0:T(8,128)S(1)}, bf16[128,256]{1,0:T(8,128)(2,1)S(1)}) custom-call(s32[1,5]{1,0:T(1,128)S(1)} %copy-done.1, f32[32,64,128]{2,1,0:T(8,128)S(1)} %bitcast.3), custom_call_target="tpu_custom_call" | custom-call | flops 26214400 | bytes 1048576 | tf_op jit(solution)/shard_map/pallas_call | solution.py:421
  6.4 2.4 %collective-permute-done.before = f32[4,64,128]{2,1,0:T(8,128)S(1)} collective-permute-done((f32[4,64,128]{2,1,0:T(8,128)S(1)}, f32[4,64,128]{2,1,0:T(8,128)S(1)}, u32[]{:S(2)}, u32[]{:S(2)}) %collective-permute-start) | collective-permute-done | bytes 131104 | tf_op jit(solution)/shard_map/ppermute | solution.py:411
  8.8 0.0 collective-permute-done.1.after
  8.8 1.9 %shard_map.48 = f32[65,8,128]{2,1,0:T(8,128)S(1)} custom-call(s32[1,5]{1,0:T(1,128)S(1)} %copy-done.1, bf16[128,256]{1,0:T(8,128)(2,1)S(1)} %get-tuple-element.21.left, f32[4,64,128]{2,1,0:T(8,128)S(1)} %collective-permute-done.before, f32[32,64,128]{2,1,0:T(8,128)S(1)} %bitcast.4, f32[5,64,128]{2,1,0:T(8,128)S(1)} %collective-permute-done.1.after), custom_call_target="tpu_custom_call" | custom-call | flops 15728640 | bytes 1048576 | tf_op jit(solution)/shard_map/pallas_call | solution.py:433
  10.7 1.6 %collective-permute-start.2 = (f32[65,8,128]{2,1,0:T(8,128)S(1)}, f32[65,8,128]{2,1,0:T(8,128)S(1)}, u32[]{:S(2)}, u32[]{:S(2)}) collective-permute-start(f32[65,8,128]{2,1,0:T(8,128)S(1)} %shard_map.48), channel_id=1, source_target_pairs={{0,4},{4,0},{8,12},{12,8},{1,5},{5,1},{9,13},{13,9},{2,6},{6,2},{1... | collective-permute-start | bytes 798728 | tf_op jit(solution)/shard_map/ppermute | solution.py:445
  12.4 0.7 collective-permute-start.3
  13.0 6.3 %collective-permute-start.5 = (f32[65,8,128]{2,1,0:T(8,128)S(1)}, f32[65,8,128]{2,1,0:T(8,128)S(1)}, u32[]{:S(2)}, u32[]{:S(2)}) collective-permute-start(f32[65,8,128]{2,1,0:T(8,128)S(1)} %get-tuple-element.28), channel_id=1, source_target_pairs={{0,4},{12,8},{1,5},{13,9},{2,6},{14,10},{3,7},{15,11},{16,20},{28,... | collective-permute-start | bytes 798728 | tf_op jit(solution)/shard_map/ppermute | solution.py:448
  19.3 1.9 %shard_map.49 = f32[65,8,128]{2,1,0:T(8,128)S(1)} custom-call(s32[1,5]{1,0:T(1,128)S(1)} %copy-done.1, bf16[128,256]{1,0:T(8,128)(2,1)S(1)} %get-tuple-element.21.left, f32[4,64,128]{2,1,0:T(8,128)S(1)} %collective-permute-done.before, f32[32,64,128]{2,1,0:T(8,128)S(1)} %bitcast.5, f32[5,64,128]{2,1,0:T(8,128)S(1)} %collective-permute-done.1.after), custom_call_target="tpu_custom_call" | custom-call | flops 15728640 | bytes 1048576 | tf_op jit(solution)/shard_map/pallas_call | solution.py:433
  21.2 1.3 %collective-permute-start.4 = (f32[65,8,128]{2,1,0:T(8,128)S(1)}, f32[65,8,128]{2,1,0:T(8,128)S(1)}, u32[]{:S(2)}, u32[]{:S(2)}) collective-permute-start(f32[65,8,128]{2,1,0:T(8,128)S(1)} %get-tuple-element.29), channel_id=1, source_target_pairs={{0,8},{12,4},{1,9},{13,5},{2,10},{14,6},{3,11},{15,7},{16,24},{28,... | collective-permute-start | bytes 798728 | tf_op jit(solution)/shard_map/ppermute | solution.py:447
  22.5 0.0 collective-permute-done.2
  22.6 1.3 %collective-permute-start.6 = (f32[65,8,128]{2,1,0:T(8,128)S(1)}, f32[65,8,128]{2,1,0:T(8,128)S(1)}, u32[]{:S(2)}, u32[]{:S(2)}) collective-permute-start(f32[65,8,128]{2,1,0:T(8,128)S(1)} %add.36), channel_id=1, source_target_pairs={{4,12},{8,0},{5,13},{9,1},{6,14},{10,2},{7,15},{11,3},{20,28},{24,... | collective-permute-start | bytes 798728 | tf_op jit(solution)/shard_map/ppermute | solution.py:451
  23.9 0.0 collective-permute-done.3
  23.9 2.2 %collective-permute-done.5 = f32[65,8,128]{2,1,0:T(8,128)S(1)} collective-permute-done((f32[65,8,128]{2,1,0:T(8,128)S(1)}, f32[65,8,128]{2,1,0:T(8,128)S(1)}, u32[]{:S(2)}, u32[]{:S(2)}) %collective-permute-start.5) | collective-permute-done | bytes 266272 | tf_op jit(solution)/shard_map/ppermute | solution.py:448
  26.1 3.8 %collective-permute-done.4 = f32[65,8,128]{2,1,0:T(8,128)S(1)} collective-permute-done((f32[65,8,128]{2,1,0:T(8,128)S(1)}, f32[65,8,128]{2,1,0:T(8,128)S(1)}, u32[]{:S(2)}, u32[]{:S(2)}) %collective-permute-start.4) | collective-permute-done | bytes 266272 | tf_op jit(solution)/shard_map/ppermute | solution.py:447
  29.9 7.5 %collective-permute-done.6 = f32[65,8,128]{2,1,0:T(8,128)S(1)} collective-permute-done((f32[65,8,128]{2,1,0:T(8,128)S(1)}, f32[65,8,128]{2,1,0:T(8,128)S(1)}, u32[]{:S(2)}, u32[]{:S(2)}) %collective-permute-start.6) | collective-permute-done | bytes 266272 | tf_op jit(solution)/shard_map/ppermute | solution.py:451
  37.4 0.1 add_add_fusion.own
  37.6 1.5 %collective-permute-start.8 = (f32[40,8,128]{2,1,0:T(8,128)S(1)}, f32[40,8,128]{2,1,0:T(8,128)S(1)}, u32[]{:S(2)}, u32[]{:S(2)}) collective-permute-start(f32[40,8,128]{2,1,0:T(8,128)S(1)} %slice.9), channel_id=1, source_target_pairs={{4,0},{8,4},{12,8},{13,12},{9,13},{5,9},{1,5},{2,1},{6,2},{10,6},{... | collective-permute-start | bytes 491528 | tf_op jit(solution)/shard_map/ppermute | solution.py:461
  39.1 0.7 collective-permute-start.7
  39.7 0.5 shard_map.50.left
  40.2 4.0 %collective-permute-done.7.before = f32[32,8,128]{2,1,0:T(8,128)S(1)} collective-permute-done((f32[32,8,128]{2,1,0:T(8,128)S(1)}, f32[32,8,128]{2,1,0:T(8,128)S(1)}, u32[]{:S(2)}, u32[]{:S(2)}) %collective-permute-start.7) | collective-permute-done | bytes 131104 | tf_op jit(solution)/shard_map/ppermute | solution.py:460
  44.3 0.0 collective-permute-done.8.after
  44.3 6.1 %shard_map.51 = f32[16,4,8,128]{3,2,1,0:T(8,128)} custom-call(bf16[4,128,256]{2,1,0:T(8,128)(2,1)S(1)} %shard_map.50.left, f32[32,8,128]{2,1,0:T(8,128)S(1)} %collective-permute-done.7.before, f32[65,8,128]{2,1,0:T(8,128)S(1)} %add_add_fusion.own, f32[40,8,128]{2,1,0:T(8,128)S(1)} %collective-permute-done.8.after), custom_call_target="tpu_custom_call" | custom-call | flops 131072000 | bytes 1048576 | tf_op jit(solution)/shard_map/pallas_call | solution.py:467
  50.3 0.0 copy-start.2
  50.4 3.7 %all-to-all-start = ((f32[16,4,8,128]{3,2,1,0:T(8,128)}), f32[16,4,8,128]{3,2,1,0:T(8,128)S(1)}, u32[]{:S(2)}, u32[]{:S(2)}) async-start(f32[16,4,8,128]{3,2,1,0:T(8,128)} %shard_map.51), calls=%async_computation | async-start | bytes 524288 | tf_op jit(solution)/shard_map/all_to_all | solution.py:480
  54.0 0.0 copy-done.2
  54.1 0.0 copy-start.3
  54.1 0.6 copy-done.3
  54.7 0.1 add_convert_fusion.matrix
  54.9 9.1 %all-to-all-done.rows = f32[16,4,8,128]{3,2,1,0:T(8,128)S(1)} async-done(((f32[16,4,8,128]{3,2,1,0:T(8,128)}), f32[16,4,8,128]{3,2,1,0:T(8,128)S(1)}, u32[]{:S(2)}, u32[]{:S(2)}) %all-to-all-start) | async-done | bytes 262176 | tf_op jit(solution)/shard_map/all_to_all | solution.py:480
  64.0 0.4 shard_map.52
  64.4 1.0 %collective-permute-start.10 = (f32[4,32,128]{2,1,0:T(8,128)S(1)}, f32[4,32,128]{2,1,0:T(8,128)S(1)}, u32[]{:S(2)}, u32[]{:S(2)}) collective-permute-start(f32[4,32,128]{2,1,0:T(8,128)S(1)} %get-tuple-element.35), channel_id=1, source_target_pairs={{0,8},{4,12},{8,0},{12,4},{1,9},{5,13},{9,1},{13,5},{2,10},{6,14},... | collective-permute-start | bytes 196616 | tf_op jit(solution)/shard_map/ppermute | solution.py:500
  65.4 0.8 %collective-permute-start.11 = (f32[4,32,128]{2,1,0:T(8,128)S(1)}, f32[4,32,128]{2,1,0:T(8,128)S(1)}, u32[]{:S(2)}, u32[]{:S(2)}) collective-permute-start(f32[4,32,128]{2,1,0:T(8,128)S(1)} %get-tuple-element.36), channel_id=1, source_target_pairs={{0,12},{4,0},{8,4},{12,8},{1,13},{5,1},{9,5},{13,9},{2,14},{6,2},{... | collective-permute-start | bytes 196616 | tf_op jit(solution)/shard_map/ppermute | solution.py:500
  66.2 1.2 %collective-permute-start.9 = (f32[4,32,128]{2,1,0:T(8,128)S(1)}, f32[4,32,128]{2,1,0:T(8,128)S(1)}, u32[]{:S(2)}, u32[]{:S(2)}) collective-permute-start(f32[4,32,128]{2,1,0:T(8,128)S(1)} %get-tuple-element.34), channel_id=1, source_target_pairs={{0,4},{4,8},{8,12},{12,0},{1,5},{5,9},{9,13},{13,1},{2,6},{6,10},{... | collective-permute-start | bytes 196616 | tf_op jit(solution)/shard_map/ppermute | solution.py:500
  67.4 3.3 %collective-permute-done.10.refs_2_ = f32[4,32,128]{2,1,0:T(8,128)S(1)} collective-permute-done((f32[4,32,128]{2,1,0:T(8,128)S(1)}, f32[4,32,128]{2,1,0:T(8,128)S(1)}, u32[]{:S(2)}, u32[]{:S(2)}) %collective-permute-start.10) | collective-permute-done | bytes 65568 | tf_op jit(solution)/shard_map/ppermute | solution.py:500
  70.7 0.3 collective-permute-done.11.refs_3_
  71.0 1.8 %collective-permute-done.9.refs_1_ = f32[4,32,128]{2,1,0:T(8,128)S(1)} collective-permute-done((f32[4,32,128]{2,1,0:T(8,128)S(1)}, f32[4,32,128]{2,1,0:T(8,128)S(1)}, u32[]{:S(2)}, u32[]{:S(2)}) %collective-permute-start.9) | collective-permute-done | bytes 65568 | tf_op jit(solution)/shard_map/ppermute | solution.py:500
  72.8 0.8 %shard_map.53 = f32[512,128]{1,0:T(8,128)} custom-call(f32[4,32,128]{2,1,0:T(8,128)S(1)} %get-tuple-element.30.refs_0_, f32[4,32,128]{2,1,0:T(8,128)S(1)} %collective-permute-done.9.refs_1_, f32[4,32,128]{2,1,0:T(8,128)S(1)} %collective-permute-done.10.refs_2_, f32[4,32,128]{2,1,0:T(8,128)S(1)} %collective-permute-done.11.refs_3_), custom_call_target="tpu_custom_call" | custom-call | bytes 1048576 | tf_op jit(solution)/shard_map/pallas_call | solution.py:503
  (5 shorter events, 0.1 us)
Async XLA Ops:
  0.0 3.6 %copy-start = (f32[1,32,64,128]{3,2,1,0:T(8,128)S(1)}, f32[1,32,64,128]{3,2,1,0:T(8,128)}, u32[]{:S(2)}) copy-start(f32[1,32,64,128]{3,2,1,0:T(8,128)} %param.4) | copy-start | bytes 3145732
  1.1 2.5 %copy-start.1 = (s32[1,5]{1,0:T(1,128)S(1)}, s32[1,5]{1,0:T(1,128)}, u32[]{:S(2)}) copy-start(s32[1,5]{1,0:T(1,128)} %level.5) | copy-start | bytes 64
  1.1 7.7 %collective-permute-start.1 = (f32[5,64,128]{2,1,0:T(8,128)S(1)}, f32[5,64,128]{2,1,0:T(8,128)S(1)}, u32[]{:S(2)}, u32[]{:S(2)}) collective-permute-start(f32[5,64,128]{2,1,0:T(8,128)S(1)} %get-tuple-element.23), channel_id=1, source_target_pairs={{1,0},{2,1},{3,2},{0,3},{5,4},{6,5},{7,6},{4,7},{9,8},{10,9},{11,1... | collective-permute-start | bytes 491528 | tf_op jit(solution)/shard_map/ppermute | solution.py:412
  3.6 5.3 %collective-permute-start = (f32[4,64,128]{2,1,0:T(8,128)S(1)}, f32[4,64,128]{2,1,0:T(8,128)S(1)}, u32[]{:S(2)}, u32[]{:S(2)}) collective-permute-start(f32[4,64,128]{2,1,0:T(8,128)S(1)} %get-tuple-element.22), channel_id=1, source_target_pairs={{0,1},{1,2},{2,3},{3,0},{4,5},{5,6},{6,7},{7,4},{8,9},{9,10},{10,1... | collective-permute-start | bytes 393224 | tf_op jit(solution)/shard_map/ppermute | solution.py:411
  10.7 11.8 %collective-permute-start.2 = (f32[65,8,128]{2,1,0:T(8,128)S(1)}, f32[65,8,128]{2,1,0:T(8,128)S(1)}, u32[]{:S(2)}, u32[]{:S(2)}) collective-permute-start(f32[65,8,128]{2,1,0:T(8,128)S(1)} %shard_map.48), channel_id=1, source_target_pairs={{0,4},{4,0},{8,12},{12,8},{1,5},{5,1},{9,13},{13,9},{2,6},{6,2},{1... | collective-permute-start | bytes 798728 | tf_op jit(solution)/shard_map/ppermute | solution.py:445
  12.4 11.5 %collective-permute-start.3 = (f32[65,8,128]{2,1,0:T(8,128)S(1)}, f32[65,8,128]{2,1,0:T(8,128)S(1)}, u32[]{:S(2)}, u32[]{:S(2)}) collective-permute-start(f32[65,8,128]{2,1,0:T(8,128)S(1)} %get-tuple-element.29), channel_id=1, source_target_pairs={{4,8},{8,4},{5,9},{9,5},{6,10},{10,6},{7,11},{11,7},{20,24},{24,20... | collective-permute-start | bytes 798728 | tf_op jit(solution)/shard_map/ppermute | solution.py:443
  13.0 13.1 %collective-permute-start.5 = (f32[65,8,128]{2,1,0:T(8,128)S(1)}, f32[65,8,128]{2,1,0:T(8,128)S(1)}, u32[]{:S(2)}, u32[]{:S(2)}) collective-permute-start(f32[65,8,128]{2,1,0:T(8,128)S(1)} %get-tuple-element.28), channel_id=1, source_target_pairs={{0,4},{12,8},{1,5},{13,9},{2,6},{14,10},{3,7},{15,11},{16,20},{28,... | collective-permute-start | bytes 798728 | tf_op jit(solution)/shard_map/ppermute | solution.py:448
  21.2 8.7 %collective-permute-start.4 = (f32[65,8,128]{2,1,0:T(8,128)S(1)}, f32[65,8,128]{2,1,0:T(8,128)S(1)}, u32[]{:S(2)}, u32[]{:S(2)}) collective-permute-start(f32[65,8,128]{2,1,0:T(8,128)S(1)} %get-tuple-element.29), channel_id=1, source_target_pairs={{0,8},{12,4},{1,9},{13,5},{2,10},{14,6},{3,11},{15,7},{16,24},{28,... | collective-permute-start | bytes 798728 | tf_op jit(solution)/shard_map/ppermute | solution.py:447
  22.6 14.8 %collective-permute-start.6 = (f32[65,8,128]{2,1,0:T(8,128)S(1)}, f32[65,8,128]{2,1,0:T(8,128)S(1)}, u32[]{:S(2)}, u32[]{:S(2)}) collective-permute-start(f32[65,8,128]{2,1,0:T(8,128)S(1)} %add.36), channel_id=1, source_target_pairs={{4,12},{8,0},{5,13},{9,1},{6,14},{10,2},{7,15},{11,3},{20,28},{24,... | collective-permute-start | bytes 798728 | tf_op jit(solution)/shard_map/ppermute | solution.py:451
  37.6 6.7 %collective-permute-start.8 = (f32[40,8,128]{2,1,0:T(8,128)S(1)}, f32[40,8,128]{2,1,0:T(8,128)S(1)}, u32[]{:S(2)}, u32[]{:S(2)}) collective-permute-start(f32[40,8,128]{2,1,0:T(8,128)S(1)} %slice.9), channel_id=1, source_target_pairs={{4,0},{8,4},{12,8},{13,12},{9,13},{5,9},{1,5},{2,1},{6,2},{10,6},{... | collective-permute-start | bytes 491528 | tf_op jit(solution)/shard_map/ppermute | solution.py:461
  39.1 5.2 %collective-permute-start.7 = (f32[32,8,128]{2,1,0:T(8,128)S(1)}, f32[32,8,128]{2,1,0:T(8,128)S(1)}, u32[]{:S(2)}, u32[]{:S(2)}) collective-permute-start(f32[32,8,128]{2,1,0:T(8,128)S(1)} %slice.8), channel_id=1, source_target_pairs={{0,4},{4,8},{8,12},{12,13},{13,9},{9,5},{5,1},{1,2},{2,6},{6,10},{... | collective-permute-start | bytes 393224 | tf_op jit(solution)/shard_map/ppermute | solution.py:460
  50.3 3.7 %copy-start.2 = (s32[128]{0:T(128)S(1)}, s32[128]{0:T(128)}, u32[]{:S(2)}) copy-start(s32[128]{0:T(128)} %param.6) | copy-start | bytes 1540
  50.4 13.7 %all-to-all-start = ((f32[16,4,8,128]{3,2,1,0:T(8,128)}), f32[16,4,8,128]{3,2,1,0:T(8,128)S(1)}, u32[]{:S(2)}, u32[]{:S(2)}) async-start(f32[16,4,8,128]{3,2,1,0:T(8,128)} %shard_map.51), calls=%async_computation | async-start | bytes 524288 | tf_op jit(solution)/shard_map/all_to_all | solution.py:480
  54.1 0.7 copy-start.3
  64.4 6.3 %collective-permute-start.10 = (f32[4,32,128]{2,1,0:T(8,128)S(1)}, f32[4,32,128]{2,1,0:T(8,128)S(1)}, u32[]{:S(2)}, u32[]{:S(2)}) collective-permute-start(f32[4,32,128]{2,1,0:T(8,128)S(1)} %get-tuple-element.35), channel_id=1, source_target_pairs={{0,8},{4,12},{8,0},{12,4},{1,9},{5,13},{9,1},{13,5},{2,10},{6,14},... | collective-permute-start | bytes 196616 | tf_op jit(solution)/shard_map/ppermute | solution.py:500
  65.4 5.6 %collective-permute-start.11 = (f32[4,32,128]{2,1,0:T(8,128)S(1)}, f32[4,32,128]{2,1,0:T(8,128)S(1)}, u32[]{:S(2)}, u32[]{:S(2)}) collective-permute-start(f32[4,32,128]{2,1,0:T(8,128)S(1)} %get-tuple-element.36), channel_id=1, source_target_pairs={{0,12},{4,0},{8,4},{12,8},{1,13},{5,1},{9,5},{13,9},{2,14},{6,2},{... | collective-permute-start | bytes 196616 | tf_op jit(solution)/shard_map/ppermute | solution.py:500
  66.2 6.6 %collective-permute-start.9 = (f32[4,32,128]{2,1,0:T(8,128)S(1)}, f32[4,32,128]{2,1,0:T(8,128)S(1)}, u32[]{:S(2)}, u32[]{:S(2)}) collective-permute-start(f32[4,32,128]{2,1,0:T(8,128)S(1)} %get-tuple-element.34), channel_id=1, source_target_pairs={{0,4},{4,8},{8,12},{12,0},{1,5},{5,9},{9,13},{13,1},{2,6},{6,10},{... | collective-permute-start | bytes 196616 | tf_op jit(solution)/shard_map/ppermute | solution.py:500

commit v8 on v7

--- a/solution.py
+++ b/solution.py
@@ -304,14 +304,17 @@
     lax.fori_loop(0, grids, grid, 0)
 
 
-def second_kernel(rows, grids, left, before, own, after, out, total, wide, *bufs):
+def second_kernel(rows, grids, left, before, own, after, *refs):
+    outs, total, bufs = refs[:-5], refs[-5], refs[-4:]
     extent = rows + LOW + HIGH
-    for i in range(LOW * TILES):
-        wide[i] = before[i]
-    for i in range(rows * TILES):
-        wide[LOW * TILES + i] = own[i]
-    for i in range(HIGH * TILES):
-        wide[(LOW + rows) * TILES + i] = after[i]
+
+    def given(row, t):
+        if row < LOW:
+            return before[row * TILES + t]
+        if row < LOW + rows:
+            return own[(row - LOW) * TILES + t]
+        return after[(row - LOW - rows) * TILES + t]
+
     total[...] = jnp.zeros_like(total)
 
     def grid(g, carry):
@@ -320,11 +323,11 @@
         start = bufs[0]
         for quad in range(0, extent - 1, 4):
             for t in range(TILES):
-                values = interpolate([wide[(quad + i) * TILES + t] for i in range(5)], fine, middle)
+                values = interpolate([given(quad + i, t) for i in range(5)], fine, middle)
                 for i, value in enumerate(values):
                     start[quad + i, t] = value
         for t in range(TILES):
-            start[extent - 1, t] = wide[(extent - 1) * TILES + t]
+            start[extent - 1, t] = given(extent - 1, t)
         done = run_steps(bufs, rows, left.at[g], [tile(d) for d in range(5)])
         for quad in range(0, rows, 4):
             for t in range(TILES):
@@ -336,19 +339,29 @@
 
     lax.fori_loop(0, grids, grid, 0)
     half = N2 // 2
-    for n3 in range(N3):
-        for n1 in range(N1):
-            for n2 in range(N2):
-                at = (n3 * N1 + n1) * 2 + n2 // half
-                out[at, n2 % half] = total[pl.ds((n1 * N3 + n3) * N2 + n2, rows, stride=TILES * N2), :]
-
-
-def hier_kernel(groups, matrix, rows, *outs):
+    for d, out in enumerate(outs):
+        slab = lax.bitwise_xor(lax.axis_index("slab"), d)
+        first = lax.div(slab, 2) * (N3 * N2) + lax.rem(slab, 2) * half
+        for n3 in range(N3):
+            for n in range(half):
+                out[n3, n] = total[pl.ds(first + n3 * N2 + n, rows, stride=TILES * N2), :]
+
+
+def regroup_kernel(groups, *refs):
+    received, outs = refs[: len(refs) // 2], refs[len(refs) // 2 :]
     me = lax.axis_index("grid")
-    lanes = rows.shape[3]
+    for e, out in enumerate(outs):
+        for d, ref in enumerate(received):
+            out[d] = ref[lax.rem(me + e, groups)]
+
+
+def hier_kernel(groups, matrix, *refs):
+    received, outs = refs[:groups], refs[groups:]
+    me = lax.axis_index("grid")
+    lanes = received[0].shape[3]
     count = matrix.shape[0] // groups
-    for n in range(rows.shape[1]):
-        whole = rows[:, n].reshape(matrix.shape[1], lanes)
+    for n in range(received[0].shape[1]):
+        whole = jnp.concatenate([ref[:, n].reshape(-1, lanes) for ref in received], axis=0)
         high = whole.astype(jnp.bfloat16)
         rest = (whole - high.astype(jnp.float32)).astype(jnp.bfloat16)
         for d, out in enumerate(outs):
@@ -466,40 +479,50 @@
     half = N2 // 2
     sent = kernel(
         functools.partial(second_kernel, block, grids),
-        floats(N3 * N1 * 2, half, block, N4),
+        [floats(N3, half, block, N4)] * slabs,
         [VMEM] * 4,
-        [
-            pltpu.VMEM((block * TILES * N2, N4), jnp.float32),
-            pltpu.VMEM(((block + LOW + HIGH) * TILES, N2, N4), jnp.float32),
-        ]
-        + spaces(block),
+        [pltpu.VMEM((block * TILES * N2, N4), jnp.float32)] + spaces(block),
         limit=8,
         flops=400 * 8192 * 40,
     )(left, before, own, after)
 
-    spread = lax.all_to_all(sent, both, split_axis=0, concat_axis=0, tiled=True)
-
-    source = np.zeros(N0, np.int32)
-    for place, device in enumerate(chain):
-        source[device * block : (device + 1) * block] = place * block + np.arange(block)
-    column = jnp.asarray(source)[None, :]
+    def shared(values, axis, partner):
+        members = range(lax.axis_size(axis))
+        others = lax.optimization_barrier(tuple(values[1:]))
+        return [values[0]] + [
+            lax.ppermute(value, axis, [(i, partner(i, d)) for i in members]) for d, value in enumerate(others, 1)
+        ]
+
+    ahead = lambda i, d: (i + d) % grids
+    by_slab = shared(sent, "slab", lambda i, d: i ^ d)
+    ready = kernel(
+        functools.partial(regroup_kernel, grids),
+        [floats(slabs, half, block, N4)] * grids,
+        [VMEM] * slabs,
+    )(*by_slab)
+    by_grid = shared(ready, "grid", ahead)
+
+    me, at = lax.axis_index("grid"), lax.axis_index("slab")
+    place = jnp.arange(N0, dtype=jnp.int32)
+    source = (me - place // (slabs * block)) % grids
+    slab = at ^ (place // block % slabs)
+    source = jnp.where(slab % 2 == 0, source, grids - 1 - source)
+    column = ((slab * grids + source) * block + place % block)[None, :]
     row = owner[:, None]
     reach = jnp.where(row > 0, row & -row, 0)
-    part = jnp.where(row > 0, -0.5, 0.0)
+    half_of = jnp.where(row > 0, -0.5, 0.0)
     matrix = (
         (column == row).astype(jnp.float32)
-        + part * (column == row - reach)
-        + part * (column == (row + reach) % N0)
+        + half_of * (column == row - reach)
+        + half_of * (column == (row + reach) % N0)
     ).astype(jnp.bfloat16)
     group = N0 // grids
     hier = kernel(
-        functools.partial(hier_kernel, grids), [floats(half, group, N4)] * grids, [VMEM, VMEM]
-    )(matrix, spread)
-    others = lax.optimization_barrier(tuple(hier[1:]))
-    received = [hier[0]] + [
-        lax.ppermute(value, "grid", [(i, (i + d) % grids) for i in range(grids)])
-        for d, value in enumerate(others, 1)
-    ]
+        functools.partial(hier_kernel, grids),
+        [floats(half, group, N4)] * grids,
+        [VMEM] * (1 + grids),
+    )(matrix, *by_grid)
+    received = shared(hier, "grid", ahead)
     out = kernel(
         functools.partial(place_kernel, grids), floats(group * half * N3, N4), [VMEM] * grids
     )(*received)

time: 73.9 us -> 73.6 us (level)
  starting transfers between devices: 22.5 us -> 25.9 us
  waiting for transfers between devices: 34.4 us -> 31.4 us
    all_to_all x1 -> x0, waiting for transfers between devices: 9.14 us -> none  [local_fast(): spread = lax.all_to_all(sent, both, split_axis=0, concat_axis=0, tiled=True)]
    ppermute x3 -> x9, starting transfers between devices: 3.05 us -> 10.1 us  [shared(): lax.ppermute(value, axis, [(i, partner(i, d)) for i in members])]
    ppermute x3 -> x9, waiting for transfers between devices: 5.35 us -> 12.1 us  [shared(): lax.ppermute(value, axis, [(i, partner(i, d)) for i in members])]
    all_to_all x1 -> x0, starting transfers between devices: 3.66 us -> none  [local_fast(): spread = lax.all_to_all(sent, both, split_axis=0, concat_axis=0, tiled=True)]
    pallas_call x1 -> x2, Pallas kernels: 6.07 us -> 5.48 us  [the longest x1 5.46 us: local_fast(): kernel(functools.partial(second_kernel, block, grids), [floats(N3, half,...]
  transfers between devices with their start and end apart: 13 -> 18, of which waited for: 9 -> 11; matrix products, arithmetic and copies ran while one was open for 0% -> 0% of each run, Pallas kernels for 7% -> 7%
where the time goes in v8:
time: 73.6 us; the launch traced here: 73.3 us
  waiting for transfers between devices  31.4 us (43%)
  starting transfers between devices  25.9 us (35%)
  Pallas kernels  14.8 us (20%)
    ppermute x9, waiting for transfers between devices, shared(): lax.ppermute(value, axis, [(i, partner(i, d)) for i in members])  12.1 us
    ppermute x9, starting transfers between devices, shared(): lax.ppermute(value, axis, [(i, partner(i, d)) for i in members])  10.1 us
    ppermute x1, waiting for transfers between devices, local_fast(): passed = lax.ppermute(joined, 'grid', [(1, 3), (2, 0)])  7.53 us
    ppermute x1, starting transfers between devices, local_fast(): inwards = lax.ppermute(near, 'grid', [(0, 1), (3, 2)])  6.31 us
    pallas_call x1, Pallas kernels, local_fast(): kernel(functools.partial(second_kernel, block, grids), [floats(N3, half,...  5.46 us
    ppermute x1, waiting for transfers between devices, local_fast(): lax.ppermute(own[(block - LOW) * TILES:block * TILES], both, forward)  4.11 us
    ppermute x1, waiting for transfers between devices, local_fast(): skipped = lax.ppermute(middle, 'grid', [(0, 2), (3, 1)])  3.79 us
    pallas_call x2, Pallas kernels, outer_block(): kernel(functools.partial(outer_kernel, later), piece, [SMEM] + [VMEM] * 4...  3.75 us
  transfers between devices with their start and end apart: 18, of which 11 were waited for; matrix products, arithmetic and copies ran while one was open for 0% of the time, Pallas kernels for 7%

profile of v8, /device:TPU:0, one launch (start us, length us, event | category | flops | bytes accessed | tf_op | source)
XLA Modules:
  0.0 73.3 jit_solution(11829734913498683246)
XLA Ops:
  0.0 0.0 copy-start
  0.0 1.1 %shard_map.38 = (f32[4,64,128]{2,1,0:T(8,128)S(1)}, f32[5,64,128]{2,1,0:T(8,128)S(1)}) custom-call(f32[32,64,128]{2,1,0:T(8,128)} %bitcast.2), custom_call_target="tpu_custom_call" | custom-call | bytes 1048576 | tf_op jit(solution)/shard_map/pallas_call | solution.py:418
  1.1 0.0 copy-start.1
  1.1 2.5 %collective-permute-start.1 = (f32[5,64,128]{2,1,0:T(8,128)S(1)}, f32[5,64,128]{2,1,0:T(8,128)S(1)}, u32[]{:S(2)}, u32[]{:S(2)}) collective-permute-start(f32[5,64,128]{2,1,0:T(8,128)S(1)} %get-tuple-element.37), channel_id=1, source_target_pairs={{1,0},{2,1},{3,2},{0,3},{5,4},{6,5},{7,6},{4,7},{9,8},{10,9},{11,1... | collective-permute-start | bytes 491528 | tf_op jit(solution)/shard_map/ppermute | solution.py:425
  3.6 0.0 collective-permute-start
  3.6 0.0 copy-done
  3.6 0.0 copy-done.1
  3.6 2.8 %shard_map.37 = (f32[65,8,128]{2,1,0:T(8,128)S(1)}, f32[65,8,128]{2,1,0:T(8,128)S(1)}, bf16[128,256]{1,0:T(8,128)(2,1)S(1)}) custom-call(s32[1,5]{1,0:T(1,128)S(1)} %copy-done.1, f32[32,64,128]{2,1,0:T(8,128)S(1)} %bitcast.3), custom_call_target="tpu_custom_call" | custom-call | flops 26214400 | bytes 1048576 | tf_op jit(solution)/shard_map/pallas_call | solution.py:434
  6.4 2.4 %collective-permute-done.before = f32[4,64,128]{2,1,0:T(8,128)S(1)} collective-permute-done((f32[4,64,128]{2,1,0:T(8,128)S(1)}, f32[4,64,128]{2,1,0:T(8,128)S(1)}, u32[]{:S(2)}, u32[]{:S(2)}) %collective-permute-start) | collective-permute-done | bytes 131104 | tf_op jit(solution)/shard_map/ppermute | solution.py:424
  8.8 0.0 collective-permute-done.1.after
  8.8 1.9 %shard_map.39 = f32[65,8,128]{2,1,0:T(8,128)S(1)} custom-call(s32[1,5]{1,0:T(1,128)S(1)} %copy-done.1, bf16[128,256]{1,0:T(8,128)(2,1)S(1)} %get-tuple-element.35.left, f32[4,64,128]{2,1,0:T(8,128)S(1)} %collective-permute-done.before, f32[32,64,128]{2,1,0:T(8,128)S(1)} %bitcast.4, f32[5,64,128]{2,1,0:T(8,128)S(1)} %collective-permute-done.1.after), custom_call_target="tpu_custom_call" | custom-call | flops 15728640 | bytes 1048576 | tf_op jit(solution)/shard_map/pallas_call | solution.py:446
  10.7 1.6 %collective-permute-start.2 = (f32[65,8,128]{2,1,0:T(8,128)S(1)}, f32[65,8,128]{2,1,0:T(8,128)S(1)}, u32[]{:S(2)}, u32[]{:S(2)}) collective-permute-start(f32[65,8,128]{2,1,0:T(8,128)S(1)} %shard_map.39), channel_id=1, source_target_pairs={{0,4},{4,0},{8,12},{12,8},{1,5},{5,1},{9,13},{13,9},{2,6},{6,2},{1... | collective-permute-start | bytes 798728 | tf_op jit(solution)/shard_map/ppermute | solution.py:458
  12.4 0.7 collective-permute-start.3
  13.0 6.3 %collective-permute-start.5 = (f32[65,8,128]{2,1,0:T(8,128)S(1)}, f32[65,8,128]{2,1,0:T(8,128)S(1)}, u32[]{:S(2)}, u32[]{:S(2)}) collective-permute-start(f32[65,8,128]{2,1,0:T(8,128)S(1)} %get-tuple-element.42), channel_id=1, source_target_pairs={{0,4},{12,8},{1,5},{13,9},{2,6},{14,10},{3,7},{15,11},{16,20},{28,... | collective-permute-start | bytes 798728 | tf_op jit(solution)/shard_map/ppermute | solution.py:461
  19.3 1.9 %shard_map.40 = f32[65,8,128]{2,1,0:T(8,128)S(1)} custom-call(s32[1,5]{1,0:T(1,128)S(1)} %copy-done.1, bf16[128,256]{1,0:T(8,128)(2,1)S(1)} %get-tuple-element.35.left, f32[4,64,128]{2,1,0:T(8,128)S(1)} %collective-permute-done.before, f32[32,64,128]{2,1,0:T(8,128)S(1)} %bitcast.5, f32[5,64,128]{2,1,0:T(8,128)S(1)} %collective-permute-done.1.after), custom_call_target="tpu_custom_call" | custom-call | flops 15728640 | bytes 1048576 | tf_op jit(solution)/shard_map/pallas_call | solution.py:446
  21.2 1.3 %collective-permute-start.4 = (f32[65,8,128]{2,1,0:T(8,128)S(1)}, f32[65,8,128]{2,1,0:T(8,128)S(1)}, u32[]{:S(2)}, u32[]{:S(2)}) collective-permute-start(f32[65,8,128]{2,1,0:T(8,128)S(1)} %get-tuple-element.43), channel_id=1, source_target_pairs={{0,8},{12,4},{1,9},{13,5},{2,10},{14,6},{3,11},{15,7},{16,24},{28,... | collective-permute-start | bytes 798728 | tf_op jit(solution)/shard_map/ppermute | solution.py:460
  22.5 0.0 collective-permute-done.2
  22.6 1.3 %collective-permute-start.6 = (f32[65,8,128]{2,1,0:T(8,128)S(1)}, f32[65,8,128]{2,1,0:T(8,128)S(1)}, u32[]{:S(2)}, u32[]{:S(2)}) collective-permute-start(f32[65,8,128]{2,1,0:T(8,128)S(1)} %add.100), channel_id=1, source_target_pairs={{4,12},{8,0},{5,13},{9,1},{6,14},{10,2},{7,15},{11,3},{20,28},{24,... | collective-permute-start | bytes 798728 | tf_op jit(solution)/shard_map/ppermute | solution.py:464
  23.9 0.0 copy-start.2
  23.9 0.6 copy-done.2
  24.6 0.0 collective-permute-done.3
  24.6 1.5 %collective-permute-done.5 = f32[65,8,128]{2,1,0:T(8,128)S(1)} collective-permute-done((f32[65,8,128]{2,1,0:T(8,128)S(1)}, f32[65,8,128]{2,1,0:T(8,128)S(1)}, u32[]{:S(2)}, u32[]{:S(2)}) %collective-permute-start.5) | collective-permute-done | bytes 266272 | tf_op jit(solution)/shard_map/ppermute | solution.py:461
  26.1 3.8 %collective-permute-done.4 = f32[65,8,128]{2,1,0:T(8,128)S(1)} collective-permute-done((f32[65,8,128]{2,1,0:T(8,128)S(1)}, f32[65,8,128]{2,1,0:T(8,128)S(1)}, u32[]{:S(2)}, u32[]{:S(2)}) %collective-permute-start.4) | collective-permute-done | bytes 266272 | tf_op jit(solution)/shard_map/ppermute | solution.py:460
  29.9 7.5 %collective-permute-done.6 = f32[65,8,128]{2,1,0:T(8,128)S(1)} collective-permute-done((f32[65,8,128]{2,1,0:T(8,128)S(1)}, f32[65,8,128]{2,1,0:T(8,128)S(1)}, u32[]{:S(2)}, u32[]{:S(2)}) %collective-permute-start.6) | collective-permute-done | bytes 266272 | tf_op jit(solution)/shard_map/ppermute | solution.py:464
  37.4 0.1 add_add_fusion.own
  37.6 1.5 %collective-permute-start.8 = (f32[40,8,128]{2,1,0:T(8,128)S(1)}, f32[40,8,128]{2,1,0:T(8,128)S(1)}, u32[]{:S(2)}, u32[]{:S(2)}) collective-permute-start(f32[40,8,128]{2,1,0:T(8,128)S(1)} %slice.9), channel_id=1, source_target_pairs={{4,0},{8,4},{12,8},{13,12},{9,13},{5,9},{1,5},{2,1},{6,2},{10,6},{... | collective-permute-start | bytes 491528 | tf_op jit(solution)/shard_map/ppermute | solution.py:474
  39.1 0.6 collective-permute-start.7
  39.7 0.5 shard_map.41.left
  40.2 4.1 %collective-permute-done.7.before = f32[32,8,128]{2,1,0:T(8,128)S(1)} collective-permute-done((f32[32,8,128]{2,1,0:T(8,128)S(1)}, f32[32,8,128]{2,1,0:T(8,128)S(1)}, u32[]{:S(2)}, u32[]{:S(2)}) %collective-permute-start.7) | collective-permute-done | bytes 131104 | tf_op jit(solution)/shard_map/ppermute | solution.py:473
  44.3 0.0 collective-permute-done.8.after
  44.3 5.5 %shard_map.42 = (f32[4,4,8,128]{3,2,1,0:T(8,128)S(1)}, f32[4,4,8,128]{3,2,1,0:T(8,128)S(1)}, f32[4,4,8,128]{3,2,1,0:T(8,128)S(1)}, f32[4,4,8,128]{3,2,1,0:T(8,128)S(1)}) custom-call(bf16[4,128,256]{2,1,0:T(8,128)(2,1)S(1)} %shard_map.41.left, f32[32,8,128]{2,1,0:T(8,128)S(1)} %collective-permute-done.7.before, f32[65,8,128]{2,1,0:T(8,128)S(1)} %add_add_fusion.own, ...), custom_call_target="tpu_custom_call" | custom-call | flops 131072000 | bytes 1048576 | tf_op jit(solution)/shard_map/pallas_call | solution.py:480
  49.8 1.2 %collective-permute-start.10 = (f32[4,4,8,128]{3,2,1,0:T(8,128)S(1)}, f32[4,4,8,128]{3,2,1,0:T(8,128)S(1)}, u32[]{:S(2)}, u32[]{:S(2)}) collective-permute-start(f32[4,4,8,128]{3,2,1,0:T(8,128)S(1)} %get-tuple-element.49), channel_id=1, source_target_pairs={{0,2},{1,3},{2,0},{3,1},{4,6},{5,7},{6,4},{7,5},{8,10},{9,11},{10,... | collective-permute-start | bytes 196616 | tf_op jit(solution)/shard_map/ppermute | solution.py:493
  51.0 0.0 collective-permute-start.11
  51.0 1.0 %collective-permute-start.9 = (f32[4,4,8,128]{3,2,1,0:T(8,128)S(1)}, f32[4,4,8,128]{3,2,1,0:T(8,128)S(1)}, u32[]{:S(2)}, u32[]{:S(2)}) collective-permute-start(f32[4,4,8,128]{3,2,1,0:T(8,128)S(1)} %get-tuple-element.48), channel_id=1, source_target_pairs={{0,1},{1,0},{2,3},{3,2},{4,5},{5,4},{6,7},{7,6},{8,9},{9,8},{10,11... | collective-permute-start | bytes 196616 | tf_op jit(solution)/shard_map/ppermute | solution.py:493
  52.0 2.2 %collective-permute-done.10.refs_2_ = f32[4,4,8,128]{3,2,1,0:T(8,128)S(1)} collective-permute-done((f32[4,4,8,128]{3,2,1,0:T(8,128)S(1)}, f32[4,4,8,128]{3,2,1,0:T(8,128)S(1)}, u32[]{:S(2)}, u32[]{:S(2)}) %collective-permute-start.10) | collective-permute-done | bytes 65568 | tf_op jit(solution)/shard_map/ppermute | solution.py:493
  54.2 1.2 %collective-permute-done.11.refs_3_ = f32[4,4,8,128]{3,2,1,0:T(8,128)S(1)} collective-permute-done((f32[4,4,8,128]{3,2,1,0:T(8,128)S(1)}, f32[4,4,8,128]{3,2,1,0:T(8,128)S(1)}, u32[]{:S(2)}, u32[]{:S(2)}) %collective-permute-start.11) | collective-permute-done | bytes 65568 | tf_op jit(solution)/shard_map/ppermute | solution.py:493
  55.4 0.0 collective-permute-done.9.refs_1_
  55.4 0.5 collective-permute-start.12
  55.9 0.7 collective-permute-start.13
  56.6 2.8 %collective-permute-start.14 = (f32[4,4,8,128]{3,2,1,0:T(8,128)S(1)}, f32[4,4,8,128]{3,2,1,0:T(8,128)S(1)}, u32[]{:S(2)}, u32[]{:S(2)}) collective-permute-start(f32[4,4,8,128]{3,2,1,0:T(8,128)S(1)} %get-tuple-element.57), channel_id=1, source_target_pairs={{0,12},{4,0},{8,4},{12,8},{1,13},{5,1},{9,5},{13,9},{2,14},{6,2},{... | collective-permute-start | bytes 196616 | tf_op jit(solution)/shard_map/ppermute | solution.py:493
  59.5 0.1 add_convert_fusion.matrix
  59.6 2.6 %collective-permute-done.12.refs_1_ = f32[4,4,8,128]{3,2,1,0:T(8,128)S(1)} collective-permute-done((f32[4,4,8,128]{3,2,1,0:T(8,128)S(1)}, f32[4,4,8,128]{3,2,1,0:T(8,128)S(1)}, u32[]{:S(2)}, u32[]{:S(2)}) %collective-permute-start.12) | collective-permute-done | bytes 65568 | tf_op jit(solution)/shard_map/ppermute | solution.py:493
  62.2 1.9 %collective-permute-done.13.refs_2_ = f32[4,4,8,128]{3,2,1,0:T(8,128)S(1)} collective-permute-done((f32[4,4,8,128]{3,2,1,0:T(8,128)S(1)}, f32[4,4,8,128]{3,2,1,0:T(8,128)S(1)}, u32[]{:S(2)}, u32[]{:S(2)}) %collective-permute-start.13) | collective-permute-done | bytes 65568 | tf_op jit(solution)/shard_map/ppermute | solution.py:493
  64.1 0.0 collective-permute-done.14.refs_3_
  64.1 0.4 shard_map.44
  64.5 1.4 %collective-permute-start.15 = (f32[4,32,128]{2,1,0:T(8,128)S(1)}, f32[4,32,128]{2,1,0:T(8,128)S(1)}, u32[]{:S(2)}, u32[]{:S(2)}) collective-permute-start(f32[4,32,128]{2,1,0:T(8,128)S(1)} %get-tuple-element.62), channel_id=1, source_target_pairs={{0,4},{4,8},{8,12},{12,0},{1,5},{5,9},{9,13},{13,1},{2,6},{6,10},{... | collective-permute-start | bytes 196616 | tf_op jit(solution)/shard_map/ppermute | solution.py:493
  65.8 1.2 %collective-permute-start.16 = (f32[4,32,128]{2,1,0:T(8,128)S(1)}, f32[4,32,128]{2,1,0:T(8,128)S(1)}, u32[]{:S(2)}, u32[]{:S(2)}) collective-permute-start(f32[4,32,128]{2,1,0:T(8,128)S(1)} %get-tuple-element.63), channel_id=1, source_target_pairs={{0,8},{4,12},{8,0},{12,4},{1,9},{5,13},{9,1},{13,5},{2,10},{6,14},... | collective-permute-start | bytes 196616 | tf_op jit(solution)/shard_map/ppermute | solution.py:493
  67.0 1.3 %collective-permute-start.17 = (f32[4,32,128]{2,1,0:T(8,128)S(1)}, f32[4,32,128]{2,1,0:T(8,128)S(1)}, u32[]{:S(2)}, u32[]{:S(2)}) collective-permute-start(f32[4,32,128]{2,1,0:T(8,128)S(1)} %get-tuple-element.64), channel_id=1, source_target_pairs={{0,12},{4,0},{8,4},{12,8},{1,13},{5,1},{9,5},{13,9},{2,14},{6,2},{... | collective-permute-start | bytes 196616 | tf_op jit(solution)/shard_map/ppermute | solution.py:493
  68.3 2.9 %collective-permute-done.15.refs_1_ = f32[4,32,128]{2,1,0:T(8,128)S(1)} collective-permute-done((f32[4,32,128]{2,1,0:T(8,128)S(1)}, f32[4,32,128]{2,1,0:T(8,128)S(1)}, u32[]{:S(2)}, u32[]{:S(2)}) %collective-permute-start.15) | collective-permute-done | bytes 65568 | tf_op jit(solution)/shard_map/ppermute | solution.py:493
  71.2 1.3 %collective-permute-done.16.refs_2_ = f32[4,32,128]{2,1,0:T(8,128)S(1)} collective-permute-done((f32[4,32,128]{2,1,0:T(8,128)S(1)}, f32[4,32,128]{2,1,0:T(8,128)S(1)}, u32[]{:S(2)}, u32[]{:S(2)}) %collective-permute-start.16) | collective-permute-done | bytes 65568 | tf_op jit(solution)/shard_map/ppermute | solution.py:493
  72.5 0.0 collective-permute-done.17.refs_3_
  72.5 0.8 %shard_map.45 = f32[512,128]{1,0:T(8,128)} custom-call(f32[4,32,128]{2,1,0:T(8,128)S(1)} %get-tuple-element.58.refs_0_, f32[4,32,128]{2,1,0:T(8,128)S(1)} %collective-permute-done.15.refs_1_, f32[4,32,128]{2,1,0:T(8,128)S(1)} %collective-permute-done.16.refs_2_, f32[4,32,128]{2,1,0:T(8,128)S(1)} %collective-permute-done.17.refs_3_), custom_call_target="tpu_custom_call" | custom-call | bytes 1048576 | tf_op jit(solution)/shard_map/pallas_call | solution.py:526
  (7 shorter events, 0.1 us)
Async XLA Ops:
  0.0 3.6 %copy-start = (f32[1,32,64,128]{3,2,1,0:T(8,128)S(1)}, f32[1,32,64,128]{3,2,1,0:T(8,128)}, u32[]{:S(2)}) copy-start(f32[1,32,64,128]{3,2,1,0:T(8,128)} %param.3) | copy-start | bytes 3145732
  1.1 2.5 %copy-start.1 = (s32[1,5]{1,0:T(1,128)S(1)}, s32[1,5]{1,0:T(1,128)}, u32[]{:S(2)}) copy-start(s32[1,5]{1,0:T(1,128)} %level.5) | copy-start | bytes 64
  1.1 7.7 %collective-permute-start.1 = (f32[5,64,128]{2,1,0:T(8,128)S(1)}, f32[5,64,128]{2,1,0:T(8,128)S(1)}, u32[]{:S(2)}, u32[]{:S(2)}) collective-permute-start(f32[5,64,128]{2,1,0:T(8,128)S(1)} %get-tuple-element.37), channel_id=1, source_target_pairs={{1,0},{2,1},{3,2},{0,3},{5,4},{6,5},{7,6},{4,7},{9,8},{10,9},{11,1... | collective-permute-start | bytes 491528 | tf_op jit(solution)/shard_map/ppermute | solution.py:425
  3.6 5.3 %collective-permute-start = (f32[4,64,128]{2,1,0:T(8,128)S(1)}, f32[4,64,128]{2,1,0:T(8,128)S(1)}, u32[]{:S(2)}, u32[]{:S(2)}) collective-permute-start(f32[4,64,128]{2,1,0:T(8,128)S(1)} %get-tuple-element.36), channel_id=1, source_target_pairs={{0,1},{1,2},{2,3},{3,0},{4,5},{5,6},{6,7},{7,4},{8,9},{9,10},{10,1... | collective-permute-start | bytes 393224 | tf_op jit(solution)/shard_map/ppermute | solution.py:424
  10.7 11.8 %collective-permute-start.2 = (f32[65,8,128]{2,1,0:T(8,128)S(1)}, f32[65,8,128]{2,1,0:T(8,128)S(1)}, u32[]{:S(2)}, u32[]{:S(2)}) collective-permute-start(f32[65,8,128]{2,1,0:T(8,128)S(1)} %shard_map.39), channel_id=1, source_target_pairs={{0,4},{4,0},{8,12},{12,8},{1,5},{5,1},{9,13},{13,9},{2,6},{6,2},{1... | collective-permute-start | bytes 798728 | tf_op jit(solution)/shard_map/ppermute | solution.py:458
  12.4 12.2 %collective-permute-start.3 = (f32[65,8,128]{2,1,0:T(8,128)S(1)}, f32[65,8,128]{2,1,0:T(8,128)S(1)}, u32[]{:S(2)}, u32[]{:S(2)}) collective-permute-start(f32[65,8,128]{2,1,0:T(8,128)S(1)} %get-tuple-element.43), channel_id=1, source_target_pairs={{4,8},{8,4},{5,9},{9,5},{6,10},{10,6},{7,11},{11,7},{20,24},{24,20... | collective-permute-start | bytes 798728 | tf_op jit(solution)/shard_map/ppermute | solution.py:456
  13.0 13.1 %collective-permute-start.5 = (f32[65,8,128]{2,1,0:T(8,128)S(1)}, f32[65,8,128]{2,1,0:T(8,128)S(1)}, u32[]{:S(2)}, u32[]{:S(2)}) collective-permute-start(f32[65,8,128]{2,1,0:T(8,128)S(1)} %get-tuple-element.42), channel_id=1, source_target_pairs={{0,4},{12,8},{1,5},{13,9},{2,6},{14,10},{3,7},{15,11},{16,20},{28,... | collective-permute-start | bytes 798728 | tf_op jit(solution)/shard_map/ppermute | solution.py:461
  21.2 8.7 %collective-permute-start.4 = (f32[65,8,128]{2,1,0:T(8,128)S(1)}, f32[65,8,128]{2,1,0:T(8,128)S(1)}, u32[]{:S(2)}, u32[]{:S(2)}) collective-permute-start(f32[65,8,128]{2,1,0:T(8,128)S(1)} %get-tuple-element.43), channel_id=1, source_target_pairs={{0,8},{12,4},{1,9},{13,5},{2,10},{14,6},{3,11},{15,7},{16,24},{28,... | collective-permute-start | bytes 798728 | tf_op jit(solution)/shard_map/ppermute | solution.py:460
  22.6 14.8 %collective-permute-start.6 = (f32[65,8,128]{2,1,0:T(8,128)S(1)}, f32[65,8,128]{2,1,0:T(8,128)S(1)}, u32[]{:S(2)}, u32[]{:S(2)}) collective-permute-start(f32[65,8,128]{2,1,0:T(8,128)S(1)} %add.100), channel_id=1, source_target_pairs={{4,12},{8,0},{5,13},{9,1},{6,14},{10,2},{7,15},{11,3},{20,28},{24,... | collective-permute-start | bytes 798728 | tf_op jit(solution)/shard_map/ppermute | solution.py:464
  23.9 0.7 copy-start.2
  37.6 6.7 %collective-permute-start.8 = (f32[40,8,128]{2,1,0:T(8,128)S(1)}, f32[40,8,128]{2,1,0:T(8,128)S(1)}, u32[]{:S(2)}, u32[]{:S(2)}) collective-permute-start(f32[40,8,128]{2,1,0:T(8,128)S(1)} %slice.9), channel_id=1, source_target_pairs={{4,0},{8,4},{12,8},{13,12},{9,13},{5,9},{1,5},{2,1},{6,2},{10,6},{... | collective-permute-start | bytes 491528 | tf_op jit(solution)/shard_map/ppermute | solution.py:474
  39.1 5.2 %collective-permute-start.7 = (f32[32,8,128]{2,1,0:T(8,128)S(1)}, f32[32,8,128]{2,1,0:T(8,128)S(1)}, u32[]{:S(2)}, u32[]{:S(2)}) collective-permute-start(f32[32,8,128]{2,1,0:T(8,128)S(1)} %slice.8), channel_id=1, source_target_pairs={{0,4},{4,8},{8,12},{12,13},{13,9},{9,5},{5,1},{1,2},{2,6},{6,10},{... | collective-permute-start | bytes 393224 | tf_op jit(solution)/shard_map/ppermute | solution.py:473
  49.8 4.4 %collective-permute-start.10 = (f32[4,4,8,128]{3,2,1,0:T(8,128)S(1)}, f32[4,4,8,128]{3,2,1,0:T(8,128)S(1)}, u32[]{:S(2)}, u32[]{:S(2)}) collective-permute-start(f32[4,4,8,128]{3,2,1,0:T(8,128)S(1)} %get-tuple-element.49), channel_id=1, source_target_pairs={{0,2},{1,3},{2,0},{3,1},{4,6},{5,7},{6,4},{7,5},{8,10},{9,11},{10,... | collective-permute-start | bytes 196616 | tf_op jit(solution)/shard_map/ppermute | solution.py:493
  51.0 4.4 %collective-permute-start.11 = (f32[4,4,8,128]{3,2,1,0:T(8,128)S(1)}, f32[4,4,8,128]{3,2,1,0:T(8,128)S(1)}, u32[]{:S(2)}, u32[]{:S(2)}) collective-permute-start(f32[4,4,8,128]{3,2,1,0:T(8,128)S(1)} %get-tuple-element.50), channel_id=1, source_target_pairs={{0,3},{1,2},{2,1},{3,0},{4,7},{5,6},{6,5},{7,4},{8,11},{9,10},{10,... | collective-permute-start | bytes 196616 | tf_op jit(solution)/shard_map/ppermute | solution.py:493
  51.0 4.4 %collective-permute-start.9 = (f32[4,4,8,128]{3,2,1,0:T(8,128)S(1)}, f32[4,4,8,128]{3,2,1,0:T(8,128)S(1)}, u32[]{:S(2)}, u32[]{:S(2)}) collective-permute-start(f32[4,4,8,128]{3,2,1,0:T(8,128)S(1)} %get-tuple-element.48), channel_id=1, source_target_pairs={{0,1},{1,0},{2,3},{3,2},{4,5},{5,4},{6,7},{7,6},{8,9},{9,8},{10,11... | collective-permute-start | bytes 196616 | tf_op jit(solution)/shard_map/ppermute | solution.py:493
  55.4 6.8 %collective-permute-start.12 = (f32[4,4,8,128]{3,2,1,0:T(8,128)S(1)}, f32[4,4,8,128]{3,2,1,0:T(8,128)S(1)}, u32[]{:S(2)}, u32[]{:S(2)}) collective-permute-start(f32[4,4,8,128]{3,2,1,0:T(8,128)S(1)} %get-tuple-element.55), channel_id=1, source_target_pairs={{0,4},{4,8},{8,12},{12,0},{1,5},{5,9},{9,13},{13,1},{2,6},{6,10},{... | collective-permute-start | bytes 196616 | tf_op jit(solution)/shard_map/ppermute | solution.py:493
  55.9 8.1 %collective-permute-start.13 = (f32[4,4,8,128]{3,2,1,0:T(8,128)S(1)}, f32[4,4,8,128]{3,2,1,0:T(8,128)S(1)}, u32[]{:S(2)}, u32[]{:S(2)}) collective-permute-start(f32[4,4,8,128]{3,2,1,0:T(8,128)S(1)} %get-tuple-element.56), channel_id=1, source_target_pairs={{0,8},{4,12},{8,0},{12,4},{1,9},{5,13},{9,1},{13,5},{2,10},{6,14},... | collective-permute-start | bytes 196616 | tf_op jit(solution)/shard_map/ppermute | solution.py:493
  56.6 7.4 %collective-permute-start.14 = (f32[4,4,8,128]{3,2,1,0:T(8,128)S(1)}, f32[4,4,8,128]{3,2,1,0:T(8,128)S(1)}, u32[]{:S(2)}, u32[]{:S(2)}) collective-permute-start(f32[4,4,8,128]{3,2,1,0:T(8,128)S(1)} %get-tuple-element.57), channel_id=1, source_target_pairs={{0,12},{4,0},{8,4},{12,8},{1,13},{5,1},{9,5},{13,9},{2,14},{6,2},{... | collective-permute-start | bytes 196616 | tf_op jit(solution)/shard_map/ppermute | solution.py:493
  64.5 6.8 %collective-permute-start.15 = (f32[4,32,128]{2,1,0:T(8,128)S(1)}, f32[4,32,128]{2,1,0:T(8,128)S(1)}, u32[]{:S(2)}, u32[]{:S(2)}) collective-permute-start(f32[4,32,128]{2,1,0:T(8,128)S(1)} %get-tuple-element.62), channel_id=1, source_target_pairs={{0,4},{4,8},{8,12},{12,0},{1,5},{5,9},{9,13},{13,1},{2,6},{6,10},{... | collective-permute-start | bytes 196616 | tf_op jit(solution)/shard_map/ppermute | solution.py:493
  65.8 6.7 %collective-permute-start.16 = (f32[4,32,128]{2,1,0:T(8,128)S(1)}, f32[4,32,128]{2,1,0:T(8,128)S(1)}, u32[]{:S(2)}, u32[]{:S(2)}) collective-permute-start(f32[4,32,128]{2,1,0:T(8,128)S(1)} %get-tuple-element.63), channel_id=1, source_target_pairs={{0,8},{4,12},{8,0},{12,4},{1,9},{5,13},{9,1},{13,5},{2,10},{6,14},... | collective-permute-start | bytes 196616 | tf_op jit(solution)/shard_map/ppermute | solution.py:493
  67.0 5.5 %collective-permute-start.17 = (f32[4,32,128]{2,1,0:T(8,128)S(1)}, f32[4,32,128]{2,1,0:T(8,128)S(1)}, u32[]{:S(2)}, u32[]{:S(2)}) collective-permute-start(f32[4,32,128]{2,1,0:T(8,128)S(1)} %get-tuple-element.64), channel_id=1, source_target_pairs={{0,12},{4,0},{8,4},{12,8},{1,13},{5,1},{9,5},{13,9},{2,14},{6,2},{... | collective-permute-start | bytes 196616 | tf_op jit(solution)/shard_map/ppermute | solution.py:493

commit v9 on v8

--- a/solution.py
+++ b/solution.py
@@ -348,7 +348,7 @@
 
 
 def regroup_kernel(groups, *refs):
-    received, outs = refs[: len(refs) // 2], refs[len(refs) // 2 :]
+    received, outs = refs[:-groups], refs[-groups:]
     me = lax.axis_index("grid")
     for e, out in enumerate(outs):
         for d, ref in enumerate(received):
@@ -356,12 +356,13 @@
 
 
 def hier_kernel(groups, matrix, *refs):
-    received, outs = refs[:groups], refs[groups:]
+    received, outs = refs[: 2 * groups], refs[2 * groups :]
     me = lax.axis_index("grid")
     lanes = received[0].shape[3]
     count = matrix.shape[0] // groups
     for n in range(received[0].shape[1]):
-        whole = jnp.concatenate([ref[:, n].reshape(-1, lanes) for ref in received], axis=0)
+        pairs = [(received[d], received[groups + d]) for d in range(groups)]
+        whole = jnp.concatenate([ref[:, n].reshape(-1, lanes) for pair in pairs for ref in pair], axis=0)
         high = whole.astype(jnp.bfloat16)
         rest = (whole - high.astype(jnp.float32)).astype(jnp.bfloat16)
         for d, out in enumerate(outs):
@@ -486,21 +487,22 @@
         flops=400 * 8192 * 40,
     )(left, before, own, after)
 
-    def shared(values, axis, partner):
-        members = range(lax.axis_size(axis))
-        others = lax.optimization_barrier(tuple(values[1:]))
-        return [values[0]] + [
-            lax.ppermute(value, axis, [(i, partner(i, d)) for i in members]) for d, value in enumerate(others, 1)
-        ]
-
+    def exchanged(value, axis, partner, d):
+        pairs = [(i, partner(i, d)) for i in range(lax.axis_size(axis))]
+        return lax.ppermute(value, axis, pairs)
+
+    other = lambda i, d: i ^ d
     ahead = lambda i, d: (i + d) % grids
-    by_slab = shared(sent, "slab", lambda i, d: i ^ d)
-    ready = kernel(
-        functools.partial(regroup_kernel, grids),
-        [floats(slabs, half, block, N4)] * grids,
-        [VMEM] * slabs,
-    )(*by_slab)
-    by_grid = shared(ready, "grid", ahead)
+    far_parts = [exchanged(sent[d], "slab", other, d) for d in (2, 3)]
+    near_parts = [sent[0], exchanged(sent[1], "slab", other, 1)]
+    by_grid = []
+    for parts in (near_parts, far_parts):
+        ready = kernel(
+            functools.partial(regroup_kernel, grids),
+            [floats(len(parts), half, block, N4)] * grids,
+            [VMEM] * len(parts),
+        )(*parts)
+        by_grid += [ready[0]] + [exchanged(ready[d], "grid", ahead, d) for d in range(1, grids)]
 
     me, at = lax.axis_index("grid"), lax.axis_index("slab")
     place = jnp.arange(N0, dtype=jnp.int32)
@@ -520,9 +522,9 @@
     hier = kernel(
         functools.partial(hier_kernel, grids),
         [floats(half, group, N4)] * grids,
-        [VMEM] * (1 + grids),
+        [VMEM] * (1 + 2 * grids),
     )(matrix, *by_grid)
-    received = shared(hier, "grid", ahead)
+    received = [hier[0]] + [exchanged(hier[d], "grid", ahead, d) for d in range(1, grids)]
     out = kernel(
         functools.partial(place_kernel, grids), floats(group * half * N3, N4), [VMEM] * grids
     )(*received)

time: 73.6 us -> 76.4 us (1.038)
  starting transfers between devices: 25.9 us -> 31.7 us
  waiting for transfers between devices: 31.4 us -> 29.1 us
    ppermute x9 -> x12, starting transfers between devices: 10.1 us -> 15.9 us  [exchanged(): return lax.ppermute(value, axis, pairs)]
    ppermute x9 -> x12, waiting for transfers between devices: 12.1 us -> 9.11 us  [exchanged(): return lax.ppermute(value, axis, pairs)]
  transfers between devices with their start and end apart: 18 -> 21, of which waited for: 11 -> 12; matrix products, arithmetic and copies ran while one was open for 0% -> 0% of each run, Pallas kernels for 7% -> 7%
where the time goes in v9:
time: 76.4 us; the launch traced here: 76.1 us
  starting transfers between devices  31.7 us (41%)
  waiting for transfers between devices  29.1 us (38%)
  Pallas kernels  14.7 us (19%)
    ppermute x12, starting transfers between devices, exchanged(): return lax.ppermute(value, axis, pairs)  15.9 us
    ppermute x12, waiting for transfers between devices, exchanged(): return lax.ppermute(value, axis, pairs)  9.11 us
    ppermute x1, waiting for transfers between devices, local_fast(): passed = lax.ppermute(joined, 'grid', [(1, 3), (2, 0)])  7.53 us
    ppermute x1, starting transfers between devices, local_fast(): inwards = lax.ppermute(near, 'grid', [(0, 1), (3, 2)])  6.31 us
    pallas_call x1, Pallas kernels, local_fast(): kernel(functools.partial(second_kernel, block, grids), [floats(N3, half,...  5.35 us
    ppermute x1, waiting for transfers between devices, local_fast(): lax.ppermute(own[(block - LOW) * TILES:block * TILES], both, forward)  4.1 us
    ppermute x1, waiting for transfers between devices, local_fast(): skipped = lax.ppermute(middle, 'grid', [(0, 2), (3, 1)])  3.79 us
    pallas_call x2, Pallas kernels, outer_block(): kernel(functools.partial(outer_kernel, later), piece, [SMEM] + [VMEM] * 4...  3.75 us
  transfers between devices with their start and end apart: 21, of which 12 were waited for; matrix products, arithmetic and copies ran while one was open for 0% of the time, Pallas kernels for 7%

profile of v9, /device:TPU:0, one launch (start us, length us, event | category | flops | bytes accessed | tf_op | source)
XLA Modules:
  0.0 76.1 jit_solution(2645450919027440950)
XLA Ops:
  0.0 0.0 copy-start
  0.0 1.1 %shard_map.38 = (f32[4,64,128]{2,1,0:T(8,128)S(1)}, f32[5,64,128]{2,1,0:T(8,128)S(1)}) custom-call(f32[32,64,128]{2,1,0:T(8,128)} %bitcast.2), custom_call_target="tpu_custom_call" | custom-call | bytes 1048576 | tf_op jit(solution)/shard_map/pallas_call | solution.py:419
  1.1 0.0 copy-start.1
  1.1 2.5 %collective-permute-start.1 = (f32[5,64,128]{2,1,0:T(8,128)S(1)}, f32[5,64,128]{2,1,0:T(8,128)S(1)}, u32[]{:S(2)}, u32[]{:S(2)}) collective-permute-start(f32[5,64,128]{2,1,0:T(8,128)S(1)} %get-tuple-element.32), channel_id=1, source_target_pairs={{1,0},{2,1},{3,2},{0,3},{5,4},{6,5},{7,6},{4,7},{9,8},{10,9},{11,1... | collective-permute-start | bytes 491528 | tf_op jit(solution)/shard_map/ppermute | solution.py:426
  3.6 0.0 collective-permute-start
  3.6 0.0 copy-done
  3.6 0.0 copy-done.1
  3.6 2.8 %shard_map.37 = (f32[65,8,128]{2,1,0:T(8,128)S(1)}, f32[65,8,128]{2,1,0:T(8,128)S(1)}, bf16[128,256]{1,0:T(8,128)(2,1)S(1)}) custom-call(s32[1,5]{1,0:T(1,128)S(1)} %copy-done.1, f32[32,64,128]{2,1,0:T(8,128)S(1)} %bitcast.3), custom_call_target="tpu_custom_call" | custom-call | flops 26214400 | bytes 1048576 | tf_op jit(solution)/shard_map/pallas_call | solution.py:435
  6.4 2.4 %collective-permute-done.before = f32[4,64,128]{2,1,0:T(8,128)S(1)} collective-permute-done((f32[4,64,128]{2,1,0:T(8,128)S(1)}, f32[4,64,128]{2,1,0:T(8,128)S(1)}, u32[]{:S(2)}, u32[]{:S(2)}) %collective-permute-start) | collective-permute-done | bytes 131104 | tf_op jit(solution)/shard_map/ppermute | solution.py:425
  8.8 0.0 collective-permute-done.1.after
  8.8 1.9 %shard_map.39 = f32[65,8,128]{2,1,0:T(8,128)S(1)} custom-call(s32[1,5]{1,0:T(1,128)S(1)} %copy-done.1, bf16[128,256]{1,0:T(8,128)(2,1)S(1)} %get-tuple-element.30.left, f32[4,64,128]{2,1,0:T(8,128)S(1)} %collective-permute-done.before, f32[32,64,128]{2,1,0:T(8,128)S(1)} %bitcast.4, f32[5,64,128]{2,1,0:T(8,128)S(1)} %collective-permute-done.1.after), custom_call_target="tpu_custom_call" | custom-call | flops 15728640 | bytes 1048576 | tf_op jit(solution)/shard_map/pallas_call | solution.py:447
  10.7 1.6 %collective-permute-start.2 = (f32[65,8,128]{2,1,0:T(8,128)S(1)}, f32[65,8,128]{2,1,0:T(8,128)S(1)}, u32[]{:S(2)}, u32[]{:S(2)}) collective-permute-start(f32[65,8,128]{2,1,0:T(8,128)S(1)} %shard_map.39), channel_id=1, source_target_pairs={{0,4},{4,0},{8,12},{12,8},{1,5},{5,1},{9,13},{13,9},{2,6},{6,2},{1... | collective-permute-start | bytes 798728 | tf_op jit(solution)/shard_map/ppermute | solution.py:459
  12.4 0.7 collective-permute-start.3
  13.0 6.3 %collective-permute-start.5 = (f32[65,8,128]{2,1,0:T(8,128)S(1)}, f32[65,8,128]{2,1,0:T(8,128)S(1)}, u32[]{:S(2)}, u32[]{:S(2)}) collective-permute-start(f32[65,8,128]{2,1,0:T(8,128)S(1)} %get-tuple-element.37), channel_id=1, source_target_pairs={{0,4},{12,8},{1,5},{13,9},{2,6},{14,10},{3,7},{15,11},{16,20},{28,... | collective-permute-start | bytes 798728 | tf_op jit(solution)/shard_map/ppermute | solution.py:462
  19.3 1.9 %shard_map.40 = f32[65,8,128]{2,1,0:T(8,128)S(1)} custom-call(s32[1,5]{1,0:T(1,128)S(1)} %copy-done.1, bf16[128,256]{1,0:T(8,128)(2,1)S(1)} %get-tuple-element.30.left, f32[4,64,128]{2,1,0:T(8,128)S(1)} %collective-permute-done.before, f32[32,64,128]{2,1,0:T(8,128)S(1)} %bitcast.5, f32[5,64,128]{2,1,0:T(8,128)S(1)} %collective-permute-done.1.after), custom_call_target="tpu_custom_call" | custom-call | flops 15728640 | bytes 1048576 | tf_op jit(solution)/shard_map/pallas_call | solution.py:447
  21.2 1.3 %collective-permute-start.4 = (f32[65,8,128]{2,1,0:T(8,128)S(1)}, f32[65,8,128]{2,1,0:T(8,128)S(1)}, u32[]{:S(2)}, u32[]{:S(2)}) collective-permute-start(f32[65,8,128]{2,1,0:T(8,128)S(1)} %get-tuple-element.38), channel_id=1, source_target_pairs={{0,8},{12,4},{1,9},{13,5},{2,10},{14,6},{3,11},{15,7},{16,24},{28,... | collective-permute-start | bytes 798728 | tf_op jit(solution)/shard_map/ppermute | solution.py:461
  22.5 0.0 collective-permute-done.2
  22.6 1.3 %collective-permute-start.6 = (f32[65,8,128]{2,1,0:T(8,128)S(1)}, f32[65,8,128]{2,1,0:T(8,128)S(1)}, u32[]{:S(2)}, u32[]{:S(2)}) collective-permute-start(f32[65,8,128]{2,1,0:T(8,128)S(1)} %add.100), channel_id=1, source_target_pairs={{4,12},{8,0},{5,13},{9,1},{6,14},{10,2},{7,15},{11,3},{20,28},{24,... | collective-permute-start | bytes 798728 | tf_op jit(solution)/shard_map/ppermute | solution.py:465
  23.9 0.0 collective-permute-done.3
  23.9 2.2 %collective-permute-done.5 = f32[65,8,128]{2,1,0:T(8,128)S(1)} collective-permute-done((f32[65,8,128]{2,1,0:T(8,128)S(1)}, f32[65,8,128]{2,1,0:T(8,128)S(1)}, u32[]{:S(2)}, u32[]{:S(2)}) %collective-permute-start.5) | collective-permute-done | bytes 266272 | tf_op jit(solution)/shard_map/ppermute | solution.py:462
  26.1 3.8 %collective-permute-done.4 = f32[65,8,128]{2,1,0:T(8,128)S(1)} collective-permute-done((f32[65,8,128]{2,1,0:T(8,128)S(1)}, f32[65,8,128]{2,1,0:T(8,128)S(1)}, u32[]{:S(2)}, u32[]{:S(2)}) %collective-permute-start.4) | collective-permute-done | bytes 266272 | tf_op jit(solution)/shard_map/ppermute | solution.py:461
  29.9 7.5 %collective-permute-done.6 = f32[65,8,128]{2,1,0:T(8,128)S(1)} collective-permute-done((f32[65,8,128]{2,1,0:T(8,128)S(1)}, f32[65,8,128]{2,1,0:T(8,128)S(1)}, u32[]{:S(2)}, u32[]{:S(2)}) %collective-permute-start.6) | collective-permute-done | bytes 266272 | tf_op jit(solution)/shard_map/ppermute | solution.py:465
  37.4 0.1 add_add_fusion.own
  37.6 0.0 copy-start.2
  37.6 1.5 %collective-permute-start.8 = (f32[40,8,128]{2,1,0:T(8,128)S(1)}, f32[40,8,128]{2,1,0:T(8,128)S(1)}, u32[]{:S(2)}, u32[]{:S(2)}) collective-permute-start(f32[40,8,128]{2,1,0:T(8,128)S(1)} %slice.9), channel_id=1, source_target_pairs={{4,0},{8,4},{12,8},{13,12},{9,13},{5,9},{1,5},{2,1},{6,2},{10,6},{... | collective-permute-start | bytes 491528 | tf_op jit(solution)/shard_map/ppermute | solution.py:475
  39.1 0.6 collective-permute-start.7
  39.7 0.0 copy-done.2
  39.7 0.5 shard_map.41.left
  40.2 4.1 %collective-permute-done.7.before = f32[32,8,128]{2,1,0:T(8,128)S(1)} collective-permute-done((f32[32,8,128]{2,1,0:T(8,128)S(1)}, f32[32,8,128]{2,1,0:T(8,128)S(1)}, u32[]{:S(2)}, u32[]{:S(2)}) %collective-permute-start.7) | collective-permute-done | bytes 131104 | tf_op jit(solution)/shard_map/ppermute | solution.py:474
  44.3 0.0 collective-permute-done.8.after
  44.3 5.4 %shard_map.42 = (f32[4,4,8,128]{3,2,1,0:T(8,128)S(1)}, f32[4,4,8,128]{3,2,1,0:T(8,128)S(1)}, f32[4,4,8,128]{3,2,1,0:T(8,128)S(1)}, f32[4,4,8,128]{3,2,1,0:T(8,128)S(1)}) custom-call(bf16[4,128,256]{2,1,0:T(8,128)(2,1)S(1)} %shard_map.41.left, f32[32,8,128]{2,1,0:T(8,128)S(1)} %collective-permute-done.7.before, f32[65,8,128]{2,1,0:T(8,128)S(1)} %add_add_fusion.own, ...), custom_call_target="tpu_custom_call" | custom-call | flops 131072000 | bytes 1048576 | tf_op jit(solution)/shard_map/pallas_call | solution.py:481
  49.7 1.2 %collective-permute-start.13 = (f32[4,4,8,128]{3,2,1,0:T(8,128)S(1)}, f32[4,4,8,128]{3,2,1,0:T(8,128)S(1)}, u32[]{:S(2)}, u32[]{:S(2)}) collective-permute-start(f32[4,4,8,128]{3,2,1,0:T(8,128)S(1)} %get-tuple-element.45), channel_id=1, source_target_pairs={{0,2},{1,3},{2,0},{3,1},{4,6},{5,7},{6,4},{7,5},{8,10},{9,11},{10,... | collective-permute-start | bytes 196616 | tf_op jit(solution)/shard_map/ppermute | solution.py:492
  50.9 0.0 collective-permute-start.14
  50.9 1.0 %collective-permute-start.9 = (f32[4,4,8,128]{3,2,1,0:T(8,128)S(1)}, f32[4,4,8,128]{3,2,1,0:T(8,128)S(1)}, u32[]{:S(2)}, u32[]{:S(2)}) collective-permute-start(f32[4,4,8,128]{3,2,1,0:T(8,128)S(1)} %get-tuple-element.40), channel_id=1, source_target_pairs={{0,1},{1,0},{2,3},{3,2},{4,5},{5,4},{6,7},{7,6},{8,9},{9,8},{10,11... | collective-permute-start | bytes 196616 | tf_op jit(solution)/shard_map/ppermute | solution.py:492
  51.9 2.2 %collective-permute-done.13.refs_0_ = f32[4,4,8,128]{3,2,1,0:T(8,128)S(1)} collective-permute-done((f32[4,4,8,128]{3,2,1,0:T(8,128)S(1)}, f32[4,4,8,128]{3,2,1,0:T(8,128)S(1)}, u32[]{:S(2)}, u32[]{:S(2)}) %collective-permute-start.13) | collective-permute-done | bytes 65568 | tf_op jit(solution)/shard_map/ppermute | solution.py:492
  54.1 1.2 %collective-permute-done.14.refs_1_ = f32[4,4,8,128]{3,2,1,0:T(8,128)S(1)} collective-permute-done((f32[4,4,8,128]{3,2,1,0:T(8,128)S(1)}, f32[4,4,8,128]{3,2,1,0:T(8,128)S(1)}, u32[]{:S(2)}, u32[]{:S(2)}) %collective-permute-start.14) | collective-permute-done | bytes 65568 | tf_op jit(solution)/shard_map/ppermute | solution.py:492
  55.3 0.5 collective-permute-start.15
  55.8 0.8 collective-permute-start.16
  56.6 2.9 %collective-permute-start.17 = (f32[2,4,8,128]{3,2,1,0:T(8,128)S(1)}, f32[2,4,8,128]{3,2,1,0:T(8,128)S(1)}, u32[]{:S(2)}, u32[]{:S(2)}) collective-permute-start(f32[2,4,8,128]{3,2,1,0:T(8,128)S(1)} %get-tuple-element.50), channel_id=1, source_target_pairs={{0,12},{4,0},{8,4},{12,8},{1,13},{5,1},{9,5},{13,9},{2,14},{6,2},{... | collective-permute-start | bytes 98312 | tf_op jit(solution)/shard_map/ppermute | solution.py:492
  59.5 0.0 collective-permute-done.9.refs_1_
  59.5 0.4 collective-permute-start.10
  59.9 1.5 %collective-permute-start.11 = (f32[2,4,8,128]{3,2,1,0:T(8,128)S(1)}, f32[2,4,8,128]{3,2,1,0:T(8,128)S(1)}, u32[]{:S(2)}, u32[]{:S(2)}) collective-permute-start(f32[2,4,8,128]{3,2,1,0:T(8,128)S(1)} %get-tuple-element.43), channel_id=1, source_target_pairs={{0,8},{4,12},{8,0},{12,4},{1,9},{5,13},{9,1},{13,5},{2,10},{6,14},... | collective-permute-start | bytes 98312 | tf_op jit(solution)/shard_map/ppermute | solution.py:492
  61.4 0.0 collective-permute-done.15.refs_5_
  61.4 2.8 %collective-permute-start.12 = (f32[2,4,8,128]{3,2,1,0:T(8,128)S(1)}, f32[2,4,8,128]{3,2,1,0:T(8,128)S(1)}, u32[]{:S(2)}, u32[]{:S(2)}) collective-permute-start(f32[2,4,8,128]{3,2,1,0:T(8,128)S(1)} %get-tuple-element.44), channel_id=1, source_target_pairs={{0,12},{4,0},{8,4},{12,8},{1,13},{5,1},{9,5},{13,9},{2,14},{6,2},{... | collective-permute-start | bytes 98312 | tf_op jit(solution)/shard_map/ppermute | solution.py:492
  64.3 0.1 add_convert_fusion.matrix
  64.4 0.0 collective-permute-done.16.refs_6_
  64.4 0.0 collective-permute-done.17.refs_7_
  64.5 0.9 %collective-permute-done.10.refs_1_ = f32[2,4,8,128]{3,2,1,0:T(8,128)S(1)} collective-permute-done((f32[2,4,8,128]{3,2,1,0:T(8,128)S(1)}, f32[2,4,8,128]{3,2,1,0:T(8,128)S(1)}, u32[]{:S(2)}, u32[]{:S(2)}) %collective-permute-start.10) | collective-permute-done | bytes 32800 | tf_op jit(solution)/shard_map/ppermute | solution.py:492
  65.4 0.0 collective-permute-done.11.refs_2_
  65.4 0.5 collective-permute-done.12.refs_3_
  65.9 0.4 shard_map.45
  66.3 2.0 %collective-permute-start.18 = (f32[4,32,128]{2,1,0:T(8,128)S(1)}, f32[4,32,128]{2,1,0:T(8,128)S(1)}, u32[]{:S(2)}, u32[]{:S(2)}) collective-permute-start(f32[4,32,128]{2,1,0:T(8,128)S(1)} %get-tuple-element.52), channel_id=1, source_target_pairs={{0,4},{4,8},{8,12},{12,0},{1,5},{5,9},{9,13},{13,1},{2,6},{6,10},{... | collective-permute-start | bytes 196616 | tf_op jit(solution)/shard_map/ppermute | solution.py:492
  68.2 2.8 %collective-permute-start.19 = (f32[4,32,128]{2,1,0:T(8,128)S(1)}, f32[4,32,128]{2,1,0:T(8,128)S(1)}, u32[]{:S(2)}, u32[]{:S(2)}) collective-permute-start(f32[4,32,128]{2,1,0:T(8,128)S(1)} %get-tuple-element.53), channel_id=1, source_target_pairs={{0,8},{4,12},{8,0},{12,4},{1,9},{5,13},{9,1},{13,5},{2,10},{6,14},... | collective-permute-start | bytes 196616 | tf_op jit(solution)/shard_map/ppermute | solution.py:492
  71.1 0.0 collective-permute-start.20
  71.1 1.7 %collective-permute-done.18.refs_1_ = f32[4,32,128]{2,1,0:T(8,128)S(1)} collective-permute-done((f32[4,32,128]{2,1,0:T(8,128)S(1)}, f32[4,32,128]{2,1,0:T(8,128)S(1)}, u32[]{:S(2)}, u32[]{:S(2)}) %collective-permute-start.18) | collective-permute-done | bytes 65568 | tf_op jit(solution)/shard_map/ppermute | solution.py:492
  72.7 1.4 %collective-permute-done.19.refs_2_ = f32[4,32,128]{2,1,0:T(8,128)S(1)} collective-permute-done((f32[4,32,128]{2,1,0:T(8,128)S(1)}, f32[4,32,128]{2,1,0:T(8,128)S(1)}, u32[]{:S(2)}, u32[]{:S(2)}) %collective-permute-start.19) | collective-permute-done | bytes 65568 | tf_op jit(solution)/shard_map/ppermute | solution.py:492
  74.1 1.2 %collective-permute-done.20.refs_3_ = f32[4,32,128]{2,1,0:T(8,128)S(1)} collective-permute-done((f32[4,32,128]{2,1,0:T(8,128)S(1)}, f32[4,32,128]{2,1,0:T(8,128)S(1)}, u32[]{:S(2)}, u32[]{:S(2)}) %collective-permute-start.20) | collective-permute-done | bytes 65568 | tf_op jit(solution)/shard_map/ppermute | solution.py:492
  75.3 0.8 %shard_map.46 = f32[512,128]{1,0:T(8,128)} custom-call(f32[4,32,128]{2,1,0:T(8,128)S(1)} %get-tuple-element.51.refs_0_, f32[4,32,128]{2,1,0:T(8,128)S(1)} %collective-permute-done.18.refs_1_, f32[4,32,128]{2,1,0:T(8,128)S(1)} %collective-permute-done.19.refs_2_, f32[4,32,128]{2,1,0:T(8,128)S(1)} %collective-permute-done.20.refs_3_), custom_call_target="tpu_custom_call" | custom-call | bytes 1048576 | tf_op jit(solution)/shard_map/pallas_call | solution.py:528
  (8 shorter events, 0.1 us)
Async XLA Ops:
  0.0 3.6 %copy-start = (f32[1,32,64,128]{3,2,1,0:T(8,128)S(1)}, f32[1,32,64,128]{3,2,1,0:T(8,128)}, u32[]{:S(2)}) copy-start(f32[1,32,64,128]{3,2,1,0:T(8,128)} %param.3) | copy-start | bytes 3145732
  1.1 2.5 %copy-start.1 = (s32[1,5]{1,0:T(1,128)S(1)}, s32[1,5]{1,0:T(1,128)}, u32[]{:S(2)}) copy-start(s32[1,5]{1,0:T(1,128)} %level.5) | copy-start | bytes 64
  1.1 7.7 %collective-permute-start.1 = (f32[5,64,128]{2,1,0:T(8,128)S(1)}, f32[5,64,128]{2,1,0:T(8,128)S(1)}, u32[]{:S(2)}, u32[]{:S(2)}) collective-permute-start(f32[5,64,128]{2,1,0:T(8,128)S(1)} %get-tuple-element.32), channel_id=1, source_target_pairs={{1,0},{2,1},{3,2},{0,3},{5,4},{6,5},{7,6},{4,7},{9,8},{10,9},{11,1... | collective-permute-start | bytes 491528 | tf_op jit(solution)/shard_map/ppermute | solution.py:426
  3.6 5.3 %collective-permute-start = (f32[4,64,128]{2,1,0:T(8,128)S(1)}, f32[4,64,128]{2,1,0:T(8,128)S(1)}, u32[]{:S(2)}, u32[]{:S(2)}) collective-permute-start(f32[4,64,128]{2,1,0:T(8,128)S(1)} %get-tuple-element.31), channel_id=1, source_target_pairs={{0,1},{1,2},{2,3},{3,0},{4,5},{5,6},{6,7},{7,4},{8,9},{9,10},{10,1... | collective-permute-start | bytes 393224 | tf_op jit(solution)/shard_map/ppermute | solution.py:425
  10.7 11.8 %collective-permute-start.2 = (f32[65,8,128]{2,1,0:T(8,128)S(1)}, f32[65,8,128]{2,1,0:T(8,128)S(1)}, u32[]{:S(2)}, u32[]{:S(2)}) collective-permute-start(f32[65,8,128]{2,1,0:T(8,128)S(1)} %shard_map.39), channel_id=1, source_target_pairs={{0,4},{4,0},{8,12},{12,8},{1,5},{5,1},{9,13},{13,9},{2,6},{6,2},{1... | collective-permute-start | bytes 798728 | tf_op jit(solution)/shard_map/ppermute | solution.py:459
  12.4 11.6 %collective-permute-start.3 = (f32[65,8,128]{2,1,0:T(8,128)S(1)}, f32[65,8,128]{2,1,0:T(8,128)S(1)}, u32[]{:S(2)}, u32[]{:S(2)}) collective-permute-start(f32[65,8,128]{2,1,0:T(8,128)S(1)} %get-tuple-element.38), channel_id=1, source_target_pairs={{4,8},{8,4},{5,9},{9,5},{6,10},{10,6},{7,11},{11,7},{20,24},{24,20... | collective-permute-start | bytes 798728 | tf_op jit(solution)/shard_map/ppermute | solution.py:457
  13.0 13.1 %collective-permute-start.5 = (f32[65,8,128]{2,1,0:T(8,128)S(1)}, f32[65,8,128]{2,1,0:T(8,128)S(1)}, u32[]{:S(2)}, u32[]{:S(2)}) collective-permute-start(f32[65,8,128]{2,1,0:T(8,128)S(1)} %get-tuple-element.37), channel_id=1, source_target_pairs={{0,4},{12,8},{1,5},{13,9},{2,6},{14,10},{3,7},{15,11},{16,20},{28,... | collective-permute-start | bytes 798728 | tf_op jit(solution)/shard_map/ppermute | solution.py:462
  21.2 8.7 %collective-permute-start.4 = (f32[65,8,128]{2,1,0:T(8,128)S(1)}, f32[65,8,128]{2,1,0:T(8,128)S(1)}, u32[]{:S(2)}, u32[]{:S(2)}) collective-permute-start(f32[65,8,128]{2,1,0:T(8,128)S(1)} %get-tuple-element.38), channel_id=1, source_target_pairs={{0,8},{12,4},{1,9},{13,5},{2,10},{14,6},{3,11},{15,7},{16,24},{28,... | collective-permute-start | bytes 798728 | tf_op jit(solution)/shard_map/ppermute | solution.py:461
  22.6 14.8 %collective-permute-start.6 = (f32[65,8,128]{2,1,0:T(8,128)S(1)}, f32[65,8,128]{2,1,0:T(8,128)S(1)}, u32[]{:S(2)}, u32[]{:S(2)}) collective-permute-start(f32[65,8,128]{2,1,0:T(8,128)S(1)} %add.100), channel_id=1, source_target_pairs={{4,12},{8,0},{5,13},{9,1},{6,14},{10,2},{7,15},{11,3},{20,28},{24,... | collective-permute-start | bytes 798728 | tf_op jit(solution)/shard_map/ppermute | solution.py:465
  37.6 2.1 %copy-start.2 = (s32[128]{0:T(128)S(1)}, s32[128]{0:T(128)}, u32[]{:S(2)}) copy-start(s32[128]{0:T(128)} %param.5) | copy-start | bytes 1540
  37.6 6.7 %collective-permute-start.8 = (f32[40,8,128]{2,1,0:T(8,128)S(1)}, f32[40,8,128]{2,1,0:T(8,128)S(1)}, u32[]{:S(2)}, u32[]{:S(2)}) collective-permute-start(f32[40,8,128]{2,1,0:T(8,128)S(1)} %slice.9), channel_id=1, source_target_pairs={{4,0},{8,4},{12,8},{13,12},{9,13},{5,9},{1,5},{2,1},{6,2},{10,6},{... | collective-permute-start | bytes 491528 | tf_op jit(solution)/shard_map/ppermute | solution.py:475
  39.1 5.2 %collective-permute-start.7 = (f32[32,8,128]{2,1,0:T(8,128)S(1)}, f32[32,8,128]{2,1,0:T(8,128)S(1)}, u32[]{:S(2)}, u32[]{:S(2)}) collective-permute-start(f32[32,8,128]{2,1,0:T(8,128)S(1)} %slice.8), channel_id=1, source_target_pairs={{0,4},{4,8},{8,12},{12,13},{13,9},{9,5},{5,1},{1,2},{2,6},{6,10},{... | collective-permute-start | bytes 393224 | tf_op jit(solution)/shard_map/ppermute | solution.py:474
  49.7 4.4 %collective-permute-start.13 = (f32[4,4,8,128]{3,2,1,0:T(8,128)S(1)}, f32[4,4,8,128]{3,2,1,0:T(8,128)S(1)}, u32[]{:S(2)}, u32[]{:S(2)}) collective-permute-start(f32[4,4,8,128]{3,2,1,0:T(8,128)S(1)} %get-tuple-element.45), channel_id=1, source_target_pairs={{0,2},{1,3},{2,0},{3,1},{4,6},{5,7},{6,4},{7,5},{8,10},{9,11},{10,... | collective-permute-start | bytes 196616 | tf_op jit(solution)/shard_map/ppermute | solution.py:492
  50.9 4.4 %collective-permute-start.14 = (f32[4,4,8,128]{3,2,1,0:T(8,128)S(1)}, f32[4,4,8,128]{3,2,1,0:T(8,128)S(1)}, u32[]{:S(2)}, u32[]{:S(2)}) collective-permute-start(f32[4,4,8,128]{3,2,1,0:T(8,128)S(1)} %get-tuple-element.46), channel_id=1, source_target_pairs={{0,3},{1,2},{2,1},{3,0},{4,7},{5,6},{6,5},{7,4},{8,11},{9,10},{10,... | collective-permute-start | bytes 196616 | tf_op jit(solution)/shard_map/ppermute | solution.py:492
  50.9 8.6 %collective-permute-start.9 = (f32[4,4,8,128]{3,2,1,0:T(8,128)S(1)}, f32[4,4,8,128]{3,2,1,0:T(8,128)S(1)}, u32[]{:S(2)}, u32[]{:S(2)}) collective-permute-start(f32[4,4,8,128]{3,2,1,0:T(8,128)S(1)} %get-tuple-element.40), channel_id=1, source_target_pairs={{0,1},{1,0},{2,3},{3,2},{4,5},{5,4},{6,7},{7,6},{8,9},{9,8},{10,11... | collective-permute-start | bytes 196616 | tf_op jit(solution)/shard_map/ppermute | solution.py:492
  55.3 6.1 %collective-permute-start.15 = (f32[2,4,8,128]{3,2,1,0:T(8,128)S(1)}, f32[2,4,8,128]{3,2,1,0:T(8,128)S(1)}, u32[]{:S(2)}, u32[]{:S(2)}) collective-permute-start(f32[2,4,8,128]{3,2,1,0:T(8,128)S(1)} %get-tuple-element.48), channel_id=1, source_target_pairs={{0,4},{4,8},{8,12},{12,0},{1,5},{5,9},{9,13},{13,1},{2,6},{6,10},{... | collective-permute-start | bytes 98312 | tf_op jit(solution)/shard_map/ppermute | solution.py:492
  55.8 8.6 %collective-permute-start.16 = (f32[2,4,8,128]{3,2,1,0:T(8,128)S(1)}, f32[2,4,8,128]{3,2,1,0:T(8,128)S(1)}, u32[]{:S(2)}, u32[]{:S(2)}) collective-permute-start(f32[2,4,8,128]{3,2,1,0:T(8,128)S(1)} %get-tuple-element.49), channel_id=1, source_target_pairs={{0,8},{4,12},{8,0},{12,4},{1,9},{5,13},{9,1},{13,5},{2,10},{6,14},... | collective-permute-start | bytes 98312 | tf_op jit(solution)/shard_map/ppermute | solution.py:492
  56.6 7.8 %collective-permute-start.17 = (f32[2,4,8,128]{3,2,1,0:T(8,128)S(1)}, f32[2,4,8,128]{3,2,1,0:T(8,128)S(1)}, u32[]{:S(2)}, u32[]{:S(2)}) collective-permute-start(f32[2,4,8,128]{3,2,1,0:T(8,128)S(1)} %get-tuple-element.50), channel_id=1, source_target_pairs={{0,12},{4,0},{8,4},{12,8},{1,13},{5,1},{9,5},{13,9},{2,14},{6,2},{... | collective-permute-start | bytes 98312 | tf_op jit(solution)/shard_map/ppermute | solution.py:492
  59.5 5.9 %collective-permute-start.10 = (f32[2,4,8,128]{3,2,1,0:T(8,128)S(1)}, f32[2,4,8,128]{3,2,1,0:T(8,128)S(1)}, u32[]{:S(2)}, u32[]{:S(2)}) collective-permute-start(f32[2,4,8,128]{3,2,1,0:T(8,128)S(1)} %get-tuple-element.42), channel_id=1, source_target_pairs={{0,4},{4,8},{8,12},{12,0},{1,5},{5,9},{9,13},{13,1},{2,6},{6,10},{... | collective-permute-start | bytes 98312 | tf_op jit(solution)/shard_map/ppermute | solution.py:492
  59.9 5.5 %collective-permute-start.11 = (f32[2,4,8,128]{3,2,1,0:T(8,128)S(1)}, f32[2,4,8,128]{3,2,1,0:T(8,128)S(1)}, u32[]{:S(2)}, u32[]{:S(2)}) collective-permute-start(f32[2,4,8,128]{3,2,1,0:T(8,128)S(1)} %get-tuple-element.43), channel_id=1, source_target_pairs={{0,8},{4,12},{8,0},{12,4},{1,9},{5,13},{9,1},{13,5},{2,10},{6,14},... | collective-permute-start | bytes 98312 | tf_op jit(solution)/shard_map/ppermute | solution.py:492
  61.4 4.4 %collective-permute-start.12 = (f32[2,4,8,128]{3,2,1,0:T(8,128)S(1)}, f32[2,4,8,128]{3,2,1,0:T(8,128)S(1)}, u32[]{:S(2)}, u32[]{:S(2)}) collective-permute-start(f32[2,4,8,128]{3,2,1,0:T(8,128)S(1)} %get-tuple-element.44), channel_id=1, source_target_pairs={{0,12},{4,0},{8,4},{12,8},{1,13},{5,1},{9,5},{13,9},{2,14},{6,2},{... | collective-permute-start | bytes 98312 | tf_op jit(solution)/shard_map/ppermute | solution.py:492
  66.3 6.5 %collective-permute-start.18 = (f32[4,32,128]{2,1,0:T(8,128)S(1)}, f32[4,32,128]{2,1,0:T(8,128)S(1)}, u32[]{:S(2)}, u32[]{:S(2)}) collective-permute-start(f32[4,32,128]{2,1,0:T(8,128)S(1)} %get-tuple-element.52), channel_id=1, source_target_pairs={{0,4},{4,8},{8,12},{12,0},{1,5},{5,9},{9,13},{13,1},{2,6},{6,10},{... | collective-permute-start | bytes 196616 | tf_op jit(solution)/shard_map/ppermute | solution.py:492
  68.2 5.9 %collective-permute-start.19 = (f32[4,32,128]{2,1,0:T(8,128)S(1)}, f32[4,32,128]{2,1,0:T(8,128)S(1)}, u32[]{:S(2)}, u32[]{:S(2)}) collective-permute-start(f32[4,32,128]{2,1,0:T(8,128)S(1)} %get-tuple-element.53), channel_id=1, source_target_pairs={{0,8},{4,12},{8,0},{12,4},{1,9},{5,13},{9,1},{13,5},{2,10},{6,14},... | collective-permute-start | bytes 196616 | tf_op jit(solution)/shard_map/ppermute | solution.py:492
  71.1 4.3 %collective-permute-start.20 = (f32[4,32,128]{2,1,0:T(8,128)S(1)}, f32[4,32,128]{2,1,0:T(8,128)S(1)}, u32[]{:S(2)}, u32[]{:S(2)}) collective-permute-start(f32[4,32,128]{2,1,0:T(8,128)S(1)} %get-tuple-element.54), channel_id=1, source_target_pairs={{0,12},{4,0},{8,4},{12,8},{1,13},{5,1},{9,5},{13,9},{2,14},{6,2},{... | collective-permute-start | bytes 196616 | tf_op jit(solution)/shard_map/ppermute | solution.py:492

commit v10 on v8

--- a/solution.py
+++ b/solution.py
@@ -488,10 +488,10 @@
 
     def shared(values, axis, partner):
         members = range(lax.axis_size(axis))
-        others = lax.optimization_barrier(tuple(values[1:]))
-        return [values[0]] + [
-            lax.ppermute(value, axis, [(i, partner(i, d)) for i in members]) for d, value in enumerate(others, 1)
-        ]
+        received = [values[0]]
+        for d, value in enumerate(values[1:], 1):
+            received.append(lax.ppermute(value, axis, [(i, partner(i, d)) for i in members]))
+        return received
 
     ahead = lambda i, d: (i + d) % grids
     by_slab = shared(sent, "slab", lambda i, d: i ^ d)

time: 73.6 us -> 73.6 us (level)
  no operation moved by 1% of the time
where the time goes in v10:
time: 73.6 us; the launch traced here: 73.3 us
  waiting for transfers between devices  31.4 us (43%)
  starting transfers between devices  25.9 us (35%)
  Pallas kernels  14.8 us (20%)
    ppermute x9, waiting for transfers between devices, shared(): lax.ppermute(value, axis, [(i, partner(i, d)) for i in members])  12.1 us
    ppermute x9, starting transfers between devices, shared(): lax.ppermute(value, axis, [(i, partner(i, d)) for i in members])  10.1 us
    ppermute x1, waiting for transfers between devices, local_fast(): passed = lax.ppermute(joined, 'grid', [(1, 3), (2, 0)])  7.53 us
    ppermute x1, starting transfers between devices, local_fast(): inwards = lax.ppermute(near, 'grid', [(0, 1), (3, 2)])  6.31 us
    pallas_call x1, Pallas kernels, local_fast(): kernel(functools.partial(second_kernel, block, grids), [floats(N3, half,...  5.46 us
    ppermute x1, waiting for transfers between devices, local_fast(): lax.ppermute(own[(block - LOW) * TILES:block * TILES], both, forward)  4.11 us
    ppermute x1, waiting for transfers between devices, local_fast(): skipped = lax.ppermute(middle, 'grid', [(0, 2), (3, 1)])  3.79 us
    pallas_call x2, Pallas kernels, outer_block(): kernel(functools.partial(outer_kernel, later), piece, [SMEM] + [VMEM] * 4...  3.75 us
  transfers between devices with their start and end apart: 18, of which 11 were waited for; matrix products, arithmetic and copies ran while one was open for 0% of the time, Pallas kernels for 7%

profile of v10, /device:TPU:0, one launch (start us, length us, event | category | flops | bytes accessed | tf_op | source)
XLA Modules:
  0.0 73.3 jit_solution(1919710854347060903)
XLA Ops:
  0.0 0.0 copy-start
  0.0 1.1 %shard_map.38 = (f32[4,64,128]{2,1,0:T(8,128)S(1)}, f32[5,64,128]{2,1,0:T(8,128)S(1)}) custom-call(f32[32,64,128]{2,1,0:T(8,128)} %bitcast.2), custom_call_target="tpu_custom_call" | custom-call | bytes 1048576 | tf_op jit(solution)/shard_map/pallas_call | solution.py:418
  1.1 0.0 copy-start.1
  1.1 2.5 %collective-permute-start.1 = (f32[5,64,128]{2,1,0:T(8,128)S(1)}, f32[5,64,128]{2,1,0:T(8,128)S(1)}, u32[]{:S(2)}, u32[]{:S(2)}) collective-permute-start(f32[5,64,128]{2,1,0:T(8,128)S(1)} %get-tuple-element.28), channel_id=1, source_target_pairs={{1,0},{2,1},{3,2},{0,3},{5,4},{6,5},{7,6},{4,7},{9,8},{10,9},{11,1... | collective-permute-start | bytes 491528 | tf_op jit(solution)/shard_map/ppermute | solution.py:425
  3.6 0.0 collective-permute-start
  3.6 0.0 copy-done
  3.6 0.0 copy-done.1
  3.6 2.8 %shard_map.37 = (f32[65,8,128]{2,1,0:T(8,128)S(1)}, f32[65,8,128]{2,1,0:T(8,128)S(1)}, bf16[128,256]{1,0:T(8,128)(2,1)S(1)}) custom-call(s32[1,5]{1,0:T(1,128)S(1)} %copy-done.1, f32[32,64,128]{2,1,0:T(8,128)S(1)} %bitcast.3), custom_call_target="tpu_custom_call" | custom-call | flops 26214400 | bytes 1048576 | tf_op jit(solution)/shard_map/pallas_call | solution.py:434
  6.4 2.4 %collective-permute-done.before = f32[4,64,128]{2,1,0:T(8,128)S(1)} collective-permute-done((f32[4,64,128]{2,1,0:T(8,128)S(1)}, f32[4,64,128]{2,1,0:T(8,128)S(1)}, u32[]{:S(2)}, u32[]{:S(2)}) %collective-permute-start) | collective-permute-done | bytes 131104 | tf_op jit(solution)/shard_map/ppermute | solution.py:424
  8.8 0.0 collective-permute-done.1.after
  8.8 1.9 %shard_map.39 = f32[65,8,128]{2,1,0:T(8,128)S(1)} custom-call(s32[1,5]{1,0:T(1,128)S(1)} %copy-done.1, bf16[128,256]{1,0:T(8,128)(2,1)S(1)} %get-tuple-element.26.left, f32[4,64,128]{2,1,0:T(8,128)S(1)} %collective-permute-done.before, f32[32,64,128]{2,1,0:T(8,128)S(1)} %bitcast.4, f32[5,64,128]{2,1,0:T(8,128)S(1)} %collective-permute-done.1.after), custom_call_target="tpu_custom_call" | custom-call | flops 15728640 | bytes 1048576 | tf_op jit(solution)/shard_map/pallas_call | solution.py:446
  10.7 1.6 %collective-permute-start.2 = (f32[65,8,128]{2,1,0:T(8,128)S(1)}, f32[65,8,128]{2,1,0:T(8,128)S(1)}, u32[]{:S(2)}, u32[]{:S(2)}) collective-permute-start(f32[65,8,128]{2,1,0:T(8,128)S(1)} %shard_map.39), channel_id=1, source_target_pairs={{0,4},{4,0},{8,12},{12,8},{1,5},{5,1},{9,13},{13,9},{2,6},{6,2},{1... | collective-permute-start | bytes 798728 | tf_op jit(solution)/shard_map/ppermute | solution.py:458
  12.4 0.7 collective-permute-start.3
  13.0 6.3 %collective-permute-start.5 = (f32[65,8,128]{2,1,0:T(8,128)S(1)}, f32[65,8,128]{2,1,0:T(8,128)S(1)}, u32[]{:S(2)}, u32[]{:S(2)}) collective-permute-start(f32[65,8,128]{2,1,0:T(8,128)S(1)} %get-tuple-element.33), channel_id=1, source_target_pairs={{0,4},{12,8},{1,5},{13,9},{2,6},{14,10},{3,7},{15,11},{16,20},{28,... | collective-permute-start | bytes 798728 | tf_op jit(solution)/shard_map/ppermute | solution.py:461
  19.3 1.9 %shard_map.40 = f32[65,8,128]{2,1,0:T(8,128)S(1)} custom-call(s32[1,5]{1,0:T(1,128)S(1)} %copy-done.1, bf16[128,256]{1,0:T(8,128)(2,1)S(1)} %get-tuple-element.26.left, f32[4,64,128]{2,1,0:T(8,128)S(1)} %collective-permute-done.before, f32[32,64,128]{2,1,0:T(8,128)S(1)} %bitcast.5, f32[5,64,128]{2,1,0:T(8,128)S(1)} %collective-permute-done.1.after), custom_call_target="tpu_custom_call" | custom-call | flops 15728640 | bytes 1048576 | tf_op jit(solution)/shard_map/pallas_call | solution.py:446
  21.2 1.3 %collective-permute-start.4 = (f32[65,8,128]{2,1,0:T(8,128)S(1)}, f32[65,8,128]{2,1,0:T(8,128)S(1)}, u32[]{:S(2)}, u32[]{:S(2)}) collective-permute-start(f32[65,8,128]{2,1,0:T(8,128)S(1)} %get-tuple-element.34), channel_id=1, source_target_pairs={{0,8},{12,4},{1,9},{13,5},{2,10},{14,6},{3,11},{15,7},{16,24},{28,... | collective-permute-start | bytes 798728 | tf_op jit(solution)/shard_map/ppermute | solution.py:460
  22.5 0.0 collective-permute-done.2
  22.6 1.3 %collective-permute-start.6 = (f32[65,8,128]{2,1,0:T(8,128)S(1)}, f32[65,8,128]{2,1,0:T(8,128)S(1)}, u32[]{:S(2)}, u32[]{:S(2)}) collective-permute-start(f32[65,8,128]{2,1,0:T(8,128)S(1)} %add.100), channel_id=1, source_target_pairs={{4,12},{8,0},{5,13},{9,1},{6,14},{10,2},{7,15},{11,3},{20,28},{24,... | collective-permute-start | bytes 798728 | tf_op jit(solution)/shard_map/ppermute | solution.py:464
  23.9 0.0 copy-start.2
  23.9 0.6 copy-done.2
  24.6 0.0 collective-permute-done.3
  24.6 1.5 %collective-permute-done.5 = f32[65,8,128]{2,1,0:T(8,128)S(1)} collective-permute-done((f32[65,8,128]{2,1,0:T(8,128)S(1)}, f32[65,8,128]{2,1,0:T(8,128)S(1)}, u32[]{:S(2)}, u32[]{:S(2)}) %collective-permute-start.5) | collective-permute-done | bytes 266272 | tf_op jit(solution)/shard_map/ppermute | solution.py:461
  26.1 3.8 %collective-permute-done.4 = f32[65,8,128]{2,1,0:T(8,128)S(1)} collective-permute-done((f32[65,8,128]{2,1,0:T(8,128)S(1)}, f32[65,8,128]{2,1,0:T(8,128)S(1)}, u32[]{:S(2)}, u32[]{:S(2)}) %collective-permute-start.4) | collective-permute-done | bytes 266272 | tf_op jit(solution)/shard_map/ppermute | solution.py:460
  29.9 7.5 %collective-permute-done.6 = f32[65,8,128]{2,1,0:T(8,128)S(1)} collective-permute-done((f32[65,8,128]{2,1,0:T(8,128)S(1)}, f32[65,8,128]{2,1,0:T(8,128)S(1)}, u32[]{:S(2)}, u32[]{:S(2)}) %collective-permute-start.6) | collective-permute-done | bytes 266272 | tf_op jit(solution)/shard_map/ppermute | solution.py:464
  37.4 0.1 add_add_fusion.own
  37.6 1.5 %collective-permute-start.8 = (f32[40,8,128]{2,1,0:T(8,128)S(1)}, f32[40,8,128]{2,1,0:T(8,128)S(1)}, u32[]{:S(2)}, u32[]{:S(2)}) collective-permute-start(f32[40,8,128]{2,1,0:T(8,128)S(1)} %slice.9), channel_id=1, source_target_pairs={{4,0},{8,4},{12,8},{13,12},{9,13},{5,9},{1,5},{2,1},{6,2},{10,6},{... | collective-permute-start | bytes 491528 | tf_op jit(solution)/shard_map/ppermute | solution.py:474
  39.1 0.6 collective-permute-start.7
  39.7 0.5 shard_map.41.left
  40.2 4.1 %collective-permute-done.7.before = f32[32,8,128]{2,1,0:T(8,128)S(1)} collective-permute-done((f32[32,8,128]{2,1,0:T(8,128)S(1)}, f32[32,8,128]{2,1,0:T(8,128)S(1)}, u32[]{:S(2)}, u32[]{:S(2)}) %collective-permute-start.7) | collective-permute-done | bytes 131104 | tf_op jit(solution)/shard_map/ppermute | solution.py:473
  44.3 0.0 collective-permute-done.8.after
  44.3 5.5 %shard_map.42 = (f32[4,4,8,128]{3,2,1,0:T(8,128)S(1)}, f32[4,4,8,128]{3,2,1,0:T(8,128)S(1)}, f32[4,4,8,128]{3,2,1,0:T(8,128)S(1)}, f32[4,4,8,128]{3,2,1,0:T(8,128)S(1)}) custom-call(bf16[4,128,256]{2,1,0:T(8,128)(2,1)S(1)} %shard_map.41.left, f32[32,8,128]{2,1,0:T(8,128)S(1)} %collective-permute-done.7.before, f32[65,8,128]{2,1,0:T(8,128)S(1)} %add_add_fusion.own, ...), custom_call_target="tpu_custom_call" | custom-call | flops 131072000 | bytes 1048576 | tf_op jit(solution)/shard_map/pallas_call | solution.py:480
  49.8 1.2 %collective-permute-start.10 = (f32[4,4,8,128]{3,2,1,0:T(8,128)S(1)}, f32[4,4,8,128]{3,2,1,0:T(8,128)S(1)}, u32[]{:S(2)}, u32[]{:S(2)}) collective-permute-start(f32[4,4,8,128]{3,2,1,0:T(8,128)S(1)} %get-tuple-element.37), channel_id=1, source_target_pairs={{0,2},{1,3},{2,0},{3,1},{4,6},{5,7},{6,4},{7,5},{8,10},{9,11},{10,... | collective-permute-start | bytes 196616 | tf_op jit(solution)/shard_map/ppermute | solution.py:493
  51.0 0.0 collective-permute-start.11
  51.0 1.0 %collective-permute-start.9 = (f32[4,4,8,128]{3,2,1,0:T(8,128)S(1)}, f32[4,4,8,128]{3,2,1,0:T(8,128)S(1)}, u32[]{:S(2)}, u32[]{:S(2)}) collective-permute-start(f32[4,4,8,128]{3,2,1,0:T(8,128)S(1)} %get-tuple-element.36), channel_id=1, source_target_pairs={{0,1},{1,0},{2,3},{3,2},{4,5},{5,4},{6,7},{7,6},{8,9},{9,8},{10,11... | collective-permute-start | bytes 196616 | tf_op jit(solution)/shard_map/ppermute | solution.py:493
  52.0 2.2 %collective-permute-done.10.refs_2_ = f32[4,4,8,128]{3,2,1,0:T(8,128)S(1)} collective-permute-done((f32[4,4,8,128]{3,2,1,0:T(8,128)S(1)}, f32[4,4,8,128]{3,2,1,0:T(8,128)S(1)}, u32[]{:S(2)}, u32[]{:S(2)}) %collective-permute-start.10) | collective-permute-done | bytes 65568 | tf_op jit(solution)/shard_map/ppermute | solution.py:493
  54.2 1.2 %collective-permute-done.11.refs_3_ = f32[4,4,8,128]{3,2,1,0:T(8,128)S(1)} collective-permute-done((f32[4,4,8,128]{3,2,1,0:T(8,128)S(1)}, f32[4,4,8,128]{3,2,1,0:T(8,128)S(1)}, u32[]{:S(2)}, u32[]{:S(2)}) %collective-permute-start.11) | collective-permute-done | bytes 65568 | tf_op jit(solution)/shard_map/ppermute | solution.py:493
  55.4 0.0 collective-permute-done.9.refs_1_
  55.4 0.5 collective-permute-start.12
  55.9 0.7 collective-permute-start.13
  56.6 2.8 %collective-permute-start.14 = (f32[4,4,8,128]{3,2,1,0:T(8,128)S(1)}, f32[4,4,8,128]{3,2,1,0:T(8,128)S(1)}, u32[]{:S(2)}, u32[]{:S(2)}) collective-permute-start(f32[4,4,8,128]{3,2,1,0:T(8,128)S(1)} %get-tuple-element.42), channel_id=1, source_target_pairs={{0,12},{4,0},{8,4},{12,8},{1,13},{5,1},{9,5},{13,9},{2,14},{6,2},{... | collective-permute-start | bytes 196616 | tf_op jit(solution)/shard_map/ppermute | solution.py:493
  59.5 0.1 add_convert_fusion.matrix
  59.6 2.6 %collective-permute-done.12.refs_1_ = f32[4,4,8,128]{3,2,1,0:T(8,128)S(1)} collective-permute-done((f32[4,4,8,128]{3,2,1,0:T(8,128)S(1)}, f32[4,4,8,128]{3,2,1,0:T(8,128)S(1)}, u32[]{:S(2)}, u32[]{:S(2)}) %collective-permute-start.12) | collective-permute-done | bytes 65568 | tf_op jit(solution)/shard_map/ppermute | solution.py:493
  62.2 1.9 %collective-permute-done.13.refs_2_ = f32[4,4,8,128]{3,2,1,0:T(8,128)S(1)} collective-permute-done((f32[4,4,8,128]{3,2,1,0:T(8,128)S(1)}, f32[4,4,8,128]{3,2,1,0:T(8,128)S(1)}, u32[]{:S(2)}, u32[]{:S(2)}) %collective-permute-start.13) | collective-permute-done | bytes 65568 | tf_op jit(solution)/shard_map/ppermute | solution.py:493
  64.1 0.0 collective-permute-done.14.refs_3_
  64.1 0.4 shard_map.44
  64.5 1.4 %collective-permute-start.15 = (f32[4,32,128]{2,1,0:T(8,128)S(1)}, f32[4,32,128]{2,1,0:T(8,128)S(1)}, u32[]{:S(2)}, u32[]{:S(2)}) collective-permute-start(f32[4,32,128]{2,1,0:T(8,128)S(1)} %get-tuple-element.44), channel_id=1, source_target_pairs={{0,4},{4,8},{8,12},{12,0},{1,5},{5,9},{9,13},{13,1},{2,6},{6,10},{... | collective-permute-start | bytes 196616 | tf_op jit(solution)/shard_map/ppermute | solution.py:493
  65.8 1.2 %collective-permute-start.16 = (f32[4,32,128]{2,1,0:T(8,128)S(1)}, f32[4,32,128]{2,1,0:T(8,128)S(1)}, u32[]{:S(2)}, u32[]{:S(2)}) collective-permute-start(f32[4,32,128]{2,1,0:T(8,128)S(1)} %get-tuple-element.45), channel_id=1, source_target_pairs={{0,8},{4,12},{8,0},{12,4},{1,9},{5,13},{9,1},{13,5},{2,10},{6,14},... | collective-permute-start | bytes 196616 | tf_op jit(solution)/shard_map/ppermute | solution.py:493
  67.0 1.3 %collective-permute-start.17 = (f32[4,32,128]{2,1,0:T(8,128)S(1)}, f32[4,32,128]{2,1,0:T(8,128)S(1)}, u32[]{:S(2)}, u32[]{:S(2)}) collective-permute-start(f32[4,32,128]{2,1,0:T(8,128)S(1)} %get-tuple-element.46), channel_id=1, source_target_pairs={{0,12},{4,0},{8,4},{12,8},{1,13},{5,1},{9,5},{13,9},{2,14},{6,2},{... | collective-permute-start | bytes 196616 | tf_op jit(solution)/shard_map/ppermute | solution.py:493
  68.3 2.9 %collective-permute-done.15.refs_1_ = f32[4,32,128]{2,1,0:T(8,128)S(1)} collective-permute-done((f32[4,32,128]{2,1,0:T(8,128)S(1)}, f32[4,32,128]{2,1,0:T(8,128)S(1)}, u32[]{:S(2)}, u32[]{:S(2)}) %collective-permute-start.15) | collective-permute-done | bytes 65568 | tf_op jit(solution)/shard_map/ppermute | solution.py:493
  71.2 1.3 %collective-permute-done.16.refs_2_ = f32[4,32,128]{2,1,0:T(8,128)S(1)} collective-permute-done((f32[4,32,128]{2,1,0:T(8,128)S(1)}, f32[4,32,128]{2,1,0:T(8,128)S(1)}, u32[]{:S(2)}, u32[]{:S(2)}) %collective-permute-start.16) | collective-permute-done | bytes 65568 | tf_op jit(solution)/shard_map/ppermute | solution.py:493
  72.5 0.0 collective-permute-done.17.refs_3_
  72.5 0.8 %shard_map.45 = f32[512,128]{1,0:T(8,128)} custom-call(f32[4,32,128]{2,1,0:T(8,128)S(1)} %get-tuple-element.43.refs_0_, f32[4,32,128]{2,1,0:T(8,128)S(1)} %collective-permute-done.15.refs_1_, f32[4,32,128]{2,1,0:T(8,128)S(1)} %collective-permute-done.16.refs_2_, f32[4,32,128]{2,1,0:T(8,128)S(1)} %collective-permute-done.17.refs_3_), custom_call_target="tpu_custom_call" | custom-call | bytes 1048576 | tf_op jit(solution)/shard_map/pallas_call | solution.py:526
  (7 shorter events, 0.1 us)
Async XLA Ops:
  0.0 3.6 %copy-start = (f32[1,32,64,128]{3,2,1,0:T(8,128)S(1)}, f32[1,32,64,128]{3,2,1,0:T(8,128)}, u32[]{:S(2)}) copy-start(f32[1,32,64,128]{3,2,1,0:T(8,128)} %param.3) | copy-start | bytes 3145732
  1.1 2.5 %copy-start.1 = (s32[1,5]{1,0:T(1,128)S(1)}, s32[1,5]{1,0:T(1,128)}, u32[]{:S(2)}) copy-start(s32[1,5]{1,0:T(1,128)} %level.5) | copy-start | bytes 64
  1.1 7.7 %collective-permute-start.1 = (f32[5,64,128]{2,1,0:T(8,128)S(1)}, f32[5,64,128]{2,1,0:T(8,128)S(1)}, u32[]{:S(2)}, u32[]{:S(2)}) collective-permute-start(f32[5,64,128]{2,1,0:T(8,128)S(1)} %get-tuple-element.28), channel_id=1, source_target_pairs={{1,0},{2,1},{3,2},{0,3},{5,4},{6,5},{7,6},{4,7},{9,8},{10,9},{11,1... | collective-permute-start | bytes 491528 | tf_op jit(solution)/shard_map/ppermute | solution.py:425
  3.6 5.3 %collective-permute-start = (f32[4,64,128]{2,1,0:T(8,128)S(1)}, f32[4,64,128]{2,1,0:T(8,128)S(1)}, u32[]{:S(2)}, u32[]{:S(2)}) collective-permute-start(f32[4,64,128]{2,1,0:T(8,128)S(1)} %get-tuple-element.27), channel_id=1, source_target_pairs={{0,1},{1,2},{2,3},{3,0},{4,5},{5,6},{6,7},{7,4},{8,9},{9,10},{10,1... | collective-permute-start | bytes 393224 | tf_op jit(solution)/shard_map/ppermute | solution.py:424
  10.7 11.8 %collective-permute-start.2 = (f32[65,8,128]{2,1,0:T(8,128)S(1)}, f32[65,8,128]{2,1,0:T(8,128)S(1)}, u32[]{:S(2)}, u32[]{:S(2)}) collective-permute-start(f32[65,8,128]{2,1,0:T(8,128)S(1)} %shard_map.39), channel_id=1, source_target_pairs={{0,4},{4,0},{8,12},{12,8},{1,5},{5,1},{9,13},{13,9},{2,6},{6,2},{1... | collective-permute-start | bytes 798728 | tf_op jit(solution)/shard_map/ppermute | solution.py:458
  12.4 12.2 %collective-permute-start.3 = (f32[65,8,128]{2,1,0:T(8,128)S(1)}, f32[65,8,128]{2,1,0:T(8,128)S(1)}, u32[]{:S(2)}, u32[]{:S(2)}) collective-permute-start(f32[65,8,128]{2,1,0:T(8,128)S(1)} %get-tuple-element.34), channel_id=1, source_target_pairs={{4,8},{8,4},{5,9},{9,5},{6,10},{10,6},{7,11},{11,7},{20,24},{24,20... | collective-permute-start | bytes 798728 | tf_op jit(solution)/shard_map/ppermute | solution.py:456
  13.0 13.1 %collective-permute-start.5 = (f32[65,8,128]{2,1,0:T(8,128)S(1)}, f32[65,8,128]{2,1,0:T(8,128)S(1)}, u32[]{:S(2)}, u32[]{:S(2)}) collective-permute-start(f32[65,8,128]{2,1,0:T(8,128)S(1)} %get-tuple-element.33), channel_id=1, source_target_pairs={{0,4},{12,8},{1,5},{13,9},{2,6},{14,10},{3,7},{15,11},{16,20},{28,... | collective-permute-start | bytes 798728 | tf_op jit(solution)/shard_map/ppermute | solution.py:461
  21.2 8.7 %collective-permute-start.4 = (f32[65,8,128]{2,1,0:T(8,128)S(1)}, f32[65,8,128]{2,1,0:T(8,128)S(1)}, u32[]{:S(2)}, u32[]{:S(2)}) collective-permute-start(f32[65,8,128]{2,1,0:T(8,128)S(1)} %get-tuple-element.34), channel_id=1, source_target_pairs={{0,8},{12,4},{1,9},{13,5},{2,10},{14,6},{3,11},{15,7},{16,24},{28,... | collective-permute-start | bytes 798728 | tf_op jit(solution)/shard_map/ppermute | solution.py:460
  22.6 14.8 %collective-permute-start.6 = (f32[65,8,128]{2,1,0:T(8,128)S(1)}, f32[65,8,128]{2,1,0:T(8,128)S(1)}, u32[]{:S(2)}, u32[]{:S(2)}) collective-permute-start(f32[65,8,128]{2,1,0:T(8,128)S(1)} %add.100), channel_id=1, source_target_pairs={{4,12},{8,0},{5,13},{9,1},{6,14},{10,2},{7,15},{11,3},{20,28},{24,... | collective-permute-start | bytes 798728 | tf_op jit(solution)/shard_map/ppermute | solution.py:464
  23.9 0.7 copy-start.2
  37.6 6.7 %collective-permute-start.8 = (f32[40,8,128]{2,1,0:T(8,128)S(1)}, f32[40,8,128]{2,1,0:T(8,128)S(1)}, u32[]{:S(2)}, u32[]{:S(2)}) collective-permute-start(f32[40,8,128]{2,1,0:T(8,128)S(1)} %slice.9), channel_id=1, source_target_pairs={{4,0},{8,4},{12,8},{13,12},{9,13},{5,9},{1,5},{2,1},{6,2},{10,6},{... | collective-permute-start | bytes 491528 | tf_op jit(solution)/shard_map/ppermute | solution.py:474
  39.1 5.2 %collective-permute-start.7 = (f32[32,8,128]{2,1,0:T(8,128)S(1)}, f32[32,8,128]{2,1,0:T(8,128)S(1)}, u32[]{:S(2)}, u32[]{:S(2)}) collective-permute-start(f32[32,8,128]{2,1,0:T(8,128)S(1)} %slice.8), channel_id=1, source_target_pairs={{0,4},{4,8},{8,12},{12,13},{13,9},{9,5},{5,1},{1,2},{2,6},{6,10},{... | collective-permute-start | bytes 393224 | tf_op jit(solution)/shard_map/ppermute | solution.py:473
  49.8 4.4 %collective-permute-start.10 = (f32[4,4,8,128]{3,2,1,0:T(8,128)S(1)}, f32[4,4,8,128]{3,2,1,0:T(8,128)S(1)}, u32[]{:S(2)}, u32[]{:S(2)}) collective-permute-start(f32[4,4,8,128]{3,2,1,0:T(8,128)S(1)} %get-tuple-element.37), channel_id=1, source_target_pairs={{0,2},{1,3},{2,0},{3,1},{4,6},{5,7},{6,4},{7,5},{8,10},{9,11},{10,... | collective-permute-start | bytes 196616 | tf_op jit(solution)/shard_map/ppermute | solution.py:493
  51.0 4.4 %collective-permute-start.11 = (f32[4,4,8,128]{3,2,1,0:T(8,128)S(1)}, f32[4,4,8,128]{3,2,1,0:T(8,128)S(1)}, u32[]{:S(2)}, u32[]{:S(2)}) collective-permute-start(f32[4,4,8,128]{3,2,1,0:T(8,128)S(1)} %get-tuple-element.38), channel_id=1, source_target_pairs={{0,3},{1,2},{2,1},{3,0},{4,7},{5,6},{6,5},{7,4},{8,11},{9,10},{10,... | collective-permute-start | bytes 196616 | tf_op jit(solution)/shard_map/ppermute | solution.py:493
  51.0 4.4 %collective-permute-start.9 = (f32[4,4,8,128]{3,2,1,0:T(8,128)S(1)}, f32[4,4,8,128]{3,2,1,0:T(8,128)S(1)}, u32[]{:S(2)}, u32[]{:S(2)}) collective-permute-start(f32[4,4,8,128]{3,2,1,0:T(8,128)S(1)} %get-tuple-element.36), channel_id=1, source_target_pairs={{0,1},{1,0},{2,3},{3,2},{4,5},{5,4},{6,7},{7,6},{8,9},{9,8},{10,11... | collective-permute-start | bytes 196616 | tf_op jit(solution)/shard_map/ppermute | solution.py:493
  55.4 6.8 %collective-permute-start.12 = (f32[4,4,8,128]{3,2,1,0:T(8,128)S(1)}, f32[4,4,8,128]{3,2,1,0:T(8,128)S(1)}, u32[]{:S(2)}, u32[]{:S(2)}) collective-permute-start(f32[4,4,8,128]{3,2,1,0:T(8,128)S(1)} %get-tuple-element.40), channel_id=1, source_target_pairs={{0,4},{4,8},{8,12},{12,0},{1,5},{5,9},{9,13},{13,1},{2,6},{6,10},{... | collective-permute-start | bytes 196616 | tf_op jit(solution)/shard_map/ppermute | solution.py:493
  55.9 8.1 %collective-permute-start.13 = (f32[4,4,8,128]{3,2,1,0:T(8,128)S(1)}, f32[4,4,8,128]{3,2,1,0:T(8,128)S(1)}, u32[]{:S(2)}, u32[]{:S(2)}) collective-permute-start(f32[4,4,8,128]{3,2,1,0:T(8,128)S(1)} %get-tuple-element.41), channel_id=1, source_target_pairs={{0,8},{4,12},{8,0},{12,4},{1,9},{5,13},{9,1},{13,5},{2,10},{6,14},... | collective-permute-start | bytes 196616 | tf_op jit(solution)/shard_map/ppermute | solution.py:493
  56.6 7.4 %collective-permute-start.14 = (f32[4,4,8,128]{3,2,1,0:T(8,128)S(1)}, f32[4,4,8,128]{3,2,1,0:T(8,128)S(1)}, u32[]{:S(2)}, u32[]{:S(2)}) collective-permute-start(f32[4,4,8,128]{3,2,1,0:T(8,128)S(1)} %get-tuple-element.42), channel_id=1, source_target_pairs={{0,12},{4,0},{8,4},{12,8},{1,13},{5,1},{9,5},{13,9},{2,14},{6,2},{... | collective-permute-start | bytes 196616 | tf_op jit(solution)/shard_map/ppermute | solution.py:493
  64.5 6.8 %collective-permute-start.15 = (f32[4,32,128]{2,1,0:T(8,128)S(1)}, f32[4,32,128]{2,1,0:T(8,128)S(1)}, u32[]{:S(2)}, u32[]{:S(2)}) collective-permute-start(f32[4,32,128]{2,1,0:T(8,128)S(1)} %get-tuple-element.44), channel_id=1, source_target_pairs={{0,4},{4,8},{8,12},{12,0},{1,5},{5,9},{9,13},{13,1},{2,6},{6,10},{... | collective-permute-start | bytes 196616 | tf_op jit(solution)/shard_map/ppermute | solution.py:493
  65.8 6.7 %collective-permute-start.16 = (f32[4,32,128]{2,1,0:T(8,128)S(1)}, f32[4,32,128]{2,1,0:T(8,128)S(1)}, u32[]{:S(2)}, u32[]{:S(2)}) collective-permute-start(f32[4,32,128]{2,1,0:T(8,128)S(1)} %get-tuple-element.45), channel_id=1, source_target_pairs={{0,8},{4,12},{8,0},{12,4},{1,9},{5,13},{9,1},{13,5},{2,10},{6,14},... | collective-permute-start | bytes 196616 | tf_op jit(solution)/shard_map/ppermute | solution.py:493
  67.0 5.5 %collective-permute-start.17 = (f32[4,32,128]{2,1,0:T(8,128)S(1)}, f32[4,32,128]{2,1,0:T(8,128)S(1)}, u32[]{:S(2)}, u32[]{:S(2)}) collective-permute-start(f32[4,32,128]{2,1,0:T(8,128)S(1)} %get-tuple-element.46), channel_id=1, source_target_pairs={{0,12},{4,0},{8,4},{12,8},{1,13},{5,1},{9,5},{13,9},{2,14},{6,2},{... | collective-permute-start | bytes 196616 | tf_op jit(solution)/shard_map/ppermute | solution.py:493

commit v11 on v9

--- a/solution.py
+++ b/solution.py
@@ -373,22 +373,32 @@
 
 
 def place_kernel(groups, *refs):
-    received, out = refs[:-1], refs[-1]
+    received, out, held, sems = refs[:-3], refs[-3], refs[-2], refs[-1]
     me = lax.axis_index("grid")
     parts, count = received[0].shape[0], received[0].shape[1]
-    for d, ref in enumerate(received):
-        n3 = lax.rem(me + groups - d, groups)
-        for n in range(parts):
-            out[pl.ds(n * N3 + n3, count, stride=parts * N3), :] = ref[n]
-
-
-def kernel(body, out_shape, in_specs, scratch=(), limit=4, flops=0):
+    chunks, stride = sems.shape[0], parts * N3
+    step = count // chunks
+    copies = []
+    for c in range(chunks):
+        for d, ref in enumerate(received):
+            n3 = lax.rem(me + groups - d, groups)
+            for n in range(parts):
+                at = pl.ds(c * step * stride + n * N3 + n3, step, stride=stride)
+                held[at, :] = ref[n, c * step : (c + 1) * step, :]
+        span = pl.ds(c * step * stride, step * stride)
+        copies.append(pltpu.make_async_copy(held.at[span], out.at[span], sems.at[c]))
+        copies[-1].start()
+    for copy in copies:
+        copy.wait()
+
+
+def kernel(body, out_shape, in_specs, scratch=(), limit=4, flops=0, space=VMEM):
     single = not isinstance(out_shape, (list, tuple))
     return pl.pallas_call(
         body,
         out_shape=out_shape,
         in_specs=in_specs,
-        out_specs=VMEM if single else [VMEM] * len(out_shape),
+        out_specs=space if single else [space] * len(out_shape),
         scratch_shapes=list(scratch),
         compiler_params=pltpu.CompilerParams(vmem_limit_bytes=limit << 20),
         cost_estimate=pl.CostEstimate(flops=flops, bytes_accessed=1 << 20, transcendentals=flops // 30),
@@ -526,7 +536,11 @@
     )(matrix, *by_grid)
     received = [hier[0]] + [exchanged(hier[d], "grid", ahead, d) for d in range(1, grids)]
     out = kernel(
-        functools.partial(place_kernel, grids), floats(group * half * N3, N4), [VMEM] * grids
+        functools.partial(place_kernel, grids),
+        floats(group * half * N3, N4),
+        [VMEM] * grids,
+        [pltpu.VMEM((group * half * N3, N4), jnp.float32), pltpu.SemaphoreType.DMA((4,))],
+        space=HBM,
     )(*received)
     return out.reshape(group, Q // slabs, N4)
 

time: 76.4 us -> 76.3 us (level)
  no operation moved by 1% of the time
where the time goes in v11:
time: 76.3 us; the launch traced here: 76.1 us
  starting transfers between devices  31.7 us (42%)
  waiting for transfers between devices  29.1 us (38%)
  Pallas kernels  14.7 us (19%)
    ppermute x12, starting transfers between devices, exchanged(): return lax.ppermute(value, axis, pairs)  15.9 us
    ppermute x12, waiting for transfers between devices, exchanged(): return lax.ppermute(value, axis, pairs)  9.11 us
    ppermute x1, waiting for transfers between devices, local_fast(): passed = lax.ppermute(joined, 'grid', [(1, 3), (2, 0)])  7.53 us
    ppermute x1, starting transfers between devices, local_fast(): inwards = lax.ppermute(near, 'grid', [(0, 1), (3, 2)])  6.31 us
    pallas_call x1, Pallas kernels, local_fast(): kernel(functools.partial(second_kernel, block, grids), [floats(N3, half,...  5.35 us
    ppermute x1, waiting for transfers between devices, local_fast(): lax.ppermute(own[(block - LOW) * TILES:block * TILES], both, forward)  4.1 us
    ppermute x1, waiting for transfers between devices, local_fast(): skipped = lax.ppermute(middle, 'grid', [(0, 2), (3, 1)])  3.79 us
    pallas_call x2, Pallas kernels, outer_block(): kernel(functools.partial(outer_kernel, later), piece, [SMEM] + [VMEM] * 4...  3.75 us
  transfers between devices with their start and end apart: 21, of which 12 were waited for; matrix products, arithmetic and copies ran while one was open for 0% of the time, Pallas kernels for 7%

profile of v11, /device:TPU:0, one launch (start us, length us, event | category | flops | bytes accessed | tf_op | source)
XLA Modules:
  0.0 76.1 jit_solution(9794919998814076966)
XLA Ops:
  0.0 0.0 copy-start
  0.0 1.1 %shard_map.38 = (f32[4,64,128]{2,1,0:T(8,128)S(1)}, f32[5,64,128]{2,1,0:T(8,128)S(1)}) custom-call(f32[32,64,128]{2,1,0:T(8,128)} %bitcast.2), custom_call_target="tpu_custom_call" | custom-call | bytes 1048576 | tf_op jit(solution)/shard_map/pallas_call | solution.py:429
  1.1 0.0 copy-start.1
  1.1 2.5 %collective-permute-start.1 = (f32[5,64,128]{2,1,0:T(8,128)S(1)}, f32[5,64,128]{2,1,0:T(8,128)S(1)}, u32[]{:S(2)}, u32[]{:S(2)}) collective-permute-start(f32[5,64,128]{2,1,0:T(8,128)S(1)} %get-tuple-element.32), channel_id=1, source_target_pairs={{1,0},{2,1},{3,2},{0,3},{5,4},{6,5},{7,6},{4,7},{9,8},{10,9},{11,1... | collective-permute-start | bytes 491528 | tf_op jit(solution)/shard_map/ppermute | solution.py:436
  3.6 0.0 collective-permute-start
  3.6 0.0 copy-done
  3.6 0.0 copy-done.1
  3.6 2.8 %shard_map.37 = (f32[65,8,128]{2,1,0:T(8,128)S(1)}, f32[65,8,128]{2,1,0:T(8,128)S(1)}, bf16[128,256]{1,0:T(8,128)(2,1)S(1)}) custom-call(s32[1,5]{1,0:T(1,128)S(1)} %copy-done.1, f32[32,64,128]{2,1,0:T(8,128)S(1)} %bitcast.3), custom_call_target="tpu_custom_call" | custom-call | flops 26214400 | bytes 1048576 | tf_op jit(solution)/shard_map/pallas_call | solution.py:445
  6.4 2.4 %collective-permute-done.before = f32[4,64,128]{2,1,0:T(8,128)S(1)} collective-permute-done((f32[4,64,128]{2,1,0:T(8,128)S(1)}, f32[4,64,128]{2,1,0:T(8,128)S(1)}, u32[]{:S(2)}, u32[]{:S(2)}) %collective-permute-start) | collective-permute-done | bytes 131104 | tf_op jit(solution)/shard_map/ppermute | solution.py:435
  8.8 0.0 collective-permute-done.1.after
  8.8 1.9 %shard_map.39 = f32[65,8,128]{2,1,0:T(8,128)S(1)} custom-call(s32[1,5]{1,0:T(1,128)S(1)} %copy-done.1, bf16[128,256]{1,0:T(8,128)(2,1)S(1)} %get-tuple-element.30.left, f32[4,64,128]{2,1,0:T(8,128)S(1)} %collective-permute-done.before, f32[32,64,128]{2,1,0:T(8,128)S(1)} %bitcast.4, f32[5,64,128]{2,1,0:T(8,128)S(1)} %collective-permute-done.1.after), custom_call_target="tpu_custom_call" | custom-call | flops 15728640 | bytes 1048576 | tf_op jit(solution)/shard_map/pallas_call | solution.py:457
  10.7 1.6 %collective-permute-start.2 = (f32[65,8,128]{2,1,0:T(8,128)S(1)}, f32[65,8,128]{2,1,0:T(8,128)S(1)}, u32[]{:S(2)}, u32[]{:S(2)}) collective-permute-start(f32[65,8,128]{2,1,0:T(8,128)S(1)} %shard_map.39), channel_id=1, source_target_pairs={{0,4},{4,0},{8,12},{12,8},{1,5},{5,1},{9,13},{13,9},{2,6},{6,2},{1... | collective-permute-start | bytes 798728 | tf_op jit(solution)/shard_map/ppermute | solution.py:469
  12.4 0.7 collective-permute-start.3
  13.0 6.3 %collective-permute-start.5 = (f32[65,8,128]{2,1,0:T(8,128)S(1)}, f32[65,8,128]{2,1,0:T(8,128)S(1)}, u32[]{:S(2)}, u32[]{:S(2)}) collective-permute-start(f32[65,8,128]{2,1,0:T(8,128)S(1)} %get-tuple-element.37), channel_id=1, source_target_pairs={{0,4},{12,8},{1,5},{13,9},{2,6},{14,10},{3,7},{15,11},{16,20},{28,... | collective-permute-start | bytes 798728 | tf_op jit(solution)/shard_map/ppermute | solution.py:472
  19.3 1.9 %shard_map.40 = f32[65,8,128]{2,1,0:T(8,128)S(1)} custom-call(s32[1,5]{1,0:T(1,128)S(1)} %copy-done.1, bf16[128,256]{1,0:T(8,128)(2,1)S(1)} %get-tuple-element.30.left, f32[4,64,128]{2,1,0:T(8,128)S(1)} %collective-permute-done.before, f32[32,64,128]{2,1,0:T(8,128)S(1)} %bitcast.5, f32[5,64,128]{2,1,0:T(8,128)S(1)} %collective-permute-done.1.after), custom_call_target="tpu_custom_call" | custom-call | flops 15728640 | bytes 1048576 | tf_op jit(solution)/shard_map/pallas_call | solution.py:457
  21.2 1.3 %collective-permute-start.4 = (f32[65,8,128]{2,1,0:T(8,128)S(1)}, f32[65,8,128]{2,1,0:T(8,128)S(1)}, u32[]{:S(2)}, u32[]{:S(2)}) collective-permute-start(f32[65,8,128]{2,1,0:T(8,128)S(1)} %get-tuple-element.38), channel_id=1, source_target_pairs={{0,8},{12,4},{1,9},{13,5},{2,10},{14,6},{3,11},{15,7},{16,24},{28,... | collective-permute-start | bytes 798728 | tf_op jit(solution)/shard_map/ppermute | solution.py:471
  22.5 0.0 collective-permute-done.2
  22.6 1.3 %collective-permute-start.6 = (f32[65,8,128]{2,1,0:T(8,128)S(1)}, f32[65,8,128]{2,1,0:T(8,128)S(1)}, u32[]{:S(2)}, u32[]{:S(2)}) collective-permute-start(f32[65,8,128]{2,1,0:T(8,128)S(1)} %add.100), channel_id=1, source_target_pairs={{4,12},{8,0},{5,13},{9,1},{6,14},{10,2},{7,15},{11,3},{20,28},{24,... | collective-permute-start | bytes 798728 | tf_op jit(solution)/shard_map/ppermute | solution.py:475
  23.9 0.0 collective-permute-done.3
  23.9 2.2 %collective-permute-done.5 = f32[65,8,128]{2,1,0:T(8,128)S(1)} collective-permute-done((f32[65,8,128]{2,1,0:T(8,128)S(1)}, f32[65,8,128]{2,1,0:T(8,128)S(1)}, u32[]{:S(2)}, u32[]{:S(2)}) %collective-permute-start.5) | collective-permute-done | bytes 266272 | tf_op jit(solution)/shard_map/ppermute | solution.py:472
  26.1 3.8 %collective-permute-done.4 = f32[65,8,128]{2,1,0:T(8,128)S(1)} collective-permute-done((f32[65,8,128]{2,1,0:T(8,128)S(1)}, f32[65,8,128]{2,1,0:T(8,128)S(1)}, u32[]{:S(2)}, u32[]{:S(2)}) %collective-permute-start.4) | collective-permute-done | bytes 266272 | tf_op jit(solution)/shard_map/ppermute | solution.py:471
  29.9 7.5 %collective-permute-done.6 = f32[65,8,128]{2,1,0:T(8,128)S(1)} collective-permute-done((f32[65,8,128]{2,1,0:T(8,128)S(1)}, f32[65,8,128]{2,1,0:T(8,128)S(1)}, u32[]{:S(2)}, u32[]{:S(2)}) %collective-permute-start.6) | collective-permute-done | bytes 266272 | tf_op jit(solution)/shard_map/ppermute | solution.py:475
  37.4 0.1 add_add_fusion.own
  37.6 0.0 copy-start.2
  37.6 1.5 %collective-permute-start.8 = (f32[40,8,128]{2,1,0:T(8,128)S(1)}, f32[40,8,128]{2,1,0:T(8,128)S(1)}, u32[]{:S(2)}, u32[]{:S(2)}) collective-permute-start(f32[40,8,128]{2,1,0:T(8,128)S(1)} %slice.9), channel_id=1, source_target_pairs={{4,0},{8,4},{12,8},{13,12},{9,13},{5,9},{1,5},{2,1},{6,2},{10,6},{... | collective-permute-start | bytes 491528 | tf_op jit(solution)/shard_map/ppermute | solution.py:485
  39.1 0.6 collective-permute-start.7
  39.7 0.0 copy-done.2
  39.7 0.5 shard_map.41.left
  40.2 4.1 %collective-permute-done.7.before = f32[32,8,128]{2,1,0:T(8,128)S(1)} collective-permute-done((f32[32,8,128]{2,1,0:T(8,128)S(1)}, f32[32,8,128]{2,1,0:T(8,128)S(1)}, u32[]{:S(2)}, u32[]{:S(2)}) %collective-permute-start.7) | collective-permute-done | bytes 131104 | tf_op jit(solution)/shard_map/ppermute | solution.py:484
  44.3 0.0 collective-permute-done.8.after
  44.3 5.4 %shard_map.42 = (f32[4,4,8,128]{3,2,1,0:T(8,128)S(1)}, f32[4,4,8,128]{3,2,1,0:T(8,128)S(1)}, f32[4,4,8,128]{3,2,1,0:T(8,128)S(1)}, f32[4,4,8,128]{3,2,1,0:T(8,128)S(1)}) custom-call(bf16[4,128,256]{2,1,0:T(8,128)(2,1)S(1)} %shard_map.41.left, f32[32,8,128]{2,1,0:T(8,128)S(1)} %collective-permute-done.7.before, f32[65,8,128]{2,1,0:T(8,128)S(1)} %add_add_fusion.own, ...), custom_call_target="tpu_custom_call" | custom-call | flops 131072000 | bytes 1048576 | tf_op jit(solution)/shard_map/pallas_call | solution.py:491
  49.7 1.2 %collective-permute-start.13 = (f32[4,4,8,128]{3,2,1,0:T(8,128)S(1)}, f32[4,4,8,128]{3,2,1,0:T(8,128)S(1)}, u32[]{:S(2)}, u32[]{:S(2)}) collective-permute-start(f32[4,4,8,128]{3,2,1,0:T(8,128)S(1)} %get-tuple-element.45), channel_id=1, source_target_pairs={{0,2},{1,3},{2,0},{3,1},{4,6},{5,7},{6,4},{7,5},{8,10},{9,11},{10,... | collective-permute-start | bytes 196616 | tf_op jit(solution)/shard_map/ppermute | solution.py:502
  50.9 0.0 collective-permute-start.14
  50.9 1.0 %collective-permute-start.9 = (f32[4,4,8,128]{3,2,1,0:T(8,128)S(1)}, f32[4,4,8,128]{3,2,1,0:T(8,128)S(1)}, u32[]{:S(2)}, u32[]{:S(2)}) collective-permute-start(f32[4,4,8,128]{3,2,1,0:T(8,128)S(1)} %get-tuple-element.40), channel_id=1, source_target_pairs={{0,1},{1,0},{2,3},{3,2},{4,5},{5,4},{6,7},{7,6},{8,9},{9,8},{10,11... | collective-permute-start | bytes 196616 | tf_op jit(solution)/shard_map/ppermute | solution.py:502
  51.9 2.2 %collective-permute-done.13.refs_0_ = f32[4,4,8,128]{3,2,1,0:T(8,128)S(1)} collective-permute-done((f32[4,4,8,128]{3,2,1,0:T(8,128)S(1)}, f32[4,4,8,128]{3,2,1,0:T(8,128)S(1)}, u32[]{:S(2)}, u32[]{:S(2)}) %collective-permute-start.13) | collective-permute-done | bytes 65568 | tf_op jit(solution)/shard_map/ppermute | solution.py:502
  54.1 1.2 %collective-permute-done.14.refs_1_ = f32[4,4,8,128]{3,2,1,0:T(8,128)S(1)} collective-permute-done((f32[4,4,8,128]{3,2,1,0:T(8,128)S(1)}, f32[4,4,8,128]{3,2,1,0:T(8,128)S(1)}, u32[]{:S(2)}, u32[]{:S(2)}) %collective-permute-start.14) | collective-permute-done | bytes 65568 | tf_op jit(solution)/shard_map/ppermute | solution.py:502
  55.3 0.5 collective-permute-start.15
  55.8 0.8 collective-permute-start.16
  56.6 2.9 %collective-permute-start.17 = (f32[2,4,8,128]{3,2,1,0:T(8,128)S(1)}, f32[2,4,8,128]{3,2,1,0:T(8,128)S(1)}, u32[]{:S(2)}, u32[]{:S(2)}) collective-permute-start(f32[2,4,8,128]{3,2,1,0:T(8,128)S(1)} %get-tuple-element.50), channel_id=1, source_target_pairs={{0,12},{4,0},{8,4},{12,8},{1,13},{5,1},{9,5},{13,9},{2,14},{6,2},{... | collective-permute-start | bytes 98312 | tf_op jit(solution)/shard_map/ppermute | solution.py:502
  59.5 0.0 collective-permute-done.9.refs_1_
  59.5 0.4 collective-permute-start.10
  59.9 1.5 %collective-permute-start.11 = (f32[2,4,8,128]{3,2,1,0:T(8,128)S(1)}, f32[2,4,8,128]{3,2,1,0:T(8,128)S(1)}, u32[]{:S(2)}, u32[]{:S(2)}) collective-permute-start(f32[2,4,8,128]{3,2,1,0:T(8,128)S(1)} %get-tuple-element.43), channel_id=1, source_target_pairs={{0,8},{4,12},{8,0},{12,4},{1,9},{5,13},{9,1},{13,5},{2,10},{6,14},... | collective-permute-start | bytes 98312 | tf_op jit(solution)/shard_map/ppermute | solution.py:502
  61.4 0.0 collective-permute-done.15.refs_5_
  61.4 2.8 %collective-permute-start.12 = (f32[2,4,8,128]{3,2,1,0:T(8,128)S(1)}, f32[2,4,8,128]{3,2,1,0:T(8,128)S(1)}, u32[]{:S(2)}, u32[]{:S(2)}) collective-permute-start(f32[2,4,8,128]{3,2,1,0:T(8,128)S(1)} %get-tuple-element.44), channel_id=1, source_target_pairs={{0,12},{4,0},{8,4},{12,8},{1,13},{5,1},{9,5},{13,9},{2,14},{6,2},{... | collective-permute-start | bytes 98312 | tf_op jit(solution)/shard_map/ppermute | solution.py:502
  64.3 0.1 add_convert_fusion.matrix
  64.4 0.0 collective-permute-done.16.refs_6_
  64.4 0.0 collective-permute-done.17.refs_7_
  64.5 0.9 %collective-permute-done.10.refs_1_ = f32[2,4,8,128]{3,2,1,0:T(8,128)S(1)} collective-permute-done((f32[2,4,8,128]{3,2,1,0:T(8,128)S(1)}, f32[2,4,8,128]{3,2,1,0:T(8,128)S(1)}, u32[]{:S(2)}, u32[]{:S(2)}) %collective-permute-start.10) | collective-permute-done | bytes 32800 | tf_op jit(solution)/shard_map/ppermute | solution.py:502
  65.4 0.0 collective-permute-done.11.refs_2_
  65.4 0.5 collective-permute-done.12.refs_3_
  65.9 0.4 shard_map.45
  66.3 2.0 %collective-permute-start.18 = (f32[4,32,128]{2,1,0:T(8,128)S(1)}, f32[4,32,128]{2,1,0:T(8,128)S(1)}, u32[]{:S(2)}, u32[]{:S(2)}) collective-permute-start(f32[4,32,128]{2,1,0:T(8,128)S(1)} %get-tuple-element.52), channel_id=1, source_target_pairs={{0,4},{4,8},{8,12},{12,0},{1,5},{5,9},{9,13},{13,1},{2,6},{6,10},{... | collective-permute-start | bytes 196616 | tf_op jit(solution)/shard_map/ppermute | solution.py:502
  68.2 2.8 %collective-permute-start.19 = (f32[4,32,128]{2,1,0:T(8,128)S(1)}, f32[4,32,128]{2,1,0:T(8,128)S(1)}, u32[]{:S(2)}, u32[]{:S(2)}) collective-permute-start(f32[4,32,128]{2,1,0:T(8,128)S(1)} %get-tuple-element.53), channel_id=1, source_target_pairs={{0,8},{4,12},{8,0},{12,4},{1,9},{5,13},{9,1},{13,5},{2,10},{6,14},... | collective-permute-start | bytes 196616 | tf_op jit(solution)/shard_map/ppermute | solution.py:502
  71.1 0.0 collective-permute-start.20
  71.1 1.7 %collective-permute-done.18.refs_1_ = f32[4,32,128]{2,1,0:T(8,128)S(1)} collective-permute-done((f32[4,32,128]{2,1,0:T(8,128)S(1)}, f32[4,32,128]{2,1,0:T(8,128)S(1)}, u32[]{:S(2)}, u32[]{:S(2)}) %collective-permute-start.18) | collective-permute-done | bytes 65568 | tf_op jit(solution)/shard_map/ppermute | solution.py:502
  72.7 1.4 %collective-permute-done.19.refs_2_ = f32[4,32,128]{2,1,0:T(8,128)S(1)} collective-permute-done((f32[4,32,128]{2,1,0:T(8,128)S(1)}, f32[4,32,128]{2,1,0:T(8,128)S(1)}, u32[]{:S(2)}, u32[]{:S(2)}) %collective-permute-start.19) | collective-permute-done | bytes 65568 | tf_op jit(solution)/shard_map/ppermute | solution.py:502
  74.1 1.2 %collective-permute-done.20.refs_3_ = f32[4,32,128]{2,1,0:T(8,128)S(1)} collective-permute-done((f32[4,32,128]{2,1,0:T(8,128)S(1)}, f32[4,32,128]{2,1,0:T(8,128)S(1)}, u32[]{:S(2)}, u32[]{:S(2)}) %collective-permute-start.20) | collective-permute-done | bytes 65568 | tf_op jit(solution)/shard_map/ppermute | solution.py:502
  75.3 0.8 shard_map.46
  (8 shorter events, 0.1 us)
Async XLA Ops:
  0.0 3.6 %copy-start = (f32[1,32,64,128]{3,2,1,0:T(8,128)S(1)}, f32[1,32,64,128]{3,2,1,0:T(8,128)}, u32[]{:S(2)}) copy-start(f32[1,32,64,128]{3,2,1,0:T(8,128)} %param.3) | copy-start | bytes 3145732
  1.1 2.5 %copy-start.1 = (s32[1,5]{1,0:T(1,128)S(1)}, s32[1,5]{1,0:T(1,128)}, u32[]{:S(2)}) copy-start(s32[1,5]{1,0:T(1,128)} %level.5) | copy-start | bytes 64
  1.1 7.7 %collective-permute-start.1 = (f32[5,64,128]{2,1,0:T(8,128)S(1)}, f32[5,64,128]{2,1,0:T(8,128)S(1)}, u32[]{:S(2)}, u32[]{:S(2)}) collective-permute-start(f32[5,64,128]{2,1,0:T(8,128)S(1)} %get-tuple-element.32), channel_id=1, source_target_pairs={{1,0},{2,1},{3,2},{0,3},{5,4},{6,5},{7,6},{4,7},{9,8},{10,9},{11,1... | collective-permute-start | bytes 491528 | tf_op jit(solution)/shard_map/ppermute | solution.py:436
  3.6 5.3 %collective-permute-start = (f32[4,64,128]{2,1,0:T(8,128)S(1)}, f32[4,64,128]{2,1,0:T(8,128)S(1)}, u32[]{:S(2)}, u32[]{:S(2)}) collective-permute-start(f32[4,64,128]{2,1,0:T(8,128)S(1)} %get-tuple-element.31), channel_id=1, source_target_pairs={{0,1},{1,2},{2,3},{3,0},{4,5},{5,6},{6,7},{7,4},{8,9},{9,10},{10,1... | collective-permute-start | bytes 393224 | tf_op jit(solution)/shard_map/ppermute | solution.py:435
  10.7 11.8 %collective-permute-start.2 = (f32[65,8,128]{2,1,0:T(8,128)S(1)}, f32[65,8,128]{2,1,0:T(8,128)S(1)}, u32[]{:S(2)}, u32[]{:S(2)}) collective-permute-start(f32[65,8,128]{2,1,0:T(8,128)S(1)} %shard_map.39), channel_id=1, source_target_pairs={{0,4},{4,0},{8,12},{12,8},{1,5},{5,1},{9,13},{13,9},{2,6},{6,2},{1... | collective-permute-start | bytes 798728 | tf_op jit(solution)/shard_map/ppermute | solution.py:469
  12.4 11.6 %collective-permute-start.3 = (f32[65,8,128]{2,1,0:T(8,128)S(1)}, f32[65,8,128]{2,1,0:T(8,128)S(1)}, u32[]{:S(2)}, u32[]{:S(2)}) collective-permute-start(f32[65,8,128]{2,1,0:T(8,128)S(1)} %get-tuple-element.38), channel_id=1, source_target_pairs={{4,8},{8,4},{5,9},{9,5},{6,10},{10,6},{7,11},{11,7},{20,24},{24,20... | collective-permute-start | bytes 798728 | tf_op jit(solution)/shard_map/ppermute | solution.py:467
  13.0 13.1 %collective-permute-start.5 = (f32[65,8,128]{2,1,0:T(8,128)S(1)}, f32[65,8,128]{2,1,0:T(8,128)S(1)}, u32[]{:S(2)}, u32[]{:S(2)}) collective-permute-start(f32[65,8,128]{2,1,0:T(8,128)S(1)} %get-tuple-element.37), channel_id=1, source_target_pairs={{0,4},{12,8},{1,5},{13,9},{2,6},{14,10},{3,7},{15,11},{16,20},{28,... | collective-permute-start | bytes 798728 | tf_op jit(solution)/shard_map/ppermute | solution.py:472
  21.2 8.7 %collective-permute-start.4 = (f32[65,8,128]{2,1,0:T(8,128)S(1)}, f32[65,8,128]{2,1,0:T(8,128)S(1)}, u32[]{:S(2)}, u32[]{:S(2)}) collective-permute-start(f32[65,8,128]{2,1,0:T(8,128)S(1)} %get-tuple-element.38), channel_id=1, source_target_pairs={{0,8},{12,4},{1,9},{13,5},{2,10},{14,6},{3,11},{15,7},{16,24},{28,... | collective-permute-start | bytes 798728 | tf_op jit(solution)/shard_map/ppermute | solution.py:471
  22.6 14.8 %collective-permute-start.6 = (f32[65,8,128]{2,1,0:T(8,128)S(1)}, f32[65,8,128]{2,1,0:T(8,128)S(1)}, u32[]{:S(2)}, u32[]{:S(2)}) collective-permute-start(f32[65,8,128]{2,1,0:T(8,128)S(1)} %add.100), channel_id=1, source_target_pairs={{4,12},{8,0},{5,13},{9,1},{6,14},{10,2},{7,15},{11,3},{20,28},{24,... | collective-permute-start | bytes 798728 | tf_op jit(solution)/shard_map/ppermute | solution.py:475
  37.6 2.1 %copy-start.2 = (s32[128]{0:T(128)S(1)}, s32[128]{0:T(128)}, u32[]{:S(2)}) copy-start(s32[128]{0:T(128)} %param.5) | copy-start | bytes 1540
  37.6 6.7 %collective-permute-start.8 = (f32[40,8,128]{2,1,0:T(8,128)S(1)}, f32[40,8,128]{2,1,0:T(8,128)S(1)}, u32[]{:S(2)}, u32[]{:S(2)}) collective-permute-start(f32[40,8,128]{2,1,0:T(8,128)S(1)} %slice.9), channel_id=1, source_target_pairs={{4,0},{8,4},{12,8},{13,12},{9,13},{5,9},{1,5},{2,1},{6,2},{10,6},{... | collective-permute-start | bytes 491528 | tf_op jit(solution)/shard_map/ppermute | solution.py:485
  39.1 5.2 %collective-permute-start.7 = (f32[32,8,128]{2,1,0:T(8,128)S(1)}, f32[32,8,128]{2,1,0:T(8,128)S(1)}, u32[]{:S(2)}, u32[]{:S(2)}) collective-permute-start(f32[32,8,128]{2,1,0:T(8,128)S(1)} %slice.8), channel_id=1, source_target_pairs={{0,4},{4,8},{8,12},{12,13},{13,9},{9,5},{5,1},{1,2},{2,6},{6,10},{... | collective-permute-start | bytes 393224 | tf_op jit(solution)/shard_map/ppermute | solution.py:484
  49.7 4.4 %collective-permute-start.13 = (f32[4,4,8,128]{3,2,1,0:T(8,128)S(1)}, f32[4,4,8,128]{3,2,1,0:T(8,128)S(1)}, u32[]{:S(2)}, u32[]{:S(2)}) collective-permute-start(f32[4,4,8,128]{3,2,1,0:T(8,128)S(1)} %get-tuple-element.45), channel_id=1, source_target_pairs={{0,2},{1,3},{2,0},{3,1},{4,6},{5,7},{6,4},{7,5},{8,10},{9,11},{10,... | collective-permute-start | bytes 196616 | tf_op jit(solution)/shard_map/ppermute | solution.py:502
  50.9 4.4 %collective-permute-start.14 = (f32[4,4,8,128]{3,2,1,0:T(8,128)S(1)}, f32[4,4,8,128]{3,2,1,0:T(8,128)S(1)}, u32[]{:S(2)}, u32[]{:S(2)}) collective-permute-start(f32[4,4,8,128]{3,2,1,0:T(8,128)S(1)} %get-tuple-element.46), channel_id=1, source_target_pairs={{0,3},{1,2},{2,1},{3,0},{4,7},{5,6},{6,5},{7,4},{8,11},{9,10},{10,... | collective-permute-start | bytes 196616 | tf_op jit(solution)/shard_map/ppermute | solution.py:502
  50.9 8.6 %collective-permute-start.9 = (f32[4,4,8,128]{3,2,1,0:T(8,128)S(1)}, f32[4,4,8,128]{3,2,1,0:T(8,128)S(1)}, u32[]{:S(2)}, u32[]{:S(2)}) collective-permute-start(f32[4,4,8,128]{3,2,1,0:T(8,128)S(1)} %get-tuple-element.40), channel_id=1, source_target_pairs={{0,1},{1,0},{2,3},{3,2},{4,5},{5,4},{6,7},{7,6},{8,9},{9,8},{10,11... | collective-permute-start | bytes 196616 | tf_op jit(solution)/shard_map/ppermute | solution.py:502
  55.3 6.1 %collective-permute-start.15 = (f32[2,4,8,128]{3,2,1,0:T(8,128)S(1)}, f32[2,4,8,128]{3,2,1,0:T(8,128)S(1)}, u32[]{:S(2)}, u32[]{:S(2)}) collective-permute-start(f32[2,4,8,128]{3,2,1,0:T(8,128)S(1)} %get-tuple-element.48), channel_id=1, source_target_pairs={{0,4},{4,8},{8,12},{12,0},{1,5},{5,9},{9,13},{13,1},{2,6},{6,10},{... | collective-permute-start | bytes 98312 | tf_op jit(solution)/shard_map/ppermute | solution.py:502
  55.8 8.6 %collective-permute-start.16 = (f32[2,4,8,128]{3,2,1,0:T(8,128)S(1)}, f32[2,4,8,128]{3,2,1,0:T(8,128)S(1)}, u32[]{:S(2)}, u32[]{:S(2)}) collective-permute-start(f32[2,4,8,128]{3,2,1,0:T(8,128)S(1)} %get-tuple-element.49), channel_id=1, source_target_pairs={{0,8},{4,12},{8,0},{12,4},{1,9},{5,13},{9,1},{13,5},{2,10},{6,14},... | collective-permute-start | bytes 98312 | tf_op jit(solution)/shard_map/ppermute | solution.py:502
  56.6 7.8 %collective-permute-start.17 = (f32[2,4,8,128]{3,2,1,0:T(8,128)S(1)}, f32[2,4,8,128]{3,2,1,0:T(8,128)S(1)}, u32[]{:S(2)}, u32[]{:S(2)}) collective-permute-start(f32[2,4,8,128]{3,2,1,0:T(8,128)S(1)} %get-tuple-element.50), channel_id=1, source_target_pairs={{0,12},{4,0},{8,4},{12,8},{1,13},{5,1},{9,5},{13,9},{2,14},{6,2},{... | collective-permute-start | bytes 98312 | tf_op jit(solution)/shard_map/ppermute | solution.py:502
  59.5 5.9 %collective-permute-start.10 = (f32[2,4,8,128]{3,2,1,0:T(8,128)S(1)}, f32[2,4,8,128]{3,2,1,0:T(8,128)S(1)}, u32[]{:S(2)}, u32[]{:S(2)}) collective-permute-start(f32[2,4,8,128]{3,2,1,0:T(8,128)S(1)} %get-tuple-element.42), channel_id=1, source_target_pairs={{0,4},{4,8},{8,12},{12,0},{1,5},{5,9},{9,13},{13,1},{2,6},{6,10},{... | collective-permute-start | bytes 98312 | tf_op jit(solution)/shard_map/ppermute | solution.py:502
  59.9 5.5 %collective-permute-start.11 = (f32[2,4,8,128]{3,2,1,0:T(8,128)S(1)}, f32[2,4,8,128]{3,2,1,0:T(8,128)S(1)}, u32[]{:S(2)}, u32[]{:S(2)}) collective-permute-start(f32[2,4,8,128]{3,2,1,0:T(8,128)S(1)} %get-tuple-element.43), channel_id=1, source_target_pairs={{0,8},{4,12},{8,0},{12,4},{1,9},{5,13},{9,1},{13,5},{2,10},{6,14},... | collective-permute-start | bytes 98312 | tf_op jit(solution)/shard_map/ppermute | solution.py:502
  61.4 4.4 %collective-permute-start.12 = (f32[2,4,8,128]{3,2,1,0:T(8,128)S(1)}, f32[2,4,8,128]{3,2,1,0:T(8,128)S(1)}, u32[]{:S(2)}, u32[]{:S(2)}) collective-permute-start(f32[2,4,8,128]{3,2,1,0:T(8,128)S(1)} %get-tuple-element.44), channel_id=1, source_target_pairs={{0,12},{4,0},{8,4},{12,8},{1,13},{5,1},{9,5},{13,9},{2,14},{6,2},{... | collective-permute-start | bytes 98312 | tf_op jit(solution)/shard_map/ppermute | solution.py:502
  66.3 6.5 %collective-permute-start.18 = (f32[4,32,128]{2,1,0:T(8,128)S(1)}, f32[4,32,128]{2,1,0:T(8,128)S(1)}, u32[]{:S(2)}, u32[]{:S(2)}) collective-permute-start(f32[4,32,128]{2,1,0:T(8,128)S(1)} %get-tuple-element.52), channel_id=1, source_target_pairs={{0,4},{4,8},{8,12},{12,0},{1,5},{5,9},{9,13},{13,1},{2,6},{6,10},{... | collective-permute-start | bytes 196616 | tf_op jit(solution)/shard_map/ppermute | solution.py:502
  68.2 5.9 %collective-permute-start.19 = (f32[4,32,128]{2,1,0:T(8,128)S(1)}, f32[4,32,128]{2,1,0:T(8,128)S(1)}, u32[]{:S(2)}, u32[]{:S(2)}) collective-permute-start(f32[4,32,128]{2,1,0:T(8,128)S(1)} %get-tuple-element.53), channel_id=1, source_target_pairs={{0,8},{4,12},{8,0},{12,4},{1,9},{5,13},{9,1},{13,5},{2,10},{6,14},... | collective-permute-start | bytes 196616 | tf_op jit(solution)/shard_map/ppermute | solution.py:502
  71.1 4.3 %collective-permute-start.20 = (f32[4,32,128]{2,1,0:T(8,128)S(1)}, f32[4,32,128]{2,1,0:T(8,128)S(1)}, u32[]{:S(2)}, u32[]{:S(2)}) collective-permute-start(f32[4,32,128]{2,1,0:T(8,128)S(1)} %get-tuple-element.54), channel_id=1, source_target_pairs={{0,12},{4,0},{8,4},{12,8},{1,13},{5,1},{9,5},{13,9},{2,14},{6,2},{... | collective-permute-start | bytes 196616 | tf_op jit(solution)/shard_map/ppermute | solution.py:502
